TPU v7x, 128 devices: a whole 4x4x4 slice. The times are simulated.
128 devices in a mesh: seq: 8 (over x, core), grp: 16 (over z, y).
Axes of the slice: x: 4, y: 4, z: 4, core: 2. Of those that a mesh axis runs over, the one named last changes fastest.
Arguments:
- tokens: bfloat16 [16, 1024, 1536], P('grp', 'seq'), may hold values from -15 to 15
- lengths: int32 [16, 3], P('grp'), may hold values from 1 to 512, 1024 in all within a row
- prompt_adapter: int32 [16, 3], P('grp'), may hold values from 0 to 15
- routes: int32 [16, 1024, 8], P('grp', 'seq'), may hold values from 0 to 39, all different within a row; in each aligned block of 128 rows (0 to 127, 128 to 255, ..., all dimensions but the last counted through in order) at most 40 rows name the same one
- routing_weight: float32 [16, 1024, 8], P('grp', 'seq'), may hold values from 0.1 to 1
- attention_gain: float32 [1536], replicated, may hold values from 0.5 to 1.5
- query_weight: bfloat16 [1536, 1536], replicated, may hold values from -25 to 25
- key_weight: bfloat16 [1536, 512], replicated, may hold values from -0.15625 to 0.15625
- value_weight: bfloat16 [1536, 512], replicated, may hold values from -0.15625 to 0.15625
- output_weight: bfloat16 [1536, 1536], replicated, may hold values from -0.15625 to 0.15625
- adapter_down_maps: bfloat16 [4, 16, 1536, 16], P(None, 'grp'), may hold values from -0.15625 to 0.15625
- adapter_up_query_output: bfloat16 [2, 16, 16, 1536], P(None, 'grp'), may hold values from -1.5 to 1.5
- adapter_up_key_value: bfloat16 [2, 16, 16, 512], P(None, 'grp'), may hold values from -1.5 to 1.5
- expert_gain: float32 [1536], replicated, may hold values from 0.5 to 1.5
- gate_weight: bfloat16 [80, 1536, 256], P('grp'), may hold values from -0.15625 to 0.15625
- up_weight: bfloat16 [80, 1536, 256], P('grp'), may hold values from -0.15625 to 0.15625
- down_weight: bfloat16 [80, 256, 1536], P('grp'), may hold values from -0.25 to 0.25
- closing_gain: float32 [1536], replicated, may hold values from 0.5 to 1.5
- vocab_projection: bfloat16 [1536, 49152], P(None, ('seq', 'grp')), may hold values from -10 to 10
Outputs:
- hidden_out: bfloat16 [16, 1024, 1536], P('grp', 'seq')
- log_probs: float32 [48, 49152], P(None, ('seq', 'grp'))
Inputs may be any that keep to these rules, and one draw needn't show every extreme that they name: The 3 lengths of a group sum to 1024; the longest is exactly 512. `routes`: A token names 8 different experts. Within the 128 tokens of one device no expert is named by more than 40 of them, and in every draw some expert is named by exactly 40 tokens of some device.
All inputs are finite; a program needn't handle non-finite values.
Results may differ from a plain program's by a relative error of at most 0.017.
The roundings to bfloat16 on the way count: a program that leaves them out, or rounds other values in their place, can miss the bound.
Values may be sent and summed in bfloat16 or wider, within the bound.
No kernel may reach another device: no remote copies, remote signals or barrier semaphores. Data moves between devices by JAX's collectives and lax.ppermute only.
A program may use at most 192 MiB of HBM per device.

v0:
```python
import jax
import jax.numpy as jnp
from jax import lax
from jax.sharding import PartitionSpec as P

HEADS = 24
KV_HEADS = 8
HEAD = 64
EXPERTS = 40
TOP = 8
CAP = 40


EPSILON = 1e-05
ROPE_BASE = 10000.0
MASKED = -1e30


def rms_scaled(features, scales):
    features = features.astype(jnp.float32)
    inverse = lax.rsqrt(jnp.mean(features * features, axis=-1, keepdims=True) + EPSILON)
    return (features * inverse * scales).astype(jnp.bfloat16)


def rotate(features, offsets):
    half_size = features.shape[-1] // 2
    frequency = ROPE_BASE ** (-jnp.arange(half_size, dtype=jnp.float32) / half_size)
    angles = offsets.astype(jnp.float32)[:, None, None] * frequency[None, None, :]
    cosine = jnp.cos(angles)
    sines = jnp.sin(angles)
    first_half = features[..., :half_size]
    second = features[..., half_size:]
    return jnp.concatenate(
        [first_half * cosine - second * sines, second * cosine + first_half * sines], axis=-1
    )


def doc_layout(prompt_lens, row_index):
    doc_ends = jnp.cumsum(prompt_lens)
    starts = doc_ends - prompt_lens
    document = jnp.sum((row_index[:, None] >= doc_ends[None, :]).astype(jnp.int32), axis=1)
    member = document[:, None] == jnp.arange(prompt_lens.shape[0], dtype=jnp.int32)[None, :]
    doc_start = jnp.sum(jnp.where(member, starts[None, :], 0), axis=1)
    return (document, row_index - doc_start, member)


def adapter_delta(normalized_rows, selected_experts, down_proj, up_weights):
    low_rank = jnp.einsum(
        "td,adr->tar", normalized_rows, down_proj, preferred_element_type=jnp.float32
    )
    low_rank = (low_rank * selected_experts[:, :, None]).astype(jnp.bfloat16)
    return jnp.einsum("tar,are->te", low_rank, up_weights, preferred_element_type=jnp.float32)


def body(
    tokens,
    lengths,
    prompt_adapter,
    routes,
    routing_weight,
    attention_gain,
    query_weight,
    key_weight,
    value_weight,
    output_weight,
    adapter_down_maps,
    adapter_up_query_output,
    adapter_up_key_value,
    expert_gain,
    gate_weight,
    up_weight,
    down_weight,
    closing_gain,
    vocab_projection,
):
    rows_in = tokens[0]
    tok_count = rows_in.shape[0]
    model_width = rows_in.shape[1]
    prompt_lens = lengths[0]
    owners = prompt_adapter[0]
    ratio = HEADS // KV_HEADS
    logit_scale = HEAD ** (-0.5)
    down_all, wide_all, narrow_all = (
        lax.all_gather(adapter_down_maps, "grp", axis=1, tiled=True),
        lax.all_gather(adapter_up_query_output, "grp", axis=1, tiled=True),
        lax.all_gather(adapter_up_key_value, "grp", axis=1, tiled=True),
    )
    row_index = lax.axis_index("seq") * tok_count + jnp.arange(tok_count, dtype=jnp.int32)
    document, offsets, member = doc_layout(prompt_lens, row_index)
    adapter = jnp.sum(jnp.where(member, owners[None, :], 0), axis=1)
    selected_experts = (
        adapter[:, None] == jnp.arange(down_all.shape[1], dtype=jnp.int32)[None, :]
    ).astype(jnp.float32)
    normalized_rows = rms_scaled(rows_in, attention_gain)
    query_matrix = jnp.dot(
        normalized_rows, query_weight, preferred_element_type=jnp.float32
    ) + adapter_delta(normalized_rows, selected_experts, down_all[0], wide_all[0])
    query_matrix = rotate(query_matrix.reshape(tok_count, HEADS, HEAD), offsets).astype(
        jnp.bfloat16
    )
    query_matrix = query_matrix.reshape(tok_count, KV_HEADS, ratio, HEAD)
    key_matrix = jnp.dot(
        normalized_rows, key_weight, preferred_element_type=jnp.float32
    ) + adapter_delta(normalized_rows, selected_experts, down_all[1], narrow_all[0])
    key_matrix = (
        rotate(key_matrix.reshape(tok_count, KV_HEADS, HEAD), offsets)
        .astype(jnp.bfloat16)
        .reshape(tok_count, KV_HEADS * HEAD)
    )
    value_matrix = (
        jnp.dot(normalized_rows, value_weight, preferred_element_type=jnp.float32)
        + adapter_delta(normalized_rows, selected_experts, down_all[2], narrow_all[1])
    ).astype(jnp.bfloat16)
    running_max = jnp.full((KV_HEADS, ratio, tok_count), MASKED, jnp.float32)
    key_part = lax.all_gather(key_matrix, "seq", axis=0, tiled=True)
    value_part = lax.all_gather(value_matrix, "seq", axis=0, tiled=True)
    key_count = key_part.shape[0]
    key_index = jnp.arange(key_count, dtype=jnp.int32)
    key_doc, _, _ = doc_layout(prompt_lens, key_index)
    allowed = (key_doc[None, :] == document[:, None]) & (key_index[None, :] <= row_index[:, None])
    attention_logits = (
        jnp.einsum(
            "jhlv,phv->hljp",
            query_matrix,
            key_part.reshape(key_count, KV_HEADS, HEAD),
            preferred_element_type=jnp.float32,
        )
        * logit_scale
    )
    attention_logits = jnp.where(allowed[None, None], attention_logits, MASKED)
    new_max = jnp.maximum(running_max, jnp.max(attention_logits, axis=-1))
    weights = jnp.where(allowed[None, None], jnp.exp(attention_logits - new_max[..., None]), 0.0)
    running_sum = jnp.sum(weights, axis=-1)
    weighted_values = jnp.einsum(
        "ukoe,euh->ukoh",
        weights.astype(jnp.bfloat16),
        value_part.reshape(key_count, KV_HEADS, HEAD),
        preferred_element_type=jnp.float32,
    )
    running_max, running_sum, weighted_values = (new_max, running_sum, weighted_values)
    attention_output = (
        (weighted_values / running_sum[..., None])
        .transpose(2, 0, 1, 3)
        .reshape(tok_count, HEADS * HEAD)
        .astype(jnp.bfloat16)
    )
    outside_mask = jnp.dot(
        attention_output, output_weight, preferred_element_type=jnp.float32
    ) + adapter_delta(attention_output, selected_experts, down_all[3], wide_all[1])
    mixed_rows = (rows_in.astype(jnp.float32) + outside_mask).astype(jnp.bfloat16)
    moe_in = rms_scaled(mixed_rows, expert_gain)
    expert_ids = routes[0].reshape(-1)
    flat_weights = routing_weight[0].reshape(-1)
    onehot = (expert_ids[:, None] == jnp.arange(EXPERTS, dtype=jnp.int32)[None, :]).astype(
        jnp.int32
    )
    slot_index = jnp.sum((jnp.cumsum(onehot, axis=0) - onehot) * onehot, axis=1)
    source_row = jnp.arange(expert_ids.shape[0], dtype=jnp.int32) // TOP
    slot_table = (
        jnp.full((EXPERTS * CAP,), tok_count, jnp.int32)
        .at[expert_ids * CAP + slot_index]
        .set(source_row)
        .reshape(EXPERTS, CAP)
    )
    padded = jnp.concatenate([moe_in, jnp.zeros((1, model_width), jnp.bfloat16)], axis=0)
    groups = lax.axis_size("grp")
    slices_here = gate_weight.shape[0]
    outgoing = padded[jnp.repeat(slot_table, 2, axis=0)].reshape(
        groups, slices_here, CAP, model_width
    )
    arrived = lax.all_to_all(outgoing, "grp", split_axis=0, concat_axis=0, tiled=True)
    gate_proj = jnp.einsum(
        "nlcd,ldf->nlcf", arrived, gate_weight, preferred_element_type=jnp.float32
    )
    up_proj = jnp.einsum("nlcd,ldf->nlcf", arrived, up_weight, preferred_element_type=jnp.float32)
    hidden = (jax.nn.silu(gate_proj) * up_proj).astype(jnp.bfloat16)
    halves = jnp.einsum(
        "nlcf,lfd->nlcd", hidden, down_weight, preferred_element_type=jnp.float32
    ).astype(jnp.bfloat16)
    returned = lax.all_to_all(halves, "grp", split_axis=0, concat_axis=0, tiled=True).reshape(
        -1, model_width
    )
    slice_ids = 2 * expert_ids[:, None] + jnp.arange(2, dtype=jnp.int32)[None, :]
    pick_index = slice_ids * CAP + slot_index[:, None]
    picked = returned[pick_index].astype(jnp.float32).reshape(tok_count, TOP * 2, model_width)
    holder = slice_ids // slices_here
    holder_hot = (holder[:, :, None] == jnp.arange(groups, dtype=jnp.int32)[None, None, :]).astype(
        jnp.float32
    )
    holder_hot = (holder_hot * flat_weights[:, None, None]).reshape(tok_count, TOP * 2, groups)
    partial_value = jnp.einsum(
        "tkg,tkd->tgd", holder_hot, picked, precision=lax.Precision.HIGHEST
    ).astype(jnp.bfloat16)
    combined = jnp.sum(partial_value.astype(jnp.float32), axis=1)
    hidden_out = (mixed_rows.astype(jnp.float32) + combined).astype(jnp.bfloat16)
    last_index = jnp.cumsum(prompt_lens) - 1
    selector = (last_index[:, None] == row_index[None, :]).astype(jnp.bfloat16)
    last_rows = jnp.dot(selector, hidden_out, preferred_element_type=jnp.float32)
    last_rows = rms_scaled(last_rows, closing_gain).astype(jnp.float32)
    own_group = (jnp.arange(groups, dtype=jnp.int32) == lax.axis_index("grp")).astype(jnp.float32)
    spread = own_group[:, None, None] * last_rows[None, :, :]
    gathered = lax.psum(spread, ("seq", "grp"))
    final_rows = gathered.reshape(-1, model_width).astype(jnp.bfloat16)
    logits = jnp.dot(final_rows, vocab_projection, preferred_element_type=jnp.float32)
    global_max = lax.pmax(jnp.max(logits, axis=1), ("seq", "grp"))
    global_sum = lax.psum(jnp.sum(jnp.exp(logits - global_max[:, None]), axis=1), ("seq", "grp"))
    log_probs = logits - (global_max + jnp.log(global_sum))[:, None]
    return (hidden_out[None], log_probs)


def solution(mesh):
    placed = (
        P("grp", "seq", None),
        P("grp", None),
        P("grp", None),
        P("grp", "seq", None),
        P("grp", "seq", None),
        P(),
        P(),
        P(),
        P(),
        P(),
        P(None, "grp", None, None),
        P(None, "grp", None, None),
        P(None, "grp", None, None),
        P(),
        P("grp", None, None),
        P("grp", None, None),
        P("grp", None, None),
        P(),
        P(None, ("seq", "grp")),
    )
    return jax.shard_map(
        body,
        mesh=mesh,
        in_specs=placed,
        out_specs=(P("grp", "seq", None), P(None, ("seq", "grp"))),
        check_vma=False,
    )
```

profile of v0, /device:TPU:1, one launch (start us, length us, event | category | flops | bytes accessed | tf_op | source)
XLA Modules:
  0.0 710.7 jit_solution(9158568903717004309)
XLA Ops:
  12.1 22.3 %all_gather.16 = bf16[2,16,16,512]{3,2,1,0:T(8,128)(2,1)S(1)} all-gather(bf16[2,1,16,512]{3,2,1,0:T(8,128)(2,1)} %param.31), channel_id=1, replica_groups=mesh['seq'=8,'grp'=16] {'grp'}, dimensions={1}, use_global_device_ids=true | all-gather | bytes 557056 | tf_op jit(solution)/shard_map/all_gather | solution.py:86
  34.4 11.3 %reduce-window.11 = s32[40,8,128]{2,1,0:T(8,128)S(1)} reduce-window(s32[40,8,128]{2,1,0:T(8,128)S(1)} %fusion.60, s32[]{:T(128)} %constant.32.clone.1), window={size=1x1x128 pad=0_0x0_0x127_0}, to_apply=%region_9.10 | reduce-window | flops 5201920 | bytes 327684 | tf_op jit(solution)/shard_map/reduce-window.1
  46.4 4.3 scatter_custom_fusion
  53.3 8.4 %all-gather.5.cloned.1.call-done = bf16[4,16,1536,16]{2,3,1,0:T(8,128)(2,1)} async-done(((bf16[4,1,1536,16]{2,3,1,0:T(8,128)(2,1)}), bf16[4,16,1536,16]{2,3,1,0:T(8,128)(2,1)}) %all-gather.5.cloned.1.call-update) | async-done | bytes 3145744 | tf_op jit(solution)/shard_map/all_gather | solution.py:84
  61.7 3.2 fusion.93
  68.8 1.6 fusion.86
  70.3 35.7 %all-gather.9.cloned.1.call-done = bf16[2,16,16,1536]{3,2,1,0:T(8,128)(2,1)} async-done(((bf16[2,1,16,1536]{3,2,1,0:T(8,128)(2,1)}), bf16[2,16,16,1536]{3,2,1,0:T(8,128)(2,1)}) %all-gather.9.cloned.1.call-update) | async-done | bytes 1572880 | tf_op jit(solution)/shard_map/all_gather | solution.py:85
  107.4 3.2 convolution_add_fusion.1
  110.9 1.6 fusion.84
  112.8 2.5 fusion.33
  115.3 16.3 %all-gather.7.cloned.1.call-done = bf16[1024,512]{0,1:T(8,128)(2,1)} async-done(((bf16[128,512]{0,1:T(8,128)(2,1)}), bf16[1024,512]{0,1:T(8,128)(2,1)}) %all-gather.7.cloned.1.call-update) | async-done | bytes 1048592 | tf_op jit(solution)/shard_map/all_gather | solution.py:115
  131.6 3.1 fusion
  134.8 4.5 copy-done.2
  139.4 3.0 fusion.2
  142.4 15.8 %all-gather.11.cloned.1.call-done = bf16[1024,512]{1,0:T(8,128)(2,1)} async-done(((bf16[128,512]{1,0:T(8,128)(2,1)}), bf16[1024,512]{1,0:T(8,128)(2,1)}) %all-gather.11.cloned.1.call-update) | async-done | bytes 1048592 | tf_op jit(solution)/shard_map/all_gather | solution.py:116
  158.2 2.3 copy.58
  160.5 8.1 %fusion.40 = bf16[128,8,3,64]{0,3,2,1:T(8,128)(2,1)S(1)} fusion(bf16[1024,8,64,1]{0,2,3,1:T(8,128)(2,1)} %bitcast.215, f32[8,1024,128,3]{2,1,3,0:T(8,128)} %copy-done.2, f32[8,3,128]{2,1,0:T(4,128)S(1)} %broadcast_maximum_fusion, pred[128,1024]{0,1:T(8,128)(4,1)S(1)} %fusion.51, f32[128,8,3]{0,2,1:T(4,128)S(1)} %bitcast.233), kind=kOutput, calls=%fused_computation.49 | convolution fusion | flops 418775040 | bytes 14180352 | tf_op jit(solution)/shard_map/ukoe,euh->ukoh/dot_general | solution.py:134
  169.2 3.3 multiply_reduce_fusion
  172.7 11.9 %gather_fusion = bf16[3200,1536]{1,0:T(8,128)(2,1)} fusion(bf16[129,1536]{1,0:T(8,128)(2,1)S(1)} %concatenate.20, s32[4096]{0:T(1024)S(1)} %pad_clamp_fusion), kind=kCustom, calls=%fused_computation | custom fusion | bytes 19673600 | tf_op jit(solution)/shard_map/gather | solution.py:168
  184.5 117.5 %all_to_all.10 = bf16[16,5,40,1536]{3,2,1,0:T(8,128)(2,1)S(1)} all-to-all(bf16[16,5,40,1536]{3,2,1,0:T(8,128)(2,1)} %bitcast.208), channel_id=1, replica_groups=mesh['seq'=8,'grp'=16] {'grp'}, dimensions={0} | all-to-all | bytes 19660800 | tf_op jit(solution)/shard_map/all_to_all | solution.py:171
  302.1 3.8 copy-done.3
  305.8 4.6 fusion.6
  310.5 13.4 %fusion.1 = bf16[16,5,40,1536]{3,2,0,1:T(8,128)(2,1)} fusion(bf16[5,256,1536]{2,1,0:T(8,128)(2,1)} %param.35, f32[5,16,40,256]{3,2,1,0:T(8,128)} %fusion.6, bf16[5,1536,256]{2,1,0:T(8,128)(2,1)} %param.34, bf16[16,5,40,1536]{3,2,1,0:T(8,128)(2,1)} %copy-done.3), kind=kOutput, calls=%fused_computation.8 | convolution fusion | flops 5042995200 | bytes 30801920 | tf_op jit(solution)/shard_map/nlcf,lfd->nlcd/dot_general | solution.py:177
  323.9 8.3 %copy.70 = bf16[16,5,40,1536]{3,2,1,0:T(8,128)(2,1)} copy(bf16[16,5,40,1536]{3,2,0,1:T(8,128)(2,1)} %fusion.1) | data formatting | bytes 19660800 | tf_op jit(solution)/shard_map/convert_element_type | solution.py:179
  332.2 4.9 all-to-all-start.1
  338.2 141.3 %all-to-all-done.1 = bf16[16,5,40,1536]{3,2,1,0:T(8,128)(2,1)} async-done(((bf16[16,5,40,1536]{3,2,1,0:T(8,128)(2,1)}), bf16[16,5,40,1536]{3,2,1,0:T(8,128)(2,1)}, u32[]{:S(2)}, u32[]{:S(2)}) %all-to-all-start.1) | async-done | bytes 9830432 | tf_op jit(solution)/shard_map/all_to_all | solution.py:180
  479.5 18.3 %gather_fusion.1 = bf16[2048,1536]{1,0:T(8,128)(2,1)} fusion(bf16[3200,1536]{1,0:T(8,128)(2,1)} %bitcast.65, s32[2048]{0:T(1024)S(1)} %broadcast_clamp_fusion), kind=kCustom, calls=%fused_computation.1 | custom fusion | bytes 12591104 | tf_op jit(solution)/shard_map/gather | solution.py:185
  497.9 9.2 %convert_reduce_fusion = f32[128,1536]{1,0:T(8,128)S(1)} fusion(bf16[128,16,1536]{2,1,0:T(8,128)(2,1)} %bitcast.209, f32[128,16]{1,0:T(8,128)S(1)} %copy.62, s32[128,16]{1,0:T(8,128)S(1)} %copy.61), kind=kOutput, calls=%fused_computation.4 | convolution fusion | flops 613285888 | bytes 7094272 | tf_op jit(solution)/shard_map/tkg,tkd->tgd/dot_general | solution.py:191
  507.7 66.8 %all-reduce.2 = bf16[16,3,1536]{2,1,0:T(4,128)(2,1)S(1)} all-reduce(f32[16,3,1536]{2,1,0:T(4,128)S(1)} %broadcast_multiply_fusion), channel_id=1, replica_groups=mesh['seq'=8,'grp'=16] {'seq','grp'}, use_global_device_ids=true, to_apply=%region_15.16 | all-reduce | flops 73728 | bytes 442368 | tf_op jit(solution)/shard_map/psum | solution.py:202
  574.7 1.7 fusion.94
  576.4 64.4 %pmax.7 = f32[48]{0:T(128)S(1)} all-reduce(f32[48]{0:T(128)S(1)} %get-tuple-element.22), channel_id=1, replica_groups=mesh['seq'=8,'grp'=16] {'seq','grp'}, use_global_device_ids=true, to_apply=%region_17.18 | all-reduce | flops 48 | bytes 384 | tf_op jit(solution)/shard_map/pmax | solution.py:205
  640.9 62.5 %psum.15 = f32[48]{0:T(128)S(1)} all-reduce(f32[48]{0:T(128)S(1)} %exponential_reduce_fusion), channel_id=1, replica_groups=mesh['seq'=8,'grp'=16] {'seq','grp'}, use_global_device_ids=true, to_apply=%region_19.20 | all-reduce | flops 48 | bytes 384 | tf_op jit(solution)/shard_map/psum | solution.py:206
  (102 shorter events, 17.3 us)
Async XLA Ops:
  7.2 58.4 %copy-start = (bf16[1536,512]{1,0:T(8,128)(2,1)S(1)}, bf16[1536,512]{1,0:T(8,128)(2,1)}, u32[]{:S(2)}) copy-start(bf16[1536,512]{1,0:T(8,128)(2,1)} %param.26) | copy-start | bytes 4718596
  7.2 57.7 %copy-start.4 = (bf16[1,128,1536]{2,1,0:T(8,128)(2,1)S(1)}, bf16[1,128,1536]{2,1,0:T(8,128)(2,1)}, u32[]{:S(2)}) copy-start(bf16[1,128,1536]{2,1,0:T(8,128)(2,1)} %param.19) | copy-start | bytes 1179652
  7.2 57.7 %copy-start.7 = (f32[1536]{0:T(1024)S(1)}, f32[1536]{0:T(1024)}, u32[]{:S(2)}) copy-start(f32[1536]{0:T(1024)} %param.24) | copy-start | bytes 18436
  7.2 54.5 %all-gather.5.cloned.1.call-start = ((), (), s32[]{:S(2)}) async-start(), calls=%async_computation.2 | async-start | bytes 3342336 | tf_op jit(solution)/shard_map/all_gather | solution.py:84
  7.9 98.1 %all-gather.9.cloned.1.call-start = ((), (), s32[]{:S(2)}) async-start(), calls=%async_computation.4 | async-start | bytes 1671168 | tf_op jit(solution)/shard_map/all_gather | solution.py:85
  8.7 122.9 %all-gather.7.cloned.1.call-start = ((), (), s32[]{:S(2)}) async-start(), calls=%async_computation.3 | async-start | bytes 1179648 | tf_op jit(solution)/shard_map/all_gather | solution.py:115
  68.5 89.7 %all-gather.11.cloned.1.call-start = ((), (), s32[]{:S(2)}) async-start(), calls=%async_computation.5 | async-start | bytes 1179648 | tf_op jit(solution)/shard_map/all_gather | solution.py:116
  134.8 4.6 copy-start.2
  160.5 8.4 %copy-start.5 = (bf16[2,16,16,1536]{3,2,1,0:T(8,128)(2,1)S(1)}, bf16[2,16,16,1536]{3,2,1,0:T(8,128)(2,1)}, u32[]{:S(2)}) copy-start(bf16[2,16,16,1536]{3,2,1,0:T(8,128)(2,1)} %all-gather.9.cloned.1.call-done) | copy-start | bytes 4718596
  168.5 4.0 copy-start.8
  184.5 121.3 %copy-start.11 = (bf16[5,1536,256]{2,1,0:T(8,128)(2,1)S(1)}, bf16[5,1536,256]{2,1,0:T(8,128)(2,1)}, u32[]{:S(2)}) copy-start(bf16[5,1536,256]{2,1,0:T(8,128)(2,1)} %param.33) | copy-start | bytes 11796484
  302.1 3.8 copy-start.3
  332.2 5.8 copy-start.10
  332.2 147.3 %all-to-all-start.1 = ((bf16[16,5,40,1536]{3,2,1,0:T(8,128)(2,1)}), bf16[16,5,40,1536]{3,2,1,0:T(8,128)(2,1)}, u32[]{:S(2)}, u32[]{:S(2)}) async-start(bf16[16,5,40,1536]{3,2,1,0:T(8,128)(2,1)} %copy.70), calls=%async_computation.1 | async-start | bytes 19660800 | tf_op jit(solution)/shard_map/all_to_all | solution.py:180
  497.9 206.3 %copy-start.1 = (bf16[1536,512]{1,0:T(8,128)(2,1)S(1)}, bf16[1536,512]{1,0:T(8,128)(2,1)}, u32[]{:S(2)}) copy-start(bf16[1536,512]{1,0:T(8,128)(2,1)} %param.26) | copy-start | bytes 4718596
  497.9 9.6 %copy-start.9 = (f32[1536]{0:T(1024)S(1)}, f32[1536]{0:T(1024)}, u32[]{:S(2)}) copy-start(f32[1536]{0:T(1024)} %param.36) | copy-start | bytes 18436
  507.1 197.1 %copy-start.6 = (bf16[128,1536]{1,0:T(8,128)(2,1)}, bf16[128,1536]{1,0:T(8,128)(2,1)S(1)}, u32[]{:S(2)}) copy-start(bf16[128,1536]{1,0:T(8,128)(2,1)S(1)} %add_convert_fusion) | copy-start | bytes 1179652
Sparse Core Ops, SparseCore 0:
  10.2 51.4 all-gather.4
  63.8 42.1 all-gather.8
  107.7 23.8 all-gather.6
  133.8 24.3 all-gather.10
where the time goes:
time: 712 us; the launch traced here: 711 us
  blocking collectives  334 us (47%)
  waiting for transfers between devices  219 us (31%)
  local copies, waits for them, and re-layouts  60.3 us (8%)
  matrix products  56.6 us (8%)
  other arithmetic  21.7 us (3%)
  between operations  14.3 us (2%)
    all_to_all x1, waiting for transfers between devices, body(): lax.all_to_all(halves, 'grp', split_axis=0, concat_axis=0, tiled=True)  141 us
    all_to_all x1, blocking collectives, body(): lax.all_to_all(outgoing, 'grp', split_axis=0, concat_axis=0, tiled=True)  118 us
    psum x1, blocking collectives, body(): gathered = lax.psum(spread, ('seq', 'grp'))  66.8 us
    pmax x1, blocking collectives, body(): global_max = lax.pmax(jnp.max(logits, axis=1), ('seq', 'grp'))  64.4 us
    psum x1, blocking collectives, body(): lax.psum(jnp.sum(jnp.exp(logits - global_max[:, None]), axis=1), ('seq',...  62.5 us
    all_gather x1, waiting for transfers between devices, body(): lax.all_gather(adapter_up_query_output, 'grp', axis=1, tiled=True)  35.7 us
    all_gather x1, blocking collectives, body(): lax.all_gather(adapter_up_key_value, 'grp', axis=1, tiled=True)  22.3 us
    gather x1, local copies, waits for them, and re-layouts, body(): returned[pick_index].astype(jnp.float32)  18.3 us
  transfers between devices with their start and end apart: 5, of which 5 were waited for; matrix products, arithmetic and copies ran while one was open for 7% of the time, Pallas kernels for 0%

commit v1 on v0

v1 whole, which is shorter than its diff:
```python
import jax
import jax.numpy as jnp
from jax import lax
from jax.experimental import pallas as pl
from jax.experimental.pallas import tpu as pltpu
from jax.sharding import PartitionSpec as P

HEADS = 24
KV_HEADS = 8
HEAD = 64
EXPERTS = 40
TOP = 8
SLOTS = 48
EPSILON = 1e-05
ROPE_BASE = 10000.0
MASKED = -1e30
SIDE = 4
BF = jnp.bfloat16
F32 = jnp.float32
WHOLE = ("seq", "grp")


def shift(rows, axis, step):
    if axis == "z":
        pairs = [(i, (i // SIDE + step) % SIDE * SIDE + i % SIDE) for i in range(16)]
    else:
        pairs = [(i, i // SIDE * SIDE + (i % SIDE + step) % SIDE) for i in range(16)]
    return lax.ppermute(rows, "grp", pairs)


def partner(rows):
    return lax.ppermute(rows, "seq", [(s, s ^ 1) for s in range(8)])


def gather_tokens(first, second):
    near = [shift(first, "y", 1), shift(second, "z", 1), shift(first, "y", -1),
            shift(second, "z", -1), shift(first, "y", 2), shift(second, "z", 2)]
    near = lax.optimization_barrier(near)
    plane_a = jnp.stack([first, near[0], near[2], near[4]])
    plane_b = jnp.stack([second, near[1], near[3], near[5]])
    far = [shift(plane_a, "z", 1), shift(plane_b, "y", 1), shift(plane_a, "z", -1),
           shift(plane_b, "y", -1)]
    far = lax.optimization_barrier(far)
    last = [shift(far[0][:2], "z", 1), shift(far[1][:2], "y", 1),
            shift(far[2][2:], "z", -1), shift(far[3][2:], "y", -1)]
    return ([plane_a, far[0], far[2], last[0], last[2]],
            [plane_b, far[1], far[3], last[1], last[3]])


def reduce_tokens(parts_a, parts_b):
    def wide(v):
        return v.astype(F32)

    far = [shift(parts_a[3][:2], "z", 1), shift(parts_b[3][:2], "y", 1),
           shift(parts_a[3][2:], "z", -1), shift(parts_b[3][2:], "y", -1)]
    far = lax.optimization_barrier(far)

    def relay(parts, down, up):
        plus = jnp.concatenate([(wide(parts[2][:2]) + wide(down)).astype(BF), parts[2][2:]])
        minus = jnp.concatenate([parts[1][:2], (wide(parts[1][2:]) + wide(up)).astype(BF)])
        return plus, minus

    plus_a, minus_a = relay(parts_a, far[0], far[2])
    plus_b, minus_b = relay(parts_b, far[1], far[3])
    near = [shift(plus_a, "z", 1), shift(plus_b, "y", 1), shift(minus_a, "z", -1),
            shift(minus_b, "y", -1)]
    near = lax.optimization_barrier(near)
    sum_a = wide(parts_a[0]) + wide(near[0]) + wide(near[2])
    sum_b = wide(parts_b[0]) + wide(near[1]) + wide(near[3])
    low_a, low_b = sum_a[1:].astype(BF), sum_b[1:].astype(BF)
    final = [shift(low_a[1], "y", 1), shift(low_b[1], "z", 1), shift(low_a[0], "y", -1),
             shift(low_b[0], "z", -1), shift(low_a[2], "y", 2), shift(low_b[2], "z", 2)]
    total_a = sum_a[0] + wide(final[0]) + wide(final[2]) + wide(final[4])
    total_b = sum_b[0] + wide(final[1]) + wide(final[3]) + wide(final[5])
    return jnp.concatenate([total_a, total_b])


def dot_t(lhs, rhs):
    return lax.dot_general(lhs, rhs, (((1,), (1,)), ((), ())), preferred_element_type=F32)


def attention_kernel(*refs):
    tok = refs[0:6]
    adapt = refs[6:14]
    (gain, gain_moe, cosine, sine, bias, doc, colp, colr, wq_hbm, wk_hbm, wv_hbm, wo_hbm,
     mixed_out, moe_a, moe_b,
     wq, wk, wv, wo, xn, ad, qbuf, kbuf, vbuf, att, sems) = refs[14:]
    copies = [pltpu.make_async_copy(src, dst, sems.at[i]) for i, (src, dst) in enumerate(
        [(wk_hbm, wk), (wv_hbm, wv), (wq_hbm, wq), (wo_hbm, wo)])]
    for copy in copies:
        copy.start()
    count = tok[0].shape[0]
    for j in range(8):
        ad[48 * j:48 * j + 48, :] = adapt[j][...]

    def norm(rows, scale):
        inverse = lax.rsqrt(jnp.mean(rows * rows, axis=-1, keepdims=True) + EPSILON)
        return (rows * inverse * scale).astype(BF)

    for b in range(6):
        xn[b * count:(b + 1) * count, :] = norm(tok[b][...].astype(F32), gain[...])
    copies[0].wait()
    copies[1].wait()
    col_prompt = colp[...]
    col_row = colr[...]

    def low(z, roll, first, docs):
        moved = pltpu.roll(z, roll, 1)
        keep = (docs == col_prompt) & (col_row >= first) & (col_row < first + 2)
        return jnp.where(keep, moved, 0.0).astype(BF)

    lane = lax.broadcasted_iota(jnp.int32, (count, 128), 1)
    lower = (lane & 63) < 32

    def rope(u, cos_t, sin_t):
        turned = jnp.where(lower, pltpu.roll(u, 96, 1), pltpu.roll(u, 32, 1))
        return (u * cos_t + turned * sin_t).astype(BF)

    def key_block(b, carry):
        at = pl.multiple_of(b * count, count)
        rows = xn[pl.ds(at, count), :]
        docs = doc[pl.ds(at, count), :]
        z = dot_t(rows, ad[...])
        keys = jnp.dot(rows, wk[...], preferred_element_type=F32) + jnp.dot(
            low(z, 10, 12, docs), ad[:, :512], preferred_element_type=F32)
        values = jnp.dot(rows, wv[...], preferred_element_type=F32) + jnp.dot(
            low(z, 8, 12, docs), ad[:, 512:1024], preferred_element_type=F32)
        vbuf[pl.ds(at, count), :] = values.astype(BF)
        cos_t = cosine[pl.ds(at, count), :]
        sin_t = sine[pl.ds(at, count), :]
        for c in range(4):
            kbuf[pl.ds(at, count), 128 * c:128 * c + 128] = rope(
                keys[:, 128 * c:128 * c + 128], cos_t, sin_t)
        return carry

    lax.fori_loop(0, 6, key_block, 0)
    copies[2].wait()
    own = xn[0:count, :]
    docs = doc[0:count, :]
    z = dot_t(own, ad[...])
    zq = low(z, 8, 8, docs)
    cos_t = cosine[0:count, :]
    sin_t = sine[0:count, :]
    low_half = lane < 64

    def query_block(c, carry):
        at = pl.multiple_of(c * 384, 128)
        u = jnp.dot(own, wq[:, pl.ds(at, 384)], preferred_element_type=F32) + jnp.dot(
            zq, ad[:, pl.ds(at, 384)], preferred_element_type=F32)
        for t in range(3):
            qbuf[:, pl.ds(pl.multiple_of(at + 128 * t, 128), 128)] = rope(
                u[:, 128 * t:128 * t + 128], cos_t, sin_t)
        return carry

    lax.fori_loop(0, 4, query_block, 0)

    def pair(j, carry):
        kv = pl.ds(pl.multiple_of(j * 128, 128), 128)
        keys = kbuf[:, kv]
        values = vbuf[:, kv]
        tiles = [qbuf[:, pl.ds(pl.multiple_of(j * 384 + 128 * t, 128), 128)] for t in range(3)]
        results = []
        for h in range(6):
            own_low, kv_low = h % 2 == 0, h < 3
            q = tiles[h // 2].astype(F32)
            if own_low != kv_low:
                q = pltpu.roll(q, 64, 1)
            q = jnp.where(low_half if kv_low else ~low_half, q, 0.0).astype(BF)
            s = dot_t(q, keys) * (HEAD ** -0.5) + bias[...]
            top = jnp.max(s, axis=-1, keepdims=True)
            w = jnp.exp(s - top)
            total = jnp.sum(w, axis=-1, keepdims=True)
            o = jnp.dot(w.astype(BF), values, preferred_element_type=F32) / total
            if own_low != kv_low:
                o = pltpu.roll(o, 64, 1)
            results.append(o)
        for t in range(3):
            att[:, pl.ds(pl.multiple_of(j * 384 + 128 * t, 128), 128)] = jnp.where(
                low_half, results[2 * t], results[2 * t + 1]).astype(BF)
        return carry

    lax.fori_loop(0, 4, pair, 0)
    copies[3].wait()
    attended = att[...]
    zo = low(dot_t(attended, ad[...]), 4, 10, docs)
    mixed = (tok[0][...].astype(F32) + jnp.dot(attended, wo[...], preferred_element_type=F32)
             + jnp.dot(zo, ad[...], preferred_element_type=F32)).astype(BF)
    mixed_out[...] = mixed
    moe = norm(mixed.astype(F32), gain_moe[...])
    moe_a[...] = moe[:count // 2]
    moe_b[...] = moe[count // 2:]


def attention(tok, adapt, gain, gain_moe, cosine, sine, bias, doc, colp, colr, wq, wk, wv, wo):
    count, width = tok[0].shape
    vm = pl.BlockSpec(memory_space=pltpu.VMEM)
    anywhere = pl.BlockSpec(memory_space=pl.ANY)
    half = jax.ShapeDtypeStruct((count // 2, width), BF)
    return pl.pallas_call(
        attention_kernel,
        out_shape=(jax.ShapeDtypeStruct((count, width), BF), half, half),
        in_specs=[vm] * 22 + [anywhere] * 4,
        out_specs=(vm, vm, vm),
        scratch_shapes=[
            pltpu.VMEM(wq.shape, BF), pltpu.VMEM(wk.shape, BF), pltpu.VMEM(wv.shape, BF),
            pltpu.VMEM(wo.shape, BF), pltpu.VMEM((6 * count, width), BF),
            pltpu.VMEM((384, width), BF), pltpu.VMEM((count, width), BF),
            pltpu.VMEM((6 * count, 512), BF), pltpu.VMEM((6 * count, 512), BF),
            pltpu.VMEM((count, width), BF), pltpu.SemaphoreType.DMA((4,)),
        ],
        compiler_params=pltpu.CompilerParams(vmem_limit_bytes=48 << 20),
        name="attention_block",
    )(*tok, *adapt, gain, gain_moe, cosine, sine, bias, doc, colp, colr, wq, wk, wv, wo)


def expert_kernel(*refs):
    pieces_a, pieces_b = refs[0:5], refs[5:10]
    high, low, gate_hbm, up_hbm, down_hbm = refs[10:15]
    out_a, out_b = refs[15:19], refs[19:23]
    x, xe, ho, gate, up, down, sem_x, sem_w, sem_o = refs[23:]
    loads = []
    where_a = [x.at[0, :, 0:64], x.at[1, :, 0:64], x.at[2, :, 0:64], x.at[3, 0:2, 0:64],
               x.at[3, 2:4, 0:64]]
    where_b = [x.at[:, 0, 64:128], x.at[:, 1, 64:128], x.at[:, 2, 64:128],
               x.at[0:2, 3, 64:128], x.at[2:4, 3, 64:128]]
    for k in range(5):
        loads.append(pltpu.make_async_copy(pieces_a[k], where_a[k], sem_x.at[k]))
        loads.append(pltpu.make_async_copy(pieces_b[k], where_b[k], sem_x.at[5 + k]))
    for copy in loads:
        copy.start()
    weights = []
    for s in range(5):
        weights.append([pltpu.make_async_copy(src.at[s], dst.at[s], sem_w.at[3 * s + k])
                        for k, (src, dst) in enumerate(
                            [(gate_hbm, gate), (up_hbm, up), (down_hbm, down)])])
        for copy in weights[-1]:
            copy.start()
    for copy in loads:
        copy.wait()
    before = (lax.broadcasted_iota(jnp.int32, (128, 128), 0)
              < lax.broadcasted_iota(jnp.int32, (128, 128), 1)).astype(BF)
    slot = lax.broadcasted_iota(jnp.int32, (SLOTS, 128), 0).astype(F32)

    def places(i):
        named = (high[i] > 0.0).astype(F32)
        rank = jnp.dot(named.astype(BF), before, preferred_element_type=F32)
        rank = jnp.where(named > 0.0, rank, -1.0)
        return [slot == rank[s:s + 1, :] for s in range(5)]

    def take(i, carry):
        block = x[i // 4, lax.rem(i, 4)]
        hot = jnp.concatenate([jnp.where(p, 1.0, 0.0) for p in places(i)]).astype(BF)
        rows = jnp.dot(hot, block, preferred_element_type=F32).astype(BF)
        for s in range(5):
            xe[s, pl.ds(pl.multiple_of(i * SLOTS, SLOTS), SLOTS), :] = rows[
                s * SLOTS:(s + 1) * SLOTS]
        return carry

    lax.fori_loop(0, 16, take, 0)
    size = 8 * SLOTS
    for s in range(5):
        for copy in weights[s]:
            copy.wait()

        def run(c, carry, s=s):
            at = pl.ds(pl.multiple_of(c * size, size), size)
            rows = xe[s, at, :]
            g = jnp.dot(rows, gate[s], preferred_element_type=F32)
            u = jnp.dot(rows, up[s], preferred_element_type=F32)
            hidden = (g / (1.0 + jnp.exp(-g)) * u).astype(BF)
            ho[s, at, :] = jnp.dot(hidden, down[s], preferred_element_type=F32).astype(BF)
            return carry

        lax.fori_loop(0, 2, run, 0)

    def combine(i, carry):
        spots = places(i)
        high_i, low_i = high[i], low[i]
        hot_high = jnp.concatenate(
            [jnp.where(p, high_i[s:s + 1, :], 0.0) for s, p in enumerate(spots)]).astype(BF)
        hot_low = jnp.concatenate(
            [jnp.where(p, low_i[s:s + 1, :], 0.0) for s, p in enumerate(spots)]).astype(BF)
        at = pl.ds(pl.multiple_of(i * SLOTS, SLOTS), SLOTS)
        rows = jnp.concatenate([ho[s, at, :] for s in range(5)])
        dims = (((0,), (0,)), ((), ()))
        total = lax.dot_general(hot_high, rows, dims, preferred_element_type=F32)
        total = total + lax.dot_general(hot_low, rows, dims, preferred_element_type=F32)
        x[i // 4, lax.rem(i, 4)] = total.astype(BF)
        return carry

    lax.fori_loop(0, 16, combine, 0)
    stores = [pltpu.make_async_copy(x.at[k, :, 0:64], out_a[k], sem_o.at[k]) for k in range(4)]
    stores += [pltpu.make_async_copy(x.at[:, k, 64:128], out_b[k], sem_o.at[4 + k])
               for k in range(4)]
    for copy in stores:
        copy.start()
    for copy in stores:
        copy.wait()


def experts(pieces_a, pieces_b, high, low, gate, up, down):
    width = gate.shape[1]
    anywhere = pl.BlockSpec(memory_space=pl.ANY)
    vm = pl.BlockSpec(memory_space=pltpu.VMEM)
    quarter = jax.ShapeDtypeStruct((4, 64, width), BF)
    outs = pl.pallas_call(
        expert_kernel,
        out_shape=(quarter,) * 8,
        in_specs=[anywhere] * 10 + [vm] * 2 + [anywhere] * 3,
        out_specs=(anywhere,) * 8,
        scratch_shapes=[
            pltpu.VMEM((4, 4, 128, width), BF), pltpu.VMEM((5, 16 * SLOTS, width), BF),
            pltpu.VMEM((5, 16 * SLOTS, width), BF), pltpu.VMEM(gate.shape, BF),
            pltpu.VMEM(up.shape, BF), pltpu.VMEM(down.shape, BF),
            pltpu.SemaphoreType.DMA((10,)), pltpu.SemaphoreType.DMA((15,)),
            pltpu.SemaphoreType.DMA((8,)),
        ],
        compiler_params=pltpu.CompilerParams(vmem_limit_bytes=58 << 20),
        name="expert_block",
    )(*pieces_a, *pieces_b, high, low, gate, up, down)
    return outs[:4], outs[4:]


def rms_scaled(features, scales):
    features = features.astype(F32)
    inverse = lax.rsqrt(jnp.mean(features * features, axis=-1, keepdims=True) + EPSILON)
    return (features * inverse * scales).astype(BF)


def body(tokens, lengths, prompt_adapter, routes, routing_weight, attention_gain, query_weight,
         key_weight, value_weight, output_weight, adapter_down_maps, adapter_up_query_output,
         adapter_up_key_value, expert_gain, gate_weight, up_weight, down_weight, closing_gain,
         vocab_projection):
    own = tokens[0]
    count, width = own.shape
    me, grp = lax.axis_index("seq"), lax.axis_index("grp")
    back1 = lax.ppermute(own, "seq", [(s, s + 2) for s in range(6)])
    back2 = lax.ppermute(own, "seq", [(s, s + 4) for s in range(4)])

    ids, given = routes[0], routing_weight[0]
    table = jnp.sum(jnp.where(
        ids[:, None, :] == jnp.arange(EXPERTS, dtype=jnp.int32)[None, :, None],
        given[:, None, :], 0.0), axis=2).T
    table = jnp.repeat(table, 2, axis=0).reshape(16, 5 * count)
    high = lax.reduce_precision(table, 8, 7)
    low = table - high
    route_rows = jnp.concatenate(
        [high, low, jnp.zeros((16, width - 10 * count), F32)], axis=1).astype(BF)

    ranks = (jnp.arange(16, dtype=jnp.int32)[:, None]
             == 2 * me + jnp.arange(2, dtype=jnp.int32)[None, :]).astype(BF)
    downs = jnp.einsum("rk,pdr->pkd", ranks, adapter_down_maps[:, 0],
                       preferred_element_type=F32).astype(BF).reshape(8, width)
    ups = lax.dynamic_slice_in_dim(adapter_up_query_output[:, 0], 2 * me, 2, 1).reshape(4, width)
    thin = lax.dynamic_slice_in_dim(adapter_up_key_value[:, 0], 2 * me, 2, 1)
    thin = jnp.concatenate([thin[0], thin[1], jnp.zeros((2, width - 1024), BF)], axis=1)
    maps = jnp.concatenate([downs, ups, thin], axis=0)
    payload = jnp.concatenate(
        [jnp.broadcast_to(maps[None], (16, 14, width)), route_rows[:, None, :],
         jnp.zeros((16, 1, width), BF)], axis=1)
    held = lax.all_to_all(payload, "grp", 0, 0, tiled=True)
    row_kind = jnp.arange(16, dtype=jnp.int32)[None, :, None]
    picked = jnp.stack([lax.dynamic_index_in_dim(held, prompt_adapter[0, p], 0, False)
                        for p in range(3)])
    picked = jnp.where(row_kind < 14, picked, 0).reshape(48, width)
    turn = [picked] + [lax.ppermute(picked, "seq", [(s, (s + d) % 8) for s in range(8)])
                       for d in (2, 6, 4)]
    adapt = turn + [partner(piece) for piece in turn]
    tok = [own, back1, back2]
    tok = tok + [partner(rows) for rows in tok]

    rel = jnp.array([0, 3, 1, 2], jnp.int32)
    source = ((grp // 4 + rel[:, None]) % 4 * 4 + (grp % 4 + rel[None, :]) % 4).reshape(16)
    order = (source[:, None] == jnp.arange(16, dtype=jnp.int32)[None, :]).astype(F32)
    route_in = jnp.dot(order, held[:, 14, :].astype(F32), precision=lax.Precision.HIGHEST)
    pad = jnp.zeros((16, 3, count), F32)
    high_in = jnp.concatenate([route_in[:, :5 * count].reshape(16, 5, count), pad], axis=1)
    low_in = jnp.concatenate(
        [route_in[:, 5 * count:10 * count].reshape(16, 5, count), pad], axis=1)

    lens = lengths[0]
    ends = jnp.cumsum(lens)
    starts = ends - lens
    other = me ^ 1
    blocks = jnp.stack([me, me - 2, me - 4, other, other - 2, other - 4])
    index = (blocks[:, None] * count + jnp.arange(count, dtype=jnp.int32)[None, :]).reshape(-1)
    document = jnp.sum((index[:, None] >= ends[None, :]).astype(jnp.int32), axis=1)
    start = jnp.where(document == 0, starts[0], jnp.where(document == 1, starts[1], starts[2]))
    half = HEAD // 2
    frequency = ROPE_BASE ** (-jnp.arange(half, dtype=F32) / half)
    angles = (index - start).astype(F32)[:, None] * frequency[None, :]
    cosine, sine = jnp.cos(angles), jnp.sin(angles)
    cosine = jnp.concatenate([cosine] * 4, axis=1)
    sine = jnp.concatenate([-sine, sine, -sine, sine], axis=1)
    row_index = index[:count]
    allowed = ((document[None, :] == document[:count, None]) & (index[None, :] >= 0)
               & (index[None, :] <= row_index[:, None]))
    bias = jnp.where(allowed, 0.0, MASKED).astype(F32)
    columns = jnp.arange(384, dtype=jnp.int32)[None, :]

    mixed, moe_a, moe_b = attention(
        tok, adapt, attention_gain[None], expert_gain[None], cosine, sine, bias,
        document[:, None], columns // 16 % 3, columns % 16, query_weight, key_weight,
        value_weight, output_weight)

    pieces_a, pieces_b = gather_tokens(moe_a, moe_b)
    parts_a, parts_b = experts(pieces_a, pieces_b, high_in, low_in, gate_weight, up_weight,
                               down_weight)
    combined = reduce_tokens(parts_a, parts_b)
    hidden_out = (mixed.astype(F32) + combined).astype(BF)

    selector = (ends[:, None] - 1 == row_index[None, :]).astype(BF)
    last = jnp.dot(selector, hidden_out, preferred_element_type=F32)
    last = rms_scaled(last, closing_gain)
    part = width // 8
    split = last.reshape(3, 8, part).transpose(1, 0, 2)
    mine = lax.all_to_all(split, "seq", 0, 0, tiled=True)
    mine = jnp.sum(mine.astype(F32), axis=0).astype(BF)
    everyone = lax.all_to_all(jnp.broadcast_to(mine[None], (128, 3, part)), WHOLE, 0, 0,
                              tiled=True)
    final_rows = everyone.reshape(8, 48, part).transpose(1, 0, 2).reshape(48, width)
    logits = jnp.dot(final_rows, vocab_projection, preferred_element_type=F32)
    top = jnp.max(logits, axis=1)
    mass = jnp.sum(jnp.exp(logits - top[:, None]), axis=1)
    stats = jnp.concatenate([top, mass, jnp.zeros((32,), F32)])
    stats = lax.all_to_all(jnp.broadcast_to(stats[None], (128, 128)), WHOLE, 0, 0, tiled=True)
    tops = stats[:, :48]
    peak = jnp.max(tops, axis=0)
    total = jnp.sum(stats[:, 48:96] * jnp.exp(tops - peak[None]), axis=0)
    log_probs = logits - (peak + jnp.log(total))[:, None]
    return hidden_out[None], log_probs


def solution(mesh):
    placed = (
        P("grp", "seq", None), P("grp", None), P("grp", None), P("grp", "seq", None),
        P("grp", "seq", None), P(), P(), P(), P(), P(), P(None, "grp", None, None),
        P(None, "grp", None, None), P(None, "grp", None, None), P(), P("grp", None, None),
        P("grp", None, None), P("grp", None, None), P(), P(None, WHOLE),
    )
    return jax.shard_map(
        body,
        mesh=mesh,
        in_specs=placed,
        out_specs=(P("grp", "seq", None), P(None, WHOLE)),
        check_vma=False,
    )
```

time: 712 us -> 266 us (0.37)
  blocking collectives: 334 us -> 40.7 us
  waiting for transfers between devices: 219 us -> 55.9 us
  starting transfers between devices: 5.27 us -> 68.8 us
  Pallas kernels: 0 us -> 60.6 us
  matrix products: 56.6 us -> 2.08 us
  local copies, waits for them, and re-layouts: 60.3 us -> 16.2 us
  other arithmetic: 21.7 us -> 14.2 us
  between operations: 14.3 us -> 7 us
    all_to_all x1 -> x2, waiting for transfers between devices: 141 us -> 8.93 us  [the longest x1 8.93 us: body(): lax.all_to_all(jnp.broadcast_to(stats[None], (128, 128)), WHOLE, 0, 0, ti...]
    psum x2 -> x0, blocking collectives: 129 us -> none  [the longest x1 66.8 us: body(): gathered = lax.psum(spread, ('seq', 'grp'))]
    all_to_all x1 -> x2, blocking collectives: 118 us -> 40.7 us  [the longest x1 24.1 us: body(): mine = lax.all_to_all(split, 'seq', 0, 0, tiled=True)]
    all_gather x4 -> x0, waiting for transfers between devices: 76.2 us -> none  [the longest x1 35.7 us: body(): lax.all_gather(adapter_up_query_output, 'grp', axis=1, tiled=True)]
    pmax x1 -> x0, blocking collectives: 64.4 us -> none  [body(): global_max = lax.pmax(jnp.max(logits, axis=1), ('seq', 'grp'))]
    pallas_call x0 -> x2, Pallas kernels: none -> 60.6 us  [the longest x1 37.3 us: experts(): pl.pallas_call(expert_kernel, out_shape=(quarter,) * 8, in_specs=[anywher...]
    ppermute x0 -> x40, starting transfers between devices: none -> 57 us  [the longest x28 40.2 us: shift(): return lax.ppermute(rows, 'grp', pairs)]
    dot_general x15 -> x4, matrix products: 52.7 us -> 2.08 us  [the longest x1 1.15 us: body(): jnp.einsum('rk,pdr->pkd', ranks, adapter_down_maps[:, 0], preferred_eleme...]
  transfers between devices with their start and end apart: 5 -> 42, of which waited for: 5 -> 20; matrix products, arithmetic and copies ran while one was open for 7% -> 10% of each run, Pallas kernels for 0% -> 0%
where the time goes in v1:
time: 266 us
  starting transfers between devices  68.8 us (26%)
  Pallas kernels  60.6 us (23%)
  waiting for transfers between devices  55.9 us (21%)
  blocking collectives  40.7 us (15%)
  local copies, waits for them, and re-layouts  16.2 us (6%)
  other arithmetic  14.2 us (5%)
  between operations  7 us (3%)
    ppermute x28, waiting for transfers between devices, shift(): return lax.ppermute(rows, 'grp', pairs)  43.2 us
    ppermute x28, starting transfers between devices, shift(): return lax.ppermute(rows, 'grp', pairs)  40.2 us
    pallas_call x1, Pallas kernels, experts(): pl.pallas_call(expert_kernel, out_shape=(quarter,) * 8, in_specs=[anywher...  37.3 us
    all_to_all x1, blocking collectives, body(): mine = lax.all_to_all(split, 'seq', 0, 0, tiled=True)  24.1 us
    pallas_call x1, Pallas kernels, attention(): pl.pallas_call(attention_kernel, out_shape=(jax.ShapeDtypeStruct((count,...  23.2 us
    all_to_all x1, blocking collectives, body(): lax.all_to_all(jnp.broadcast_to(mine[None], (128, 3, part)), WHOLE, 0, 0,...  16.6 us
    all_to_all x1, waiting for transfers between devices, body(): lax.all_to_all(jnp.broadcast_to(stats[None], (128, 128)), WHOLE, 0, 0, ti...  8.93 us
    all_to_all x1, starting transfers between devices, body(): held = lax.all_to_all(payload, 'grp', 0, 0, tiled=True)  7.81 us
  transfers between devices with their start and end apart: 42, of which 20 were waited for; matrix products, arithmetic and copies ran while one was open for 10% of the time, Pallas kernels for 0%

profile of v1, /device:TPU:1, one launch (start us, length us, event | category | flops | bytes accessed | tf_op | source)
XLA Modules:
  0.0 265.5 jit_solution(18275187320426413786)
XLA Ops:
  0.6 4.1 %collective-permute-start = (bf16[128,1536]{1,0:T(8,128)(2,1)}, bf16[128,1536]{1,0:T(8,128)(2,1)S(1)}, u32[]{:S(2)}, u32[]{:S(2)}) collective-permute-start(bf16[128,1536]{1,0:T(8,128)(2,1)} %bitcast.97), channel_id=1, source_target_pairs={{0,32},{16,48},{32,64},{48,80},{64,96},{80,112},{1,33},{17,49},{33... | collective-permute-start | bytes 1179656 | tf_op jit(solution)/shard_map/ppermute | solution.py:337
  4.8 4.4 %collective-permute-start.1 = (bf16[128,1536]{1,0:T(8,128)(2,1)}, bf16[128,1536]{1,0:T(8,128)(2,1)S(1)}, u32[]{:S(2)}, u32[]{:S(2)}) collective-permute-start(bf16[128,1536]{1,0:T(8,128)(2,1)} %bitcast.98), channel_id=1, source_target_pairs={{0,64},{16,80},{32,96},{48,112},{1,65},{17,81},{33,97},{49,113},{2... | collective-permute-start | bytes 1179656 | tf_op jit(solution)/shard_map/ppermute | solution.py:338
  15.5 7.8 %all-to-all-start = ((bf16[16,16,1536]{2,1,0:T(8,128)(2,1)}), bf16[16,16,1536]{2,1,0:T(8,128)(2,1)}, u32[]{:S(2)}, u32[]{:S(2)}) async-start(bf16[16,16,1536]{2,1,0:T(8,128)(2,1)} %maximum_maximum_fusion), calls=%async_computation | async-start | bytes 1572864 | tf_op jit(solution)/shard_map/all_to_all | solution.py:361
  26.7 2.0 subtract_convert_fusion
  35.4 2.5 fusion.9
  43.5 1.8 collective-permute-done.6.refs_8_
  45.3 1.9 collective-permute-start.10
  48.8 1.9 collective-permute-done.5.refs_7_
  52.2 23.2 %attention_block.1 = (bf16[128,1536]{1,0:T(8,128)(2,1)S(1)}, bf16[64,1536]{1,0:T(8,128)(2,1)S(1)}, bf16[64,1536]{1,0:T(8,128)(2,1)S(1)}) custom-call(bf16[128,1536]{1,0:T(8,128)(2,1)S(1)} %bitcast.100, bf16[128,1536]{1,0:T(8,128)(2,1)S(1)} %collective-permute-done.refs_1_, bf16[128,1536]{1,0:T(8,128)(2,1)S(1)} %collective-permute-done.1.refs_2_, ...), custom_call_target="tpu_custom_call" | custom-call | tf_op jit(solution)/shard_map/attention_block/pallas_call | solution.py:199
  75.4 1.7 collective-permute-start.12
  83.1 2.9 %collective-permute-start.17 = (bf16[64,1536]{1,0:T(8,128)(2,1)S(1)}, bf16[64,1536]{1,0:T(8,128)(2,1)S(1)}, u32[]{:S(2)}, u32[]{:S(2)}) collective-permute-start(bf16[64,1536]{1,0:T(8,128)(2,1)S(1)} %get-tuple-element.33), channel_id=1, source_target_pairs={{0,8},{1,9},{2,10},{3,11},{4,12},{5,13},{6,14},{7,15},{8,0},{9,1},... | collective-permute-start | bytes 589832 | tf_op jit(solution)/shard_map/ppermute | solution.py:28
  87.7 2.6 collective-permute-done.17
  90.5 2.7 %collective-permute-start.21 = (bf16[4,64,1536]{2,1,0:T(8,128)(2,1)S(1)}, bf16[4,64,1536]{2,1,0:T(8,128)(2,1)}, u32[]{:S(2)}, u32[]{:S(2)}) collective-permute-start(bf16[4,64,1536]{2,1,0:T(8,128)(2,1)S(1)} %pad_maximum_fusion.1.refs_5_), channel_id=1, source_target_pairs={{0,3},{1,0},{2,1},{3,2},{4,7},{5,4},{6,5},{7,6},{8,11},{9,8},{10,9... | collective-permute-start | bytes 2359304 | tf_op jit(solution)/shard_map/ppermute | solution.py:28
  97.3 11.5 %collective-permute-done.19.refs_6_ = bf16[4,64,1536]{2,1,0:T(8,128)(2,1)} collective-permute-done((bf16[4,64,1536]{2,1,0:T(8,128)(2,1)S(1)}, bf16[4,64,1536]{2,1,0:T(8,128)(2,1)}, u32[]{:S(2)}, u32[]{:S(2)}) %collective-permute-start.19) | collective-permute-done | bytes 786464 | tf_op jit(solution)/shard_map/ppermute | solution.py:28
  108.8 2.3 collective-permute-done.18.refs_1_
  112.8 1.8 slice.141
  114.5 2.1 collective-permute-start.23
  118.8 2.7 %collective-permute-start.25 = (bf16[2,64,1536]{2,1,0:T(8,128)(2,1)S(1)}, bf16[2,64,1536]{2,1,0:T(8,128)(2,1)}, u32[]{:S(2)}, u32[]{:S(2)}) collective-permute-start(bf16[2,64,1536]{2,1,0:T(8,128)(2,1)S(1)} %slice.143), channel_id=1, source_target_pairs={{0,3},{1,0},{2,1},{3,2},{4,7},{5,4},{6,5},{7,6},{8,11},{9,8},{10,9... | collective-permute-start | bytes 1179656 | tf_op jit(solution)/shard_map/ppermute | solution.py:28
  123.1 2.6 collective-permute-done.24.refs_8_
  126.3 37.3 %expert_block.1 = (bf16[4,64,1536]{2,1,0:T(8,128)(2,1)}, bf16[4,64,1536]{2,1,0:T(8,128)(2,1)}, bf16[4,64,1536]{2,1,0:T(8,128)(2,1)}, bf16[4,64,1536]{2,1,0:T(8,1...) custom-call(bf16[4,64,1536]{2,1,0:T(8,128)(2,1)} %copy-done.3, ...), custom_call_target="tpu_custom_call" | custom-call | tf_op jit(solution)/shard_map/expert_block/pallas_call | solution.py:306
  165.2 2.7 %collective-permute-start.28 = (bf16[2,64,1536]{2,1,0:T(8,128)(2,1)S(1)}, bf16[2,64,1536]{2,1,0:T(8,128)(2,1)S(1)}, u32[]{:S(2)}, u32[]{:S(2)}) collective-permute-start(bf16[2,64,1536]{2,1,0:T(8,128)(2,1)S(1)} %get-tuple-element.72), channel_id=1, source_target_pairs={{0,12},{1,13},{2,14},{3,15},{4,0},{5,1},{6,2},{7,3},{8,4},{9,5},{1... | collective-permute-start | bytes 1179656 | tf_op jit(solution)/shard_map/ppermute | solution.py:28
  167.9 3.3 %collective-permute-start.29 = (bf16[2,64,1536]{2,1,0:T(8,128)(2,1)S(1)}, bf16[2,64,1536]{2,1,0:T(8,128)(2,1)S(1)}, u32[]{:S(2)}, u32[]{:S(2)}) collective-permute-start(bf16[2,64,1536]{2,1,0:T(8,128)(2,1)S(1)} %get-tuple-element.70), channel_id=1, source_target_pairs={{0,3},{1,0},{2,1},{3,2},{4,7},{5,4},{6,5},{7,6},{8,11},{9,8},{10,9... | collective-permute-start | bytes 1179656 | tf_op jit(solution)/shard_map/ppermute | solution.py:28
  173.6 2.3 collective-permute-done.29
  176.1 3.5 %collective-permute-start.33 = (bf16[4,64,1536]{2,1,0:T(8,128)(2,1)S(1)}, bf16[4,64,1536]{2,1,0:T(8,128)(2,1)S(1)}, u32[]{:S(2)}, u32[]{:S(2)}) collective-permute-start(bf16[4,64,1536]{2,1,0:T(8,128)(2,1)S(1)} %pad_maximum_fusion.5), channel_id=1, source_target_pairs={{0,3},{1,0},{2,1},{3,2},{4,7},{5,4},{6,5},{7,6},{8,11},{9,8},{10,9... | collective-permute-start | bytes 2359304 | tf_op jit(solution)/shard_map/ppermute | solution.py:28
  181.8 10.1 %collective-permute-done.33 = bf16[4,64,1536]{2,1,0:T(8,128)(2,1)S(1)} collective-permute-done((bf16[4,64,1536]{2,1,0:T(8,128)(2,1)S(1)}, bf16[4,64,1536]{2,1,0:T(8,128)(2,1)S(1)}, u32[]{:S(2)}, u32[]{:S(2)}) %collective-permute-start.33) | collective-permute-done | bytes 786464 | tf_op jit(solution)/shard_map/ppermute | solution.py:28
  193.5 2.4 collective-permute-start.35
  197.7 2.4 collective-permute-start.38
  202.8 3.6 %collective-permute-done.36 = bf16[64,1536]{1,0:T(8,128)(2,1)S(1)} collective-permute-done((bf16[64,1536]{1,0:T(8,128)(2,1)S(1)}, bf16[64,1536]{1,0:T(8,128)(2,1)S(1)}, u32[]{:S(2)}, u32[]{:S(2)}) %collective-permute-start.36) | collective-permute-done | bytes 196640 | tf_op jit(solution)/shard_map/ppermute | solution.py:28
  208.0 24.1 %all_to_all.24 = bf16[8,3,192]{2,1,0:T(4,128)(2,1)S(1)} all-to-all(bf16[8,3,192]{2,1,0:T(4,128)(2,1)S(1)} %bitcast.113), channel_id=1, replica_groups=mesh['seq'=8,'grp'=16] {'seq'}, dimensions={0} | all-to-all | bytes 18432 | tf_op jit(solution)/shard_map/all_to_all | solution.py:417
  232.2 16.6 %all_to_all.25 = bf16[128,3,192]{2,1,0:T(4,128)(2,1)S(1)} all-to-all(bf16[128,3,192]{2,1,0:T(4,128)(2,1)S(1)} %broadcast_in_dim.138), channel_id=1, replica_groups=mesh['seq'=8,'grp'=16] {'seq','grp'}, dimensions={0} | all-to-all | bytes 294912 | tf_op jit(solution)/shard_map/all_to_all | solution.py:419
  250.6 4.0 %all-to-all-start.3 = ((f32[128,1,128]{2,1,0:T(1,128)}), f32[128,1,128]{2,1,0:T(1,128)S(1)}, u32[]{:S(2)}, u32[]{:S(2)}) async-start(f32[128,1,128]{2,1,0:T(1,128)} %broadcast_in_dim.140), calls=%async_computation.3 | async-start | bytes 131072 | tf_op jit(solution)/shard_map/all_to_all | solution.py:426
  255.5 8.9 %all-to-all-done.3 = f32[128,1,128]{2,1,0:T(1,128)S(1)} async-done(((f32[128,1,128]{2,1,0:T(1,128)}), f32[128,1,128]{2,1,0:T(1,128)S(1)}, u32[]{:S(2)}, u32[]{:S(2)}) %all-to-all-start.3) | async-done | bytes 65568 | tf_op jit(solution)/shard_map/all_to_all | solution.py:426
  (200 shorter events, 54.5 us)
Async XLA Ops:
  0.6 37.2 %collective-permute-start = (bf16[128,1536]{1,0:T(8,128)(2,1)}, bf16[128,1536]{1,0:T(8,128)(2,1)S(1)}, u32[]{:S(2)}, u32[]{:S(2)}) collective-permute-start(bf16[128,1536]{1,0:T(8,128)(2,1)} %bitcast.97), channel_id=1, source_target_pairs={{0,32},{16,48},{32,64},{48,80},{64,96},{80,112},{1,33},{17,49},{33... | collective-permute-start | bytes 1179656 | tf_op jit(solution)/shard_map/ppermute | solution.py:337
  4.8 33.4 %collective-permute-start.1 = (bf16[128,1536]{1,0:T(8,128)(2,1)}, bf16[128,1536]{1,0:T(8,128)(2,1)S(1)}, u32[]{:S(2)}, u32[]{:S(2)}) collective-permute-start(bf16[128,1536]{1,0:T(8,128)(2,1)} %bitcast.98), channel_id=1, source_target_pairs={{0,64},{16,80},{32,96},{48,112},{1,65},{17,81},{33,97},{49,113},{2... | collective-permute-start | bytes 1179656 | tf_op jit(solution)/shard_map/ppermute | solution.py:338
  9.1 31.3 %collective-permute-start.2 = (bf16[128,1536]{1,0:T(8,128)(2,1)}, bf16[128,1536]{1,0:T(8,128)(2,1)S(1)}, u32[]{:S(2)}, u32[]{:S(2)}) collective-permute-start(bf16[128,1536]{1,0:T(8,128)(2,1)} %bitcast.99), channel_id=1, source_target_pairs={{0,16},{16,0},{32,48},{48,32},{64,80},{80,64},{96,112},{112,96},{1... | collective-permute-start | bytes 1179656 | tf_op jit(solution)/shard_map/ppermute | solution.py:32
  15.5 22.8 %all-to-all-start = ((bf16[16,16,1536]{2,1,0:T(8,128)(2,1)}), bf16[16,16,1536]{2,1,0:T(8,128)(2,1)}, u32[]{:S(2)}, u32[]{:S(2)}) async-start(bf16[16,16,1536]{2,1,0:T(8,128)(2,1)} %maximum_maximum_fusion), calls=%async_computation | async-start | bytes 1572864 | tf_op jit(solution)/shard_map/all_to_all | solution.py:361
  38.2 13.9 %collective-permute-start.4 = (bf16[128,1536]{1,0:T(8,128)(2,1)S(1)}, bf16[128,1536]{1,0:T(8,128)(2,1)S(1)}, u32[]{:S(2)}, u32[]{:S(2)}) collective-permute-start(bf16[128,1536]{1,0:T(8,128)(2,1)S(1)} %collective-permute-done.1.refs_2_), channel_id=1, source_target_pairs={{0,16},{16,0},{32,48},{48,32},{64,80},{80,64},{96,112},{112,96},{1... | collective-permute-start | bytes 1179656 | tf_op jit(solution)/shard_map/ppermute | solution.py:32
  40.4 10.2 %collective-permute-start.5 = (bf16[48,1536]{1,0:T(8,128)(2,1)S(1)}, bf16[48,1536]{1,0:T(8,128)(2,1)S(1)}, u32[]{:S(2)}, u32[]{:S(2)}) collective-permute-start(bf16[48,1536]{1,0:T(8,128)(2,1)S(1)} %bitcast_select_fusion.refs_6_), channel_id=1, source_target_pairs={{0,32},{16,48},{32,64},{48,80},{64,96},{80,112},{96,0},{112,16},{1... | collective-permute-start | bytes 442376 | tf_op jit(solution)/shard_map/ppermute | solution.py:366
  42.5 9.6 %collective-permute-start.8 = (bf16[48,1536]{1,0:T(8,128)(2,1)S(1)}, bf16[48,1536]{1,0:T(8,128)(2,1)S(1)}, u32[]{:S(2)}, u32[]{:S(2)}) collective-permute-start(bf16[48,1536]{1,0:T(8,128)(2,1)S(1)} %bitcast_select_fusion.refs_6_), channel_id=1, source_target_pairs={{0,16},{16,0},{32,48},{48,32},{64,80},{80,64},{96,112},{112,96},{1... | collective-permute-start | bytes 442376 | tf_op jit(solution)/shard_map/ppermute | solution.py:32
  75.4 7.7 %collective-permute-start.12 = (bf16[64,1536]{1,0:T(8,128)(2,1)S(1)}, bf16[64,1536]{1,0:T(8,128)(2,1)S(1)}, u32[]{:S(2)}, u32[]{:S(2)}) collective-permute-start(bf16[64,1536]{1,0:T(8,128)(2,1)S(1)} %get-tuple-element.32), channel_id=1, source_target_pairs={{0,1},{1,2},{2,3},{3,0},{4,5},{5,6},{6,7},{7,4},{8,9},{9,10},{10,1... | collective-permute-start | bytes 589832 | tf_op jit(solution)/shard_map/ppermute | solution.py:28
  77.2 8.9 %collective-permute-start.14 = (bf16[64,1536]{1,0:T(8,128)(2,1)S(1)}, bf16[64,1536]{1,0:T(8,128)(2,1)S(1)}, u32[]{:S(2)}, u32[]{:S(2)}) collective-permute-start(bf16[64,1536]{1,0:T(8,128)(2,1)S(1)} %get-tuple-element.32), channel_id=1, source_target_pairs={{0,3},{1,0},{2,1},{3,2},{4,7},{5,4},{6,5},{7,6},{8,11},{9,8},{10,9... | collective-permute-start | bytes 589832 | tf_op jit(solution)/shard_map/ppermute | solution.py:28
  78.5 7.6 %collective-permute-start.13 = (bf16[64,1536]{1,0:T(8,128)(2,1)S(1)}, bf16[64,1536]{1,0:T(8,128)(2,1)S(1)}, u32[]{:S(2)}, u32[]{:S(2)}) collective-permute-start(bf16[64,1536]{1,0:T(8,128)(2,1)S(1)} %get-tuple-element.33), channel_id=1, source_target_pairs={{0,4},{1,5},{2,6},{3,7},{4,8},{5,9},{6,10},{7,11},{8,12},{9,13},{1... | collective-permute-start | bytes 589832 | tf_op jit(solution)/shard_map/ppermute | solution.py:28
  90.4 18.4 %collective-permute-start.19 = (bf16[4,64,1536]{2,1,0:T(8,128)(2,1)S(1)}, bf16[4,64,1536]{2,1,0:T(8,128)(2,1)}, u32[]{:S(2)}, u32[]{:S(2)}) collective-permute-start(bf16[4,64,1536]{2,1,0:T(8,128)(2,1)S(1)} %pad_maximum_fusion.1.refs_5_), channel_id=1, source_target_pairs={{0,1},{1,2},{2,3},{3,0},{4,5},{5,6},{6,7},{7,4},{8,9},{9,10},{10,1... | collective-permute-start | bytes 2359304 | tf_op jit(solution)/shard_map/ppermute | solution.py:28
  90.5 18.3 %collective-permute-start.21 = (bf16[4,64,1536]{2,1,0:T(8,128)(2,1)S(1)}, bf16[4,64,1536]{2,1,0:T(8,128)(2,1)}, u32[]{:S(2)}, u32[]{:S(2)}) collective-permute-start(bf16[4,64,1536]{2,1,0:T(8,128)(2,1)S(1)} %pad_maximum_fusion.1.refs_5_), channel_id=1, source_target_pairs={{0,3},{1,0},{2,1},{3,2},{4,7},{5,4},{6,5},{7,6},{8,11},{9,8},{10,9... | collective-permute-start | bytes 2359304 | tf_op jit(solution)/shard_map/ppermute | solution.py:28
  93.3 17.8 %collective-permute-start.18 = (bf16[4,64,1536]{2,1,0:T(8,128)(2,1)S(1)}, bf16[4,64,1536]{2,1,0:T(8,128)(2,1)}, u32[]{:S(2)}, u32[]{:S(2)}) collective-permute-start(bf16[4,64,1536]{2,1,0:T(8,128)(2,1)S(1)} %pad_maximum_fusion.refs_0_), channel_id=1, source_target_pairs={{0,4},{1,5},{2,6},{3,7},{4,8},{5,9},{6,10},{7,11},{8,12},{9,13},{1... | collective-permute-start | bytes 2359304 | tf_op jit(solution)/shard_map/ppermute | solution.py:28
  94.3 16.8 %collective-permute-start.20 = (bf16[4,64,1536]{2,1,0:T(8,128)(2,1)S(1)}, bf16[4,64,1536]{2,1,0:T(8,128)(2,1)}, u32[]{:S(2)}, u32[]{:S(2)}) collective-permute-start(bf16[4,64,1536]{2,1,0:T(8,128)(2,1)S(1)} %pad_maximum_fusion.refs_0_), channel_id=1, source_target_pairs={{0,12},{1,13},{2,14},{3,15},{4,0},{5,1},{6,2},{7,3},{8,4},{9,5},{1... | collective-permute-start | bytes 2359304 | tf_op jit(solution)/shard_map/ppermute | solution.py:28
  112.1 10.9 %collective-permute-start.22 = (bf16[2,64,1536]{2,1,0:T(8,128)(2,1)S(1)}, bf16[2,64,1536]{2,1,0:T(8,128)(2,1)}, u32[]{:S(2)}, u32[]{:S(2)}) collective-permute-start(bf16[2,64,1536]{2,1,0:T(8,128)(2,1)S(1)} %slice.140), channel_id=1, source_target_pairs={{0,4},{1,5},{2,6},{3,7},{4,8},{5,9},{6,10},{7,11},{8,12},{9,13},{1... | collective-permute-start | bytes 1179656 | tf_op jit(solution)/shard_map/ppermute | solution.py:28
  114.5 8.5 %collective-permute-start.23 = (bf16[2,64,1536]{2,1,0:T(8,128)(2,1)}, bf16[2,64,1536]{2,1,0:T(8,128)(2,1)}, u32[]{:S(2)}, u32[]{:S(2)}) collective-permute-start(bf16[2,64,1536]{2,1,0:T(8,128)(2,1)} %slice.141), channel_id=1, source_target_pairs={{0,12},{1,13},{2,14},{3,15},{4,0},{5,1},{6,2},{7,3},{8,4},{9,5},{1... | collective-permute-start | bytes 1179656 | tf_op jit(solution)/shard_map/ppermute | solution.py:28
  117.7 8.0 %collective-permute-start.24 = (bf16[2,64,1536]{2,1,0:T(8,128)(2,1)S(1)}, bf16[2,64,1536]{2,1,0:T(8,128)(2,1)}, u32[]{:S(2)}, u32[]{:S(2)}) collective-permute-start(bf16[2,64,1536]{2,1,0:T(8,128)(2,1)S(1)} %slice.142), channel_id=1, source_target_pairs={{0,1},{1,2},{2,3},{3,0},{4,5},{5,6},{6,7},{7,4},{8,9},{9,10},{10,1... | collective-permute-start | bytes 1179656 | tf_op jit(solution)/shard_map/ppermute | solution.py:28
  118.8 7.5 %collective-permute-start.25 = (bf16[2,64,1536]{2,1,0:T(8,128)(2,1)S(1)}, bf16[2,64,1536]{2,1,0:T(8,128)(2,1)}, u32[]{:S(2)}, u32[]{:S(2)}) collective-permute-start(bf16[2,64,1536]{2,1,0:T(8,128)(2,1)S(1)} %slice.143), channel_id=1, source_target_pairs={{0,3},{1,0},{2,1},{3,2},{4,7},{5,4},{6,5},{7,6},{8,11},{9,8},{10,9... | collective-permute-start | bytes 1179656 | tf_op jit(solution)/shard_map/ppermute | solution.py:28
  164.9 7.9 %collective-permute-start.26 = (bf16[2,64,1536]{2,1,0:T(8,128)(2,1)S(1)}, bf16[2,64,1536]{2,1,0:T(8,128)(2,1)S(1)}, u32[]{:S(2)}, u32[]{:S(2)}) collective-permute-start(bf16[2,64,1536]{2,1,0:T(8,128)(2,1)S(1)} %get-tuple-element.73), channel_id=1, source_target_pairs={{0,4},{1,5},{2,6},{3,7},{4,8},{5,9},{6,10},{7,11},{8,12},{9,13},{1... | collective-permute-start | bytes 1179656 | tf_op jit(solution)/shard_map/ppermute | solution.py:28
  165.1 8.5 %collective-permute-start.27 = (bf16[2,64,1536]{2,1,0:T(8,128)(2,1)S(1)}, bf16[2,64,1536]{2,1,0:T(8,128)(2,1)S(1)}, u32[]{:S(2)}, u32[]{:S(2)}) collective-permute-start(bf16[2,64,1536]{2,1,0:T(8,128)(2,1)S(1)} %get-tuple-element.71), channel_id=1, source_target_pairs={{0,1},{1,2},{2,3},{3,0},{4,5},{5,6},{6,7},{7,4},{8,9},{9,10},{10,1... | collective-permute-start | bytes 1179656 | tf_op jit(solution)/shard_map/ppermute | solution.py:28
  165.2 8.5 %collective-permute-start.28 = (bf16[2,64,1536]{2,1,0:T(8,128)(2,1)S(1)}, bf16[2,64,1536]{2,1,0:T(8,128)(2,1)S(1)}, u32[]{:S(2)}, u32[]{:S(2)}) collective-permute-start(bf16[2,64,1536]{2,1,0:T(8,128)(2,1)S(1)} %get-tuple-element.72), channel_id=1, source_target_pairs={{0,12},{1,13},{2,14},{3,15},{4,0},{5,1},{6,2},{7,3},{8,4},{9,5},{1... | collective-permute-start | bytes 1179656 | tf_op jit(solution)/shard_map/ppermute | solution.py:28
  167.9 8.0 %collective-permute-start.29 = (bf16[2,64,1536]{2,1,0:T(8,128)(2,1)S(1)}, bf16[2,64,1536]{2,1,0:T(8,128)(2,1)S(1)}, u32[]{:S(2)}, u32[]{:S(2)}) collective-permute-start(bf16[2,64,1536]{2,1,0:T(8,128)(2,1)S(1)} %get-tuple-element.70), channel_id=1, source_target_pairs={{0,3},{1,0},{2,1},{3,2},{4,7},{5,4},{6,5},{7,6},{8,11},{9,8},{10,9... | collective-permute-start | bytes 1179656 | tf_op jit(solution)/shard_map/ppermute | solution.py:28
  176.1 15.8 %collective-permute-start.33 = (bf16[4,64,1536]{2,1,0:T(8,128)(2,1)S(1)}, bf16[4,64,1536]{2,1,0:T(8,128)(2,1)S(1)}, u32[]{:S(2)}, u32[]{:S(2)}) collective-permute-start(bf16[4,64,1536]{2,1,0:T(8,128)(2,1)S(1)} %pad_maximum_fusion.5), channel_id=1, source_target_pairs={{0,3},{1,0},{2,1},{3,2},{4,7},{5,4},{6,5},{7,6},{8,11},{9,8},{10,9... | collective-permute-start | bytes 2359304 | tf_op jit(solution)/shard_map/ppermute | solution.py:28
  179.7 12.2 %collective-permute-start.32 = (bf16[4,64,1536]{2,1,0:T(8,128)(2,1)S(1)}, bf16[4,64,1536]{2,1,0:T(8,128)(2,1)S(1)}, u32[]{:S(2)}, u32[]{:S(2)}) collective-permute-start(bf16[4,64,1536]{2,1,0:T(8,128)(2,1)S(1)} %pad_maximum_fusion.4), channel_id=1, source_target_pairs={{0,12},{1,13},{2,14},{3,15},{4,0},{5,1},{6,2},{7,3},{8,4},{9,5},{1... | collective-permute-start | bytes 2359304 | tf_op jit(solution)/shard_map/ppermute | solution.py:28
  180.0 12.1 %collective-permute-start.31 = (bf16[4,64,1536]{2,1,0:T(8,128)(2,1)S(1)}, bf16[4,64,1536]{2,1,0:T(8,128)(2,1)S(1)}, u32[]{:S(2)}, u32[]{:S(2)}) collective-permute-start(bf16[4,64,1536]{2,1,0:T(8,128)(2,1)S(1)} %pad_maximum_fusion.3), channel_id=1, source_target_pairs={{0,1},{1,2},{2,3},{3,0},{4,5},{5,6},{6,7},{7,4},{8,9},{9,10},{10,1... | collective-permute-start | bytes 2359304 | tf_op jit(solution)/shard_map/ppermute | solution.py:28
  180.3 12.1 %collective-permute-start.30 = (bf16[4,64,1536]{2,1,0:T(8,128)(2,1)S(1)}, bf16[4,64,1536]{2,1,0:T(8,128)(2,1)S(1)}, u32[]{:S(2)}, u32[]{:S(2)}) collective-permute-start(bf16[4,64,1536]{2,1,0:T(8,128)(2,1)S(1)} %pad_maximum_fusion.2), channel_id=1, source_target_pairs={{0,4},{1,5},{2,6},{3,7},{4,8},{5,9},{6,10},{7,11},{8,12},{9,13},{1... | collective-permute-start | bytes 2359304 | tf_op jit(solution)/shard_map/ppermute | solution.py:28
  192.8 8.5 %collective-permute-start.34 = (bf16[64,1536]{1,0:T(8,128)(2,1)S(1)}, bf16[64,1536]{1,0:T(8,128)(2,1)S(1)}, u32[]{:S(2)}, u32[]{:S(2)}) collective-permute-start(bf16[64,1536]{1,0:T(8,128)(2,1)S(1)} %get-tuple-element.64), channel_id=1, source_target_pairs={{0,1},{1,2},{2,3},{3,0},{4,5},{5,6},{6,7},{7,4},{8,9},{9,10},{10,1... | collective-permute-start | bytes 589832 | tf_op jit(solution)/shard_map/ppermute | solution.py:28
  193.5 9.3 %collective-permute-start.35 = (bf16[64,1536]{1,0:T(8,128)(2,1)S(1)}, bf16[64,1536]{1,0:T(8,128)(2,1)S(1)}, u32[]{:S(2)}, u32[]{:S(2)}) collective-permute-start(bf16[64,1536]{1,0:T(8,128)(2,1)S(1)} %get-tuple-element.66), channel_id=1, source_target_pairs={{0,3},{1,0},{2,1},{3,2},{4,7},{5,4},{6,5},{7,6},{8,11},{9,8},{10,9... | collective-permute-start | bytes 589832 | tf_op jit(solution)/shard_map/ppermute | solution.py:28
  195.9 10.5 %collective-permute-start.36 = (bf16[64,1536]{1,0:T(8,128)(2,1)S(1)}, bf16[64,1536]{1,0:T(8,128)(2,1)S(1)}, u32[]{:S(2)}, u32[]{:S(2)}) collective-permute-start(bf16[64,1536]{1,0:T(8,128)(2,1)S(1)} %get-tuple-element.65), channel_id=1, source_target_pairs={{0,2},{1,3},{2,0},{3,1},{4,6},{5,7},{6,4},{7,5},{8,10},{9,11},{10,... | collective-permute-start | bytes 589832 | tf_op jit(solution)/shard_map/ppermute | solution.py:28
  197.4 9.1 %collective-permute-start.37 = (bf16[64,1536]{1,0:T(8,128)(2,1)S(1)}, bf16[64,1536]{1,0:T(8,128)(2,1)S(1)}, u32[]{:S(2)}, u32[]{:S(2)}) collective-permute-start(bf16[64,1536]{1,0:T(8,128)(2,1)S(1)} %get-tuple-element.67), channel_id=1, source_target_pairs={{0,4},{1,5},{2,6},{3,7},{4,8},{5,9},{6,10},{7,11},{8,12},{9,13},{1... | collective-permute-start | bytes 589832 | tf_op jit(solution)/shard_map/ppermute | solution.py:28
  197.7 8.8 %collective-permute-start.38 = (bf16[64,1536]{1,0:T(8,128)(2,1)S(1)}, bf16[64,1536]{1,0:T(8,128)(2,1)S(1)}, u32[]{:S(2)}, u32[]{:S(2)}) collective-permute-start(bf16[64,1536]{1,0:T(8,128)(2,1)S(1)} %get-tuple-element.69), channel_id=1, source_target_pairs={{0,12},{1,13},{2,14},{3,15},{4,0},{5,1},{6,2},{7,3},{8,4},{9,5},{1... | collective-permute-start | bytes 589832 | tf_op jit(solution)/shard_map/ppermute | solution.py:28
  250.6 13.7 %all-to-all-start.3 = ((f32[128,1,128]{2,1,0:T(1,128)}), f32[128,1,128]{2,1,0:T(1,128)S(1)}, u32[]{:S(2)}, u32[]{:S(2)}) async-start(f32[128,1,128]{2,1,0:T(1,128)} %broadcast_in_dim.140), calls=%async_computation.3 | async-start | bytes 131072 | tf_op jit(solution)/shard_map/all_to_all | solution.py:426
  (31 other events, 526.2 us)

commit v2 on v1

v2 whole, which is shorter than its diff:
```python
import functools

import jax
import jax.numpy as jnp
import numpy as np
from jax import lax
from jax.experimental import pallas as pl
from jax.experimental.pallas import tpu as pltpu
from jax.sharding import PartitionSpec as P

HEADS = 24
KV_HEADS = 8
HEAD = 64
EXPERTS = 40
TOP = 8
CAP = 40
EPSILON = 1e-05
ROPE_BASE = 10000.0
MASKED = -1e30
SIDE = 4
BF = jnp.bfloat16
F32 = jnp.float32
WHOLE = ("seq", "grp")


def shift(rows, phase, step):
    pairs = []
    for s in range(8):
        for i in range(16):
            if s % 2 == phase:
                to = i // SIDE * SIDE + (i % SIDE + step) % SIDE
            else:
                to = (i // SIDE + step) % SIDE * SIDE + i % SIDE
            pairs.append((s * 16 + i, s * 16 + to))
    return lax.ppermute(rows, WHOLE, pairs)


def partner(rows):
    return lax.ppermute(rows, "seq", [(s, s ^ 1) for s in range(8)])


def wide(v):
    return v.astype(F32)


def dot_t(lhs, rhs):
    return lax.dot_general(lhs, rhs, (((1,), (1,)), ((), ())), preferred_element_type=F32)


def attention_kernel(*refs):
    tok = refs[0:6]
    adapt = refs[6:14]
    (gain, gain_moe, cosine, sine, key_doc, key_index, doc, index, colp, colr, wq_hbm, wk_hbm,
     wv_hbm, wo_hbm, mixed_out, moe_out,
     wq, wk, wv, wo, xn, ad, qbuf, kbuf, vbuf, att, sems) = refs[14:]
    copies = [pltpu.make_async_copy(src, dst, sems.at[i]) for i, (src, dst) in enumerate(
        [(wk_hbm, wk), (wv_hbm, wv), (wq_hbm, wq), (wo_hbm, wo)])]
    for copy in copies:
        copy.start()
    count = tok[0].shape[0]
    for j in range(8):
        ad[48 * j:48 * j + 48, :] = adapt[j][...]

    def norm(rows, scale):
        inverse = lax.rsqrt(jnp.mean(rows * rows, axis=-1, keepdims=True) + EPSILON)
        return (rows * inverse * scale).astype(BF)

    for b in range(6):
        xn[b * count:(b + 1) * count, :] = norm(tok[b][...].astype(F32), gain[...])
    copies[0].wait()
    copies[1].wait()
    col_prompt = colp[...]
    col_row = colr[...]

    def low(z, roll, first, docs):
        moved = pltpu.roll(z, roll, 1)
        keep = (docs == col_prompt) & (col_row >= first) & (col_row < first + 2)
        return jnp.where(keep, moved, 0.0).astype(BF)

    lane = lax.broadcasted_iota(jnp.int32, (count, 128), 1)
    lower = (lane & 63) < 32

    def rope(u, cos_t, sin_t):
        turned = jnp.where(lower, pltpu.roll(u, 96, 1), pltpu.roll(u, 32, 1))
        return (u * cos_t + turned * sin_t).astype(BF)

    def key_block(b, carry):
        at = pl.multiple_of(b * count, count)
        rows = xn[pl.ds(at, count), :]
        docs = doc[pl.ds(at, count), :]
        z = dot_t(rows, ad[...])
        keys = jnp.dot(rows, wk[...], preferred_element_type=F32) + jnp.dot(
            low(z, 10, 12, docs), ad[:, :512], preferred_element_type=F32)
        values = jnp.dot(rows, wv[...], preferred_element_type=F32) + jnp.dot(
            low(z, 8, 12, docs), ad[:, 512:1024], preferred_element_type=F32)
        vbuf[pl.ds(at, count), :] = values.astype(BF)
        cos_t = cosine[pl.ds(at, count), :]
        sin_t = sine[pl.ds(at, count), :]
        for c in range(4):
            kbuf[pl.ds(at, count), 128 * c:128 * c + 128] = rope(
                keys[:, 128 * c:128 * c + 128], cos_t, sin_t)
        return carry

    lax.fori_loop(0, 6, key_block, 0)
    copies[2].wait()
    own = xn[0:count, :]
    docs = doc[0:count, :]
    z = dot_t(own, ad[...])
    zq = low(z, 8, 8, docs)
    cos_t = cosine[0:count, :]
    sin_t = sine[0:count, :]
    low_half = lane < 64
    allowed = (docs == key_doc[...]) & (key_index[...] <= index[...])
    bias = jnp.where(allowed, 0.0, MASKED)

    def query_block(c, carry):
        at = pl.multiple_of(c * 384, 128)
        u = jnp.dot(own, wq[:, pl.ds(at, 384)], preferred_element_type=F32) + jnp.dot(
            zq, ad[:, pl.ds(at, 384)], preferred_element_type=F32)
        for t in range(3):
            qbuf[:, pl.ds(pl.multiple_of(at + 128 * t, 128), 128)] = rope(
                u[:, 128 * t:128 * t + 128], cos_t, sin_t)
        return carry

    lax.fori_loop(0, 4, query_block, 0)

    def pair(j, carry):
        kv = pl.ds(pl.multiple_of(j * 128, 128), 128)
        keys = kbuf[:, kv]
        values = vbuf[:, kv]
        tiles = [qbuf[:, pl.ds(pl.multiple_of(j * 384 + 128 * t, 128), 128)] for t in range(3)]
        results = []
        for h in range(6):
            own_low, kv_low = h % 2 == 0, h < 3
            q = tiles[h // 2].astype(F32)
            if own_low != kv_low:
                q = pltpu.roll(q, 64, 1)
            q = jnp.where(low_half if kv_low else ~low_half, q, 0.0).astype(BF)
            s = dot_t(q, keys) * (HEAD ** -0.5) + bias
            top = jnp.max(s, axis=-1, keepdims=True)
            w = jnp.exp(s - top)
            total = jnp.sum(w, axis=-1, keepdims=True)
            o = jnp.dot(w.astype(BF), values, preferred_element_type=F32) / total
            if own_low != kv_low:
                o = pltpu.roll(o, 64, 1)
            results.append(o)
        for t in range(3):
            att[:, pl.ds(pl.multiple_of(j * 384 + 128 * t, 128), 128)] = jnp.where(
                low_half, results[2 * t], results[2 * t + 1]).astype(BF)
        return carry

    lax.fori_loop(0, 4, pair, 0)
    copies[3].wait()
    attended = att[...]
    zo = low(dot_t(attended, ad[...]), 4, 10, docs)
    mixed = (tok[0][...].astype(F32) + jnp.dot(attended, wo[...], preferred_element_type=F32)
             + jnp.dot(zo, ad[...], preferred_element_type=F32)).astype(BF)
    mixed_out[...] = mixed
    moe_out[...] = norm(mixed.astype(F32), gain_moe[...])


def attention(tok, adapt, *others):
    count, width = tok[0].shape
    wq, wk, wv, wo = others[-4:]
    vm = pl.BlockSpec(memory_space=pltpu.VMEM)
    anywhere = pl.BlockSpec(memory_space=pl.ANY)
    rows = jax.ShapeDtypeStruct((count, width), BF)
    return pl.pallas_call(
        attention_kernel,
        out_shape=(rows, rows),
        in_specs=[vm] * (10 + len(others)) + [anywhere] * 4,
        out_specs=(vm, vm),
        scratch_shapes=[
            pltpu.VMEM(wq.shape, BF), pltpu.VMEM(wk.shape, BF), pltpu.VMEM(wv.shape, BF),
            pltpu.VMEM(wo.shape, BF), pltpu.VMEM((6 * count, width), BF),
            pltpu.VMEM((384, width), BF), pltpu.VMEM((count, width), BF),
            pltpu.VMEM((6 * count, 512), BF), pltpu.VMEM((6 * count, 512), BF),
            pltpu.VMEM((count, width), BF), pltpu.SemaphoreType.DMA((4,)),
        ],
        compiler_params=pltpu.CompilerParams(vmem_limit_bytes=48 << 20),
        cost_estimate=pl.CostEstimate(flops=6 << 30, transcendentals=0,
                                      bytes_accessed=16 << 20),
        name="attention_block",
    )(*tok, *adapt, *others)


def expert_kernel(sizes, *refs):
    n = len(sizes)
    pieces, (first, table, gate_hbm, up_hbm, down_hbm) = refs[:n], refs[n:n + 5]
    outs = refs[n + 5:2 * n + 5]
    x, xe, ho, scale, gate, up, down, sem_x, sem_w, sem_o = refs[2 * n + 5:]
    pairs = sum(sizes) // 2
    rows_all = pairs * 2 * CAP
    starts = [sum(sizes[:k]) for k in range(n)]
    loads = [pltpu.make_async_copy(pieces[k], x.at[pl.ds(starts[k], sizes[k])], sem_x.at[k])
             for k in range(n)]
    for copy in loads:
        copy.start()
    odd = first[0]
    order = [odd, odd + 1, odd + 2, odd + 3, 4 - 4 * odd]
    weights = []
    for s in range(5):
        weights.append([pltpu.make_async_copy(src.at[order[s]], dst, sem_w.at[3 * s + k])
                        for k, (src, dst) in enumerate(
                            [(gate_hbm, gate.at[s]), (up_hbm, up.at[s]),
                             (down_hbm, down.at[pl.ds(256 * s, 256)])])])
        for copy in weights[-1]:
            copy.start()
    row = lax.broadcasted_iota(jnp.int32, (256, 256), 0)
    col = lax.broadcasted_iota(jnp.int32, (256, 256), 1)
    before = ((row < col) & ((row < 128) == (col < 128))).astype(BF)
    slot = lax.broadcasted_iota(jnp.int32, (2 * CAP, 256), 0).astype(F32)
    base = jnp.where(lax.broadcasted_iota(jnp.int32, (8, 256), 1) < 128, 0.0, float(CAP))
    for copy in loads:
        copy.wait()

    def places(i):
        named = table[i] > 0.0
        rank = jnp.dot(named.astype(F32).astype(BF), before, preferred_element_type=F32) + base
        rank = jnp.where(named, rank, -1.0)
        return [slot == rank[e:e + 1, :] for e in range(3)]

    def take(i, carry):
        spots = places(i)
        block = jnp.concatenate([x[2 * i], x[2 * i + 1]])
        hot = jnp.concatenate([jnp.where(p, 1.0, 0.0) for p in spots]).astype(BF)
        rows = jnp.dot(hot, block, preferred_element_type=F32).astype(BF)
        at = pl.ds(pl.multiple_of(i * 2 * CAP, 16), 2 * CAP)
        given = table[i]
        for e in range(3):
            xe[e, at, :] = rows[e * 2 * CAP:(e + 1) * 2 * CAP]
            scale[e, at, :] = jnp.sum(jnp.where(spots[e], given[e:e + 1, :], 0.0), axis=1,
                                      keepdims=True)
        return carry

    lax.fori_loop(0, pairs, take, 0)
    size = min(rows_all, 320)
    for e in range(3):
        halves = [2 * e, 2 * e + 1] if e < 2 else [4]
        for s in halves:
            for copy in weights[s]:
                copy.wait()

        def run(c, carry, e=e, halves=halves):
            at = pl.ds(pl.multiple_of(c * size, 16), size)
            rows = xe[e, at, :]
            hidden = []
            for s in halves:
                g = jnp.dot(rows, gate[s], preferred_element_type=F32)
                u = jnp.dot(rows, up[s], preferred_element_type=F32)
                hidden.append((g / (1.0 + jnp.exp(-g)) * u).astype(BF))
            hidden = jnp.concatenate(hidden, axis=1)
            maps = down[512 * e:512 * e + 256 * len(halves), :]
            out = jnp.dot(hidden, maps, preferred_element_type=F32)
            ho[e, at, :] = (out * scale[e, at, :]).astype(BF)
            return carry

        lax.fori_loop(0, rows_all // size, run, 0)

    def combine(i, carry):
        hot = jnp.concatenate([jnp.where(p, 1.0, 0.0) for p in places(i)]).astype(BF)
        at = pl.ds(pl.multiple_of(i * 2 * CAP, 16), 2 * CAP)
        rows = jnp.concatenate([ho[e, at, :] for e in range(3)])
        total = lax.dot_general(hot, rows, (((0,), (0,)), ((), ())),
                                preferred_element_type=F32).astype(BF)
        x[2 * i] = total[:128]
        x[2 * i + 1] = total[128:]
        return carry

    lax.fori_loop(0, pairs, combine, 0)
    stores = [pltpu.make_async_copy(x.at[pl.ds(starts[k], sizes[k])], outs[k], sem_o.at[k])
              for k in range(n)]
    for copy in stores:
        copy.start()
    for copy in stores:
        copy.wait()


def experts(pieces, first, table, gate, up, down):
    sizes = [piece.shape[0] for piece in pieces]
    total, width = sum(sizes), gate.shape[1]
    rows = total * CAP
    anywhere = pl.BlockSpec(memory_space=pl.ANY)
    vm = pl.BlockSpec(memory_space=pltpu.VMEM)
    return pl.pallas_call(
        functools.partial(expert_kernel, sizes),
        out_shape=tuple(jax.ShapeDtypeStruct(piece.shape, BF) for piece in pieces),
        in_specs=[anywhere] * len(sizes) + [pl.BlockSpec(memory_space=pltpu.SMEM), vm]
        + [anywhere] * 3,
        out_specs=(anywhere,) * len(sizes),
        scratch_shapes=[
            pltpu.VMEM((total, 128, width), BF), pltpu.VMEM((3, rows, width), BF),
            pltpu.VMEM((3, rows, width), BF), pltpu.VMEM((3, rows, 1), F32),
            pltpu.VMEM(gate.shape, BF), pltpu.VMEM(up.shape, BF),
            pltpu.VMEM((5 * 256, width), BF),
            pltpu.SemaphoreType.DMA((len(sizes),)), pltpu.SemaphoreType.DMA((15,)),
            pltpu.SemaphoreType.DMA((len(sizes),)),
        ],
        compiler_params=pltpu.CompilerParams(vmem_limit_bytes=44 << 20),
        cost_estimate=pl.CostEstimate(flops=rows * 6 * 1536 * 256 * 5, transcendentals=0,
                                      bytes_accessed=12 << 20),
        name="expert_block",
    )(*pieces, first, table, gate, up, down)


def rms_scaled(features, scales):
    features = features.astype(F32)
    inverse = lax.rsqrt(jnp.mean(features * features, axis=-1, keepdims=True) + EPSILON)
    return (features * inverse * scales).astype(BF)


def body(tokens, lengths, prompt_adapter, routes, routing_weight, attention_gain, query_weight,
         key_weight, value_weight, output_weight, adapter_down_maps, adapter_up_query_output,
         adapter_up_key_value, expert_gain, gate_weight, up_weight, down_weight, closing_gain,
         vocab_projection):
    own = tokens[0]
    count, width = own.shape
    me, grp = lax.axis_index("seq"), lax.axis_index("grp")

    listing = np.concatenate([np.array([0, 1, 2] if g % 2 == 0 else [1, 2, 0]) + 5 * g // 2
                              for g in range(16)]).astype(np.int32)
    ids, given = routes[0], routing_weight[0]
    table = jnp.sum(jnp.where(ids.T[None] == jnp.asarray(listing)[:, None, None],
                              given.T[None], 0.0), axis=1).reshape(16, 3 * count)
    high = lax.reduce_precision(table, 8, 7)
    low = table - high
    route_rows = jnp.concatenate(
        [high, low, jnp.zeros((16, width - 6 * count), F32)], axis=1).astype(BF)

    ranks = (jnp.arange(16, dtype=jnp.int32)[:, None]
             == 2 * me + jnp.arange(2, dtype=jnp.int32)[None, :]).astype(BF)
    downs = jnp.einsum("rk,pdr->pkd", ranks, adapter_down_maps[:, 0],
                       preferred_element_type=F32).astype(BF).reshape(8, width)
    ups = lax.dynamic_slice_in_dim(adapter_up_query_output[:, 0], 2 * me, 2, 1).reshape(4, width)
    thin = lax.dynamic_slice_in_dim(adapter_up_key_value[:, 0], 2 * me, 2, 1)
    thin = jnp.concatenate([thin[0], thin[1], jnp.zeros((2, width - 1024), BF)], axis=1)
    maps = jnp.concatenate([downs, ups, thin], axis=0)
    payload = jnp.concatenate(
        [jnp.broadcast_to(maps[None], (16, 14, width)), route_rows[:, None, :],
         jnp.zeros((16, 1, width), BF)], axis=1)
    payload, own = lax.optimization_barrier((payload, own))
    held = lax.all_to_all(payload, "grp", 0, 0, tiled=True)
    back1 = lax.ppermute(own, "seq", [(s, s + 2) for s in range(6)])
    back2 = lax.ppermute(own, "seq", [(s, s + 4) for s in range(4)])
    picked = jnp.stack([lax.dynamic_index_in_dim(held, prompt_adapter[0, p], 0, False)
                        for p in range(3)]).reshape(48, width)
    turn = [picked] + [lax.ppermute(picked, "seq", [(s, (s + d) % 8) for s in range(8)])
                       for d in (2, 6, 4)]
    adapt = turn + [partner(piece) for piece in turn]
    tok = [own, back1, back2]
    tok = tok + [partner(rows) for rows in tok]

    lens = lengths[0]
    ends = jnp.cumsum(lens)
    starts = ends - lens
    other = me ^ 1
    blocks = jnp.stack([me, me - 2, me - 4, other, other - 2, other - 4])
    row = jnp.arange(count, dtype=jnp.int32)
    index = (blocks[:, None] * count + row[None, :]).reshape(-1)
    document = jnp.sum((index[:, None] >= ends[None, :]).astype(jnp.int32), axis=1)
    half = HEAD // 2
    frequency = ROPE_BASE ** (-(jnp.arange(128, dtype=jnp.int32) % half).astype(F32) / half)
    sign = jnp.where(jnp.arange(128) % HEAD < half, -1.0, 1.0).astype(F32)
    near = row.astype(F32)[:, None] * frequency[None, :]
    far = (blocks[:, None] * count - starts[None, :]).astype(F32)[:, :, None] * frequency
    near_cos, near_sin = jnp.cos(near)[None], jnp.sin(near)[None]
    far_cos, far_sin = jnp.cos(far), jnp.sin(far)

    def by_document(values):
        docs = document.reshape(6, count, 1)
        return jnp.where(docs == 0, values[:, None, 0], jnp.where(
            docs == 1, values[:, None, 1], values[:, None, 2]))

    far_cos, far_sin = by_document(far_cos), by_document(far_sin)
    cosine = (far_cos * near_cos - far_sin * near_sin).reshape(6 * count, 128)
    sine = ((far_sin * near_cos + far_cos * near_sin) * sign).reshape(6 * count, 128)
    row_index = index[:count]
    columns = jnp.arange(384, dtype=jnp.int32)[None, :]
    key_document = jnp.where(index >= 0, document, -1)

    mixed, moe_in = attention(
        tok, adapt, attention_gain[None], expert_gain[None], cosine, sine, key_document[None],
        index[None], document[:, None], row_index[:, None], columns // 16 % 3, columns % 16,
        query_weight, key_weight, value_weight, output_weight)

    rel = jnp.array([0, 3, 1, 2], jnp.int32)
    first, second = jnp.where(me % 2 == 0, grp % 4, grp // 4), jnp.where(
        me % 2 == 0, grp // 4, grp % 4)
    first, second = (first + rel[None, :]) % 4, (second + rel[:, None]) % 4
    source = jnp.where(me % 2 == 0, second * 4 + first, first * 4 + second).reshape(16)
    order = (source[:, None] == jnp.arange(16, dtype=jnp.int32)[None, :]).astype(F32)
    route_in = jnp.dot(order, held[:, 14, :].astype(F32), precision=lax.Precision.HIGHEST)
    route_in = (route_in[:, :3 * count] + route_in[:, 3 * count:6 * count]).reshape(8, 2, 3, count)
    route_in = jnp.concatenate([route_in, jnp.zeros((8, 2, 5, count), F32)], axis=2)
    route_in = route_in.transpose(0, 2, 1, 3).reshape(8, 8, 2 * count)
    odd = (grp % 2).astype(jnp.int32)[None]
    weights = (gate_weight, up_weight, down_weight)

    line = lax.optimization_barrier(
        [shift(moe_in, 0, 1), shift(moe_in, 0, -1), shift(moe_in, 0, 2)])
    plane = jnp.stack([moe_in] + line)
    minus, plus = shift(plane, 1, 1), shift(plane, 1, -1)
    (done_own,) = experts([plane], odd, route_in[:2], *weights)
    minus, plus, done_own = lax.optimization_barrier((minus, plus, done_own))
    ahead, behind = shift(minus[:2], 1, 1), shift(plus[2:], 1, -1)
    done_minus, done_plus = experts([minus, plus], odd, route_in[2:6], *weights)
    ahead, behind, done_minus, done_plus = lax.optimization_barrier(
        (ahead, behind, done_minus, done_plus))
    done_ahead, done_behind = experts([ahead, behind], odd, route_in[6:], *weights)

    ahead, behind = lax.optimization_barrier(
        (shift(done_ahead, 1, 1), shift(done_behind, 1, -1)))
    plus = jnp.concatenate([(wide(done_plus[:2]) + wide(ahead)).astype(BF), done_plus[2:]])
    minus = jnp.concatenate([done_minus[:2], (wide(done_minus[2:]) + wide(behind)).astype(BF)])
    plus, minus = lax.optimization_barrier((shift(plus, 1, 1), shift(minus, 1, -1)))
    plane = wide(done_own) + wide(plus) + wide(minus)
    low = plane[1:].astype(BF)
    line = lax.optimization_barrier(
        [shift(low[1], 0, 1), shift(low[0], 0, -1), shift(low[2], 0, 2)])
    combined = plane[0] + wide(line[0]) + wide(line[1]) + wide(line[2])
    hidden_out = (mixed.astype(F32) + combined).astype(BF)

    selector = (ends[:, None] - 1 == row_index[None, :]).astype(BF)
    last = jnp.dot(selector, hidden_out, preferred_element_type=F32)
    last = rms_scaled(last, closing_gain)
    part = width // 8
    split = last.reshape(3, 8, part).transpose(1, 0, 2)
    mine = lax.all_to_all(split, "seq", 0, 0, tiled=True)
    mine = jnp.sum(mine.astype(F32), axis=0).astype(BF)
    everyone = lax.all_to_all(jnp.broadcast_to(mine[None], (128, 3, part)), WHOLE, 0, 0,
                              tiled=True)
    final_rows = everyone.reshape(8, 48, part).transpose(1, 0, 2).reshape(48, width)
    logits = jnp.dot(final_rows, vocab_projection, preferred_element_type=F32)
    top = jnp.max(logits, axis=1)
    mass = jnp.sum(jnp.exp(logits - top[:, None]), axis=1)
    stats = jnp.concatenate([top, mass, jnp.zeros((32,), F32)])
    stats = lax.all_to_all(jnp.broadcast_to(stats[None], (128, 128)), WHOLE, 0, 0, tiled=True)
    tops = stats[:, :48]
    peak = jnp.max(tops, axis=0)
    total = jnp.sum(stats[:, 48:96] * jnp.exp(tops - peak[None]), axis=0)
    log_probs = logits - (peak + jnp.log(total))[:, None]
    return hidden_out[None], log_probs


def solution(mesh):
    placed = (
        P("grp", "seq", None), P("grp", None), P("grp", None), P("grp", "seq", None),
        P("grp", "seq", None), P(), P(), P(), P(), P(), P(None, "grp", None, None),
        P(None, "grp", None, None), P(None, "grp", None, None), P(), P("grp", None, None),
        P("grp", None, None), P("grp", None, None), P(), P(None, WHOLE),
    )
    return jax.shard_map(
        body,
        mesh=mesh,
        in_specs=placed,
        out_specs=(P("grp", "seq", None), P(None, WHOLE)),
        check_vma=False,
    )
```

time: 266 us -> 241 us (0.906)
  starting transfers between devices: 68.8 us -> 44.8 us
  Pallas kernels: 60.6 us -> 48.1 us
  blocking collectives: 40.7 us -> 49.8 us
  waiting for transfers between devices: 55.9 us -> 63 us
  other arithmetic: 14.2 us -> 9.81 us
    ppermute x28 -> x14, starting transfers between devices: 40.2 us -> 17.7 us  [shift(): return lax.ppermute(rows, WHOLE, pairs)]
    ppermute x28 -> x14, waiting for transfers between devices: 43.2 us -> 57.8 us  [shift(): return lax.ppermute(rows, WHOLE, pairs)]
    all_to_all x0 -> x1, blocking collectives: none -> 13.6 us  [body(): lax.all_to_all(jnp.broadcast_to(stats[None], (128, 128)), WHOLE, 0, 0, ti...]
    pallas_call x2 -> x4, Pallas kernels: 60.6 us -> 48.1 us  [the longest x1 24.8 us: attention(): pl.pallas_call(attention_kernel, out_shape=(rows, rows), in_specs=[vm] *...]
    all_to_all x1 -> x0, waiting for transfers between devices: 8.93 us -> none  [body(): lax.all_to_all(jnp.broadcast_to(stats[None], (128, 128)), WHOLE, 0, 0, ti...]
    unnamed x42 -> x40, local copies, waits for them, and re-layouts: 0.1 us -> 5.93 us
    slice x13 -> x6, local copies, waits for them, and re-layouts: 7.48 us -> 2.48 us  [the longest x2 2.37 us: body(): ahead, behind = (shift(minus[:2], 1, 1), shift(plus[2:], 1, -1))]
    all_to_all x1, waiting for transfers between devices: 0.01 us -> 4.38 us  [body(): held = lax.all_to_all(payload, 'grp', 0, 0, tiled=True)]
  transfers between devices with their start and end apart: 42 -> 27, of which waited for: 20 -> 10; matrix products, arithmetic and copies ran while one was open for 10% -> 5% of each run, Pallas kernels for 0% -> 7%
where the time goes in v2:
time: 241 us; the launch traced here: 240 us
  waiting for transfers between devices  63 us (26%)
  blocking collectives  49.8 us (21%)
  Pallas kernels  48.1 us (20%)
  starting transfers between devices  44.8 us (19%)
  local copies, waits for them, and re-layouts  15.9 us (7%)
  other arithmetic  9.81 us (4%)
  between operations  6.95 us (3%)
    ppermute x14, waiting for transfers between devices, shift(): return lax.ppermute(rows, WHOLE, pairs)  57.8 us
    pallas_call x1, Pallas kernels, attention(): pl.pallas_call(attention_kernel, out_shape=(rows, rows), in_specs=[vm] *...  24.8 us
    pallas_call x3, Pallas kernels, experts(): pl.pallas_call(functools.partial(expert_kernel, sizes), out_shape=tuple((...  23.4 us
    all_to_all x1, blocking collectives, body(): mine = lax.all_to_all(split, 'seq', 0, 0, tiled=True)  20.9 us
    ppermute x14, starting transfers between devices, shift(): return lax.ppermute(rows, WHOLE, pairs)  17.7 us
    all_to_all x1, blocking collectives, body(): lax.all_to_all(jnp.broadcast_to(mine[None], (128, 3, part)), WHOLE, 0, 0,...  15.3 us
    all_to_all x1, blocking collectives, body(): lax.all_to_all(jnp.broadcast_to(stats[None], (128, 128)), WHOLE, 0, 0, ti...  13.6 us
    ppermute x7, starting transfers between devices, partner(): return lax.ppermute(rows, 'seq', [(s, s ^ 1) for s in range(8)])  9.32 us
  transfers between devices with their start and end apart: 27, of which 10 were waited for; matrix products, arithmetic and copies ran while one was open for 5% of the time, Pallas kernels for 7%

profile of v2, /device:TPU:1, one launch (start us, length us, event | category | flops | bytes accessed | tf_op | source)
XLA Modules:
  0.0 240.5 jit_solution(1021460603682189659)
XLA Ops:
  4.7 1.2 maximum_maximum_fusion
  5.9 4.1 %collective-permute-start = (bf16[128,1536]{1,0:T(8,128)(2,1)S(1)}, bf16[128,1536]{1,0:T(8,128)(2,1)S(1)}, u32[]{:S(2)}, u32[]{:S(2)}) collective-permute-start(bf16[128,1536]{1,0:T(8,128)(2,1)S(1)} %bitcast.172), channel_id=1, source_target_pairs={{0,32},{16,48},{32,64},{48,80},{64,96},{80,112},{1,33},{17,49},{33... | collective-permute-start | bytes 1179656 | tf_op jit(solution)/shard_map/ppermute | solution.py:343
  10.0 4.4 %collective-permute-start.1 = (bf16[128,1536]{1,0:T(8,128)(2,1)S(1)}, bf16[128,1536]{1,0:T(8,128)(2,1)S(1)}, u32[]{:S(2)}, u32[]{:S(2)}) collective-permute-start(bf16[128,1536]{1,0:T(8,128)(2,1)S(1)} %bitcast.173), channel_id=1, source_target_pairs={{0,64},{16,80},{32,96},{48,112},{1,65},{17,81},{33,97},{49,113},{2... | collective-permute-start | bytes 1179656 | tf_op jit(solution)/shard_map/ppermute | solution.py:344
  14.4 1.3 collective-permute-start.2
  15.7 7.8 %all-to-all-start = ((bf16[16,16,1536]{2,1,0:T(8,128)(2,1)}), bf16[16,16,1536]{2,1,0:T(8,128)(2,1)}, u32[]{:S(2)}, u32[]{:S(2)}) async-start(bf16[16,16,1536]{2,1,0:T(8,128)(2,1)} %maximum_maximum_fusion), calls=%async_computation | async-start | bytes 1572864 | tf_op jit(solution)/shard_map/all_to_all | solution.py:342
  33.1 4.4 %all-to-all-done = bf16[16,16,1536]{2,1,0:T(8,128)(2,1)} async-done(((bf16[16,16,1536]{2,1,0:T(8,128)(2,1)}), bf16[16,16,1536]{2,1,0:T(8,128)(2,1)}, u32[]{:S(2)}, u32[]{:S(2)}) %all-to-all-start) | async-done | bytes 786464 | tf_op jit(solution)/shard_map/all_to_all | solution.py:342
  41.2 2.0 collective-permute-start.8
  43.2 3.0 %collective-permute-start.10 = (bf16[48,1536]{1,0:T(8,128)(2,1)S(1)}, bf16[48,1536]{1,0:T(8,128)(2,1)}, u32[]{:S(2)}, u32[]{:S(2)}) collective-permute-start(bf16[48,1536]{1,0:T(8,128)(2,1)S(1)} %collective-permute-done.6.refs_8_), channel_id=1, source_target_pairs={{0,16},{16,0},{32,48},{48,32},{64,80},{80,64},{96,112},{112,96},{1... | collective-permute-start | bytes 442376 | tf_op jit(solution)/shard_map/ppermute | solution.py:39
  48.3 1.3 collective-permute-start.9
  49.6 1.2 slice_bitcast_fusion.13
  55.9 24.8 %attention_block.1 = (bf16[128,1536]{1,0:T(8,128)(2,1)S(1)}, bf16[128,1536]{1,0:T(8,128)(2,1)S(1)}) custom-call(bf16[128,1536]{1,0:T(8,128)(2,1)S(1)} %bitcast.175, bf16[128,1536]{1,0:T(8,128)(2,1)S(1)} %collective-permute-done.refs_1_, bf16[128,1536]{1,0:T(8,128)(2,1)S(1)} %collective-permute-done.1.refs_2_, bf16[128,1536]{1,0:T(8,128)(2,1)S(1)} %copy-done.5, ...), custom_call_target="tpu_custom_call" | custom-call | flops 6442450944 | bytes 16777216 | tf_op jit(solution)/shard_map/attention_block/pallas_call | solution.py:168
  80.7 2.7 %collective-permute-start.13 = (bf16[128,1536]{1,0:T(8,128)(2,1)S(1)}, bf16[128,1536]{1,0:T(8,128)(2,1)S(1)}, u32[]{:S(2)}, u32[]{:S(2)}) collective-permute-start(bf16[128,1536]{1,0:T(8,128)(2,1)S(1)} %get-tuple-element.30), channel_id=1, source_target_pairs={{0,3},{1,0},{2,1},{3,2},{4,7},{5,4},{6,5},{7,6},{8,11},{9,8},{10,9... | collective-permute-start | bytes 1179656 | tf_op jit(solution)/shard_map/ppermute | solution.py:35
  83.4 9.7 %collective-permute-done.12 = bf16[128,1536]{1,0:T(8,128)(2,1)S(1)} collective-permute-done((bf16[128,1536]{1,0:T(8,128)(2,1)S(1)}, bf16[128,1536]{1,0:T(8,128)(2,1)S(1)}, u32[]{:S(2)}, u32[]{:S(2)}) %collective-permute-start.12) | collective-permute-done | bytes 393248 | tf_op jit(solution)/shard_map/ppermute | solution.py:35
  93.5 2.5 %collective-permute-start.16 = (bf16[4,128,1536]{2,1,0:T(8,128)(2,1)S(1)}, bf16[4,128,1536]{2,1,0:T(8,128)(2,1)}, u32[]{:S(2)}, u32[]{:S(2)}) collective-permute-start(bf16[4,128,1536]{2,1,0:T(8,128)(2,1)S(1)} %pad_maximum_fusion.refs_0_), channel_id=1, source_target_pairs={{0,12},{1,13},{2,14},{3,15},{4,0},{5,1},{6,2},{7,3},{8,4},{9,5},{1... | collective-permute-start | bytes 4718600 | tf_op jit(solution)/shard_map/ppermute | solution.py:35
  97.6 2.1 copy-done.1
  99.7 6.1 %expert_block.3 = bf16[4,128,1536]{2,1,0:T(8,128)(2,1)S(1)} custom-call(bf16[4,128,1536]{2,1,0:T(8,128)(2,1)S(1)} %pad_maximum_fusion.refs_0_, s32[1]{0:T(128)} %bitcast.46.refs_1_.refs_2_, f32[2,8,256]{2,1,0:T(8,128)S(1)} %get-tuple-element.69.refs_2_, bf16[5,1536,256]{2,1,0:T(8,128)(2,1)S(1)} %copy-done.1, bf16[5,1536,256]{2,1,0:T(8,128)(2,1)} %refs_5_.5, ...), custom_call_target="tpu_custom_call" | custom-call | flops 1887436800 | bytes 12582912 | tf_op jit(solution)/shard_map/expert_block/pallas_call | solution.py:285
  105.8 8.4 %collective-permute-done.15.refs_0_ = bf16[4,128,1536]{2,1,0:T(8,128)(2,1)} collective-permute-done((bf16[4,128,1536]{2,1,0:T(8,128)(2,1)S(1)}, bf16[4,128,1536]{2,1,0:T(8,128)(2,1)}, u32[]{:S(2)}, u32[]{:S(2)}) %collective-permute-start.15) | collective-permute-done | bytes 1572896 | tf_op jit(solution)/shard_map/ppermute | solution.py:35
  116.7 2.7 %collective-permute-start.18 = (bf16[2,128,1536]{2,1,0:T(8,128)(2,1)S(1)}, bf16[2,128,1536]{2,1,0:T(8,128)(2,1)S(1)}, u32[]{:S(2)}, u32[]{:S(2)}) collective-permute-start(bf16[2,128,1536]{2,1,0:T(8,128)(2,1)S(1)} %slice.125), channel_id=1, source_target_pairs={{0,12},{1,13},{2,14},{3,15},{4,0},{5,1},{6,2},{7,3},{8,4},{9,5},{1... | collective-permute-start | bytes 2359304 | tf_op jit(solution)/shard_map/ppermute | solution.py:35
  119.4 11.1 %expert_block.4 = (bf16[4,128,1536]{2,1,0:T(8,128)(2,1)S(1)}, bf16[4,128,1536]{2,1,0:T(8,128)(2,1)S(1)}) custom-call(bf16[4,128,1536]{2,1,0:T(8,128)(2,1)} %collective-permute-done.15.refs_0_, bf16[4,128,1536]{2,1,0:T(8,128)(2,1)} %collective-permute-done.16.refs_1_, s32[1]{0:T(128)} %bitcast.46.refs_1_.refs_2_, ...), custom_call_target="tpu_custom_call" | custom-call | flops 3774873600 | bytes 12582912 | tf_op jit(solution)/shard_map/expert_block/pallas_call | solution.py:285
  130.6 6.1 %expert_block.5 = (bf16[2,128,1536]{2,1,0:T(8,128)(2,1)S(1)}, bf16[2,128,1536]{2,1,0:T(8,128)(2,1)S(1)}) custom-call(bf16[2,128,1536]{2,1,0:T(8,128)(2,1)S(1)} %collective-permute-done.17.refs_0_, bf16[2,128,1536]{2,1,0:T(8,128)(2,1)S(1)} %collective-permute-done.18.refs_1_, s32[1]{0:T(128)} %bitcast.46.refs_1_.refs_2_, ...), custom_call_target="tpu_custom_call" | custom-call | flops 1887436800 | bytes 12582912 | tf_op jit(solution)/shard_map/expert_block/pallas_call | solution.py:285
  137.0 2.7 %collective-permute-start.20 = (bf16[2,128,1536]{2,1,0:T(8,128)(2,1)S(1)}, bf16[2,128,1536]{2,1,0:T(8,128)(2,1)S(1)}, u32[]{:S(2)}, u32[]{:S(2)}) collective-permute-start(bf16[2,128,1536]{2,1,0:T(8,128)(2,1)S(1)} %get-tuple-element.43), channel_id=1, source_target_pairs={{0,12},{1,13},{2,14},{3,15},{4,0},{5,1},{6,2},{7,3},{8,4},{9,5},{1... | collective-permute-start | bytes 2359304 | tf_op jit(solution)/shard_map/ppermute | solution.py:35
  139.8 9.6 %collective-permute-done.19 = bf16[2,128,1536]{2,1,0:T(8,128)(2,1)S(1)} collective-permute-done((bf16[2,128,1536]{2,1,0:T(8,128)(2,1)S(1)}, bf16[2,128,1536]{2,1,0:T(8,128)(2,1)S(1)}, u32[]{:S(2)}, u32[]{:S(2)}) %collective-permute-start.19) | collective-permute-done | bytes 786464 | tf_op jit(solution)/shard_map/ppermute | solution.py:35
  149.7 2.7 %collective-permute-start.22 = (bf16[4,128,1536]{2,1,0:T(8,128)(2,1)S(1)}, bf16[4,128,1536]{2,1,0:T(8,128)(2,1)S(1)}, u32[]{:S(2)}, u32[]{:S(2)}) collective-permute-start(bf16[4,128,1536]{2,1,0:T(8,128)(2,1)S(1)} %pad_maximum_fusion.2), channel_id=1, source_target_pairs={{0,12},{1,13},{2,14},{3,15},{4,0},{5,1},{6,2},{7,3},{8,4},{9,5},{1... | collective-permute-start | bytes 4718600 | tf_op jit(solution)/shard_map/ppermute | solution.py:35
  152.9 16.9 %collective-permute-done.22 = bf16[4,128,1536]{2,1,0:T(8,128)(2,1)S(1)} collective-permute-done((bf16[4,128,1536]{2,1,0:T(8,128)(2,1)S(1)}, bf16[4,128,1536]{2,1,0:T(8,128)(2,1)S(1)}, u32[]{:S(2)}, u32[]{:S(2)}) %collective-permute-start.22) | collective-permute-done | bytes 1572896 | tf_op jit(solution)/shard_map/ppermute | solution.py:35
  169.8 3.8 %collective-permute-done.21 = bf16[4,128,1536]{2,1,0:T(8,128)(2,1)S(1)} collective-permute-done((bf16[4,128,1536]{2,1,0:T(8,128)(2,1)S(1)}, bf16[4,128,1536]{2,1,0:T(8,128)(2,1)S(1)}, u32[]{:S(2)}, u32[]{:S(2)}) %collective-permute-start.21) | collective-permute-done | bytes 1572896 | tf_op jit(solution)/shard_map/ppermute | solution.py:35
  174.5 2.7 %collective-permute-start.24 = (bf16[128,1536]{1,0:T(8,128)(2,1)S(1)}, bf16[128,1536]{1,0:T(8,128)(2,1)S(1)}, u32[]{:S(2)}, u32[]{:S(2)}) collective-permute-start(bf16[128,1536]{1,0:T(8,128)(2,1)S(1)} %get-tuple-element.61), channel_id=1, source_target_pairs={{0,3},{1,0},{2,1},{3,2},{4,7},{5,4},{6,5},{7,6},{8,11},{9,8},{10,9... | collective-permute-start | bytes 1179656 | tf_op jit(solution)/shard_map/ppermute | solution.py:35
  178.1 4.3 %collective-permute-done.23 = bf16[128,1536]{1,0:T(8,128)(2,1)S(1)} collective-permute-done((bf16[128,1536]{1,0:T(8,128)(2,1)S(1)}, bf16[128,1536]{1,0:T(8,128)(2,1)S(1)}, u32[]{:S(2)}, u32[]{:S(2)}) %collective-permute-start.23) | collective-permute-done | bytes 393248 | tf_op jit(solution)/shard_map/ppermute | solution.py:35
  182.4 3.8 %collective-permute-done.24 = bf16[128,1536]{1,0:T(8,128)(2,1)S(1)} collective-permute-done((bf16[128,1536]{1,0:T(8,128)(2,1)S(1)}, bf16[128,1536]{1,0:T(8,128)(2,1)S(1)}, u32[]{:S(2)}, u32[]{:S(2)}) %collective-permute-start.24) | collective-permute-done | bytes 393248 | tf_op jit(solution)/shard_map/ppermute | solution.py:35
  186.1 1.3 collective-permute-done.25
  188.3 20.9 %all_to_all.24 = bf16[8,3,192]{2,1,0:T(4,128)(2,1)S(1)} all-to-all(bf16[8,3,192]{2,1,0:T(4,128)(2,1)S(1)} %bitcast.183), channel_id=1, replica_groups=mesh['seq'=8,'grp'=16] {'seq'}, dimensions={0} | all-to-all | bytes 18432 | tf_op jit(solution)/shard_map/all_to_all | solution.py:428
  209.3 15.3 %all_to_all.25 = bf16[128,3,192]{2,1,0:T(4,128)(2,1)S(1)} all-to-all(bf16[128,3,192]{2,1,0:T(4,128)(2,1)S(1)} %broadcast_in_dim.223), channel_id=1, replica_groups=mesh['seq'=8,'grp'=16] {'seq','grp'}, dimensions={0} | all-to-all | bytes 294912 | tf_op jit(solution)/shard_map/all_to_all | solution.py:430
  225.8 13.6 %all_to_all.26 = f32[128,1,128]{2,1,0:T(1,128)S(1)} all-to-all(f32[128,1,128]{2,1,0:T(1,128)S(1)} %broadcast_in_dim.225), channel_id=1, replica_groups=mesh['seq'=8,'grp'=16] {'seq','grp'}, dimensions={0} | all-to-all | bytes 131072 | tf_op jit(solution)/shard_map/all_to_all | solution.py:437
  (155 shorter events, 29.1 us)
Async XLA Ops:
  0.6 224.4 %copy-start = (bf16[1536,384]{1,0:T(8,128)(2,1)S(1)}, bf16[1536,384]{1,0:T(8,128)(2,1)}, u32[]{:S(2)}) copy-start(bf16[1536,384]{1,0:T(8,128)(2,1)} %param.39) | copy-start | bytes 3538948
  4.7 20.7 %copy-start.14 = (s32[1,3]{1,0:T(1,128)S(1)}, s32[1,3]{1,0:T(1,128)}, u32[]{:S(2)}) copy-start(s32[1,3]{1,0:T(1,128)} %param.23) | copy-start | bytes 40
  5.9 45.7 %copy-start.11 = (f32[1536]{0:T(1024)S(1)}, f32[1536]{0:T(1024)}, u32[]{:S(2)}) copy-start(f32[1536]{0:T(1024)} %param.26) | copy-start | bytes 18436
  5.9 45.7 %copy-start.12 = (f32[1536]{0:T(1024)S(1)}, f32[1536]{0:T(1024)}, u32[]{:S(2)}) copy-start(f32[1536]{0:T(1024)} %param.34) | copy-start | bytes 18436
  5.9 26.6 %collective-permute-start = (bf16[128,1536]{1,0:T(8,128)(2,1)S(1)}, bf16[128,1536]{1,0:T(8,128)(2,1)S(1)}, u32[]{:S(2)}, u32[]{:S(2)}) collective-permute-start(bf16[128,1536]{1,0:T(8,128)(2,1)S(1)} %bitcast.172), channel_id=1, source_target_pairs={{0,32},{16,48},{32,64},{48,80},{64,96},{80,112},{1,33},{17,49},{33... | collective-permute-start | bytes 1179656 | tf_op jit(solution)/shard_map/ppermute | solution.py:343
  10.0 22.9 %collective-permute-start.1 = (bf16[128,1536]{1,0:T(8,128)(2,1)S(1)}, bf16[128,1536]{1,0:T(8,128)(2,1)S(1)}, u32[]{:S(2)}, u32[]{:S(2)}) collective-permute-start(bf16[128,1536]{1,0:T(8,128)(2,1)S(1)} %bitcast.173), channel_id=1, source_target_pairs={{0,64},{16,80},{32,96},{48,112},{1,65},{17,81},{33,97},{49,113},{2... | collective-permute-start | bytes 1179656 | tf_op jit(solution)/shard_map/ppermute | solution.py:344
  14.4 24.3 %collective-permute-start.2 = (bf16[128,1536]{1,0:T(8,128)(2,1)S(1)}, bf16[128,1536]{1,0:T(8,128)(2,1)S(1)}, u32[]{:S(2)}, u32[]{:S(2)}) collective-permute-start(bf16[128,1536]{1,0:T(8,128)(2,1)S(1)} %bitcast.174), channel_id=1, source_target_pairs={{0,16},{16,0},{32,48},{48,32},{64,80},{80,64},{96,112},{112,96},{1... | collective-permute-start | bytes 1179656 | tf_op jit(solution)/shard_map/ppermute | solution.py:39
  15.7 21.8 %all-to-all-start = ((bf16[16,16,1536]{2,1,0:T(8,128)(2,1)}), bf16[16,16,1536]{2,1,0:T(8,128)(2,1)}, u32[]{:S(2)}, u32[]{:S(2)}) async-start(bf16[16,16,1536]{2,1,0:T(8,128)(2,1)} %maximum_maximum_fusion), calls=%async_computation | async-start | bytes 1572864 | tf_op jit(solution)/shard_map/all_to_all | solution.py:342
  32.6 8.7 %collective-permute-start.3 = (bf16[128,1536]{1,0:T(8,128)(2,1)S(1)}, bf16[128,1536]{1,0:T(8,128)(2,1)S(1)}, u32[]{:S(2)}, u32[]{:S(2)}) collective-permute-start(bf16[128,1536]{1,0:T(8,128)(2,1)S(1)} %collective-permute-done.refs_1_), channel_id=1, source_target_pairs={{0,16},{16,0},{32,48},{48,32},{64,80},{80,64},{96,112},{112,96},{1... | collective-permute-start | bytes 1179656 | tf_op jit(solution)/shard_map/ppermute | solution.py:39
  32.9 20.0 %collective-permute-start.4 = (bf16[128,1536]{1,0:T(8,128)(2,1)S(1)}, bf16[128,1536]{1,0:T(8,128)(2,1)}, u32[]{:S(2)}, u32[]{:S(2)}) collective-permute-start(bf16[128,1536]{1,0:T(8,128)(2,1)S(1)} %collective-permute-done.1.refs_2_), channel_id=1, source_target_pairs={{0,16},{16,0},{32,48},{48,32},{64,80},{80,64},{96,112},{112,96},{1... | collective-permute-start | bytes 1179656 | tf_op jit(solution)/shard_map/ppermute | solution.py:39
  38.4 4.9 %collective-permute-start.6 = (bf16[48,1536]{1,0:T(8,128)(2,1)S(1)}, bf16[48,1536]{1,0:T(8,128)(2,1)S(1)}, u32[]{:S(2)}, u32[]{:S(2)}) collective-permute-start(bf16[48,1536]{1,0:T(8,128)(2,1)S(1)} %bitcast.167), channel_id=1, source_target_pairs={{0,96},{16,112},{32,0},{48,16},{64,32},{80,48},{96,64},{112,80},{1... | collective-permute-start | bytes 442376 | tf_op jit(solution)/shard_map/ppermute | solution.py:347
  38.4 7.8 %collective-permute-start.7 = (bf16[48,1536]{1,0:T(8,128)(2,1)S(1)}, bf16[48,1536]{1,0:T(8,128)(2,1)}, u32[]{:S(2)}, u32[]{:S(2)}) collective-permute-start(bf16[48,1536]{1,0:T(8,128)(2,1)S(1)} %bitcast.168), channel_id=1, source_target_pairs={{0,64},{16,80},{32,96},{48,112},{64,0},{80,16},{96,32},{112,48},{1... | collective-permute-start | bytes 442376 | tf_op jit(solution)/shard_map/ppermute | solution.py:347
  39.5 8.8 %collective-permute-start.5 = (bf16[48,1536]{1,0:T(8,128)(2,1)S(1)}, bf16[48,1536]{1,0:T(8,128)(2,1)}, u32[]{:S(2)}, u32[]{:S(2)}) collective-permute-start(bf16[48,1536]{1,0:T(8,128)(2,1)S(1)} %bitcast.169), channel_id=1, source_target_pairs={{0,32},{16,48},{32,64},{48,80},{64,96},{80,112},{96,0},{112,16},{1... | collective-permute-start | bytes 442376 | tf_op jit(solution)/shard_map/ppermute | solution.py:347
  41.2 11.7 %collective-permute-start.8 = (bf16[48,1536]{1,0:T(8,128)(2,1)S(1)}, bf16[48,1536]{1,0:T(8,128)(2,1)}, u32[]{:S(2)}, u32[]{:S(2)}) collective-permute-start(bf16[48,1536]{1,0:T(8,128)(2,1)S(1)} %bitcast.170), channel_id=1, source_target_pairs={{0,16},{16,0},{32,48},{48,32},{64,80},{80,64},{96,112},{112,96},{1... | collective-permute-start | bytes 442376 | tf_op jit(solution)/shard_map/ppermute | solution.py:39
  43.2 9.7 %collective-permute-start.10 = (bf16[48,1536]{1,0:T(8,128)(2,1)S(1)}, bf16[48,1536]{1,0:T(8,128)(2,1)}, u32[]{:S(2)}, u32[]{:S(2)}) collective-permute-start(bf16[48,1536]{1,0:T(8,128)(2,1)S(1)} %collective-permute-done.6.refs_8_), channel_id=1, source_target_pairs={{0,16},{16,0},{32,48},{48,32},{64,80},{80,64},{96,112},{112,96},{1... | collective-permute-start | bytes 442376 | tf_op jit(solution)/shard_map/ppermute | solution.py:39
  46.3 6.6 %collective-permute-start.11 = (bf16[48,1536]{1,0:T(8,128)(2,1)}, bf16[48,1536]{1,0:T(8,128)(2,1)}, u32[]{:S(2)}, u32[]{:S(2)}) collective-permute-start(bf16[48,1536]{1,0:T(8,128)(2,1)} %collective-permute-done.7.refs_9_), channel_id=1, source_target_pairs={{0,16},{16,0},{32,48},{48,32},{64,80},{80,64},{96,112},{112,96},{1... | collective-permute-start | bytes 442376 | tf_op jit(solution)/shard_map/ppermute | solution.py:39
  48.3 4.7 %collective-permute-start.9 = (bf16[48,1536]{1,0:T(8,128)(2,1)}, bf16[48,1536]{1,0:T(8,128)(2,1)}, u32[]{:S(2)}, u32[]{:S(2)}) collective-permute-start(bf16[48,1536]{1,0:T(8,128)(2,1)} %collective-permute-done.5.refs_7_), channel_id=1, source_target_pairs={{0,16},{16,0},{32,48},{48,32},{64,80},{80,64},{96,112},{112,96},{1... | collective-permute-start | bytes 442376 | tf_op jit(solution)/shard_map/ppermute | solution.py:39
  80.6 12.4 %collective-permute-start.12 = (bf16[128,1536]{1,0:T(8,128)(2,1)S(1)}, bf16[128,1536]{1,0:T(8,128)(2,1)S(1)}, u32[]{:S(2)}, u32[]{:S(2)}) collective-permute-start(bf16[128,1536]{1,0:T(8,128)(2,1)S(1)} %get-tuple-element.30), channel_id=1, source_target_pairs={{0,1},{1,2},{2,3},{3,0},{4,5},{5,6},{6,7},{7,4},{8,9},{9,10},{10,1... | collective-permute-start | bytes 1179656 | tf_op jit(solution)/shard_map/ppermute | solution.py:35
  80.7 12.3 %collective-permute-start.13 = (bf16[128,1536]{1,0:T(8,128)(2,1)S(1)}, bf16[128,1536]{1,0:T(8,128)(2,1)S(1)}, u32[]{:S(2)}, u32[]{:S(2)}) collective-permute-start(bf16[128,1536]{1,0:T(8,128)(2,1)S(1)} %get-tuple-element.30), channel_id=1, source_target_pairs={{0,3},{1,0},{2,1},{3,2},{4,7},{5,4},{6,5},{7,6},{8,11},{9,8},{10,9... | collective-permute-start | bytes 1179656 | tf_op jit(solution)/shard_map/ppermute | solution.py:35
  83.4 9.7 %collective-permute-start.14 = (bf16[128,1536]{1,0:T(8,128)(2,1)S(1)}, bf16[128,1536]{1,0:T(8,128)(2,1)S(1)}, u32[]{:S(2)}, u32[]{:S(2)}) collective-permute-start(bf16[128,1536]{1,0:T(8,128)(2,1)S(1)} %get-tuple-element.30), channel_id=1, source_target_pairs={{0,2},{1,3},{2,0},{3,1},{4,6},{5,7},{6,4},{7,5},{8,10},{9,11},{10,... | collective-permute-start | bytes 1179656 | tf_op jit(solution)/shard_map/ppermute | solution.py:35
  93.3 20.9 %collective-permute-start.15 = (bf16[4,128,1536]{2,1,0:T(8,128)(2,1)S(1)}, bf16[4,128,1536]{2,1,0:T(8,128)(2,1)}, u32[]{:S(2)}, u32[]{:S(2)}) collective-permute-start(bf16[4,128,1536]{2,1,0:T(8,128)(2,1)S(1)} %pad_maximum_fusion.refs_0_), channel_id=1, source_target_pairs={{0,4},{1,5},{2,6},{3,7},{4,8},{5,9},{6,10},{7,11},{8,12},{9,13},{1... | collective-permute-start | bytes 4718600 | tf_op jit(solution)/shard_map/ppermute | solution.py:35
  93.5 20.7 %collective-permute-start.16 = (bf16[4,128,1536]{2,1,0:T(8,128)(2,1)S(1)}, bf16[4,128,1536]{2,1,0:T(8,128)(2,1)}, u32[]{:S(2)}, u32[]{:S(2)}) collective-permute-start(bf16[4,128,1536]{2,1,0:T(8,128)(2,1)S(1)} %pad_maximum_fusion.refs_0_), channel_id=1, source_target_pairs={{0,12},{1,13},{2,14},{3,15},{4,0},{5,1},{6,2},{7,3},{8,4},{9,5},{1... | collective-permute-start | bytes 4718600 | tf_op jit(solution)/shard_map/ppermute | solution.py:35
  115.4 15.1 %collective-permute-start.17 = (bf16[2,128,1536]{2,1,0:T(8,128)(2,1)S(1)}, bf16[2,128,1536]{2,1,0:T(8,128)(2,1)S(1)}, u32[]{:S(2)}, u32[]{:S(2)}) collective-permute-start(bf16[2,128,1536]{2,1,0:T(8,128)(2,1)S(1)} %slice.124), channel_id=1, source_target_pairs={{0,4},{1,5},{2,6},{3,7},{4,8},{5,9},{6,10},{7,11},{8,12},{9,13},{1... | collective-permute-start | bytes 2359304 | tf_op jit(solution)/shard_map/ppermute | solution.py:35
  116.7 13.9 %collective-permute-start.18 = (bf16[2,128,1536]{2,1,0:T(8,128)(2,1)S(1)}, bf16[2,128,1536]{2,1,0:T(8,128)(2,1)S(1)}, u32[]{:S(2)}, u32[]{:S(2)}) collective-permute-start(bf16[2,128,1536]{2,1,0:T(8,128)(2,1)S(1)} %slice.125), channel_id=1, source_target_pairs={{0,12},{1,13},{2,14},{3,15},{4,0},{5,1},{6,2},{7,3},{8,4},{9,5},{1... | collective-permute-start | bytes 2359304 | tf_op jit(solution)/shard_map/ppermute | solution.py:35
  136.7 12.6 %collective-permute-start.19 = (bf16[2,128,1536]{2,1,0:T(8,128)(2,1)S(1)}, bf16[2,128,1536]{2,1,0:T(8,128)(2,1)S(1)}, u32[]{:S(2)}, u32[]{:S(2)}) collective-permute-start(bf16[2,128,1536]{2,1,0:T(8,128)(2,1)S(1)} %get-tuple-element.42), channel_id=1, source_target_pairs={{0,4},{1,5},{2,6},{3,7},{4,8},{5,9},{6,10},{7,11},{8,12},{9,13},{1... | collective-permute-start | bytes 2359304 | tf_op jit(solution)/shard_map/ppermute | solution.py:35
  137.0 12.3 %collective-permute-start.20 = (bf16[2,128,1536]{2,1,0:T(8,128)(2,1)S(1)}, bf16[2,128,1536]{2,1,0:T(8,128)(2,1)S(1)}, u32[]{:S(2)}, u32[]{:S(2)}) collective-permute-start(bf16[2,128,1536]{2,1,0:T(8,128)(2,1)S(1)} %get-tuple-element.43), channel_id=1, source_target_pairs={{0,12},{1,13},{2,14},{3,15},{4,0},{5,1},{6,2},{7,3},{8,4},{9,5},{1... | collective-permute-start | bytes 2359304 | tf_op jit(solution)/shard_map/ppermute | solution.py:35
  149.7 20.1 %collective-permute-start.22 = (bf16[4,128,1536]{2,1,0:T(8,128)(2,1)S(1)}, bf16[4,128,1536]{2,1,0:T(8,128)(2,1)S(1)}, u32[]{:S(2)}, u32[]{:S(2)}) collective-permute-start(bf16[4,128,1536]{2,1,0:T(8,128)(2,1)S(1)} %pad_maximum_fusion.2), channel_id=1, source_target_pairs={{0,12},{1,13},{2,14},{3,15},{4,0},{5,1},{6,2},{7,3},{8,4},{9,5},{1... | collective-permute-start | bytes 4718600 | tf_op jit(solution)/shard_map/ppermute | solution.py:35
  152.8 20.8 %collective-permute-start.21 = (bf16[4,128,1536]{2,1,0:T(8,128)(2,1)S(1)}, bf16[4,128,1536]{2,1,0:T(8,128)(2,1)S(1)}, u32[]{:S(2)}, u32[]{:S(2)}) collective-permute-start(bf16[4,128,1536]{2,1,0:T(8,128)(2,1)S(1)} %pad_maximum_fusion.1), channel_id=1, source_target_pairs={{0,4},{1,5},{2,6},{3,7},{4,8},{5,9},{6,10},{7,11},{8,12},{9,13},{1... | collective-permute-start | bytes 4718600 | tf_op jit(solution)/shard_map/ppermute | solution.py:35
  174.4 7.9 %collective-permute-start.23 = (bf16[128,1536]{1,0:T(8,128)(2,1)S(1)}, bf16[128,1536]{1,0:T(8,128)(2,1)S(1)}, u32[]{:S(2)}, u32[]{:S(2)}) collective-permute-start(bf16[128,1536]{1,0:T(8,128)(2,1)S(1)} %get-tuple-element.62), channel_id=1, source_target_pairs={{0,1},{1,2},{2,3},{3,0},{4,5},{5,6},{6,7},{7,4},{8,9},{9,10},{10,1... | collective-permute-start | bytes 1179656 | tf_op jit(solution)/shard_map/ppermute | solution.py:35
  174.5 11.6 %collective-permute-start.24 = (bf16[128,1536]{1,0:T(8,128)(2,1)S(1)}, bf16[128,1536]{1,0:T(8,128)(2,1)S(1)}, u32[]{:S(2)}, u32[]{:S(2)}) collective-permute-start(bf16[128,1536]{1,0:T(8,128)(2,1)S(1)} %get-tuple-element.61), channel_id=1, source_target_pairs={{0,3},{1,0},{2,1},{3,2},{4,7},{5,4},{6,5},{7,6},{8,11},{9,8},{10,9... | collective-permute-start | bytes 1179656 | tf_op jit(solution)/shard_map/ppermute | solution.py:35
  177.2 10.2 %collective-permute-start.25 = (bf16[128,1536]{1,0:T(8,128)(2,1)S(1)}, bf16[128,1536]{1,0:T(8,128)(2,1)S(1)}, u32[]{:S(2)}, u32[]{:S(2)}) collective-permute-start(bf16[128,1536]{1,0:T(8,128)(2,1)S(1)} %get-tuple-element.60), channel_id=1, source_target_pairs={{0,2},{1,3},{2,0},{3,1},{4,6},{5,7},{6,4},{7,5},{8,10},{9,11},{10,... | collective-permute-start | bytes 1179656 | tf_op jit(solution)/shard_map/ppermute | solution.py:35
  187.7 37.8 %copy-start.10 = (bf16[128,1536]{1,0:T(8,128)(2,1)}, bf16[128,1536]{1,0:T(8,128)(2,1)S(1)}, u32[]{:S(2)}) copy-start(bf16[128,1536]{1,0:T(8,128)(2,1)S(1)} %fusion.5) | copy-start | bytes 1179652
  (15 other events, 83.8 us)

commit v3 on v2

--- a/solution.py
+++ b/solution.py
@@ -47,28 +47,75 @@
     return lax.dot_general(lhs, rhs, (((1,), (1,)), ((), ())), preferred_element_type=F32)
 
 
-def attention_kernel(*refs):
-    tok = refs[0:6]
-    adapt = refs[6:14]
-    (gain, gain_moe, cosine, sine, key_doc, key_index, doc, index, colp, colr, wq_hbm, wk_hbm,
-     wv_hbm, wo_hbm, mixed_out, moe_out,
-     wq, wk, wv, wo, xn, ad, qbuf, kbuf, vbuf, att, sems) = refs[14:]
+def norm(rows, scale):
+    inverse = lax.rsqrt(jnp.mean(rows * rows, axis=-1, keepdims=True) + EPSILON)
+    return (rows * inverse * scale).astype(BF)
+
+
+def base_kernel(t0, t1, t2, t3, t4, gain, wq_hbm, wk_hbm, wv_hbm, xn, base_q, base_k, base_v,
+                wq, wk, wv, sems):
     copies = [pltpu.make_async_copy(src, dst, sems.at[i]) for i, (src, dst) in enumerate(
-        [(wk_hbm, wk), (wv_hbm, wv), (wq_hbm, wq), (wo_hbm, wo)])]
+        [(wk_hbm, wk), (wv_hbm, wv), (wq_hbm, wq)])]
     for copy in copies:
         copy.start()
-    count = tok[0].shape[0]
+    count = t0.shape[0]
+    for b, rows in enumerate((t0, t1, t2, t3, t4)):
+        xn[b * count:(b + 1) * count, :] = norm(rows[...].astype(F32), gain[...])
+    copies[0].wait()
+    copies[1].wait()
+
+    def key_block(b, carry):
+        at = pl.ds(pl.multiple_of(b * 320, 320), 320)
+        rows = xn[at, :]
+        base_k[at, :] = jnp.dot(rows, wk[...], preferred_element_type=F32)
+        base_v[at, :] = jnp.dot(rows, wv[...], preferred_element_type=F32)
+        return carry
+
+    lax.fori_loop(0, 2, key_block, 0)
+    copies[2].wait()
+    own = xn[0:count, :]
+
+    def query_block(c, carry):
+        at = pl.ds(pl.multiple_of(c * 512, 512), 512)
+        base_q[:, at] = jnp.dot(own, wq[:, at], preferred_element_type=F32)
+        return carry
+
+    lax.fori_loop(0, 3, query_block, 0)
+
+
+def base_projections(tok, gain, wq, wk, wv):
+    count, width = tok[0].shape
+    vm = pl.BlockSpec(memory_space=pltpu.VMEM)
+    anywhere = pl.BlockSpec(memory_space=pl.ANY)
+    return pl.pallas_call(
+        base_kernel,
+        out_shape=(jax.ShapeDtypeStruct((5 * count, width), BF),
+                   jax.ShapeDtypeStruct((count, width), F32),
+                   jax.ShapeDtypeStruct((5 * count, 512), F32),
+                   jax.ShapeDtypeStruct((5 * count, 512), F32)),
+        in_specs=[vm] * 6 + [anywhere] * 3,
+        out_specs=(vm,) * 4,
+        scratch_shapes=[
+            pltpu.VMEM(wq.shape, BF), pltpu.VMEM(wk.shape, BF), pltpu.VMEM(wv.shape, BF),
+            pltpu.SemaphoreType.DMA((3,)),
+        ],
+        compiler_params=pltpu.CompilerParams(vmem_limit_bytes=32 << 20),
+        cost_estimate=pl.CostEstimate(flops=5 << 30, transcendentals=0,
+                                      bytes_accessed=14 << 20),
+        name="base_block",
+    )(*tok, gain, wq, wk, wv)
+
+
+def attention_kernel(*refs):
+    adapt = refs[0:8]
+    (tok, xn, base_q, base_k, base_v, gain_moe, cosine, sine, key_doc, key_index, doc, index,
+     colp, colr, wo_hbm, mixed_out, moe_out, wo, ad, qbuf, kbuf, vbuf, att, score, prob,
+     sem) = refs[8:]
+    load = pltpu.make_async_copy(wo_hbm, wo, sem)
+    load.start()
+    count = tok.shape[0]
     for j in range(8):
         ad[48 * j:48 * j + 48, :] = adapt[j][...]
-
-    def norm(rows, scale):
-        inverse = lax.rsqrt(jnp.mean(rows * rows, axis=-1, keepdims=True) + EPSILON)
-        return (rows * inverse * scale).astype(BF)
-
-    for b in range(6):
-        xn[b * count:(b + 1) * count, :] = norm(tok[b][...].astype(F32), gain[...])
-    copies[0].wait()
-    copies[1].wait()
     col_prompt = colp[...]
     col_row = colr[...]
 
@@ -82,31 +129,27 @@
 
     def rope(u, cos_t, sin_t):
         turned = jnp.where(lower, pltpu.roll(u, 96, 1), pltpu.roll(u, 32, 1))
-        return (u * cos_t + turned * sin_t).astype(BF)
+        return u * cos_t + turned * sin_t
 
     def key_block(b, carry):
-        at = pl.multiple_of(b * count, count)
-        rows = xn[pl.ds(at, count), :]
-        docs = doc[pl.ds(at, count), :]
-        z = dot_t(rows, ad[...])
-        keys = jnp.dot(rows, wk[...], preferred_element_type=F32) + jnp.dot(
+        at = pl.ds(pl.multiple_of(b * count, count), count)
+        docs = doc[at, :]
+        z = dot_t(xn[at, :], ad[...])
+        keys = base_k[at, :] + jnp.dot(
             low(z, 10, 12, docs), ad[:, :512], preferred_element_type=F32)
-        values = jnp.dot(rows, wv[...], preferred_element_type=F32) + jnp.dot(
+        values = base_v[at, :] + jnp.dot(
             low(z, 8, 12, docs), ad[:, 512:1024], preferred_element_type=F32)
-        vbuf[pl.ds(at, count), :] = values.astype(BF)
-        cos_t = cosine[pl.ds(at, count), :]
-        sin_t = sine[pl.ds(at, count), :]
+        vbuf[at, :] = values.astype(BF)
+        cos_t = cosine[at, :]
+        sin_t = sine[at, :]
         for c in range(4):
-            kbuf[pl.ds(at, count), 128 * c:128 * c + 128] = rope(
-                keys[:, 128 * c:128 * c + 128], cos_t, sin_t)
-        return carry
-
-    lax.fori_loop(0, 6, key_block, 0)
-    copies[2].wait()
-    own = xn[0:count, :]
+            kbuf[at, 128 * c:128 * c + 128] = rope(
+                keys[:, 128 * c:128 * c + 128], cos_t, sin_t).astype(BF)
+        return carry
+
+    lax.fori_loop(0, 5, key_block, 0)
     docs = doc[0:count, :]
-    z = dot_t(own, ad[...])
-    zq = low(z, 8, 8, docs)
+    zq = low(dot_t(xn[0:count, :], ad[...]), 8, 8, docs)
     cos_t = cosine[0:count, :]
     sin_t = sine[0:count, :]
     low_half = lane < 64
@@ -115,73 +158,76 @@
 
     def query_block(c, carry):
         at = pl.multiple_of(c * 384, 128)
-        u = jnp.dot(own, wq[:, pl.ds(at, 384)], preferred_element_type=F32) + jnp.dot(
+        u = base_q[:, pl.ds(at, 384)] + jnp.dot(
             zq, ad[:, pl.ds(at, 384)], preferred_element_type=F32)
         for t in range(3):
-            qbuf[:, pl.ds(pl.multiple_of(at + 128 * t, 128), 128)] = rope(
-                u[:, 128 * t:128 * t + 128], cos_t, sin_t)
+            q = rope(u[:, 128 * t:128 * t + 128], cos_t, sin_t).astype(BF).astype(F32)
+            q = q * (HEAD ** -0.5)
+            turned = pltpu.roll(q, 64, 1)
+            for own_low in (True, False):
+                h = 2 * t + (0 if own_low else 1)
+                kv_low = h < 3
+                rows = q if own_low == kv_low else turned
+                keep = low_half if kv_low else ~low_half
+                qbuf[c, count * h:count * h + count, :] = jnp.where(keep, rows, 0.0).astype(BF)
         return carry
 
     lax.fori_loop(0, 4, query_block, 0)
 
     def pair(j, carry):
         kv = pl.ds(pl.multiple_of(j * 128, 128), 128)
-        keys = kbuf[:, kv]
-        values = vbuf[:, kv]
-        tiles = [qbuf[:, pl.ds(pl.multiple_of(j * 384 + 128 * t, 128), 128)] for t in range(3)]
+        score[...] = dot_t(qbuf[j], kbuf[:, kv])
+        totals = []
+        for h in range(6):
+            at = slice(count * h, count * h + count)
+            s = score[at, :] + bias
+            top = jnp.max(s, axis=-1, keepdims=True)
+            w = jnp.exp(s - top)
+            totals.append(jnp.sum(w, axis=-1, keepdims=True))
+            prob[at, :] = w.astype(BF)
+        out = jnp.dot(prob[...], vbuf[:, kv], preferred_element_type=F32)
         results = []
         for h in range(6):
-            own_low, kv_low = h % 2 == 0, h < 3
-            q = tiles[h // 2].astype(F32)
-            if own_low != kv_low:
-                q = pltpu.roll(q, 64, 1)
-            q = jnp.where(low_half if kv_low else ~low_half, q, 0.0).astype(BF)
-            s = dot_t(q, keys) * (HEAD ** -0.5) + bias
-            top = jnp.max(s, axis=-1, keepdims=True)
-            w = jnp.exp(s - top)
-            total = jnp.sum(w, axis=-1, keepdims=True)
-            o = jnp.dot(w.astype(BF), values, preferred_element_type=F32) / total
-            if own_low != kv_low:
-                o = pltpu.roll(o, 64, 1)
-            results.append(o)
+            o = out[count * h:count * h + count] / totals[h]
+            results.append(pltpu.roll(o, 64, 1) if (h % 2 == 0) != (h < 3) else o)
         for t in range(3):
             att[:, pl.ds(pl.multiple_of(j * 384 + 128 * t, 128), 128)] = jnp.where(
                 low_half, results[2 * t], results[2 * t + 1]).astype(BF)
         return carry
 
     lax.fori_loop(0, 4, pair, 0)
-    copies[3].wait()
+    load.wait()
     attended = att[...]
     zo = low(dot_t(attended, ad[...]), 4, 10, docs)
-    mixed = (tok[0][...].astype(F32) + jnp.dot(attended, wo[...], preferred_element_type=F32)
+    mixed = (tok[...].astype(F32) + jnp.dot(attended, wo[...], preferred_element_type=F32)
              + jnp.dot(zo, ad[...], preferred_element_type=F32)).astype(BF)
     mixed_out[...] = mixed
     moe_out[...] = norm(mixed.astype(F32), gain_moe[...])
 
 
-def attention(tok, adapt, *others):
-    count, width = tok[0].shape
-    wq, wk, wv, wo = others[-4:]
+def attention(adapt, own, *others):
+    count, width = own.shape
+    wo = others[-1]
     vm = pl.BlockSpec(memory_space=pltpu.VMEM)
     anywhere = pl.BlockSpec(memory_space=pl.ANY)
     rows = jax.ShapeDtypeStruct((count, width), BF)
     return pl.pallas_call(
         attention_kernel,
         out_shape=(rows, rows),
-        in_specs=[vm] * (10 + len(others)) + [anywhere] * 4,
+        in_specs=[vm] * (8 + len(others)) + [anywhere],
         out_specs=(vm, vm),
         scratch_shapes=[
-            pltpu.VMEM(wq.shape, BF), pltpu.VMEM(wk.shape, BF), pltpu.VMEM(wv.shape, BF),
-            pltpu.VMEM(wo.shape, BF), pltpu.VMEM((6 * count, width), BF),
-            pltpu.VMEM((384, width), BF), pltpu.VMEM((count, width), BF),
-            pltpu.VMEM((6 * count, 512), BF), pltpu.VMEM((6 * count, 512), BF),
-            pltpu.VMEM((count, width), BF), pltpu.SemaphoreType.DMA((4,)),
+            pltpu.VMEM(wo.shape, BF), pltpu.VMEM((384, width), BF),
+            pltpu.VMEM((4, 6 * count, 128), BF), pltpu.VMEM((5 * count, 512), BF),
+            pltpu.VMEM((5 * count, 512), BF), pltpu.VMEM((count, width), BF),
+            pltpu.VMEM((6 * count, 5 * count), F32), pltpu.VMEM((6 * count, 5 * count), BF),
+            pltpu.SemaphoreType.DMA,
         ],
-        compiler_params=pltpu.CompilerParams(vmem_limit_bytes=48 << 20),
+        compiler_params=pltpu.CompilerParams(vmem_limit_bytes=40 << 20),
         cost_estimate=pl.CostEstimate(flops=6 << 30, transcendentals=0,
                                       bytes_accessed=16 << 20),
         name="attention_block",
-    )(*tok, *adapt, *others)
+    )(*adapt, own, *others)
 
 
 def expert_kernel(sizes, *refs):
@@ -235,27 +281,36 @@
 
     lax.fori_loop(0, pairs, take, 0)
     size = min(rows_all, 320)
-    for e in range(3):
-        halves = [2 * e, 2 * e + 1] if e < 2 else [4]
-        for s in halves:
-            for copy in weights[s]:
-                copy.wait()
-
-        def run(c, carry, e=e, halves=halves):
+
+    def ffn(e, count):
+        for h in range(count):
+            for k, (src, dst) in enumerate([(gate_hbm, gate), (up_hbm, up)]):
+                pltpu.make_async_copy(src.at[0], dst.at[0], sem_w.at[6 * e + 3 * h + k]).wait()
+            pltpu.make_async_copy(down_hbm.at[0], down.at[pl.ds(0, 256)],
+                                  sem_w.at[6 * e + 3 * h + 2]).wait()
+
+        def run(c, carry):
             at = pl.ds(pl.multiple_of(c * size, 16), size)
             rows = xe[e, at, :]
             hidden = []
-            for s in halves:
-                g = jnp.dot(rows, gate[s], preferred_element_type=F32)
-                u = jnp.dot(rows, up[s], preferred_element_type=F32)
+            for h in range(count):
+                g = jnp.dot(rows, gate[2 * e + h], preferred_element_type=F32)
+                u = jnp.dot(rows, up[2 * e + h], preferred_element_type=F32)
                 hidden.append((g / (1.0 + jnp.exp(-g)) * u).astype(BF))
             hidden = jnp.concatenate(hidden, axis=1)
-            maps = down[512 * e:512 * e + 256 * len(halves), :]
+            maps = down[pl.ds(pl.multiple_of(512 * e, 256), 256 * count), :]
             out = jnp.dot(hidden, maps, preferred_element_type=F32)
             ho[e, at, :] = (out * scale[e, at, :]).astype(BF)
             return carry
 
         lax.fori_loop(0, rows_all // size, run, 0)
+
+    def whole(e, carry):
+        ffn(e, 2)
+        return carry
+
+    lax.fori_loop(0, 2, whole, 0)
+    ffn(2, 1)
 
     def combine(i, carry):
         hot = jnp.concatenate([jnp.where(p, 1.0, 0.0) for p in places(i)]).astype(BF)
@@ -342,19 +397,10 @@
     held = lax.all_to_all(payload, "grp", 0, 0, tiled=True)
     back1 = lax.ppermute(own, "seq", [(s, s + 2) for s in range(6)])
     back2 = lax.ppermute(own, "seq", [(s, s + 4) for s in range(4)])
-    picked = jnp.stack([lax.dynamic_index_in_dim(held, prompt_adapter[0, p], 0, False)
-                        for p in range(3)]).reshape(48, width)
-    turn = [picked] + [lax.ppermute(picked, "seq", [(s, (s + d) % 8) for s in range(8)])
-                       for d in (2, 6, 4)]
-    adapt = turn + [partner(piece) for piece in turn]
-    tok = [own, back1, back2]
-    tok = tok + [partner(rows) for rows in tok]
-
     lens = lengths[0]
     ends = jnp.cumsum(lens)
     starts = ends - lens
-    other = me ^ 1
-    blocks = jnp.stack([me, me - 2, me - 4, other, other - 2, other - 4])
+    blocks = me - jnp.array([0, 2, 4, 1, 3], jnp.int32)
     row = jnp.arange(count, dtype=jnp.int32)
     index = (blocks[:, None] * count + row[None, :]).reshape(-1)
     document = jnp.sum((index[:, None] >= ends[None, :]).astype(jnp.int32), axis=1)
@@ -367,21 +413,32 @@
     far_cos, far_sin = jnp.cos(far), jnp.sin(far)
 
     def by_document(values):
-        docs = document.reshape(6, count, 1)
+        docs = document.reshape(5, count, 1)
         return jnp.where(docs == 0, values[:, None, 0], jnp.where(
             docs == 1, values[:, None, 1], values[:, None, 2]))
 
     far_cos, far_sin = by_document(far_cos), by_document(far_sin)
-    cosine = (far_cos * near_cos - far_sin * near_sin).reshape(6 * count, 128)
-    sine = ((far_sin * near_cos + far_cos * near_sin) * sign).reshape(6 * count, 128)
+    cosine = (far_cos * near_cos - far_sin * near_sin).reshape(5 * count, 128)
+    sine = ((far_sin * near_cos + far_cos * near_sin) * sign).reshape(5 * count, 128)
     row_index = index[:count]
     columns = jnp.arange(384, dtype=jnp.int32)[None, :]
     key_document = jnp.where(index >= 0, document, -1)
 
+    held, cosine, sine, document, index, key_document, row_index = lax.optimization_barrier(
+        (held, cosine, sine, document, index, key_document, row_index))
+    picked = jnp.stack([lax.dynamic_index_in_dim(held, prompt_adapter[0, p], 0, False)
+                        for p in range(3)]).reshape(48, width)
+    turn = [picked] + [lax.ppermute(picked, "seq", [(s, (s + d) % 8) for s in range(8)])
+                       for d in (2, 6, 4)]
+    adapt = turn + [partner(piece) for piece in turn]
+    odd_core = me % 2 == 1
+    tok = [own, back1, back2, partner(jnp.where(odd_core, back1, own)),
+           partner(jnp.where(odd_core, back2, back1))]
+    base = base_projections(tok, attention_gain[None], query_weight, key_weight, value_weight)
+
     mixed, moe_in = attention(
-        tok, adapt, attention_gain[None], expert_gain[None], cosine, sine, key_document[None],
-        index[None], document[:, None], row_index[:, None], columns // 16 % 3, columns % 16,
-        query_weight, key_weight, value_weight, output_weight)
+        adapt, own, *base, expert_gain[None], cosine, sine, key_document[None], index[None],
+        document[:, None], row_index[:, None], columns // 16 % 3, columns % 16, output_weight)
 
     rel = jnp.array([0, 3, 1, 2], jnp.int32)
     first, second = jnp.where(me % 2 == 0, grp % 4, grp // 4), jnp.where(
@@ -396,28 +453,40 @@
     odd = (grp % 2).astype(jnp.int32)[None]
     weights = (gate_weight, up_weight, down_weight)
 
+    def share(pieces, which):
+        return experts(pieces, odd, jnp.stack([route_in[k] for k in which]), *weights)
+
     line = lax.optimization_barrier(
         [shift(moe_in, 0, 1), shift(moe_in, 0, -1), shift(moe_in, 0, 2)])
-    plane = jnp.stack([moe_in] + line)
-    minus, plus = shift(plane, 1, 1), shift(plane, 1, -1)
-    (done_own,) = experts([plane], odd, route_in[:2], *weights)
-    minus, plus, done_own = lax.optimization_barrier((minus, plus, done_own))
-    ahead, behind = shift(minus[:2], 1, 1), shift(plus[2:], 1, -1)
-    done_minus, done_plus = experts([minus, plus], odd, route_in[2:6], *weights)
-    ahead, behind, done_minus, done_plus = lax.optimization_barrier(
-        (ahead, behind, done_minus, done_plus))
-    done_ahead, done_behind = experts([ahead, behind], odd, route_in[6:], *weights)
-
-    ahead, behind = lax.optimization_barrier(
-        (shift(done_ahead, 1, 1), shift(done_behind, 1, -1)))
-    plus = jnp.concatenate([(wide(done_plus[:2]) + wide(ahead)).astype(BF), done_plus[2:]])
-    minus = jnp.concatenate([done_minus[:2], (wide(done_minus[2:]) + wide(behind)).astype(BF)])
-    plus, minus = lax.optimization_barrier((shift(plus, 1, 1), shift(minus, 1, -1)))
-    plane = wide(done_own) + wide(plus) + wide(minus)
-    low = plane[1:].astype(BF)
+    own_lo, own_hi = jnp.stack([moe_in, line[0]]), jnp.stack([line[1], line[2]])
+    minus_lo, plus_hi = shift(own_lo, 1, 1), shift(own_hi, 1, -1)
+    minus_hi, plus_lo = shift(own_hi, 1, 1), shift(own_lo, 1, -1)
+    own_lo, own_hi = share([own_lo, own_hi], (0, 1))
+    minus_lo, plus_hi, own_lo, own_hi = lax.optimization_barrier(
+        (minus_lo, plus_hi, own_lo, own_hi))
+    first_lo, first_hi = share([minus_lo, plus_hi], (2, 5))
+    minus_lo, plus_hi, minus_hi, plus_lo, first_lo, first_hi = lax.optimization_barrier(
+        (minus_lo, plus_hi, minus_hi, plus_lo, first_lo, first_hi))
+    far_lo, far_hi = shift(minus_lo, 1, 1), shift(plus_hi, 1, -1)
+    minus_hi, plus_lo = share([minus_hi, plus_lo], (3, 4))
+    minus_lo, plus_hi, minus_hi, plus_lo, far_lo, far_hi = lax.optimization_barrier(
+        (first_lo, first_hi, minus_hi, plus_lo, far_lo, far_hi))
+
+    minus_lo, plus_hi = shift(minus_lo, 1, -1), shift(plus_hi, 1, 1)
+    far_lo, far_hi = share([far_lo, far_hi], (6, 7))
+    minus_lo, plus_hi, far_lo, far_hi = lax.optimization_barrier(
+        (minus_lo, plus_hi, far_lo, far_hi))
+    far_lo, far_hi = lax.optimization_barrier((shift(far_lo, 1, 1), shift(far_hi, 1, -1)))
+    plus_lo = shift((wide(plus_lo) + wide(far_lo)).astype(BF), 1, 1)
+    minus_hi = shift((wide(minus_hi) + wide(far_hi)).astype(BF), 1, -1)
+    minus_lo, plus_hi, minus_hi, plus_lo = lax.optimization_barrier(
+        (minus_lo, plus_hi, minus_hi, plus_lo))
+    own_lo = wide(own_lo) + wide(plus_lo) + wide(minus_lo)
+    own_hi = wide(own_hi) + wide(plus_hi) + wide(minus_hi)
     line = lax.optimization_barrier(
-        [shift(low[1], 0, 1), shift(low[0], 0, -1), shift(low[2], 0, 2)])
-    combined = plane[0] + wide(line[0]) + wide(line[1]) + wide(line[2])
+        [shift(own_hi[0].astype(BF), 0, 1), shift(own_lo[1].astype(BF), 0, -1),
+         shift(own_hi[1].astype(BF), 0, 2)])
+    combined = own_lo[0] + wide(line[0]) + wide(line[1]) + wide(line[2])
     hidden_out = (mixed.astype(F32) + combined).astype(BF)
 
     selector = (ends[:, None] - 1 == row_index[None, :]).astype(BF)

time: 241 us -> 240 us (level)
  waiting for transfers between devices: 63 us -> 49.2 us
  local copies, waits for them, and re-layouts: 15.9 us -> 22 us
  starting transfers between devices: 44.8 us -> 48.6 us
  blocking collectives: 49.8 us -> 52.3 us
    ppermute x14 -> x18, waiting for transfers between devices: 57.8 us -> 48.2 us  [shift(): return lax.ppermute(rows, WHOLE, pairs)]
    pallas_call x1, Pallas kernels: 24.8 us -> 15.6 us  [attention(): pl.pallas_call(attention_kernel, out_shape=(rows, rows), in_specs=[vm] *...]
    pallas_call x0 -> x1, Pallas kernels: none -> 6.09 us  [base_projections(): pl.pallas_call(base_kernel, out_shape=(jax.ShapeDtypeStruct((5 * count, w...]
    unnamed x40 -> x66, local copies, waits for them, and re-layouts: 5.93 us -> 11.9 us
    all_to_all x1, blocking collectives: 15.3 us -> 19.2 us  [body(): lax.all_to_all(jnp.broadcast_to(mine[None], (128, 3, part)), WHOLE, 0, 0,...]
    all_to_all x1, waiting for transfers between devices: 4.38 us -> 0.98 us  [body(): held = lax.all_to_all(payload, 'grp', 0, 0, tiled=True)]
    slice x7 -> x2, local copies, waits for them, and re-layouts: 3.58 us -> 0.52 us  [the longest x1 0.52 us: body(): row_index = index[:count]]
    ppermute x14 -> x18, starting transfers between devices: 17.7 us -> 20.6 us  [shift(): return lax.ppermute(rows, WHOLE, pairs)]
  transfers between devices with their start and end apart: 27 -> 30, of which waited for: 10 -> 9; matrix products, arithmetic and copies ran while one was open for 5% -> 6% of each run, Pallas kernels for 7% -> 13%
where the time goes in v3:
time: 240 us; the launch traced here: 239 us
  blocking collectives  52.3 us (22%)
  waiting for transfers between devices  49.2 us (20%)
  starting transfers between devices  48.6 us (20%)
  Pallas kernels  46.5 us (19%)
  local copies, waits for them, and re-layouts  22 us (9%)
  other arithmetic  10.9 us (5%)
  between operations  7.48 us (3%)
    ppermute x18, waiting for transfers between devices, shift(): return lax.ppermute(rows, WHOLE, pairs)  48.2 us
    pallas_call x4, Pallas kernels, experts(): pl.pallas_call(functools.partial(expert_kernel, sizes), out_shape=tuple((...  24.8 us
    ppermute x18, starting transfers between devices, shift(): return lax.ppermute(rows, WHOLE, pairs)  20.6 us
    all_to_all x1, blocking collectives, body(): mine = lax.all_to_all(split, 'seq', 0, 0, tiled=True)  19.5 us
    all_to_all x1, blocking collectives, body(): lax.all_to_all(jnp.broadcast_to(mine[None], (128, 3, part)), WHOLE, 0, 0,...  19.2 us
    pallas_call x1, Pallas kernels, attention(): pl.pallas_call(attention_kernel, out_shape=(rows, rows), in_specs=[vm] *...  15.6 us
    all_to_all x1, blocking collectives, body(): lax.all_to_all(jnp.broadcast_to(stats[None], (128, 128)), WHOLE, 0, 0, ti...  13.6 us
    unnamed x66, local copies, waits for them, and re-layouts  11.9 us
  transfers between devices with their start and end apart: 30, of which 9 were waited for; matrix products, arithmetic and copies ran while one was open for 6% of the time, Pallas kernels for 13%

profile of v3, /device:TPU:1, one launch (start us, length us, event | category | flops | bytes accessed | tf_op | source)
XLA Modules:
  0.0 239.1 jit_solution(5664980227682596647)
XLA Ops:
  5.9 4.0 %collective-permute-start.7 = (bf16[128,1536]{1,0:T(8,128)(2,1)S(1)}, bf16[128,1536]{1,0:T(8,128)(2,1)S(1)}, u32[]{:S(2)}, u32[]{:S(2)}) collective-permute-start(bf16[128,1536]{1,0:T(8,128)(2,1)S(1)} %bitcast.165), channel_id=1, source_target_pairs={{0,32},{16,48},{32,64},{48,80},{64,96},{80,112},{1,33},{17,49},{33... | collective-permute-start | bytes 1179656 | tf_op jit(solution)/shard_map/ppermute | solution.py:398
  9.9 4.4 %collective-permute-start.8 = (bf16[128,1536]{1,0:T(8,128)(2,1)S(1)}, bf16[128,1536]{1,0:T(8,128)(2,1)S(1)}, u32[]{:S(2)}, u32[]{:S(2)}) collective-permute-start(bf16[128,1536]{1,0:T(8,128)(2,1)S(1)} %bitcast.166), channel_id=1, source_target_pairs={{0,64},{16,80},{32,96},{48,112},{1,65},{17,81},{33,97},{49,113},{2... | collective-permute-start | bytes 1179656 | tf_op jit(solution)/shard_map/ppermute | solution.py:399
  14.3 7.8 %all-to-all-start = ((bf16[16,16,1536]{2,1,0:T(8,128)(2,1)}), bf16[16,16,1536]{2,1,0:T(8,128)(2,1)}, u32[]{:S(2)}, u32[]{:S(2)}) async-start(bf16[16,16,1536]{2,1,0:T(8,128)(2,1)} %maximum_maximum_fusion), calls=%async_computation | async-start | bytes 1572864 | tf_op jit(solution)/shard_map/all_to_all | solution.py:397
  35.9 2.7 %collective-permute-start.1 = (bf16[48,1536]{1,0:T(8,128)(2,1)S(1)}, bf16[48,1536]{1,0:T(8,128)(2,1)S(1)}, u32[]{:S(2)}, u32[]{:S(2)}) collective-permute-start(bf16[48,1536]{1,0:T(8,128)(2,1)S(1)} %bitcast.172), channel_id=1, source_target_pairs={{0,96},{16,112},{32,0},{48,16},{64,32},{80,48},{96,64},{112,80},{1... | collective-permute-start | bytes 442376 | tf_op jit(solution)/shard_map/ppermute | solution.py:431
  40.8 3.2 %collective-permute-start.3 = (bf16[48,1536]{1,0:T(8,128)(2,1)S(1)}, bf16[48,1536]{1,0:T(8,128)(2,1)S(1)}, u32[]{:S(2)}, u32[]{:S(2)}) collective-permute-start(bf16[48,1536]{1,0:T(8,128)(2,1)S(1)} %bitcast.174), channel_id=1, source_target_pairs={{0,16},{16,0},{32,48},{48,32},{64,80},{80,64},{96,112},{112,96},{1... | collective-permute-start | bytes 442376 | tf_op jit(solution)/shard_map/ppermute | solution.py:39
  44.0 2.3 collective-permute-start.4
  48.4 2.3 copy-done.9
  53.6 6.1 %base_block.1 = (bf16[640,1536]{1,0:T(8,128)(2,1)S(1)}, f32[128,1536]{1,0:T(8,128)S(1)}, f32[640,512]{1,0:T(8,128)S(1)}, f32[640,512]{1,0:T(8,128)S(1)}) custom-call(bf16[128,1536]{1,0:T(8,128)(2,1)S(1)} %bitcast.168, bf16[128,1536]{1,0:T(8,128)(2,1)S(1)} %collective-permute-done.7.t1, bf16[128,1536]{1,0:T(8,128)(2,1)S(1)} %collective-permute-done.8.t2, ...), custom_call_target="tpu_custom_call" | custom-call | flops 5368709120 | bytes 14680064 | tf_op jit(solution)/shard_map/base_block/pallas_call | solution.py:90
  62.5 15.6 %attention_block.1 = (bf16[128,1536]{1,0:T(8,128)(2,1)S(1)}, bf16[128,1536]{1,0:T(8,128)(2,1)S(1)}) custom-call(bf16[48,1536]{1,0:T(8,128)(2,1)S(1)} %bitcast.175, bf16[48,1536]{1,0:T(8,128)(2,1)S(1)} %copy-done.14, bf16[48,1536]{1,0:T(8,128)(2,1)S(1)} %copy-done.16, bf16[48,1536]{1,0:T(8,128)(2,1)} %collective-permute-done.2.refs_3_, ...), custom_call_target="tpu_custom_call" | custom-call | flops 6442450944 | bytes 16777216 | tf_op jit(solution)/shard_map/attention_block/pallas_call | solution.py:214
  78.8 2.7 %collective-permute-start.12 = (bf16[128,1536]{1,0:T(8,128)(2,1)S(1)}, bf16[128,1536]{1,0:T(8,128)(2,1)S(1)}, u32[]{:S(2)}, u32[]{:S(2)}) collective-permute-start(bf16[128,1536]{1,0:T(8,128)(2,1)S(1)} %get-tuple-element.71), channel_id=1, source_target_pairs={{0,3},{1,0},{2,1},{3,2},{4,7},{5,4},{6,5},{7,6},{8,11},{9,8},{10,9... | collective-permute-start | bytes 1179656 | tf_op jit(solution)/shard_map/ppermute | solution.py:35
  83.5 7.7 %collective-permute-done.11 = bf16[128,1536]{1,0:T(8,128)(2,1)S(1)} collective-permute-done((bf16[128,1536]{1,0:T(8,128)(2,1)S(1)}, bf16[128,1536]{1,0:T(8,128)(2,1)S(1)}, u32[]{:S(2)}, u32[]{:S(2)}) %collective-permute-start.11) | collective-permute-done | bytes 393248 | tf_op jit(solution)/shard_map/ppermute | solution.py:35
  98.8 2.4 %collective-permute-start.17 = (bf16[2,128,1536]{2,1,0:T(8,128)(2,1)S(1)}, bf16[2,128,1536]{2,1,0:T(8,128)(2,1)S(1)}, u32[]{:S(2)}, u32[]{:S(2)}) collective-permute-start(bf16[2,128,1536]{2,1,0:T(8,128)(2,1)S(1)} %pad_maximum_fusion.refs_0_), channel_id=1, source_target_pairs={{0,12},{1,13},{2,14},{3,15},{4,0},{5,1},{6,2},{7,3},{8,4},{9,5},{1... | collective-permute-start | bytes 2359304 | tf_op jit(solution)/shard_map/ppermute | solution.py:35
  101.2 2.1 copy-done.1
  103.3 6.3 %expert_block.4 = (bf16[2,128,1536]{2,1,0:T(8,128)(2,1)S(1)}, bf16[2,128,1536]{2,1,0:T(8,128)(2,1)S(1)}) custom-call(bf16[2,128,1536]{2,1,0:T(8,128)(2,1)S(1)} %pad_maximum_fusion.refs_0_, bf16[2,128,1536]{2,1,0:T(8,128)(2,1)S(1)} %pad_maximum_fusion.1.refs_1_, s32[1]{0:T(128)} %bitcast.41.refs_2_, f32[2,8,256]{2,1,0:T(8,128)S(1)} %pad_maximum_fusion.3.refs_3_, ...), custom_call_target="tpu_custom_call" | custom-call | flops 1887436800 | bytes 12582912 | tf_op jit(solution)/shard_map/expert_block/pallas_call | solution.py:340
  109.7 6.3 %expert_block.5 = (bf16[2,128,1536]{2,1,0:T(8,128)(2,1)S(1)}, bf16[2,128,1536]{2,1,0:T(8,128)(2,1)S(1)}) custom-call(bf16[2,128,1536]{2,1,0:T(8,128)(2,1)} %collective-permute-done.14.refs_0_, bf16[2,128,1536]{2,1,0:T(8,128)(2,1)S(1)} %collective-permute-done.15.refs_1_, s32[1]{0:T(128)} %bitcast.41.refs_2_, f32[2,8,256]{2,1,0:T(8,128)S(1)} %pad_maximum_fusion.4.refs_3_, ...), custom_call_target="tpu_custom_call" | custom-call | flops 1887436800 | bytes 12582912 | tf_op jit(solution)/shard_map/expert_block/pallas_call | solution.py:340
  116.0 2.7 %collective-permute-start.19 = (bf16[2,128,1536]{2,1,0:T(8,128)(2,1)S(1)}, bf16[2,128,1536]{2,1,0:T(8,128)(2,1)S(1)}, u32[]{:S(2)}, u32[]{:S(2)}) collective-permute-start(bf16[2,128,1536]{2,1,0:T(8,128)(2,1)S(1)} %collective-permute-done.15.refs_1_), channel_id=1, source_target_pairs={{0,12},{1,13},{2,14},{3,15},{4,0},{5,1},{6,2},{7,3},{8,4},{9,5},{1... | collective-permute-start | bytes 2359304 | tf_op jit(solution)/shard_map/ppermute | solution.py:35
  118.7 6.1 %expert_block.6 = (bf16[2,128,1536]{2,1,0:T(8,128)(2,1)S(1)}, bf16[2,128,1536]{2,1,0:T(8,128)(2,1)S(1)}) custom-call(bf16[2,128,1536]{2,1,0:T(8,128)(2,1)S(1)} %collective-permute-done.16.refs_0_, bf16[2,128,1536]{2,1,0:T(8,128)(2,1)S(1)} %collective-permute-done.17.refs_1_, s32[1]{0:T(128)} %bitcast.41.refs_2_, f32[2,8,256]{2,1,0:T(8,128)S(1)} %pad_maximum_fusion.5.refs_3_, ...), custom_call_target="tpu_custom_call" | custom-call | flops 1887436800 | bytes 12582912 | tf_op jit(solution)/shard_map/expert_block/pallas_call | solution.py:340
  124.9 3.7 %collective-permute-done.18.refs_0_ = bf16[2,128,1536]{2,1,0:T(8,128)(2,1)S(1)} collective-permute-done((bf16[2,128,1536]{2,1,0:T(8,128)(2,1)}, bf16[2,128,1536]{2,1,0:T(8,128)(2,1)S(1)}, u32[]{:S(2)}, u32[]{:S(2)}) %collective-permute-start.18) | collective-permute-done | bytes 786464 | tf_op jit(solution)/shard_map/ppermute | solution.py:35
  128.6 2.5 %collective-permute-start.20 = (bf16[2,128,1536]{2,1,0:T(8,128)(2,1)S(1)}, bf16[2,128,1536]{2,1,0:T(8,128)(2,1)S(1)}, u32[]{:S(2)}, u32[]{:S(2)}) collective-permute-start(bf16[2,128,1536]{2,1,0:T(8,128)(2,1)S(1)} %get-tuple-element.90), channel_id=1, source_target_pairs={{0,12},{1,13},{2,14},{3,15},{4,0},{5,1},{6,2},{7,3},{8,4},{9,5},{1... | collective-permute-start | bytes 2359304 | tf_op jit(solution)/shard_map/ppermute | solution.py:35
  131.1 6.1 %expert_block.7 = (bf16[2,128,1536]{2,1,0:T(8,128)(2,1)S(1)}, bf16[2,128,1536]{2,1,0:T(8,128)(2,1)S(1)}) custom-call(bf16[2,128,1536]{2,1,0:T(8,128)(2,1)S(1)} %collective-permute-done.18.refs_0_, bf16[2,128,1536]{2,1,0:T(8,128)(2,1)S(1)} %collective-permute-done.19.refs_1_, s32[1]{0:T(128)} %bitcast.41.refs_2_, f32[2,8,256]{2,1,0:T(8,128)S(1)} %pad_maximum_fusion.6.refs_3_, ...), custom_call_target="tpu_custom_call" | custom-call | flops 1887436800 | bytes 12582912 | tf_op jit(solution)/shard_map/expert_block/pallas_call | solution.py:340
  137.2 2.8 %collective-permute-done.20 = bf16[2,128,1536]{2,1,0:T(8,128)(2,1)S(1)} collective-permute-done((bf16[2,128,1536]{2,1,0:T(8,128)(2,1)S(1)}, bf16[2,128,1536]{2,1,0:T(8,128)(2,1)S(1)}, u32[]{:S(2)}, u32[]{:S(2)}) %collective-permute-start.20) | collective-permute-done | bytes 786464 | tf_op jit(solution)/shard_map/ppermute | solution.py:35
  140.0 3.4 %collective-permute-done.21 = bf16[2,128,1536]{2,1,0:T(8,128)(2,1)S(1)} collective-permute-done((bf16[2,128,1536]{2,1,0:T(8,128)(2,1)S(1)}, bf16[2,128,1536]{2,1,0:T(8,128)(2,1)S(1)}, u32[]{:S(2)}, u32[]{:S(2)}) %collective-permute-start.21) | collective-permute-done | bytes 786464 | tf_op jit(solution)/shard_map/ppermute | solution.py:35
  143.4 2.7 %collective-permute-start.23 = (bf16[2,128,1536]{2,1,0:T(8,128)(2,1)S(1)}, bf16[2,128,1536]{2,1,0:T(8,128)(2,1)S(1)}, u32[]{:S(2)}, u32[]{:S(2)}) collective-permute-start(bf16[2,128,1536]{2,1,0:T(8,128)(2,1)S(1)} %get-tuple-element.100), channel_id=1, source_target_pairs={{0,12},{1,13},{2,14},{3,15},{4,0},{5,1},{6,2},{7,3},{8,4},{9,5},{1... | collective-permute-start | bytes 2359304 | tf_op jit(solution)/shard_map/ppermute | solution.py:35
  146.1 9.7 %collective-permute-done.22 = bf16[2,128,1536]{2,1,0:T(8,128)(2,1)S(1)} collective-permute-done((bf16[2,128,1536]{2,1,0:T(8,128)(2,1)S(1)}, bf16[2,128,1536]{2,1,0:T(8,128)(2,1)S(1)}, u32[]{:S(2)}, u32[]{:S(2)}) %collective-permute-start.22) | collective-permute-done | bytes 786464 | tf_op jit(solution)/shard_map/ppermute | solution.py:35
  156.2 2.7 %collective-permute-start.24 = (bf16[2,128,1536]{2,1,0:T(8,128)(2,1)S(1)}, bf16[2,128,1536]{2,1,0:T(8,128)(2,1)S(1)}, u32[]{:S(2)}, u32[]{:S(2)}) collective-permute-start(bf16[2,128,1536]{2,1,0:T(8,128)(2,1)S(1)} %add_convert_fusion.2), channel_id=1, source_target_pairs={{0,12},{1,13},{2,14},{3,15},{4,0},{5,1},{6,2},{7,3},{8,4},{9,5},{1... | collective-permute-start | bytes 2359304 | tf_op jit(solution)/shard_map/ppermute | solution.py:35
  159.0 9.4 %collective-permute-done.25 = bf16[2,128,1536]{2,1,0:T(8,128)(2,1)S(1)} collective-permute-done((bf16[2,128,1536]{2,1,0:T(8,128)(2,1)S(1)}, bf16[2,128,1536]{2,1,0:T(8,128)(2,1)S(1)}, u32[]{:S(2)}, u32[]{:S(2)}) %collective-permute-start.25) | collective-permute-done | bytes 786464 | tf_op jit(solution)/shard_map/ppermute | solution.py:35
  168.8 2.8 %collective-permute-start.28 = (bf16[128,1536]{1,0:T(8,128)(2,1)S(1)}, bf16[128,1536]{1,0:T(8,128)(2,1)S(1)}, u32[]{:S(2)}, u32[]{:S(2)}) collective-permute-start(bf16[128,1536]{1,0:T(8,128)(2,1)S(1)} %get-tuple-element.116), channel_id=1, source_target_pairs={{0,2},{1,3},{2,0},{3,1},{4,6},{5,7},{6,4},{7,5},{8,10},{9,11},{10,... | collective-permute-start | bytes 1179656 | tf_op jit(solution)/shard_map/ppermute | solution.py:35
  172.1 5.8 %collective-permute-done.26 = bf16[128,1536]{1,0:T(8,128)(2,1)S(1)} collective-permute-done((bf16[128,1536]{1,0:T(8,128)(2,1)S(1)}, bf16[128,1536]{1,0:T(8,128)(2,1)S(1)}, u32[]{:S(2)}, u32[]{:S(2)}) %collective-permute-start.26) | collective-permute-done | bytes 393248 | tf_op jit(solution)/shard_map/ppermute | solution.py:35
  177.8 5.7 %collective-permute-done.28 = bf16[128,1536]{1,0:T(8,128)(2,1)S(1)} collective-permute-done((bf16[128,1536]{1,0:T(8,128)(2,1)S(1)}, bf16[128,1536]{1,0:T(8,128)(2,1)S(1)}, u32[]{:S(2)}, u32[]{:S(2)}) %collective-permute-start.28) | collective-permute-done | bytes 393248 | tf_op jit(solution)/shard_map/ppermute | solution.py:35
  184.4 19.5 %all_to_all.24 = bf16[8,3,192]{2,1,0:T(4,128)(2,1)S(1)} all-to-all(bf16[8,3,192]{2,1,0:T(4,128)(2,1)S(1)} %bitcast.182), channel_id=1, replica_groups=mesh['seq'=8,'grp'=16] {'seq'}, dimensions={0} | all-to-all | bytes 18432 | tf_op jit(solution)/shard_map/all_to_all | solution.py:497
  204.0 19.2 %all_to_all.25 = bf16[128,3,192]{2,1,0:T(4,128)(2,1)S(1)} all-to-all(bf16[128,3,192]{2,1,0:T(4,128)(2,1)S(1)} %broadcast_in_dim.230), channel_id=1, replica_groups=mesh['seq'=8,'grp'=16] {'seq','grp'}, dimensions={0} | all-to-all | bytes 294912 | tf_op jit(solution)/shard_map/all_to_all | solution.py:499
  224.4 13.6 %all_to_all.26 = f32[128,1,128]{2,1,0:T(1,128)S(1)} all-to-all(f32[128,1,128]{2,1,0:T(1,128)S(1)} %broadcast_in_dim.232), channel_id=1, replica_groups=mesh['seq'=8,'grp'=16] {'seq','grp'}, dimensions={0} | all-to-all | bytes 131072 | tf_op jit(solution)/shard_map/all_to_all | solution.py:506
  (191 shorter events, 37.5 us)
Async XLA Ops:
  0.6 223.0 %copy-start = (bf16[1536,384]{1,0:T(8,128)(2,1)S(1)}, bf16[1536,384]{1,0:T(8,128)(2,1)}, u32[]{:S(2)}) copy-start(bf16[1536,384]{1,0:T(8,128)(2,1)} %param.40) | copy-start | bytes 3538948
  5.9 25.5 %collective-permute-start.7 = (bf16[128,1536]{1,0:T(8,128)(2,1)S(1)}, bf16[128,1536]{1,0:T(8,128)(2,1)S(1)}, u32[]{:S(2)}, u32[]{:S(2)}) collective-permute-start(bf16[128,1536]{1,0:T(8,128)(2,1)S(1)} %bitcast.165), channel_id=1, source_target_pairs={{0,32},{16,48},{32,64},{48,80},{64,96},{80,112},{1,33},{17,49},{33... | collective-permute-start | bytes 1179656 | tf_op jit(solution)/shard_map/ppermute | solution.py:398
  9.9 21.6 %collective-permute-start.8 = (bf16[128,1536]{1,0:T(8,128)(2,1)S(1)}, bf16[128,1536]{1,0:T(8,128)(2,1)S(1)}, u32[]{:S(2)}, u32[]{:S(2)}) collective-permute-start(bf16[128,1536]{1,0:T(8,128)(2,1)S(1)} %bitcast.166), channel_id=1, source_target_pairs={{0,64},{16,80},{32,96},{48,112},{1,65},{17,81},{33,97},{49,113},{2... | collective-permute-start | bytes 1179656 | tf_op jit(solution)/shard_map/ppermute | solution.py:399
  14.3 20.6 %all-to-all-start = ((bf16[16,16,1536]{2,1,0:T(8,128)(2,1)}), bf16[16,16,1536]{2,1,0:T(8,128)(2,1)}, u32[]{:S(2)}, u32[]{:S(2)}) async-start(bf16[16,16,1536]{2,1,0:T(8,128)(2,1)} %maximum_maximum_fusion), calls=%async_computation | async-start | bytes 1572864 | tf_op jit(solution)/shard_map/all_to_all | solution.py:397
  32.4 8.4 %collective-permute-start.10 = (bf16[128,1536]{1,0:T(8,128)(2,1)}, bf16[128,1536]{1,0:T(8,128)(2,1)}, u32[]{:S(2)}, u32[]{:S(2)}) collective-permute-start(bf16[128,1536]{1,0:T(8,128)(2,1)} %get-tuple-element.121), channel_id=1, source_target_pairs={{0,16},{16,0},{32,48},{48,32},{64,80},{80,64},{96,112},{112,96},{1... | collective-permute-start | bytes 1179656 | tf_op jit(solution)/shard_map/ppermute | solution.py:39
  33.9 14.5 %collective-permute-start.9 = (bf16[128,1536]{1,0:T(8,128)(2,1)}, bf16[128,1536]{1,0:T(8,128)(2,1)}, u32[]{:S(2)}, u32[]{:S(2)}) collective-permute-start(bf16[128,1536]{1,0:T(8,128)(2,1)} %get-tuple-element.122), channel_id=1, source_target_pairs={{0,16},{16,0},{32,48},{48,32},{64,80},{80,64},{96,112},{112,96},{1... | collective-permute-start | bytes 1179656 | tf_op jit(solution)/shard_map/ppermute | solution.py:39
  35.8 8.2 %collective-permute-start = (bf16[48,1536]{1,0:T(8,128)(2,1)S(1)}, bf16[48,1536]{1,0:T(8,128)(2,1)S(1)}, u32[]{:S(2)}, u32[]{:S(2)}) collective-permute-start(bf16[48,1536]{1,0:T(8,128)(2,1)S(1)} %bitcast.171), channel_id=1, source_target_pairs={{0,32},{16,48},{32,64},{48,80},{64,96},{80,112},{96,0},{112,16},{1... | collective-permute-start | bytes 442376 | tf_op jit(solution)/shard_map/ppermute | solution.py:431
  35.9 10.4 %collective-permute-start.1 = (bf16[48,1536]{1,0:T(8,128)(2,1)S(1)}, bf16[48,1536]{1,0:T(8,128)(2,1)S(1)}, u32[]{:S(2)}, u32[]{:S(2)}) collective-permute-start(bf16[48,1536]{1,0:T(8,128)(2,1)S(1)} %bitcast.172), channel_id=1, source_target_pairs={{0,96},{16,112},{32,0},{48,16},{64,32},{80,48},{96,64},{112,80},{1... | collective-permute-start | bytes 442376 | tf_op jit(solution)/shard_map/ppermute | solution.py:431
  38.6 7.9 %collective-permute-start.2 = (bf16[48,1536]{1,0:T(8,128)(2,1)S(1)}, bf16[48,1536]{1,0:T(8,128)(2,1)}, u32[]{:S(2)}, u32[]{:S(2)}) collective-permute-start(bf16[48,1536]{1,0:T(8,128)(2,1)S(1)} %bitcast.173), channel_id=1, source_target_pairs={{0,64},{16,80},{32,96},{48,112},{64,0},{80,16},{96,32},{112,48},{1... | collective-permute-start | bytes 442376 | tf_op jit(solution)/shard_map/ppermute | solution.py:431
  40.8 18.9 %collective-permute-start.3 = (bf16[48,1536]{1,0:T(8,128)(2,1)S(1)}, bf16[48,1536]{1,0:T(8,128)(2,1)S(1)}, u32[]{:S(2)}, u32[]{:S(2)}) collective-permute-start(bf16[48,1536]{1,0:T(8,128)(2,1)S(1)} %bitcast.174), channel_id=1, source_target_pairs={{0,16},{16,0},{32,48},{48,32},{64,80},{80,64},{96,112},{112,96},{1... | collective-permute-start | bytes 442376 | tf_op jit(solution)/shard_map/ppermute | solution.py:39
  44.0 15.7 %collective-permute-start.4 = (bf16[48,1536]{1,0:T(8,128)(2,1)S(1)}, bf16[48,1536]{1,0:T(8,128)(2,1)S(1)}, u32[]{:S(2)}, u32[]{:S(2)}) collective-permute-start(bf16[48,1536]{1,0:T(8,128)(2,1)S(1)} %collective-permute-done.refs_1_), channel_id=1, source_target_pairs={{0,16},{16,0},{32,48},{48,32},{64,80},{80,64},{96,112},{112,96},{1... | collective-permute-start | bytes 442376 | tf_op jit(solution)/shard_map/ppermute | solution.py:39
  46.3 13.4 %collective-permute-start.5 = (bf16[48,1536]{1,0:T(8,128)(2,1)S(1)}, bf16[48,1536]{1,0:T(8,128)(2,1)S(1)}, u32[]{:S(2)}, u32[]{:S(2)}) collective-permute-start(bf16[48,1536]{1,0:T(8,128)(2,1)S(1)} %collective-permute-done.1.refs_2_), channel_id=1, source_target_pairs={{0,16},{16,0},{32,48},{48,32},{64,80},{80,64},{96,112},{112,96},{1... | collective-permute-start | bytes 442376 | tf_op jit(solution)/shard_map/ppermute | solution.py:39
  46.4 13.3 %collective-permute-start.6 = (bf16[48,1536]{1,0:T(8,128)(2,1)}, bf16[48,1536]{1,0:T(8,128)(2,1)S(1)}, u32[]{:S(2)}, u32[]{:S(2)}) collective-permute-start(bf16[48,1536]{1,0:T(8,128)(2,1)} %collective-permute-done.2.refs_3_), channel_id=1, source_target_pairs={{0,16},{16,0},{32,48},{48,32},{64,80},{80,64},{96,112},{112,96},{1... | collective-permute-start | bytes 442376 | tf_op jit(solution)/shard_map/ppermute | solution.py:39
  78.8 12.3 %collective-permute-start.11 = (bf16[128,1536]{1,0:T(8,128)(2,1)S(1)}, bf16[128,1536]{1,0:T(8,128)(2,1)S(1)}, u32[]{:S(2)}, u32[]{:S(2)}) collective-permute-start(bf16[128,1536]{1,0:T(8,128)(2,1)S(1)} %get-tuple-element.71), channel_id=1, source_target_pairs={{0,1},{1,2},{2,3},{3,0},{4,5},{5,6},{6,7},{7,4},{8,9},{9,10},{10,1... | collective-permute-start | bytes 1179656 | tf_op jit(solution)/shard_map/ppermute | solution.py:35
  78.8 12.3 %collective-permute-start.12 = (bf16[128,1536]{1,0:T(8,128)(2,1)S(1)}, bf16[128,1536]{1,0:T(8,128)(2,1)S(1)}, u32[]{:S(2)}, u32[]{:S(2)}) collective-permute-start(bf16[128,1536]{1,0:T(8,128)(2,1)S(1)} %get-tuple-element.71), channel_id=1, source_target_pairs={{0,3},{1,0},{2,1},{3,2},{4,7},{5,4},{6,5},{7,6},{8,11},{9,8},{10,9... | collective-permute-start | bytes 1179656 | tf_op jit(solution)/shard_map/ppermute | solution.py:35
  81.5 9.7 %collective-permute-start.13 = (bf16[128,1536]{1,0:T(8,128)(2,1)S(1)}, bf16[128,1536]{1,0:T(8,128)(2,1)}, u32[]{:S(2)}, u32[]{:S(2)}) collective-permute-start(bf16[128,1536]{1,0:T(8,128)(2,1)S(1)} %get-tuple-element.71), channel_id=1, source_target_pairs={{0,2},{1,3},{2,0},{3,1},{4,6},{5,7},{6,4},{7,5},{8,10},{9,11},{10,... | collective-permute-start | bytes 1179656 | tf_op jit(solution)/shard_map/ppermute | solution.py:35
  93.0 16.6 %collective-permute-start.15 = (bf16[2,128,1536]{2,1,0:T(8,128)(2,1)S(1)}, bf16[2,128,1536]{2,1,0:T(8,128)(2,1)S(1)}, u32[]{:S(2)}, u32[]{:S(2)}) collective-permute-start(bf16[2,128,1536]{2,1,0:T(8,128)(2,1)S(1)} %pad_maximum_fusion.1.refs_1_), channel_id=1, source_target_pairs={{0,12},{1,13},{2,14},{3,15},{4,0},{5,1},{6,2},{7,3},{8,4},{9,5},{1... | collective-permute-start | bytes 2359304 | tf_op jit(solution)/shard_map/ppermute | solution.py:35
  95.0 14.7 %collective-permute-start.14 = (bf16[2,128,1536]{2,1,0:T(8,128)(2,1)S(1)}, bf16[2,128,1536]{2,1,0:T(8,128)(2,1)}, u32[]{:S(2)}, u32[]{:S(2)}) collective-permute-start(bf16[2,128,1536]{2,1,0:T(8,128)(2,1)S(1)} %pad_maximum_fusion.refs_0_), channel_id=1, source_target_pairs={{0,4},{1,5},{2,6},{3,7},{4,8},{5,9},{6,10},{7,11},{8,12},{9,13},{1... | collective-permute-start | bytes 2359304 | tf_op jit(solution)/shard_map/ppermute | solution.py:35
  98.5 17.4 %collective-permute-start.16 = (bf16[2,128,1536]{2,1,0:T(8,128)(2,1)S(1)}, bf16[2,128,1536]{2,1,0:T(8,128)(2,1)S(1)}, u32[]{:S(2)}, u32[]{:S(2)}) collective-permute-start(bf16[2,128,1536]{2,1,0:T(8,128)(2,1)S(1)} %pad_maximum_fusion.1.refs_1_), channel_id=1, source_target_pairs={{0,4},{1,5},{2,6},{3,7},{4,8},{5,9},{6,10},{7,11},{8,12},{9,13},{1... | collective-permute-start | bytes 2359304 | tf_op jit(solution)/shard_map/ppermute | solution.py:35
  98.8 17.2 %collective-permute-start.17 = (bf16[2,128,1536]{2,1,0:T(8,128)(2,1)S(1)}, bf16[2,128,1536]{2,1,0:T(8,128)(2,1)S(1)}, u32[]{:S(2)}, u32[]{:S(2)}) collective-permute-start(bf16[2,128,1536]{2,1,0:T(8,128)(2,1)S(1)} %pad_maximum_fusion.refs_0_), channel_id=1, source_target_pairs={{0,12},{1,13},{2,14},{3,15},{4,0},{5,1},{6,2},{7,3},{8,4},{9,5},{1... | collective-permute-start | bytes 2359304 | tf_op jit(solution)/shard_map/ppermute | solution.py:35
  116.0 12.6 %collective-permute-start.18 = (bf16[2,128,1536]{2,1,0:T(8,128)(2,1)}, bf16[2,128,1536]{2,1,0:T(8,128)(2,1)S(1)}, u32[]{:S(2)}, u32[]{:S(2)}) collective-permute-start(bf16[2,128,1536]{2,1,0:T(8,128)(2,1)} %collective-permute-done.14.refs_0_), channel_id=1, source_target_pairs={{0,4},{1,5},{2,6},{3,7},{4,8},{5,9},{6,10},{7,11},{8,12},{9,13},{1... | collective-permute-start | bytes 2359304 | tf_op jit(solution)/shard_map/ppermute | solution.py:35
  116.0 12.5 %collective-permute-start.19 = (bf16[2,128,1536]{2,1,0:T(8,128)(2,1)S(1)}, bf16[2,128,1536]{2,1,0:T(8,128)(2,1)S(1)}, u32[]{:S(2)}, u32[]{:S(2)}) collective-permute-start(bf16[2,128,1536]{2,1,0:T(8,128)(2,1)S(1)} %collective-permute-done.15.refs_1_), channel_id=1, source_target_pairs={{0,12},{1,13},{2,14},{3,15},{4,0},{5,1},{6,2},{7,3},{8,4},{9,5},{1... | collective-permute-start | bytes 2359304 | tf_op jit(solution)/shard_map/ppermute | solution.py:35
  128.6 11.4 %collective-permute-start.20 = (bf16[2,128,1536]{2,1,0:T(8,128)(2,1)S(1)}, bf16[2,128,1536]{2,1,0:T(8,128)(2,1)S(1)}, u32[]{:S(2)}, u32[]{:S(2)}) collective-permute-start(bf16[2,128,1536]{2,1,0:T(8,128)(2,1)S(1)} %get-tuple-element.90), channel_id=1, source_target_pairs={{0,12},{1,13},{2,14},{3,15},{4,0},{5,1},{6,2},{7,3},{8,4},{9,5},{1... | collective-permute-start | bytes 2359304 | tf_op jit(solution)/shard_map/ppermute | solution.py:35
  131.1 12.3 %collective-permute-start.21 = (bf16[2,128,1536]{2,1,0:T(8,128)(2,1)S(1)}, bf16[2,128,1536]{2,1,0:T(8,128)(2,1)S(1)}, u32[]{:S(2)}, u32[]{:S(2)}) collective-permute-start(bf16[2,128,1536]{2,1,0:T(8,128)(2,1)S(1)} %get-tuple-element.91), channel_id=1, source_target_pairs={{0,4},{1,5},{2,6},{3,7},{4,8},{5,9},{6,10},{7,11},{8,12},{9,13},{1... | collective-permute-start | bytes 2359304 | tf_op jit(solution)/shard_map/ppermute | solution.py:35
  143.4 12.3 %collective-permute-start.22 = (bf16[2,128,1536]{2,1,0:T(8,128)(2,1)S(1)}, bf16[2,128,1536]{2,1,0:T(8,128)(2,1)S(1)}, u32[]{:S(2)}, u32[]{:S(2)}) collective-permute-start(bf16[2,128,1536]{2,1,0:T(8,128)(2,1)S(1)} %get-tuple-element.99), channel_id=1, source_target_pairs={{0,4},{1,5},{2,6},{3,7},{4,8},{5,9},{6,10},{7,11},{8,12},{9,13},{1... | collective-permute-start | bytes 2359304 | tf_op jit(solution)/shard_map/ppermute | solution.py:35
  143.4 12.3 %collective-permute-start.23 = (bf16[2,128,1536]{2,1,0:T(8,128)(2,1)S(1)}, bf16[2,128,1536]{2,1,0:T(8,128)(2,1)S(1)}, u32[]{:S(2)}, u32[]{:S(2)}) collective-permute-start(bf16[2,128,1536]{2,1,0:T(8,128)(2,1)S(1)} %get-tuple-element.100), channel_id=1, source_target_pairs={{0,12},{1,13},{2,14},{3,15},{4,0},{5,1},{6,2},{7,3},{8,4},{9,5},{1... | collective-permute-start | bytes 2359304 | tf_op jit(solution)/shard_map/ppermute | solution.py:35
  155.9 12.4 %collective-permute-start.25 = (bf16[2,128,1536]{2,1,0:T(8,128)(2,1)S(1)}, bf16[2,128,1536]{2,1,0:T(8,128)(2,1)S(1)}, u32[]{:S(2)}, u32[]{:S(2)}) collective-permute-start(bf16[2,128,1536]{2,1,0:T(8,128)(2,1)S(1)} %add_convert_fusion.1), channel_id=1, source_target_pairs={{0,4},{1,5},{2,6},{3,7},{4,8},{5,9},{6,10},{7,11},{8,12},{9,13},{1... | collective-permute-start | bytes 2359304 | tf_op jit(solution)/shard_map/ppermute | solution.py:35
  156.2 12.1 %collective-permute-start.24 = (bf16[2,128,1536]{2,1,0:T(8,128)(2,1)S(1)}, bf16[2,128,1536]{2,1,0:T(8,128)(2,1)S(1)}, u32[]{:S(2)}, u32[]{:S(2)}) collective-permute-start(bf16[2,128,1536]{2,1,0:T(8,128)(2,1)S(1)} %add_convert_fusion.2), channel_id=1, source_target_pairs={{0,12},{1,13},{2,14},{3,15},{4,0},{5,1},{6,2},{7,3},{8,4},{9,5},{1... | collective-permute-start | bytes 2359304 | tf_op jit(solution)/shard_map/ppermute | solution.py:35
  168.7 9.1 %collective-permute-start.26 = (bf16[128,1536]{1,0:T(8,128)(2,1)S(1)}, bf16[128,1536]{1,0:T(8,128)(2,1)S(1)}, u32[]{:S(2)}, u32[]{:S(2)}) collective-permute-start(bf16[128,1536]{1,0:T(8,128)(2,1)S(1)} %get-tuple-element.117), channel_id=1, source_target_pairs={{0,1},{1,2},{2,3},{3,0},{4,5},{5,6},{6,7},{7,4},{8,9},{9,10},{10,1... | collective-permute-start | bytes 1179656 | tf_op jit(solution)/shard_map/ppermute | solution.py:35
  168.8 14.7 %collective-permute-start.28 = (bf16[128,1536]{1,0:T(8,128)(2,1)S(1)}, bf16[128,1536]{1,0:T(8,128)(2,1)S(1)}, u32[]{:S(2)}, u32[]{:S(2)}) collective-permute-start(bf16[128,1536]{1,0:T(8,128)(2,1)S(1)} %get-tuple-element.116), channel_id=1, source_target_pairs={{0,2},{1,3},{2,0},{3,1},{4,6},{5,7},{6,4},{7,5},{8,10},{9,11},{10,... | collective-permute-start | bytes 1179656 | tf_op jit(solution)/shard_map/ppermute | solution.py:35
  172.0 11.6 %collective-permute-start.27 = (bf16[128,1536]{1,0:T(8,128)(2,1)S(1)}, bf16[128,1536]{1,0:T(8,128)(2,1)S(1)}, u32[]{:S(2)}, u32[]{:S(2)}) collective-permute-start(bf16[128,1536]{1,0:T(8,128)(2,1)S(1)} %fusion.6), channel_id=1, source_target_pairs={{0,3},{1,0},{2,1},{3,2},{4,7},{5,4},{6,5},{7,6},{8,11},{9,8},{10,9... | collective-permute-start | bytes 1179656 | tf_op jit(solution)/shard_map/ppermute | solution.py:35
  183.8 40.3 %copy-start.17 = (bf16[128,1536]{1,0:T(8,128)(2,1)}, bf16[128,1536]{1,0:T(8,128)(2,1)S(1)}, u32[]{:S(2)}) copy-start(bf16[128,1536]{1,0:T(8,128)(2,1)S(1)} %fusion.5) | copy-start | bytes 1179652
  (31 other events, 291.1 us)

commit v4 on v3

--- a/solution.py
+++ b/solution.py
@@ -14,6 +14,7 @@
 EXPERTS = 40
 TOP = 8
 CAP = 40
+KERNEL_VMEM = 63 << 20
 EPSILON = 1e-05
 ROPE_BASE = 10000.0
 MASKED = -1e30
@@ -99,7 +100,7 @@
             pltpu.VMEM(wq.shape, BF), pltpu.VMEM(wk.shape, BF), pltpu.VMEM(wv.shape, BF),
             pltpu.SemaphoreType.DMA((3,)),
         ],
-        compiler_params=pltpu.CompilerParams(vmem_limit_bytes=32 << 20),
+        compiler_params=pltpu.CompilerParams(vmem_limit_bytes=KERNEL_VMEM),
         cost_estimate=pl.CostEstimate(flops=5 << 30, transcendentals=0,
                                       bytes_accessed=14 << 20),
         name="base_block",
@@ -108,11 +109,13 @@
 
 def attention_kernel(*refs):
     adapt = refs[0:8]
-    (tok, xn, base_q, base_k, base_v, gain_moe, cosine, sine, key_doc, key_index, doc, index,
-     colp, colr, wo_hbm, mixed_out, moe_out, wo, ad, qbuf, kbuf, vbuf, att, score, prob,
-     sem) = refs[8:]
-    load = pltpu.make_async_copy(wo_hbm, wo, sem)
-    load.start()
+    (tok, gain_moe, cosine, sine, key_doc, key_index, doc, index, colp, colr, xn_hbm, q_hbm,
+     k_hbm, v_hbm, wo_hbm, mixed_out, moe_out, wo, xn, base_q, base_k, base_v, ad, qbuf, kbuf,
+     vbuf, att, score, prob, sems) = refs[8:]
+    loads = [pltpu.make_async_copy(src, dst, sems.at[i]) for i, (src, dst) in enumerate(
+        [(xn_hbm, xn), (k_hbm, base_k), (v_hbm, base_v), (q_hbm, base_q), (wo_hbm, wo)])]
+    for load in loads:
+        load.start()
     count = tok.shape[0]
     for j in range(8):
         ad[48 * j:48 * j + 48, :] = adapt[j][...]
@@ -147,6 +150,8 @@
                 keys[:, 128 * c:128 * c + 128], cos_t, sin_t).astype(BF)
         return carry
 
+    for load in loads[:3]:
+        load.wait()
     lax.fori_loop(0, 5, key_block, 0)
     docs = doc[0:count, :]
     zq = low(dot_t(xn[0:count, :], ad[...]), 8, 8, docs)
@@ -172,6 +177,7 @@
                 qbuf[c, count * h:count * h + count, :] = jnp.where(keep, rows, 0.0).astype(BF)
         return carry
 
+    loads[3].wait()
     lax.fori_loop(0, 4, query_block, 0)
 
     def pair(j, carry):
@@ -196,7 +202,7 @@
         return carry
 
     lax.fori_loop(0, 4, pair, 0)
-    load.wait()
+    loads[4].wait()
     attended = att[...]
     zo = low(dot_t(attended, ad[...]), 4, 10, docs)
     mixed = (tok[...].astype(F32) + jnp.dot(attended, wo[...], preferred_element_type=F32)
@@ -205,29 +211,30 @@
     moe_out[...] = norm(mixed.astype(F32), gain_moe[...])
 
 
-def attention(adapt, own, *others):
+def attention(adapt, own, tables, base, wo):
     count, width = own.shape
-    wo = others[-1]
     vm = pl.BlockSpec(memory_space=pltpu.VMEM)
     anywhere = pl.BlockSpec(memory_space=pl.ANY)
     rows = jax.ShapeDtypeStruct((count, width), BF)
     return pl.pallas_call(
         attention_kernel,
         out_shape=(rows, rows),
-        in_specs=[vm] * (8 + len(others)) + [anywhere],
+        in_specs=[vm] * (9 + len(tables)) + [anywhere] * 5,
         out_specs=(vm, vm),
         scratch_shapes=[
-            pltpu.VMEM(wo.shape, BF), pltpu.VMEM((384, width), BF),
+            pltpu.VMEM(wo.shape, BF), pltpu.VMEM(base[0].shape, BF),
+            pltpu.VMEM(base[1].shape, F32), pltpu.VMEM(base[2].shape, F32),
+            pltpu.VMEM(base[3].shape, F32), pltpu.VMEM((384, width), BF),
             pltpu.VMEM((4, 6 * count, 128), BF), pltpu.VMEM((5 * count, 512), BF),
             pltpu.VMEM((5 * count, 512), BF), pltpu.VMEM((count, width), BF),
             pltpu.VMEM((6 * count, 5 * count), F32), pltpu.VMEM((6 * count, 5 * count), BF),
-            pltpu.SemaphoreType.DMA,
+            pltpu.SemaphoreType.DMA((5,)),
         ],
-        compiler_params=pltpu.CompilerParams(vmem_limit_bytes=40 << 20),
+        compiler_params=pltpu.CompilerParams(vmem_limit_bytes=KERNEL_VMEM),
         cost_estimate=pl.CostEstimate(flops=6 << 30, transcendentals=0,
                                       bytes_accessed=16 << 20),
         name="attention_block",
-    )(*adapt, own, *others)
+    )(*adapt, own, *tables, *base, wo)
 
 
 def expert_kernel(sizes, *refs):
@@ -351,7 +358,7 @@
             pltpu.SemaphoreType.DMA((len(sizes),)), pltpu.SemaphoreType.DMA((15,)),
             pltpu.SemaphoreType.DMA((len(sizes),)),
         ],
-        compiler_params=pltpu.CompilerParams(vmem_limit_bytes=44 << 20),
+        compiler_params=pltpu.CompilerParams(vmem_limit_bytes=KERNEL_VMEM),
         cost_estimate=pl.CostEstimate(flops=rows * 6 * 1536 * 256 * 5, transcendentals=0,
                                       bytes_accessed=12 << 20),
         name="expert_block",
@@ -397,6 +404,10 @@
     held = lax.all_to_all(payload, "grp", 0, 0, tiled=True)
     back1 = lax.ppermute(own, "seq", [(s, s + 2) for s in range(6)])
     back2 = lax.ppermute(own, "seq", [(s, s + 4) for s in range(4)])
+    odd_core = me % 2 == 1
+    tok = [own, back1, back2, partner(jnp.where(odd_core, back1, own)),
+           partner(jnp.where(odd_core, back2, back1))]
+
     lens = lengths[0]
     ends = jnp.cumsum(lens)
     starts = ends - lens
@@ -430,16 +441,7 @@
                         for p in range(3)]).reshape(48, width)
     turn = [picked] + [lax.ppermute(picked, "seq", [(s, (s + d) % 8) for s in range(8)])
                        for d in (2, 6, 4)]
-    adapt = turn + [partner(piece) for piece in turn]
-    odd_core = me % 2 == 1
-    tok = [own, back1, back2, partner(jnp.where(odd_core, back1, own)),
-           partner(jnp.where(odd_core, back2, back1))]
     base = base_projections(tok, attention_gain[None], query_weight, key_weight, value_weight)
-
-    mixed, moe_in = attention(
-        adapt, own, *base, expert_gain[None], cosine, sine, key_document[None], index[None],
-        document[:, None], row_index[:, None], columns // 16 % 3, columns % 16, output_weight)
-
     rel = jnp.array([0, 3, 1, 2], jnp.int32)
     first, second = jnp.where(me % 2 == 0, grp % 4, grp // 4), jnp.where(
         me % 2 == 0, grp // 4, grp % 4)
@@ -453,8 +455,17 @@
     odd = (grp % 2).astype(jnp.int32)[None]
     weights = (gate_weight, up_weight, down_weight)
 
+    shares = {pair: jnp.stack([route_in[k] for k in pair])
+              for pair in ((0, 1), (2, 5), (3, 4), (6, 7))}
+    turn, base, shares = lax.optimization_barrier((turn, base, shares))
+    adapt = turn + [partner(piece) for piece in turn]
+
+    tables = [expert_gain[None], cosine, sine, key_document[None], index[None],
+              document[:, None], row_index[:, None], columns // 16 % 3, columns % 16]
+    mixed, moe_in = attention(adapt, own, tables, base, output_weight)
+
     def share(pieces, which):
-        return experts(pieces, odd, jnp.stack([route_in[k] for k in which]), *weights)
+        return experts(pieces, odd, shares[which], *weights)
 
     line = lax.optimization_barrier(
         [shift(moe_in, 0, 1), shift(moe_in, 0, -1), shift(moe_in, 0, 2)])
@@ -474,8 +485,6 @@
 
     minus_lo, plus_hi = shift(minus_lo, 1, -1), shift(plus_hi, 1, 1)
     far_lo, far_hi = share([far_lo, far_hi], (6, 7))
-    minus_lo, plus_hi, far_lo, far_hi = lax.optimization_barrier(
-        (minus_lo, plus_hi, far_lo, far_hi))
     far_lo, far_hi = lax.optimization_barrier((shift(far_lo, 1, 1), shift(far_hi, 1, -1)))
     plus_lo = shift((wide(plus_lo) + wide(far_lo)).astype(BF), 1, 1)
     minus_hi = shift((wide(minus_hi) + wide(far_hi)).astype(BF), 1, -1)

time: 240 us -> 242 us (level)
  Pallas kernels: 46.5 us -> 74.1 us
  local copies, waits for them, and re-layouts: 22 us -> 10.7 us
  waiting for transfers between devices: 49.2 us -> 42.2 us
  starting transfers between devices: 48.6 us -> 44.7 us
    pallas_call x4, Pallas kernels: 24.8 us -> 46 us  [experts(): pl.pallas_call(functools.partial(expert_kernel, sizes), out_shape=tuple((...]
    unnamed x66 -> x64, local copies, waits for them, and re-layouts: 11.9 us -> 2.89 us
    ppermute x18, waiting for transfers between devices: 48.2 us -> 40.8 us  [shift(): return lax.ppermute(rows, WHOLE, pairs)]
    all_to_all x1, blocking collectives: 19.5 us -> 15.5 us  [body(): mine = lax.all_to_all(split, 'seq', 0, 0, tiled=True)]
    ppermute x6, starting transfers between devices: 9.13 us -> 5.48 us  [partner(): return lax.ppermute(rows, 'seq', [(s, s ^ 1) for s in range(8)])]
    pallas_call x1, Pallas kernels: 15.6 us -> 19.1 us  [attention(): pl.pallas_call(attention_kernel, out_shape=(rows, rows), in_specs=[vm] *...]
    pallas_call x1, Pallas kernels: 6.09 us -> 8.91 us  [base_projections(): pl.pallas_call(base_kernel, out_shape=(jax.ShapeDtypeStruct((5 * count, w...]
  transfers between devices with their start and end apart: 30 -> 30, of which waited for: 9 -> 8; matrix products, arithmetic and copies ran while one was open for 6% -> 5% of each run, Pallas kernels for 13% -> 18%
where the time goes in v4:
time: 242 us; the launch traced here: 241 us
  Pallas kernels  74.1 us (31%)
  blocking collectives  49.9 us (21%)
  starting transfers between devices  44.7 us (18%)
  waiting for transfers between devices  42.2 us (17%)
  other arithmetic  10.9 us (5%)
  local copies, waits for them, and re-layouts  10.7 us (4%)
  between operations  7.29 us (3%)
    pallas_call x4, Pallas kernels, experts(): pl.pallas_call(functools.partial(expert_kernel, sizes), out_shape=tuple((...  46 us
    ppermute x18, waiting for transfers between devices, shift(): return lax.ppermute(rows, WHOLE, pairs)  40.8 us
    all_to_all x1, blocking collectives, body(): lax.all_to_all(jnp.broadcast_to(mine[None], (128, 3, part)), WHOLE, 0, 0,...  20.7 us
    ppermute x18, starting transfers between devices, shift(): return lax.ppermute(rows, WHOLE, pairs)  20.4 us
    pallas_call x1, Pallas kernels, attention(): pl.pallas_call(attention_kernel, out_shape=(rows, rows), in_specs=[vm] *...  19.1 us
    all_to_all x1, blocking collectives, body(): mine = lax.all_to_all(split, 'seq', 0, 0, tiled=True)  15.5 us
    all_to_all x1, blocking collectives, body(): lax.all_to_all(jnp.broadcast_to(stats[None], (128, 128)), WHOLE, 0, 0, ti...  13.6 us
    pallas_call x1, Pallas kernels, base_projections(): pl.pallas_call(base_kernel, out_shape=(jax.ShapeDtypeStruct((5 * count, w...  8.91 us
  transfers between devices with their start and end apart: 30, of which 8 were waited for; matrix products, arithmetic and copies ran while one was open for 5% of the time, Pallas kernels for 18%

profile of v4, /device:TPU:1, one launch (start us, length us, event | category | flops | bytes accessed | tf_op | source)
XLA Modules:
  0.0 240.9 jit_solution(10891800322182655603)
XLA Ops:
  3.8 1.2 maximum_maximum_fusion
  5.0 4.0 %collective-permute-start.3 = (bf16[128,1536]{1,0:T(8,128)(2,1)S(1)}, bf16[128,1536]{1,0:T(8,128)(2,1)S(1)}, u32[]{:S(2)}, u32[]{:S(2)}) collective-permute-start(bf16[128,1536]{1,0:T(8,128)(2,1)S(1)} %bitcast.169), channel_id=1, source_target_pairs={{0,32},{16,48},{32,64},{48,80},{64,96},{80,112},{1,33},{17,49},{33... | collective-permute-start | bytes 1179656 | tf_op jit(solution)/shard_map/ppermute | solution.py:405
  9.0 4.4 %collective-permute-start.4 = (bf16[128,1536]{1,0:T(8,128)(2,1)S(1)}, bf16[128,1536]{1,0:T(8,128)(2,1)S(1)}, u32[]{:S(2)}, u32[]{:S(2)}) collective-permute-start(bf16[128,1536]{1,0:T(8,128)(2,1)S(1)} %bitcast.170), channel_id=1, source_target_pairs={{0,64},{16,80},{32,96},{48,112},{1,65},{17,81},{33,97},{49,113},{2... | collective-permute-start | bytes 1179656 | tf_op jit(solution)/shard_map/ppermute | solution.py:406
  13.3 7.8 %all-to-all-start = ((bf16[16,16,1536]{2,1,0:T(8,128)(2,1)}), bf16[16,16,1536]{2,1,0:T(8,128)(2,1)S(1)}, u32[]{:S(2)}, u32[]{:S(2)}) async-start(bf16[16,16,1536]{2,1,0:T(8,128)(2,1)} %maximum_maximum_fusion), calls=%async_computation | async-start | bytes 1572864 | tf_op jit(solution)/shard_map/all_to_all | solution.py:404
  29.6 1.1 fusion.9
  30.9 1.6 collective-permute-start.5
  32.6 1.3 all-to-all-done
  34.5 2.7 %collective-permute-start.1 = (bf16[48,1536]{1,0:T(8,128)(2,1)S(1)}, bf16[48,1536]{1,0:T(8,128)(2,1)}, u32[]{:S(2)}, u32[]{:S(2)}) collective-permute-start(bf16[48,1536]{1,0:T(8,128)(2,1)S(1)} %bitcast.179), channel_id=1, source_target_pairs={{0,96},{16,112},{32,0},{48,16},{64,32},{80,48},{96,64},{112,80},{1... | collective-permute-start | bytes 442376 | tf_op jit(solution)/shard_map/ppermute | solution.py:442
  40.6 8.9 %base_block.1 = (bf16[640,1536]{1,0:T(8,128)(2,1)}, f32[128,1536]{1,0:T(8,128)}, f32[640,512]{1,0:T(8,128)}, f32[640,512]{1,0:T(8,128)}) custom-call(bf16[128,1536]{1,0:T(8,128)(2,1)} %bitcast.167, bf16[128,1536]{1,0:T(8,128)(2,1)} %copy-done.11, bf16[128,1536]{1,0:T(8,128)(2,1)} %copy-done.12, bf16[128,1536]{1,0:T(8,128)(2,1)} %copy-done.25, ...), custom_call_target="tpu_custom_call" | custom-call | flops 5368709120 | bytes 14680064 | tf_op jit(solution)/shard_map/base_block/pallas_call | solution.py:91
  49.5 3.2 %collective-permute-start.10 = (bf16[48,1536]{1,0:T(8,128)(2,1)}, bf16[48,1536]{1,0:T(8,128)(2,1)S(1)}, u32[]{:S(2)}, u32[]{:S(2)}) collective-permute-start(bf16[48,1536]{1,0:T(8,128)(2,1)} %collective-permute-done.2.refs_3_), channel_id=1, source_target_pairs={{0,16},{16,0},{32,48},{48,32},{64,80},{80,64},{96,112},{112,96},{1... | collective-permute-start | bytes 442376 | tf_op jit(solution)/shard_map/ppermute | solution.py:40
  58.1 19.1 %attention_block.1 = (bf16[128,1536]{1,0:T(8,128)(2,1)}, bf16[128,1536]{1,0:T(8,128)(2,1)}) custom-call(bf16[48,1536]{1,0:T(8,128)(2,1)} %bitcast.182, bf16[48,1536]{1,0:T(8,128)(2,1)} %copy-done.26, bf16[48,1536]{1,0:T(8,128)(2,1)} %collective-permute-done.1.refs_2_, bf16[48,1536]{1,0:T(8,128)(2,1)} %collective-permute-done.2.refs_3_, ...), custom_call_target="tpu_custom_call" | custom-call | flops 6442450944 | bytes 16777216 | tf_op jit(solution)/shard_map/attention_block/pallas_call | solution.py:219
  77.3 2.7 %collective-permute-start.12 = (bf16[128,1536]{1,0:T(8,128)(2,1)}, bf16[128,1536]{1,0:T(8,128)(2,1)S(1)}, u32[]{:S(2)}, u32[]{:S(2)}) collective-permute-start(bf16[128,1536]{1,0:T(8,128)(2,1)} %get-tuple-element.87), channel_id=1, source_target_pairs={{0,3},{1,0},{2,1},{3,2},{4,7},{5,4},{6,5},{7,6},{8,11},{9,8},{10,9... | collective-permute-start | bytes 1179656 | tf_op jit(solution)/shard_map/ppermute | solution.py:36
  80.0 9.9 %collective-permute-done.11 = bf16[128,1536]{1,0:T(8,128)(2,1)S(1)} collective-permute-done((bf16[128,1536]{1,0:T(8,128)(2,1)}, bf16[128,1536]{1,0:T(8,128)(2,1)S(1)}, u32[]{:S(2)}, u32[]{:S(2)}) %collective-permute-start.11) | collective-permute-done | bytes 393248 | tf_op jit(solution)/shard_map/ppermute | solution.py:36
  91.2 1.2 collective-permute-start.14
  92.6 2.5 %collective-permute-start.17 = (bf16[2,128,1536]{2,1,0:T(8,128)(2,1)}, bf16[2,128,1536]{2,1,0:T(8,128)(2,1)}, u32[]{:S(2)}, u32[]{:S(2)}) collective-permute-start(bf16[2,128,1536]{2,1,0:T(8,128)(2,1)} %pad_maximum_fusion.refs_0_), channel_id=1, source_target_pairs={{0,12},{1,13},{2,14},{3,15},{4,0},{5,1},{6,2},{7,3},{8,4},{9,5},{1... | collective-permute-start | bytes 2359304 | tf_op jit(solution)/shard_map/ppermute | solution.py:36
  95.1 11.5 %expert_block.4 = (bf16[2,128,1536]{2,1,0:T(8,128)(2,1)}, bf16[2,128,1536]{2,1,0:T(8,128)(2,1)}) custom-call(bf16[2,128,1536]{2,1,0:T(8,128)(2,1)} %pad_maximum_fusion.refs_0_, bf16[2,128,1536]{2,1,0:T(8,128)(2,1)} %copy-done.2, s32[1]{0:T(128)} %bitcast.51.refs_2_, f32[2,8,256]{2,1,0:T(8,128)} %pad_maximum_fusion.3.refs_3_, bf16[5,1536,256]{2,1,0:T(8,128)(2,1)} %refs_4_.7, ...), custom_call_target="tpu_custom_call" | custom-call | flops 1887436800 | bytes 12582912 | tf_op jit(solution)/shard_map/expert_block/pallas_call | solution.py:347
  106.6 11.5 %expert_block.5 = (bf16[2,128,1536]{2,1,0:T(8,128)(2,1)}, bf16[2,128,1536]{2,1,0:T(8,128)(2,1)}) custom-call(bf16[2,128,1536]{2,1,0:T(8,128)(2,1)} %collective-permute-done.14.refs_0_, bf16[2,128,1536]{2,1,0:T(8,128)(2,1)} %collective-permute-done.15.refs_1_, s32[1]{0:T(128)} %bitcast.51.refs_2_, f32[2,8,256]{2,1,0:T(8,128)} %pad_maximum_fusion.4.refs_3_, ...), custom_call_target="tpu_custom_call" | custom-call | flops 1887436800 | bytes 12582912 | tf_op jit(solution)/shard_map/expert_block/pallas_call | solution.py:347
  118.2 2.7 %collective-permute-start.19 = (bf16[2,128,1536]{2,1,0:T(8,128)(2,1)}, bf16[2,128,1536]{2,1,0:T(8,128)(2,1)}, u32[]{:S(2)}, u32[]{:S(2)}) collective-permute-start(bf16[2,128,1536]{2,1,0:T(8,128)(2,1)} %collective-permute-done.15.refs_1_), channel_id=1, source_target_pairs={{0,12},{1,13},{2,14},{3,15},{4,0},{5,1},{6,2},{7,3},{8,4},{9,5},{1... | collective-permute-start | bytes 2359304 | tf_op jit(solution)/shard_map/ppermute | solution.py:36
  120.9 11.5 %expert_block.6 = (bf16[2,128,1536]{2,1,0:T(8,128)(2,1)}, bf16[2,128,1536]{2,1,0:T(8,128)(2,1)}) custom-call(bf16[2,128,1536]{2,1,0:T(8,128)(2,1)} %collective-permute-done.16.refs_0_, bf16[2,128,1536]{2,1,0:T(8,128)(2,1)} %collective-permute-done.17.refs_1_, s32[1]{0:T(128)} %bitcast.51.refs_2_, f32[2,8,256]{2,1,0:T(8,128)} %pad_maximum_fusion.5.refs_3_, ...), custom_call_target="tpu_custom_call" | custom-call | flops 1887436800 | bytes 12582912 | tf_op jit(solution)/shard_map/expert_block/pallas_call | solution.py:347
  133.4 11.5 %expert_block.7 = (bf16[2,128,1536]{2,1,0:T(8,128)(2,1)}, bf16[2,128,1536]{2,1,0:T(8,128)(2,1)}) custom-call(bf16[2,128,1536]{2,1,0:T(8,128)(2,1)} %copy-done.9, bf16[2,128,1536]{2,1,0:T(8,128)(2,1)} %collective-permute-done.19.refs_1_, s32[1]{0:T(128)} %bitcast.51.refs_2_, f32[2,8,256]{2,1,0:T(8,128)} %pad_maximum_fusion.6.refs_3_, ...), custom_call_target="tpu_custom_call" | custom-call | flops 1887436800 | bytes 12582912 | tf_op jit(solution)/shard_map/expert_block/pallas_call | solution.py:347
  145.0 2.7 %collective-permute-start.23 = (bf16[2,128,1536]{2,1,0:T(8,128)(2,1)}, bf16[2,128,1536]{2,1,0:T(8,128)(2,1)S(1)}, u32[]{:S(2)}, u32[]{:S(2)}) collective-permute-start(bf16[2,128,1536]{2,1,0:T(8,128)(2,1)} %get-tuple-element.116), channel_id=1, source_target_pairs={{0,12},{1,13},{2,14},{3,15},{4,0},{5,1},{6,2},{7,3},{8,4},{9,5},{1... | collective-permute-start | bytes 2359304 | tf_op jit(solution)/shard_map/ppermute | solution.py:36
  147.7 1.4 collective-permute-start.21
  149.1 8.4 %collective-permute-done.22 = bf16[2,128,1536]{2,1,0:T(8,128)(2,1)S(1)} collective-permute-done((bf16[2,128,1536]{2,1,0:T(8,128)(2,1)}, bf16[2,128,1536]{2,1,0:T(8,128)(2,1)S(1)}, u32[]{:S(2)}, u32[]{:S(2)}) %collective-permute-start.22) | collective-permute-done | bytes 786464 | tf_op jit(solution)/shard_map/ppermute | solution.py:36
  158.0 2.7 %collective-permute-start.24 = (bf16[2,128,1536]{2,1,0:T(8,128)(2,1)S(1)}, bf16[2,128,1536]{2,1,0:T(8,128)(2,1)S(1)}, u32[]{:S(2)}, u32[]{:S(2)}) collective-permute-start(bf16[2,128,1536]{2,1,0:T(8,128)(2,1)S(1)} %add_convert_fusion.2), channel_id=1, source_target_pairs={{0,12},{1,13},{2,14},{3,15},{4,0},{5,1},{6,2},{7,3},{8,4},{9,5},{1... | collective-permute-start | bytes 2359304 | tf_op jit(solution)/shard_map/ppermute | solution.py:36
  160.8 4.6 %collective-permute-done.20 = bf16[2,128,1536]{2,1,0:T(8,128)(2,1)S(1)} collective-permute-done((bf16[2,128,1536]{2,1,0:T(8,128)(2,1)}, bf16[2,128,1536]{2,1,0:T(8,128)(2,1)S(1)}, u32[]{:S(2)}, u32[]{:S(2)}) %collective-permute-start.20) | collective-permute-done | bytes 786464 | tf_op jit(solution)/shard_map/ppermute | solution.py:36
  165.9 8.4 %collective-permute-done.25 = bf16[2,128,1536]{2,1,0:T(8,128)(2,1)S(1)} collective-permute-done((bf16[2,128,1536]{2,1,0:T(8,128)(2,1)S(1)}, bf16[2,128,1536]{2,1,0:T(8,128)(2,1)S(1)}, u32[]{:S(2)}, u32[]{:S(2)}) %collective-permute-start.25) | collective-permute-done | bytes 786464 | tf_op jit(solution)/shard_map/ppermute | solution.py:36
  174.8 3.5 %collective-permute-start.28 = (bf16[128,1536]{1,0:T(8,128)(2,1)S(1)}, bf16[128,1536]{1,0:T(8,128)(2,1)S(1)}, u32[]{:S(2)}, u32[]{:S(2)}) collective-permute-start(bf16[128,1536]{1,0:T(8,128)(2,1)S(1)} %get-tuple-element.132), channel_id=1, source_target_pairs={{0,2},{1,3},{2,0},{3,1},{4,6},{5,7},{6,4},{7,5},{8,10},{9,11},{10,... | collective-permute-start | bytes 1179656 | tf_op jit(solution)/shard_map/ppermute | solution.py:36
  178.8 3.8 %collective-permute-done.26 = bf16[128,1536]{1,0:T(8,128)(2,1)S(1)} collective-permute-done((bf16[128,1536]{1,0:T(8,128)(2,1)S(1)}, bf16[128,1536]{1,0:T(8,128)(2,1)S(1)}, u32[]{:S(2)}, u32[]{:S(2)}) %collective-permute-start.26) | collective-permute-done | bytes 393248 | tf_op jit(solution)/shard_map/ppermute | solution.py:36
  182.7 5.1 %collective-permute-done.28 = bf16[128,1536]{1,0:T(8,128)(2,1)S(1)} collective-permute-done((bf16[128,1536]{1,0:T(8,128)(2,1)S(1)}, bf16[128,1536]{1,0:T(8,128)(2,1)S(1)}, u32[]{:S(2)}, u32[]{:S(2)}) %collective-permute-start.28) | collective-permute-done | bytes 393248 | tf_op jit(solution)/shard_map/ppermute | solution.py:36
  188.6 15.5 %all_to_all.24 = bf16[8,3,192]{2,1,0:T(4,128)(2,1)S(1)} all-to-all(bf16[8,3,192]{2,1,0:T(4,128)(2,1)S(1)} %bitcast.183), channel_id=1, replica_groups=mesh['seq'=8,'grp'=16] {'seq'}, dimensions={0} | all-to-all | bytes 18432 | tf_op jit(solution)/shard_map/all_to_all | solution.py:506
  204.3 20.7 %all_to_all.25 = bf16[128,3,192]{2,1,0:T(4,128)(2,1)S(1)} all-to-all(bf16[128,3,192]{2,1,0:T(4,128)(2,1)S(1)} %broadcast_in_dim.230), channel_id=1, replica_groups=mesh['seq'=8,'grp'=16] {'seq','grp'}, dimensions={0} | all-to-all | bytes 294912 | tf_op jit(solution)/shard_map/all_to_all | solution.py:508
  226.2 13.6 %all_to_all.26 = f32[128,1,128]{2,1,0:T(1,128)S(1)} all-to-all(f32[128,1,128]{2,1,0:T(1,128)S(1)} %broadcast_in_dim.232), channel_id=1, replica_groups=mesh['seq'=8,'grp'=16] {'seq','grp'}, dimensions={0} | all-to-all | bytes 131072 | tf_op jit(solution)/shard_map/all_to_all | solution.py:515
  (189 shorter events, 22.9 us)
Async XLA Ops:
  5.0 25.8 %collective-permute-start.3 = (bf16[128,1536]{1,0:T(8,128)(2,1)S(1)}, bf16[128,1536]{1,0:T(8,128)(2,1)S(1)}, u32[]{:S(2)}, u32[]{:S(2)}) collective-permute-start(bf16[128,1536]{1,0:T(8,128)(2,1)S(1)} %bitcast.169), channel_id=1, source_target_pairs={{0,32},{16,48},{32,64},{48,80},{64,96},{80,112},{1,33},{17,49},{33... | collective-permute-start | bytes 1179656 | tf_op jit(solution)/shard_map/ppermute | solution.py:405
  9.0 21.8 %collective-permute-start.4 = (bf16[128,1536]{1,0:T(8,128)(2,1)S(1)}, bf16[128,1536]{1,0:T(8,128)(2,1)S(1)}, u32[]{:S(2)}, u32[]{:S(2)}) collective-permute-start(bf16[128,1536]{1,0:T(8,128)(2,1)S(1)} %bitcast.170), channel_id=1, source_target_pairs={{0,64},{16,80},{32,96},{48,112},{1,65},{17,81},{33,97},{49,113},{2... | collective-permute-start | bytes 1179656 | tf_op jit(solution)/shard_map/ppermute | solution.py:406
  13.3 20.5 %all-to-all-start = ((bf16[16,16,1536]{2,1,0:T(8,128)(2,1)}), bf16[16,16,1536]{2,1,0:T(8,128)(2,1)S(1)}, u32[]{:S(2)}, u32[]{:S(2)}) async-start(bf16[16,16,1536]{2,1,0:T(8,128)(2,1)} %maximum_maximum_fusion), calls=%async_computation | async-start | bytes 1572864 | tf_op jit(solution)/shard_map/all_to_all | solution.py:404
  30.9 8.9 %collective-permute-start.5 = (bf16[128,1536]{1,0:T(8,128)(2,1)S(1)}, bf16[128,1536]{1,0:T(8,128)(2,1)S(1)}, u32[]{:S(2)}, u32[]{:S(2)}) collective-permute-start(bf16[128,1536]{1,0:T(8,128)(2,1)S(1)} %get-tuple-element.138), channel_id=1, source_target_pairs={{0,16},{16,0},{32,48},{48,32},{64,80},{80,64},{96,112},{112,96},{1... | collective-permute-start | bytes 1179656 | tf_op jit(solution)/shard_map/ppermute | solution.py:40
  32.5 7.3 %collective-permute-start.6 = (bf16[128,1536]{1,0:T(8,128)(2,1)S(1)}, bf16[128,1536]{1,0:T(8,128)(2,1)}, u32[]{:S(2)}, u32[]{:S(2)}) collective-permute-start(bf16[128,1536]{1,0:T(8,128)(2,1)S(1)} %get-tuple-element.137), channel_id=1, source_target_pairs={{0,16},{16,0},{32,48},{48,32},{64,80},{80,64},{96,112},{112,96},{1... | collective-permute-start | bytes 1179656 | tf_op jit(solution)/shard_map/ppermute | solution.py:40
  34.4 15.1 %collective-permute-start = (bf16[48,1536]{1,0:T(8,128)(2,1)S(1)}, bf16[48,1536]{1,0:T(8,128)(2,1)S(1)}, u32[]{:S(2)}, u32[]{:S(2)}) collective-permute-start(bf16[48,1536]{1,0:T(8,128)(2,1)S(1)} %bitcast.178), channel_id=1, source_target_pairs={{0,32},{16,48},{32,64},{48,80},{64,96},{80,112},{96,0},{112,16},{1... | collective-permute-start | bytes 442376 | tf_op jit(solution)/shard_map/ppermute | solution.py:442
  34.5 15.0 %collective-permute-start.1 = (bf16[48,1536]{1,0:T(8,128)(2,1)S(1)}, bf16[48,1536]{1,0:T(8,128)(2,1)}, u32[]{:S(2)}, u32[]{:S(2)}) collective-permute-start(bf16[48,1536]{1,0:T(8,128)(2,1)S(1)} %bitcast.179), channel_id=1, source_target_pairs={{0,96},{16,112},{32,0},{48,16},{64,32},{80,48},{96,64},{112,80},{1... | collective-permute-start | bytes 442376 | tf_op jit(solution)/shard_map/ppermute | solution.py:442
  37.1 12.4 %collective-permute-start.2 = (bf16[48,1536]{1,0:T(8,128)(2,1)S(1)}, bf16[48,1536]{1,0:T(8,128)(2,1)}, u32[]{:S(2)}, u32[]{:S(2)}) collective-permute-start(bf16[48,1536]{1,0:T(8,128)(2,1)S(1)} %bitcast.180), channel_id=1, source_target_pairs={{0,64},{16,80},{32,96},{48,112},{64,0},{80,16},{96,32},{112,48},{1... | collective-permute-start | bytes 442376 | tf_op jit(solution)/shard_map/ppermute | solution.py:442
  49.5 7.8 %collective-permute-start.10 = (bf16[48,1536]{1,0:T(8,128)(2,1)}, bf16[48,1536]{1,0:T(8,128)(2,1)S(1)}, u32[]{:S(2)}, u32[]{:S(2)}) collective-permute-start(bf16[48,1536]{1,0:T(8,128)(2,1)} %collective-permute-done.2.refs_3_), channel_id=1, source_target_pairs={{0,16},{16,0},{32,48},{48,32},{64,80},{80,64},{96,112},{112,96},{1... | collective-permute-start | bytes 442376 | tf_op jit(solution)/shard_map/ppermute | solution.py:40
  52.7 4.6 %collective-permute-start.7 = (bf16[48,1536]{1,0:T(8,128)(2,1)S(1)}, bf16[48,1536]{1,0:T(8,128)(2,1)S(1)}, u32[]{:S(2)}, u32[]{:S(2)}) collective-permute-start(bf16[48,1536]{1,0:T(8,128)(2,1)S(1)} %bitcast.181), channel_id=1, source_target_pairs={{0,16},{16,0},{32,48},{48,32},{64,80},{80,64},{96,112},{112,96},{1... | collective-permute-start | bytes 442376 | tf_op jit(solution)/shard_map/ppermute | solution.py:40
  52.8 4.5 %collective-permute-start.8 = (bf16[48,1536]{1,0:T(8,128)(2,1)S(1)}, bf16[48,1536]{1,0:T(8,128)(2,1)S(1)}, u32[]{:S(2)}, u32[]{:S(2)}) collective-permute-start(bf16[48,1536]{1,0:T(8,128)(2,1)S(1)} %collective-permute-done.refs_1_), channel_id=1, source_target_pairs={{0,16},{16,0},{32,48},{48,32},{64,80},{80,64},{96,112},{112,96},{1... | collective-permute-start | bytes 442376 | tf_op jit(solution)/shard_map/ppermute | solution.py:40
  53.2 4.1 %collective-permute-start.9 = (bf16[48,1536]{1,0:T(8,128)(2,1)}, bf16[48,1536]{1,0:T(8,128)(2,1)}, u32[]{:S(2)}, u32[]{:S(2)}) collective-permute-start(bf16[48,1536]{1,0:T(8,128)(2,1)} %collective-permute-done.1.refs_2_), channel_id=1, source_target_pairs={{0,16},{16,0},{32,48},{48,32},{64,80},{80,64},{96,112},{112,96},{1... | collective-permute-start | bytes 442376 | tf_op jit(solution)/shard_map/ppermute | solution.py:40
  77.2 12.6 %collective-permute-start.11 = (bf16[128,1536]{1,0:T(8,128)(2,1)}, bf16[128,1536]{1,0:T(8,128)(2,1)S(1)}, u32[]{:S(2)}, u32[]{:S(2)}) collective-permute-start(bf16[128,1536]{1,0:T(8,128)(2,1)} %get-tuple-element.87), channel_id=1, source_target_pairs={{0,1},{1,2},{2,3},{3,0},{4,5},{5,6},{6,7},{7,4},{8,9},{9,10},{10,1... | collective-permute-start | bytes 1179656 | tf_op jit(solution)/shard_map/ppermute | solution.py:36
  77.3 12.5 %collective-permute-start.12 = (bf16[128,1536]{1,0:T(8,128)(2,1)}, bf16[128,1536]{1,0:T(8,128)(2,1)S(1)}, u32[]{:S(2)}, u32[]{:S(2)}) collective-permute-start(bf16[128,1536]{1,0:T(8,128)(2,1)} %get-tuple-element.87), channel_id=1, source_target_pairs={{0,3},{1,0},{2,1},{3,2},{4,7},{5,4},{6,5},{7,6},{8,11},{9,8},{10,9... | collective-permute-start | bytes 1179656 | tf_op jit(solution)/shard_map/ppermute | solution.py:36
  80.0 9.9 %collective-permute-start.13 = (bf16[128,1536]{1,0:T(8,128)(2,1)}, bf16[128,1536]{1,0:T(8,128)(2,1)S(1)}, u32[]{:S(2)}, u32[]{:S(2)}) collective-permute-start(bf16[128,1536]{1,0:T(8,128)(2,1)} %get-tuple-element.87), channel_id=1, source_target_pairs={{0,2},{1,3},{2,0},{3,1},{4,6},{5,7},{6,4},{7,5},{8,10},{9,11},{10,... | collective-permute-start | bytes 1179656 | tf_op jit(solution)/shard_map/ppermute | solution.py:36
  89.9 16.7 %collective-permute-start.15 = (bf16[2,128,1536]{2,1,0:T(8,128)(2,1)S(1)}, bf16[2,128,1536]{2,1,0:T(8,128)(2,1)}, u32[]{:S(2)}, u32[]{:S(2)}) collective-permute-start(bf16[2,128,1536]{2,1,0:T(8,128)(2,1)S(1)} %pad_maximum_fusion.1.refs_1_), channel_id=1, source_target_pairs={{0,12},{1,13},{2,14},{3,15},{4,0},{5,1},{6,2},{7,3},{8,4},{9,5},{1... | collective-permute-start | bytes 2359304 | tf_op jit(solution)/shard_map/ppermute | solution.py:36
  91.2 15.4 %collective-permute-start.14 = (bf16[2,128,1536]{2,1,0:T(8,128)(2,1)}, bf16[2,128,1536]{2,1,0:T(8,128)(2,1)}, u32[]{:S(2)}, u32[]{:S(2)}) collective-permute-start(bf16[2,128,1536]{2,1,0:T(8,128)(2,1)} %pad_maximum_fusion.refs_0_), channel_id=1, source_target_pairs={{0,4},{1,5},{2,6},{3,7},{4,8},{5,9},{6,10},{7,11},{8,12},{9,13},{1... | collective-permute-start | bytes 2359304 | tf_op jit(solution)/shard_map/ppermute | solution.py:36
  92.4 25.7 %collective-permute-start.16 = (bf16[2,128,1536]{2,1,0:T(8,128)(2,1)S(1)}, bf16[2,128,1536]{2,1,0:T(8,128)(2,1)}, u32[]{:S(2)}, u32[]{:S(2)}) collective-permute-start(bf16[2,128,1536]{2,1,0:T(8,128)(2,1)S(1)} %pad_maximum_fusion.1.refs_1_), channel_id=1, source_target_pairs={{0,4},{1,5},{2,6},{3,7},{4,8},{5,9},{6,10},{7,11},{8,12},{9,13},{1... | collective-permute-start | bytes 2359304 | tf_op jit(solution)/shard_map/ppermute | solution.py:36
  92.6 25.6 %collective-permute-start.17 = (bf16[2,128,1536]{2,1,0:T(8,128)(2,1)}, bf16[2,128,1536]{2,1,0:T(8,128)(2,1)}, u32[]{:S(2)}, u32[]{:S(2)}) collective-permute-start(bf16[2,128,1536]{2,1,0:T(8,128)(2,1)} %pad_maximum_fusion.refs_0_), channel_id=1, source_target_pairs={{0,12},{1,13},{2,14},{3,15},{4,0},{5,1},{6,2},{7,3},{8,4},{9,5},{1... | collective-permute-start | bytes 2359304 | tf_op jit(solution)/shard_map/ppermute | solution.py:36
  118.1 14.3 %collective-permute-start.18 = (bf16[2,128,1536]{2,1,0:T(8,128)(2,1)}, bf16[2,128,1536]{2,1,0:T(8,128)(2,1)S(1)}, u32[]{:S(2)}, u32[]{:S(2)}) collective-permute-start(bf16[2,128,1536]{2,1,0:T(8,128)(2,1)} %collective-permute-done.14.refs_0_), channel_id=1, source_target_pairs={{0,4},{1,5},{2,6},{3,7},{4,8},{5,9},{6,10},{7,11},{8,12},{9,13},{1... | collective-permute-start | bytes 2359304 | tf_op jit(solution)/shard_map/ppermute | solution.py:36
  118.2 14.2 %collective-permute-start.19 = (bf16[2,128,1536]{2,1,0:T(8,128)(2,1)}, bf16[2,128,1536]{2,1,0:T(8,128)(2,1)}, u32[]{:S(2)}, u32[]{:S(2)}) collective-permute-start(bf16[2,128,1536]{2,1,0:T(8,128)(2,1)} %collective-permute-done.15.refs_1_), channel_id=1, source_target_pairs={{0,12},{1,13},{2,14},{3,15},{4,0},{5,1},{6,2},{7,3},{8,4},{9,5},{1... | collective-permute-start | bytes 2359304 | tf_op jit(solution)/shard_map/ppermute | solution.py:36
  144.9 12.6 %collective-permute-start.22 = (bf16[2,128,1536]{2,1,0:T(8,128)(2,1)}, bf16[2,128,1536]{2,1,0:T(8,128)(2,1)S(1)}, u32[]{:S(2)}, u32[]{:S(2)}) collective-permute-start(bf16[2,128,1536]{2,1,0:T(8,128)(2,1)} %get-tuple-element.115), channel_id=1, source_target_pairs={{0,4},{1,5},{2,6},{3,7},{4,8},{5,9},{6,10},{7,11},{8,12},{9,13},{1... | collective-permute-start | bytes 2359304 | tf_op jit(solution)/shard_map/ppermute | solution.py:36
  145.0 12.5 %collective-permute-start.23 = (bf16[2,128,1536]{2,1,0:T(8,128)(2,1)}, bf16[2,128,1536]{2,1,0:T(8,128)(2,1)S(1)}, u32[]{:S(2)}, u32[]{:S(2)}) collective-permute-start(bf16[2,128,1536]{2,1,0:T(8,128)(2,1)} %get-tuple-element.116), channel_id=1, source_target_pairs={{0,12},{1,13},{2,14},{3,15},{4,0},{5,1},{6,2},{7,3},{8,4},{9,5},{1... | collective-permute-start | bytes 2359304 | tf_op jit(solution)/shard_map/ppermute | solution.py:36
  147.6 17.7 %collective-permute-start.20 = (bf16[2,128,1536]{2,1,0:T(8,128)(2,1)}, bf16[2,128,1536]{2,1,0:T(8,128)(2,1)S(1)}, u32[]{:S(2)}, u32[]{:S(2)}) collective-permute-start(bf16[2,128,1536]{2,1,0:T(8,128)(2,1)} %get-tuple-element.109), channel_id=1, source_target_pairs={{0,12},{1,13},{2,14},{3,15},{4,0},{5,1},{6,2},{7,3},{8,4},{9,5},{1... | collective-permute-start | bytes 2359304 | tf_op jit(solution)/shard_map/ppermute | solution.py:36
  147.7 18.3 %collective-permute-start.21 = (bf16[2,128,1536]{2,1,0:T(8,128)(2,1)}, bf16[2,128,1536]{2,1,0:T(8,128)(2,1)S(1)}, u32[]{:S(2)}, u32[]{:S(2)}) collective-permute-start(bf16[2,128,1536]{2,1,0:T(8,128)(2,1)} %get-tuple-element.110), channel_id=1, source_target_pairs={{0,4},{1,5},{2,6},{3,7},{4,8},{5,9},{6,10},{7,11},{8,12},{9,13},{1... | collective-permute-start | bytes 2359304 | tf_op jit(solution)/shard_map/ppermute | solution.py:36
  157.7 16.6 %collective-permute-start.25 = (bf16[2,128,1536]{2,1,0:T(8,128)(2,1)S(1)}, bf16[2,128,1536]{2,1,0:T(8,128)(2,1)S(1)}, u32[]{:S(2)}, u32[]{:S(2)}) collective-permute-start(bf16[2,128,1536]{2,1,0:T(8,128)(2,1)S(1)} %add_convert_fusion.1), channel_id=1, source_target_pairs={{0,4},{1,5},{2,6},{3,7},{4,8},{5,9},{6,10},{7,11},{8,12},{9,13},{1... | collective-permute-start | bytes 2359304 | tf_op jit(solution)/shard_map/ppermute | solution.py:36
  158.0 16.4 %collective-permute-start.24 = (bf16[2,128,1536]{2,1,0:T(8,128)(2,1)S(1)}, bf16[2,128,1536]{2,1,0:T(8,128)(2,1)S(1)}, u32[]{:S(2)}, u32[]{:S(2)}) collective-permute-start(bf16[2,128,1536]{2,1,0:T(8,128)(2,1)S(1)} %add_convert_fusion.2), channel_id=1, source_target_pairs={{0,12},{1,13},{2,14},{3,15},{4,0},{5,1},{6,2},{7,3},{8,4},{9,5},{1... | collective-permute-start | bytes 2359304 | tf_op jit(solution)/shard_map/ppermute | solution.py:36
  174.7 7.9 %collective-permute-start.26 = (bf16[128,1536]{1,0:T(8,128)(2,1)S(1)}, bf16[128,1536]{1,0:T(8,128)(2,1)S(1)}, u32[]{:S(2)}, u32[]{:S(2)}) collective-permute-start(bf16[128,1536]{1,0:T(8,128)(2,1)S(1)} %get-tuple-element.133), channel_id=1, source_target_pairs={{0,1},{1,2},{2,3},{3,0},{4,5},{5,6},{6,7},{7,4},{8,9},{9,10},{10,1... | collective-permute-start | bytes 1179656 | tf_op jit(solution)/shard_map/ppermute | solution.py:36
  174.8 12.9 %collective-permute-start.28 = (bf16[128,1536]{1,0:T(8,128)(2,1)S(1)}, bf16[128,1536]{1,0:T(8,128)(2,1)S(1)}, u32[]{:S(2)}, u32[]{:S(2)}) collective-permute-start(bf16[128,1536]{1,0:T(8,128)(2,1)S(1)} %get-tuple-element.132), channel_id=1, source_target_pairs={{0,2},{1,3},{2,0},{3,1},{4,6},{5,7},{6,4},{7,5},{8,10},{9,11},{10,... | collective-permute-start | bytes 1179656 | tf_op jit(solution)/shard_map/ppermute | solution.py:36
  178.7 9.0 %collective-permute-start.27 = (bf16[128,1536]{1,0:T(8,128)(2,1)S(1)}, bf16[128,1536]{1,0:T(8,128)(2,1)S(1)}, u32[]{:S(2)}, u32[]{:S(2)}) collective-permute-start(bf16[128,1536]{1,0:T(8,128)(2,1)S(1)} %fusion.6), channel_id=1, source_target_pairs={{0,3},{1,0},{2,1},{3,2},{4,7},{5,4},{6,5},{7,6},{8,11},{9,8},{10,9... | collective-permute-start | bytes 1179656 | tf_op jit(solution)/shard_map/ppermute | solution.py:36
  188.0 37.8 %copy-start.3 = (bf16[128,1536]{1,0:T(8,128)(2,1)}, bf16[128,1536]{1,0:T(8,128)(2,1)S(1)}, u32[]{:S(2)}) copy-start(bf16[128,1536]{1,0:T(8,128)(2,1)S(1)} %fusion.5) | copy-start | bytes 1179652
  188.0 37.4 %copy-start.4 = (bf16[1536,384]{1,0:T(8,128)(2,1)S(1)}, bf16[1536,384]{1,0:T(8,128)(2,1)}, u32[]{:S(2)}) copy-start(bf16[1536,384]{1,0:T(8,128)(2,1)} %param.40) | copy-start | bytes 3538948
  (30 other events, 326.0 us)

commit v5 on v4

v5 whole, which is shorter than its diff:
```python
import jax
import jax.numpy as jnp
import numpy as np
from jax import lax
from jax.experimental import pallas as pl
from jax.experimental.pallas import tpu as pltpu
from jax.sharding import PartitionSpec as P

HEADS = 24
KV_HEADS = 8
HEAD = 64
EXPERTS = 40
TOP = 8
CAP = 40
ATTENTION_VMEM = 63 << 20
EPSILON = 1e-05
ROPE_BASE = 10000.0
MASKED = -1e30
SIDE = 4
BF = jnp.bfloat16
F32 = jnp.float32
WHOLE = ("seq", "grp")


def shift(rows, phase, step):
    pairs = []
    for s in range(8):
        for i in range(16):
            if s % 2 == phase:
                to = i // SIDE * SIDE + (i % SIDE + step) % SIDE
            else:
                to = (i // SIDE + step) % SIDE * SIDE + i % SIDE
            pairs.append((s * 16 + i, s * 16 + to))
    return lax.ppermute(rows, WHOLE, pairs)


def partner(rows):
    return lax.ppermute(rows, "seq", [(s, s ^ 1) for s in range(8)])


def wide(v):
    return v.astype(F32)


def dot_t(lhs, rhs):
    return lax.dot_general(lhs, rhs, (((1,), (1,)), ((), ())), preferred_element_type=F32)


def norm(rows, scale):
    inverse = lax.rsqrt(jnp.mean(rows * rows, axis=-1, keepdims=True) + EPSILON)
    return (rows * inverse * scale).astype(BF)


def attention_kernel(*refs):
    tok = refs[0:5]
    adapt = refs[5:13]
    (place, gain, gain_moe, cosine, sine, wq_hbm, wk_hbm, wv_hbm, wo_hbm, mixed_out, moe_out,
     wq, wk, wv, wo, xn, ad, qbuf, kbuf, vbuf, att, score, prob, sems) = refs[13:]
    loads = [pltpu.make_async_copy(src, dst, sems.at[i]) for i, (src, dst) in enumerate(
        [(wk_hbm, wk), (wv_hbm, wv), (wq_hbm, wq), (wo_hbm, wo)])]
    for load in loads:
        load.start()
    count = tok[0].shape[0]
    ends = [place[0], place[1], place[2]]
    me = place[3]

    def document(index):
        return sum((index >= end).astype(jnp.int32) for end in ends)

    def block_start(b):
        return (me - jnp.where(b < 3, 2 * b, 2 * b - 5)) * count

    for j in range(8):
        ad[48 * j:48 * j + 48, :] = adapt[j][...]
    for b in range(5):
        xn[b * count:(b + 1) * count, :] = norm(tok[b][...].astype(F32), gain[...])
    column = lax.broadcasted_iota(jnp.int32, (1, 384), 1)
    col_row = column & 15
    col_prompt = column >> 4
    col_prompt = col_prompt - 3 * ((col_prompt * 171) >> 9)

    def low(z, roll, first, docs):
        moved = pltpu.roll(z, roll, 1)
        keep = (docs == col_prompt) & (col_row >= first) & (col_row < first + 2)
        return jnp.where(keep, moved, 0.0).astype(BF)

    lane = lax.broadcasted_iota(jnp.int32, (count, 128), 1)
    lower = (lane & 63) < 32
    down_rows = lax.broadcasted_iota(jnp.int32, (count, 1), 0)

    def rope(u, cos_t, sin_t):
        turned = jnp.where(lower, pltpu.roll(u, 96, 1), pltpu.roll(u, 32, 1))
        return u * cos_t + turned * sin_t

    loads[0].wait()
    loads[1].wait()

    def key_block(b, carry):
        at = pl.ds(pl.multiple_of(b * count, count), count)
        docs = document(block_start(b) + down_rows)
        rows = xn[at, :]
        z = dot_t(rows, ad[...])
        keys = jnp.dot(rows, wk[...], preferred_element_type=F32) + jnp.dot(
            low(z, 10, 12, docs), ad[:, :512], preferred_element_type=F32)
        values = jnp.dot(rows, wv[...], preferred_element_type=F32) + jnp.dot(
            low(z, 8, 12, docs), ad[:, 512:1024], preferred_element_type=F32)
        vbuf[at, :] = values.astype(BF)
        cos_t = cosine[at, :]
        sin_t = sine[at, :]
        for c in range(4):
            kbuf[at, 128 * c:128 * c + 128] = rope(
                keys[:, 128 * c:128 * c + 128], cos_t, sin_t).astype(BF)
        return carry

    lax.fori_loop(0, 5, key_block, 0)
    own_index = me * count + down_rows
    docs = document(own_index)
    own = xn[0:count, :]
    zq = low(dot_t(own, ad[...]), 8, 8, docs)
    cos_t = cosine[0:count, :]
    sin_t = sine[0:count, :]
    low_half = lane < 64
    along = lax.broadcasted_iota(jnp.int32, (1, count), 1)
    key_index = jnp.concatenate([block_start(b) + along for b in range(5)], axis=1)
    allowed = ((docs == document(key_index)) & (key_index <= own_index) & (key_index >= 0))
    bias = jnp.where(allowed, 0.0, MASKED)
    loads[2].wait()

    def query_block(c, carry):
        at = pl.multiple_of(c * 384, 128)
        u = jnp.dot(own, wq[:, pl.ds(at, 384)], preferred_element_type=F32) + jnp.dot(
            zq, ad[:, pl.ds(at, 384)], preferred_element_type=F32)
        for t in range(3):
            q = rope(u[:, 128 * t:128 * t + 128], cos_t, sin_t).astype(BF).astype(F32)
            q = q * (HEAD ** -0.5)
            turned = pltpu.roll(q, 64, 1)
            for own_low in (True, False):
                h = 2 * t + (0 if own_low else 1)
                kv_low = h < 3
                rows = q if own_low == kv_low else turned
                keep = low_half if kv_low else ~low_half
                qbuf[c, count * h:count * h + count, :] = jnp.where(keep, rows, 0.0).astype(BF)
        return carry

    lax.fori_loop(0, 4, query_block, 0)

    def pair(j, carry):
        kv = pl.ds(pl.multiple_of(j * 128, 128), 128)
        score[...] = dot_t(qbuf[j], kbuf[:, kv])
        totals = []
        for h in range(6):
            at = slice(count * h, count * h + count)
            s = score[at, :] + bias
            top = jnp.max(s, axis=-1, keepdims=True)
            w = jnp.exp(s - top)
            totals.append(jnp.sum(w, axis=-1, keepdims=True))
            prob[at, :] = w.astype(BF)
        out = jnp.dot(prob[...], vbuf[:, kv], preferred_element_type=F32)
        results = []
        for h in range(6):
            o = out[count * h:count * h + count] / totals[h]
            results.append(pltpu.roll(o, 64, 1) if (h % 2 == 0) != (h < 3) else o)
        for t in range(3):
            att[:, pl.ds(pl.multiple_of(j * 384 + 128 * t, 128), 128)] = jnp.where(
                low_half, results[2 * t], results[2 * t + 1]).astype(BF)
        return carry

    lax.fori_loop(0, 4, pair, 0)
    loads[3].wait()
    attended = att[...]
    zo = low(dot_t(attended, ad[...]), 4, 10, docs)
    mixed = (tok[0][...].astype(F32) + jnp.dot(attended, wo[...], preferred_element_type=F32)
             + jnp.dot(zo, ad[...], preferred_element_type=F32)).astype(BF)
    mixed_out[...] = mixed
    moe_out[...] = norm(mixed.astype(F32), gain_moe[...])


def attention(tok, adapt, place, gain, gain_moe, cosine, sine, wq, wk, wv, wo):
    count, width = tok[0].shape
    vm = pl.BlockSpec(memory_space=pltpu.VMEM)
    anywhere = pl.BlockSpec(memory_space=pl.ANY)
    rows = jax.ShapeDtypeStruct((count, width), BF)
    return pl.pallas_call(
        attention_kernel,
        out_shape=(rows, rows),
        in_specs=[vm] * 13 + [pl.BlockSpec(memory_space=pltpu.SMEM)] + [vm] * 4
        + [anywhere] * 4,
        out_specs=(vm, vm),
        scratch_shapes=[
            pltpu.VMEM(wq.shape, BF), pltpu.VMEM(wk.shape, BF), pltpu.VMEM(wv.shape, BF),
            pltpu.VMEM(wo.shape, BF), pltpu.VMEM((5 * count, width), BF),
            pltpu.VMEM((384, width), BF), pltpu.VMEM((4, 6 * count, 128), BF),
            pltpu.VMEM((5 * count, 512), BF), pltpu.VMEM((5 * count, 512), BF),
            pltpu.VMEM((count, width), BF), pltpu.VMEM((6 * count, 5 * count), F32),
            pltpu.VMEM((6 * count, 5 * count), BF), pltpu.SemaphoreType.DMA((4,)),
        ],
        compiler_params=pltpu.CompilerParams(vmem_limit_bytes=ATTENTION_VMEM),
        cost_estimate=pl.CostEstimate(flops=8 << 30, transcendentals=0,
                                      bytes_accessed=20 << 20),
        name="attention_block",
    )(*tok, *adapt, place, gain, gain_moe, cosine, sine, wq, wk, wv, wo)


def expert_kernel(p0, p1, first, table, gate, up, down, out0, out1, xe, ho, scale):
    odd, part = first[0], first[1]
    row = lax.broadcasted_iota(jnp.int32, (256, 256), 0)
    col = lax.broadcasted_iota(jnp.int32, (256, 256), 1)
    before = ((row < col) & ((row < 128) == (col < 128))).astype(BF)
    slot = lax.broadcasted_iota(jnp.int32, (2 * CAP, 256), 0).astype(F32)
    base = jnp.where(lax.broadcasted_iota(jnp.int32, (8, 256), 1) < 128, 0.0, float(CAP))

    def places(i):
        named = table[part, i] > 0.0
        rank = jnp.dot(named.astype(F32).astype(BF), before, preferred_element_type=F32) + base
        rank = jnp.where(named, rank, -1.0)
        return [slot == rank[e:e + 1, :] for e in range(3)]

    hots = []
    for i, piece in enumerate((p0, p1)):
        spots = places(i)
        hot = jnp.concatenate([jnp.where(p, 1.0, 0.0) for p in spots]).astype(BF)
        hots.append(hot)
        rows = jnp.dot(hot, piece[...], preferred_element_type=F32).astype(BF)
        given = table[part, i]
        for e in range(3):
            at = slice(i * 2 * CAP, (i + 1) * 2 * CAP)
            xe[e, at, :] = rows[e * 2 * CAP:(e + 1) * 2 * CAP]
            scale[e, at, :] = jnp.sum(jnp.where(spots[e], given[e:e + 1, :], 0.0), axis=1,
                                      keepdims=True)

    def ffn(e, half, count):
        rows = xe[e]
        hidden = []
        for h in range(count):
            g = jnp.dot(rows, gate[half + h], preferred_element_type=F32)
            u = jnp.dot(rows, up[half + h], preferred_element_type=F32)
            hidden.append((g / (1.0 + jnp.exp(-g)) * u).astype(BF))
        hidden = jnp.concatenate(hidden, axis=1)
        maps = down[pl.ds(pl.multiple_of(256 * half, 256), 256 * count), :]
        out = jnp.dot(hidden, maps, preferred_element_type=F32)
        ho[e] = (out * scale[e]).astype(BF)

    def whole(e, carry):
        ffn(e, odd + 2 * e, 2)
        return carry

    lax.fori_loop(0, 2, whole, 0)
    ffn(2, 4 - 4 * odd, 1)
    for i, out in enumerate((out0, out1)):
        rows = jnp.concatenate([ho[e, i * 2 * CAP:(i + 1) * 2 * CAP, :] for e in range(3)])
        out[...] = lax.dot_general(hots[i], rows, (((0,), (0,)), ((), ())),
                                   preferred_element_type=F32).astype(BF)


def experts(pieces, first, table, gate, up, down):
    width = gate.shape[1]
    shape = pieces[0].shape
    vm = pl.BlockSpec(memory_space=pltpu.VMEM)
    piece = jax.ShapeDtypeStruct((256, width), BF)
    outs = pl.pallas_call(
        expert_kernel,
        out_shape=(piece, piece),
        in_specs=[vm, vm, pl.BlockSpec(memory_space=pltpu.SMEM), vm, vm, vm, vm],
        out_specs=(vm, vm),
        scratch_shapes=[
            pltpu.VMEM((3, 4 * CAP, width), BF), pltpu.VMEM((3, 4 * CAP, width), BF),
            pltpu.VMEM((3, 4 * CAP, 1), F32),
        ],
        compiler_params=pltpu.CompilerParams(vmem_limit_bytes=24 << 20),
        cost_estimate=pl.CostEstimate(flops=7 << 30, transcendentals=0,
                                      bytes_accessed=12 << 20),
        name="expert_block",
    )(*[rows.reshape(256, width) for rows in pieces], first, table, gate, up,
      down.reshape(5 * 256, width))
    return [rows.reshape(shape) for rows in outs]


def rms_scaled(features, scales):
    features = features.astype(F32)
    inverse = lax.rsqrt(jnp.mean(features * features, axis=-1, keepdims=True) + EPSILON)
    return (features * inverse * scales).astype(BF)


def body(tokens, lengths, prompt_adapter, routes, routing_weight, attention_gain, query_weight,
         key_weight, value_weight, output_weight, adapter_down_maps, adapter_up_query_output,
         adapter_up_key_value, expert_gain, gate_weight, up_weight, down_weight, closing_gain,
         vocab_projection):
    own = tokens[0]
    count, width = own.shape
    me, grp = lax.axis_index("seq"), lax.axis_index("grp")

    listing = np.concatenate([np.array([0, 1, 2] if g % 2 == 0 else [1, 2, 0]) + 5 * g // 2
                              for g in range(16)]).astype(np.int32)
    ids, given = routes[0], routing_weight[0]
    table = jnp.sum(jnp.where(ids.T[None] == jnp.asarray(listing)[:, None, None],
                              given.T[None], 0.0), axis=1).reshape(16, 3 * count)
    high = lax.reduce_precision(table, 8, 7)
    low = table - high
    route_rows = jnp.concatenate(
        [high, low, jnp.zeros((16, width - 6 * count), F32)], axis=1).astype(BF)

    ranks = (jnp.arange(16, dtype=jnp.int32)[:, None]
             == 2 * me + jnp.arange(2, dtype=jnp.int32)[None, :]).astype(BF)
    downs = jnp.einsum("rk,pdr->pkd", ranks, adapter_down_maps[:, 0],
                       preferred_element_type=F32).astype(BF).reshape(8, width)
    ups = lax.dynamic_slice_in_dim(adapter_up_query_output[:, 0], 2 * me, 2, 1).reshape(4, width)
    thin = lax.dynamic_slice_in_dim(adapter_up_key_value[:, 0], 2 * me, 2, 1)
    thin = jnp.concatenate([thin[0], thin[1], jnp.zeros((2, width - 1024), BF)], axis=1)
    maps = jnp.concatenate([downs, ups, thin], axis=0)
    payload = jnp.concatenate(
        [jnp.broadcast_to(maps[None], (16, 14, width)), route_rows[:, None, :],
         jnp.zeros((16, 1, width), BF)], axis=1)
    payload, own = lax.optimization_barrier((payload, own))
    held = lax.all_to_all(payload, "grp", 0, 0, tiled=True)
    back1 = lax.ppermute(own, "seq", [(s, s + 2) for s in range(6)])
    back2 = lax.ppermute(own, "seq", [(s, s + 4) for s in range(4)])
    odd_core = me % 2 == 1
    tok = [own, back1, back2, partner(jnp.where(odd_core, back1, own)),
           partner(jnp.where(odd_core, back2, back1))]

    lens = lengths[0]
    ends = jnp.cumsum(lens)
    starts = ends - lens
    blocks = me - jnp.array([0, 2, 4, 1, 3], jnp.int32)
    row = jnp.arange(count, dtype=jnp.int32)
    index = (blocks[:, None] * count + row[None, :]).reshape(-1)
    document = jnp.sum((index[:, None] >= ends[None, :]).astype(jnp.int32), axis=1)
    half = HEAD // 2
    frequency = ROPE_BASE ** (-(jnp.arange(128, dtype=jnp.int32) % half).astype(F32) / half)
    sign = jnp.where(jnp.arange(128) % HEAD < half, -1.0, 1.0).astype(F32)
    near = row.astype(F32)[:, None] * frequency[None, :]
    far = (blocks[:, None] * count - starts[None, :]).astype(F32)[:, :, None] * frequency
    near_cos, near_sin = jnp.cos(near)[None], jnp.sin(near)[None]
    far_cos, far_sin = jnp.cos(far), jnp.sin(far)

    def by_document(values):
        docs = document.reshape(5, count, 1)
        return jnp.where(docs == 0, values[:, None, 0], jnp.where(
            docs == 1, values[:, None, 1], values[:, None, 2]))

    far_cos, far_sin = by_document(far_cos), by_document(far_sin)
    cosine = (far_cos * near_cos - far_sin * near_sin).reshape(5 * count, 128)
    sine = ((far_sin * near_cos + far_cos * near_sin) * sign).reshape(5 * count, 128)
    row_index = index[:count]
    place = jnp.concatenate([ends, me[None]]).astype(jnp.int32)
    gain, gain_moe = attention_gain[None], expert_gain[None]
    held, cosine, sine, place, gain, gain_moe = lax.optimization_barrier(
        (held, cosine, sine, place, gain, gain_moe))
    picked = jnp.stack([lax.dynamic_index_in_dim(held, prompt_adapter[0, p], 0, False)
                        for p in range(3)]).reshape(48, width)
    turn = [picked] + [lax.ppermute(picked, "seq", [(s, (s + d) % 8) for s in range(8)])
                       for d in (2, 6, 4)]
    rel = jnp.array([0, 3, 1, 2], jnp.int32)
    first, second = jnp.where(me % 2 == 0, grp % 4, grp // 4), jnp.where(
        me % 2 == 0, grp // 4, grp % 4)
    first, second = (first + rel[None, :]) % 4, (second + rel[:, None]) % 4
    source = jnp.where(me % 2 == 0, second * 4 + first, first * 4 + second).reshape(8, 2)
    source = jnp.concatenate([source[:3], source[5:6], source[3:5], source[6:]]).reshape(16)
    order = (source[:, None] == jnp.arange(16, dtype=jnp.int32)[None, :]).astype(F32)
    route_in = jnp.dot(order, held[:, 14, :].astype(F32), precision=lax.Precision.HIGHEST)
    route_in = (route_in[:, :3 * count] + route_in[:, 3 * count:6 * count]).reshape(8, 2, 3, count)
    route_in = jnp.concatenate([route_in, jnp.zeros((8, 2, 5, count), F32)], axis=2)
    route_in = route_in.transpose(0, 2, 1, 3).reshape(4, 2, 8, 2 * count)
    odd = (grp % 2).astype(jnp.int32)
    weights = (gate_weight, up_weight, down_weight)

    turn, route_in = lax.optimization_barrier((turn, route_in))
    adapt = turn + [partner(piece) for piece in turn]
    mixed, moe_in = attention(tok, adapt, place, gain, gain_moe, cosine, sine, query_weight,
                              key_weight, value_weight, output_weight)

    def share(pieces, which):
        return experts(pieces, jnp.stack([odd, jnp.int32(which)]), route_in, *weights)

    line = lax.optimization_barrier(
        [shift(moe_in, 0, 1), shift(moe_in, 0, -1), shift(moe_in, 0, 2)])
    own_lo, own_hi = jnp.stack([moe_in, line[0]]), jnp.stack([line[1], line[2]])
    minus_lo, plus_hi = shift(own_lo, 1, 1), shift(own_hi, 1, -1)
    minus_hi, plus_lo = shift(own_hi, 1, 1), shift(own_lo, 1, -1)
    own_lo, own_hi = share([own_lo, own_hi], 0)
    minus_lo, plus_hi, own_lo, own_hi = lax.optimization_barrier(
        (minus_lo, plus_hi, own_lo, own_hi))
    first_lo, first_hi = share([minus_lo, plus_hi], 1)
    minus_lo, plus_hi, minus_hi, plus_lo, first_lo, first_hi = lax.optimization_barrier(
        (minus_lo, plus_hi, minus_hi, plus_lo, first_lo, first_hi))
    far_lo, far_hi = shift(minus_lo, 1, 1), shift(plus_hi, 1, -1)
    minus_hi, plus_lo = share([minus_hi, plus_lo], 2)
    minus_lo, plus_hi, minus_hi, plus_lo, far_lo, far_hi = lax.optimization_barrier(
        (first_lo, first_hi, minus_hi, plus_lo, far_lo, far_hi))

    minus_lo, plus_hi = shift(minus_lo, 1, -1), shift(plus_hi, 1, 1)
    far_lo, far_hi = share([far_lo, far_hi], 3)
    far_lo, far_hi = lax.optimization_barrier((shift(far_lo, 1, 1), shift(far_hi, 1, -1)))
    plus_lo = shift((wide(plus_lo) + wide(far_lo)).astype(BF), 1, 1)
    minus_hi = shift((wide(minus_hi) + wide(far_hi)).astype(BF), 1, -1)
    minus_lo, plus_hi, minus_hi, plus_lo = lax.optimization_barrier(
        (minus_lo, plus_hi, minus_hi, plus_lo))
    own_lo = wide(own_lo) + wide(plus_lo) + wide(minus_lo)
    own_hi = wide(own_hi) + wide(plus_hi) + wide(minus_hi)
    line = lax.optimization_barrier(
        [shift(own_hi[0].astype(BF), 0, 1), shift(own_lo[1].astype(BF), 0, -1),
         shift(own_hi[1].astype(BF), 0, 2)])
    combined = own_lo[0] + wide(line[0]) + wide(line[1]) + wide(line[2])
    hidden_out = (mixed.astype(F32) + combined).astype(BF)

    selector = (ends[:, None] - 1 == row_index[None, :]).astype(BF)
    last = jnp.dot(selector, hidden_out, preferred_element_type=F32)
    last = rms_scaled(last, closing_gain)
    part = width // 8
    split = last.reshape(3, 8, part).transpose(1, 0, 2)
    mine = lax.all_to_all(split, "seq", 0, 0, tiled=True)
    mine = jnp.sum(mine.astype(F32), axis=0).astype(BF)
    everyone = lax.all_to_all(jnp.broadcast_to(mine[None], (128, 3, part)), WHOLE, 0, 0,
                              tiled=True)
    final_rows = everyone.reshape(8, 48, part).transpose(1, 0, 2).reshape(48, width)
    logits = jnp.dot(final_rows, vocab_projection, preferred_element_type=F32)
    top = jnp.max(logits, axis=1)
    mass = jnp.sum(jnp.exp(logits - top[:, None]), axis=1)
    stats = jnp.concatenate([top, mass, jnp.zeros((32,), F32)])
    stats = lax.all_to_all(jnp.broadcast_to(stats[None], (128, 128)), WHOLE, 0, 0, tiled=True)
    tops = stats[:, :48]
    peak = jnp.max(tops, axis=0)
    total = jnp.sum(stats[:, 48:96] * jnp.exp(tops - peak[None]), axis=0)
    log_probs = logits - (peak + jnp.log(total))[:, None]
    return hidden_out[None], log_probs


def solution(mesh):
    placed = (
        P("grp", "seq", None), P("grp", None), P("grp", None), P("grp", "seq", None),
        P("grp", "seq", None), P(), P(), P(), P(), P(), P(None, "grp", None, None),
        P(None, "grp", None, None), P(None, "grp", None, None), P(), P("grp", None, None),
        P("grp", None, None), P("grp", None, None), P(), P(None, WHOLE),
    )
    return jax.shard_map(
        body,
        mesh=mesh,
        in_specs=placed,
        out_specs=(P("grp", "seq", None), P(None, WHOLE)),
        check_vma=False,
    )
```

time: 242 us -> 221 us (0.913)
  Pallas kernels: 74.1 us -> 39.7 us
  waiting for transfers between devices: 42.2 us -> 59.1 us
  blocking collectives: 49.9 us -> 45.7 us
  local copies, waits for them, and re-layouts: 10.7 us -> 13.9 us
  other arithmetic: 10.9 us -> 7.78 us
    pallas_call x5 -> x4, Pallas kernels: 55 us -> 18.1 us  [experts(): pl.pallas_call(expert_kernel, out_shape=(piece, piece), in_specs=[vm, vm,...]
    ppermute x18, waiting for transfers between devices: 40.8 us -> 51.3 us  [shift(): return lax.ppermute(rows, WHOLE, pairs)]
    ppermute x3, waiting for transfers between devices: 0.01 us -> 6.6 us  [body(): lax.ppermute(picked, 'seq', [(s, (s + d) % 8) for s in range(8)])]
    unnamed x64 -> x52, local copies, waits for them, and re-layouts: 2.89 us -> 7.59 us
    all_to_all x1, blocking collectives: 20.7 us -> 16.8 us  [body(): lax.all_to_all(jnp.broadcast_to(mine[None], (128, 3, part)), WHOLE, 0, 0,...]
    ppermute x18, starting transfers between devices: 20.4 us -> 23.6 us  [shift(): return lax.ppermute(rows, WHOLE, pairs)]
    broadcast_in_dim x6 -> x2, local copies, waits for them, and re-layouts: 3.94 us -> 1.2 us  [body(): gain, gain_moe = (attention_gain[None], expert_gain[None])]
    pallas_call x1, Pallas kernels: 19.1 us -> 21.6 us  [attention(): pl.pallas_call(attention_kernel, out_shape=(rows, rows), in_specs=[vm] *...]
  transfers between devices with their start and end apart: 30 -> 30, of which waited for: 8 -> 17; matrix products, arithmetic and copies ran while one was open for 5% -> 3% of each run, Pallas kernels for 18% -> 6%
where the time goes in v5:
time: 221 us; the launch traced here: 220 us
  waiting for transfers between devices  59.1 us (27%)
  starting transfers between devices  45.7 us (21%)
  blocking collectives  45.7 us (21%)
  Pallas kernels  39.7 us (18%)
  local copies, waits for them, and re-layouts  13.9 us (6%)
  other arithmetic  7.78 us (4%)
  between operations  6.9 us (3%)
    ppermute x18, waiting for transfers between devices, shift(): return lax.ppermute(rows, WHOLE, pairs)  51.3 us
    ppermute x18, starting transfers between devices, shift(): return lax.ppermute(rows, WHOLE, pairs)  23.6 us
    pallas_call x1, Pallas kernels, attention(): pl.pallas_call(attention_kernel, out_shape=(rows, rows), in_specs=[vm] *...  21.6 us
    pallas_call x4, Pallas kernels, experts(): pl.pallas_call(expert_kernel, out_shape=(piece, piece), in_specs=[vm, vm,...  18.1 us
    all_to_all x1, blocking collectives, body(): lax.all_to_all(jnp.broadcast_to(mine[None], (128, 3, part)), WHOLE, 0, 0,...  16.8 us
    all_to_all x1, blocking collectives, body(): mine = lax.all_to_all(split, 'seq', 0, 0, tiled=True)  15.3 us
    all_to_all x1, blocking collectives, body(): lax.all_to_all(jnp.broadcast_to(stats[None], (128, 128)), WHOLE, 0, 0, ti...  13.6 us
    all_to_all x1, starting transfers between devices, body(): held = lax.all_to_all(payload, 'grp', 0, 0, tiled=True)  7.78 us
  transfers between devices with their start and end apart: 30, of which 17 were waited for; matrix products, arithmetic and copies ran while one was open for 3% of the time, Pallas kernels for 6%

profile of v5, /device:TPU:1, one launch (start us, length us, event | category | flops | bytes accessed | tf_op | source)
XLA Modules:
  0.0 220.0 jit_solution(8079605176806559388)
XLA Ops:
  5.0 5.5 %collective-permute-start.1 = (bf16[128,1536]{1,0:T(8,128)(2,1)S(1)}, bf16[128,1536]{1,0:T(8,128)(2,1)S(1)}, u32[]{:S(2)}, u32[]{:S(2)}) collective-permute-start(bf16[128,1536]{1,0:T(8,128)(2,1)S(1)} %bitcast.197), channel_id=1, source_target_pairs={{0,64},{16,80},{32,96},{48,112},{1,65},{17,81},{33,97},{49,113},{2... | collective-permute-start | bytes 1179656 | tf_op jit(solution)/shard_map/ppermute | solution.py:316
  10.5 2.2 %collective-permute-start = (bf16[128,1536]{1,0:T(8,128)(2,1)S(1)}, bf16[128,1536]{1,0:T(8,128)(2,1)S(1)}, u32[]{:S(2)}, u32[]{:S(2)}) collective-permute-start(bf16[128,1536]{1,0:T(8,128)(2,1)S(1)} %bitcast.198), channel_id=1, source_target_pairs={{0,32},{16,48},{32,64},{48,80},{64,96},{80,112},{1,33},{17,49},{33... | collective-permute-start | bytes 1179656 | tf_op jit(solution)/shard_map/ppermute | solution.py:315
  12.7 7.8 %all-to-all-start = ((bf16[16,16,1536]{2,1,0:T(8,128)(2,1)}), bf16[16,16,1536]{2,1,0:T(8,128)(2,1)S(1)}, u32[]{:S(2)}, u32[]{:S(2)}) async-start(bf16[16,16,1536]{2,1,0:T(8,128)(2,1)} %maximum_maximum_fusion), calls=%async_computation | async-start | bytes 1572864 | tf_op jit(solution)/shard_map/all_to_all | solution.py:314
  36.9 3.1 %collective-permute-done.6.refs_8_ = bf16[48,1536]{1,0:T(8,128)(2,1)S(1)} collective-permute-done((bf16[48,1536]{1,0:T(8,128)(2,1)S(1)}, bf16[48,1536]{1,0:T(8,128)(2,1)S(1)}, u32[]{:S(2)}, u32[]{:S(2)}) %collective-permute-start.6) | collective-permute-done | bytes 147488 | tf_op jit(solution)/shard_map/ppermute | solution.py:351
  40.1 3.4 %collective-permute-done.4.refs_6_ = bf16[48,1536]{1,0:T(8,128)(2,1)S(1)} collective-permute-done((bf16[48,1536]{1,0:T(8,128)(2,1)S(1)}, bf16[48,1536]{1,0:T(8,128)(2,1)S(1)}, u32[]{:S(2)}, u32[]{:S(2)}) %collective-permute-start.4) | collective-permute-done | bytes 147488 | tf_op jit(solution)/shard_map/ppermute | solution.py:351
  43.5 2.2 %collective-permute-start.7 = (bf16[48,1536]{1,0:T(8,128)(2,1)S(1)}, bf16[48,1536]{1,0:T(8,128)(2,1)S(1)}, u32[]{:S(2)}, u32[]{:S(2)}) collective-permute-start(bf16[48,1536]{1,0:T(8,128)(2,1)S(1)} %bitcast.209), channel_id=1, source_target_pairs={{0,16},{16,0},{32,48},{48,32},{64,80},{80,64},{96,112},{112,96},{1... | collective-permute-start | bytes 442376 | tf_op jit(solution)/shard_map/ppermute | solution.py:38
  48.5 21.6 %attention_block.1 = (bf16[128,1536]{1,0:T(8,128)(2,1)}, bf16[128,1536]{1,0:T(8,128)(2,1)}) custom-call(bf16[128,1536]{1,0:T(8,128)(2,1)} %bitcast.196, bf16[128,1536]{1,0:T(8,128)(2,1)} %copy-done.9, bf16[128,1536]{1,0:T(8,128)(2,1)} %copy-done.8, bf16[128,1536]{1,0:T(8,128)(2,1)} %collective-permute-done.2.refs_3_, ...), custom_call_target="tpu_custom_call" | custom-call | flops 8589934592 | bytes 20971520 | tf_op jit(solution)/shard_map/attention_block/pallas_call | solution.py:183
  70.1 3.0 %collective-permute-start.13 = (bf16[128,1536]{1,0:T(8,128)(2,1)}, bf16[128,1536]{1,0:T(8,128)(2,1)S(1)}, u32[]{:S(2)}, u32[]{:S(2)}) collective-permute-start(bf16[128,1536]{1,0:T(8,128)(2,1)} %get-tuple-element.66), channel_id=1, source_target_pairs={{0,2},{1,3},{2,0},{3,1},{4,6},{5,7},{6,4},{7,5},{8,10},{9,11},{10,... | collective-permute-start | bytes 1179656 | tf_op jit(solution)/shard_map/ppermute | solution.py:34
  74.5 4.3 %collective-permute-done.13 = bf16[128,1536]{1,0:T(8,128)(2,1)S(1)} collective-permute-done((bf16[128,1536]{1,0:T(8,128)(2,1)}, bf16[128,1536]{1,0:T(8,128)(2,1)S(1)}, u32[]{:S(2)}, u32[]{:S(2)}) %collective-permute-start.13) | collective-permute-done | bytes 393248 | tf_op jit(solution)/shard_map/ppermute | solution.py:34
  78.8 4.4 %collective-permute-done.12 = bf16[128,1536]{1,0:T(8,128)(2,1)S(1)} collective-permute-done((bf16[128,1536]{1,0:T(8,128)(2,1)}, bf16[128,1536]{1,0:T(8,128)(2,1)S(1)}, u32[]{:S(2)}, u32[]{:S(2)}) %collective-permute-start.12) | collective-permute-done | bytes 393248 | tf_op jit(solution)/shard_map/ppermute | solution.py:34
  83.3 2.5 %collective-permute-start.15 = (bf16[2,128,1536]{2,1,0:T(8,128)(2,1)S(1)}, bf16[2,128,1536]{2,1,0:T(8,128)(2,1)S(1)}, u32[]{:S(2)}, u32[]{:S(2)}) collective-permute-start(bf16[2,128,1536]{2,1,0:T(8,128)(2,1)S(1)} %pad_maximum_fusion.1), channel_id=1, source_target_pairs={{0,12},{1,13},{2,14},{3,15},{4,0},{5,1},{6,2},{7,3},{8,4},{9,5},{1... | collective-permute-start | bytes 2359304 | tf_op jit(solution)/shard_map/ppermute | solution.py:34
  86.3 2.5 %collective-permute-start.17 = (bf16[2,128,1536]{2,1,0:T(8,128)(2,1)S(1)}, bf16[2,128,1536]{2,1,0:T(8,128)(2,1)S(1)}, u32[]{:S(2)}, u32[]{:S(2)}) collective-permute-start(bf16[2,128,1536]{2,1,0:T(8,128)(2,1)S(1)} %pad_maximum_fusion), channel_id=1, source_target_pairs={{0,12},{1,13},{2,14},{3,15},{4,0},{5,1},{6,2},{7,3},{8,4},{9,5},{1... | collective-permute-start | bytes 2359304 | tf_op jit(solution)/shard_map/ppermute | solution.py:34
  95.1 4.5 %expert_block.4 = (bf16[256,1536]{1,0:T(8,128)(2,1)S(1)}, bf16[256,1536]{1,0:T(8,128)(2,1)S(1)}) custom-call(bf16[256,1536]{1,0:T(8,128)(2,1)S(1)} %bitcast.171, bf16[256,1536]{1,0:T(8,128)(2,1)S(1)} %bitcast.170, s32[2]{0:T(128)S(1)} %get-tuple-element.146.first, f32[4,2,8,256]{3,2,1,0:T(8,128)S(1)} %bitcast.176, bf16[5,1536,256]{2,1,0:T(8,128)(2,1)S(1)} %copy-done.1, ...), custom_call_target="tpu_custom_call" | custom-call | flops 7516192768 | bytes 12582912 | tf_op jit(solution)/shard_map/expert_block/pallas_call | solution.py:260
  99.7 4.5 %expert_block.5 = (bf16[256,1536]{1,0:T(8,128)(2,1)S(1)}, bf16[256,1536]{1,0:T(8,128)(2,1)S(1)}) custom-call(bf16[256,1536]{1,0:T(8,128)(2,1)S(1)} %bitcast.187, bf16[256,1536]{1,0:T(8,128)(2,1)S(1)} %bitcast.186, s32[2]{0:T(128)S(1)} %get-tuple-element.147.first, f32[4,2,8,256]{3,2,1,0:T(8,128)S(1)} %bitcast.177, bf16[5,1536,256]{2,1,0:T(8,128)(2,1)S(1)} %copy-done.2, ...), custom_call_target="tpu_custom_call" | custom-call | flops 7516192768 | bytes 12582912 | tf_op jit(solution)/shard_map/expert_block/pallas_call | solution.py:260
  104.2 2.5 %collective-permute-done.16 = bf16[2,128,1536]{2,1,0:T(8,128)(2,1)S(1)} collective-permute-done((bf16[2,128,1536]{2,1,0:T(8,128)(2,1)S(1)}, bf16[2,128,1536]{2,1,0:T(8,128)(2,1)S(1)}, u32[]{:S(2)}, u32[]{:S(2)}) %collective-permute-start.16) | collective-permute-done | bytes 786464 | tf_op jit(solution)/shard_map/ppermute | solution.py:34
  106.7 2.7 %collective-permute-start.19 = (bf16[2,128,1536]{2,1,0:T(8,128)(2,1)S(1)}, bf16[2,128,1536]{2,1,0:T(8,128)(2,1)S(1)}, u32[]{:S(2)}, u32[]{:S(2)}) collective-permute-start(bf16[2,128,1536]{2,1,0:T(8,128)(2,1)S(1)} %collective-permute-done.15), channel_id=1, source_target_pairs={{0,12},{1,13},{2,14},{3,15},{4,0},{5,1},{6,2},{7,3},{8,4},{9,5},{1... | collective-permute-start | bytes 2359304 | tf_op jit(solution)/shard_map/ppermute | solution.py:34
  109.5 4.5 %expert_block.6 = (bf16[256,1536]{1,0:T(8,128)(2,1)S(1)}, bf16[256,1536]{1,0:T(8,128)(2,1)S(1)}) custom-call(bf16[256,1536]{1,0:T(8,128)(2,1)S(1)} %bitcast.188, bf16[256,1536]{1,0:T(8,128)(2,1)S(1)} %bitcast.189, s32[2]{0:T(128)S(1)} %get-tuple-element.148.first, f32[4,2,8,256]{3,2,1,0:T(8,128)S(1)} %bitcast.178, bf16[5,1536,256]{2,1,0:T(8,128)(2,1)S(1)} %copy-done.2, ...), custom_call_target="tpu_custom_call" | custom-call | flops 7516192768 | bytes 12582912 | tf_op jit(solution)/shard_map/expert_block/pallas_call | solution.py:260
  114.0 5.1 %collective-permute-done.18 = bf16[2,128,1536]{2,1,0:T(8,128)(2,1)S(1)} collective-permute-done((bf16[2,128,1536]{2,1,0:T(8,128)(2,1)S(1)}, bf16[2,128,1536]{2,1,0:T(8,128)(2,1)S(1)}, u32[]{:S(2)}, u32[]{:S(2)}) %collective-permute-start.18) | collective-permute-done | bytes 786464 | tf_op jit(solution)/shard_map/ppermute | solution.py:34
  119.1 4.5 %expert_block.7 = (bf16[256,1536]{1,0:T(8,128)(2,1)S(1)}, bf16[256,1536]{1,0:T(8,128)(2,1)S(1)}) custom-call(bf16[256,1536]{1,0:T(8,128)(2,1)S(1)} %bitcast.190, bf16[256,1536]{1,0:T(8,128)(2,1)S(1)} %bitcast.191, s32[2]{0:T(128)S(1)} %get-tuple-element.149.first, f32[4,2,8,256]{3,2,1,0:T(8,128)S(1)} %bitcast.179, bf16[5,1536,256]{2,1,0:T(8,128)(2,1)S(1)} %copy-done.2, ...), custom_call_target="tpu_custom_call" | custom-call | flops 7516192768 | bytes 12582912 | tf_op jit(solution)/shard_map/expert_block/pallas_call | solution.py:260
  123.6 2.9 %collective-permute-start.23 = (bf16[2,128,1536]{2,1,0:T(8,128)(2,1)S(1)}, bf16[2,128,1536]{2,1,0:T(8,128)(2,1)S(1)}, u32[]{:S(2)}, u32[]{:S(2)}) collective-permute-start(bf16[2,128,1536]{2,1,0:T(8,128)(2,1)S(1)} %bitcast.193), channel_id=1, source_target_pairs={{0,12},{1,13},{2,14},{3,15},{4,0},{5,1},{6,2},{7,3},{8,4},{9,5},{1... | collective-permute-start | bytes 2359304 | tf_op jit(solution)/shard_map/ppermute | solution.py:34
  126.6 2.7 %collective-permute-start.20 = (bf16[2,128,1536]{2,1,0:T(8,128)(2,1)S(1)}, bf16[2,128,1536]{2,1,0:T(8,128)(2,1)S(1)}, u32[]{:S(2)}, u32[]{:S(2)}) collective-permute-start(bf16[2,128,1536]{2,1,0:T(8,128)(2,1)S(1)} %bitcast.185), channel_id=1, source_target_pairs={{0,12},{1,13},{2,14},{3,15},{4,0},{5,1},{6,2},{7,3},{8,4},{9,5},{1... | collective-permute-start | bytes 2359304 | tf_op jit(solution)/shard_map/ppermute | solution.py:34
  129.3 6.3 %collective-permute-done.23 = bf16[2,128,1536]{2,1,0:T(8,128)(2,1)S(1)} collective-permute-done((bf16[2,128,1536]{2,1,0:T(8,128)(2,1)S(1)}, bf16[2,128,1536]{2,1,0:T(8,128)(2,1)S(1)}, u32[]{:S(2)}, u32[]{:S(2)}) %collective-permute-start.23) | collective-permute-done | bytes 786464 | tf_op jit(solution)/shard_map/ppermute | solution.py:34
  135.5 3.4 %collective-permute-done.22 = bf16[2,128,1536]{2,1,0:T(8,128)(2,1)S(1)} collective-permute-done((bf16[2,128,1536]{2,1,0:T(8,128)(2,1)S(1)}, bf16[2,128,1536]{2,1,0:T(8,128)(2,1)S(1)}, u32[]{:S(2)}, u32[]{:S(2)}) %collective-permute-start.22) | collective-permute-done | bytes 786464 | tf_op jit(solution)/shard_map/ppermute | solution.py:34
  139.4 2.7 %collective-permute-start.24 = (bf16[2,128,1536]{2,1,0:T(8,128)(2,1)S(1)}, bf16[2,128,1536]{2,1,0:T(8,128)(2,1)S(1)}, u32[]{:S(2)}, u32[]{:S(2)}) collective-permute-start(bf16[2,128,1536]{2,1,0:T(8,128)(2,1)S(1)} %add_convert_fusion.2), channel_id=1, source_target_pairs={{0,12},{1,13},{2,14},{3,15},{4,0},{5,1},{6,2},{7,3},{8,4},{9,5},{1... | collective-permute-start | bytes 2359304 | tf_op jit(solution)/shard_map/ppermute | solution.py:34
  143.9 3.4 %collective-permute-done.21 = bf16[2,128,1536]{2,1,0:T(8,128)(2,1)S(1)} collective-permute-done((bf16[2,128,1536]{2,1,0:T(8,128)(2,1)S(1)}, bf16[2,128,1536]{2,1,0:T(8,128)(2,1)S(1)}, u32[]{:S(2)}, u32[]{:S(2)}) %collective-permute-start.21) | collective-permute-done | bytes 786464 | tf_op jit(solution)/shard_map/ppermute | solution.py:34
  147.3 8.4 %collective-permute-done.25 = bf16[2,128,1536]{2,1,0:T(8,128)(2,1)S(1)} collective-permute-done((bf16[2,128,1536]{2,1,0:T(8,128)(2,1)S(1)}, bf16[2,128,1536]{2,1,0:T(8,128)(2,1)S(1)}, u32[]{:S(2)}, u32[]{:S(2)}) %collective-permute-start.25) | collective-permute-done | bytes 786464 | tf_op jit(solution)/shard_map/ppermute | solution.py:34
  156.5 2.1 collective-permute-start.27
  159.3 8.3 %collective-permute-done.27 = bf16[128,1536]{1,0:T(8,128)(2,1)S(1)} collective-permute-done((bf16[128,1536]{1,0:T(8,128)(2,1)S(1)}, bf16[128,1536]{1,0:T(8,128)(2,1)S(1)}, u32[]{:S(2)}, u32[]{:S(2)}) %collective-permute-start.27) | collective-permute-done | bytes 393248 | tf_op jit(solution)/shard_map/ppermute | solution.py:34
  167.5 3.4 %collective-permute-done.26 = bf16[128,1536]{1,0:T(8,128)(2,1)S(1)} collective-permute-done((bf16[128,1536]{1,0:T(8,128)(2,1)S(1)}, bf16[128,1536]{1,0:T(8,128)(2,1)S(1)}, u32[]{:S(2)}, u32[]{:S(2)}) %collective-permute-start.26) | collective-permute-done | bytes 393248 | tf_op jit(solution)/shard_map/ppermute | solution.py:34
  171.8 15.3 %all_to_all.24 = bf16[8,3,192]{2,1,0:T(4,128)(2,1)S(1)} all-to-all(bf16[8,3,192]{2,1,0:T(4,128)(2,1)S(1)} %bitcast.211), channel_id=1, replica_groups=mesh['seq'=8,'grp'=16] {'seq'}, dimensions={0} | all-to-all | bytes 18432 | tf_op jit(solution)/shard_map/all_to_all | solution.py:411
  187.3 16.8 %all_to_all.25 = bf16[128,3,192]{2,1,0:T(4,128)(2,1)S(1)} all-to-all(bf16[128,3,192]{2,1,0:T(4,128)(2,1)S(1)} %broadcast_in_dim.208), channel_id=1, replica_groups=mesh['seq'=8,'grp'=16] {'seq','grp'}, dimensions={0} | all-to-all | bytes 294912 | tf_op jit(solution)/shard_map/all_to_all | solution.py:413
  205.3 13.6 %all_to_all.26 = f32[128,1,128]{2,1,0:T(1,128)S(1)} all-to-all(f32[128,1,128]{2,1,0:T(1,128)S(1)} %broadcast_in_dim.210), channel_id=1, replica_groups=mesh['seq'=8,'grp'=16] {'seq','grp'}, dimensions={0} | all-to-all | bytes 131072 | tf_op jit(solution)/shard_map/all_to_all | solution.py:420
  (188 shorter events, 32.8 us)
Async XLA Ops:
  5.0 27.2 %collective-permute-start.1 = (bf16[128,1536]{1,0:T(8,128)(2,1)S(1)}, bf16[128,1536]{1,0:T(8,128)(2,1)S(1)}, u32[]{:S(2)}, u32[]{:S(2)}) collective-permute-start(bf16[128,1536]{1,0:T(8,128)(2,1)S(1)} %bitcast.197), channel_id=1, source_target_pairs={{0,64},{16,80},{32,96},{48,112},{1,65},{17,81},{33,97},{49,113},{2... | collective-permute-start | bytes 1179656 | tf_op jit(solution)/shard_map/ppermute | solution.py:316
  10.5 21.7 %collective-permute-start = (bf16[128,1536]{1,0:T(8,128)(2,1)S(1)}, bf16[128,1536]{1,0:T(8,128)(2,1)S(1)}, u32[]{:S(2)}, u32[]{:S(2)}) collective-permute-start(bf16[128,1536]{1,0:T(8,128)(2,1)S(1)} %bitcast.198), channel_id=1, source_target_pairs={{0,32},{16,48},{32,64},{48,80},{64,96},{80,112},{1,33},{17,49},{33... | collective-permute-start | bytes 1179656 | tf_op jit(solution)/shard_map/ppermute | solution.py:315
  12.7 21.3 %all-to-all-start = ((bf16[16,16,1536]{2,1,0:T(8,128)(2,1)}), bf16[16,16,1536]{2,1,0:T(8,128)(2,1)S(1)}, u32[]{:S(2)}, u32[]{:S(2)}) async-start(bf16[16,16,1536]{2,1,0:T(8,128)(2,1)} %maximum_maximum_fusion), calls=%async_computation | async-start | bytes 1572864 | tf_op jit(solution)/shard_map/all_to_all | solution.py:314
  32.3 14.0 %collective-permute-start.3 = (bf16[128,1536]{1,0:T(8,128)(2,1)S(1)}, bf16[128,1536]{1,0:T(8,128)(2,1)}, u32[]{:S(2)}, u32[]{:S(2)}) collective-permute-start(bf16[128,1536]{1,0:T(8,128)(2,1)S(1)} %get-tuple-element.113), channel_id=1, source_target_pairs={{0,16},{16,0},{32,48},{48,32},{64,80},{80,64},{96,112},{112,96},{1... | collective-permute-start | bytes 1179656 | tf_op jit(solution)/shard_map/ppermute | solution.py:38
  33.9 12.4 %collective-permute-start.2 = (bf16[128,1536]{1,0:T(8,128)(2,1)S(1)}, bf16[128,1536]{1,0:T(8,128)(2,1)}, u32[]{:S(2)}, u32[]{:S(2)}) collective-permute-start(bf16[128,1536]{1,0:T(8,128)(2,1)S(1)} %get-tuple-element.114), channel_id=1, source_target_pairs={{0,16},{16,0},{32,48},{48,32},{64,80},{80,64},{96,112},{112,96},{1... | collective-permute-start | bytes 1179656 | tf_op jit(solution)/shard_map/ppermute | solution.py:38
  34.5 5.6 %collective-permute-start.6 = (bf16[48,1536]{1,0:T(8,128)(2,1)S(1)}, bf16[48,1536]{1,0:T(8,128)(2,1)S(1)}, u32[]{:S(2)}, u32[]{:S(2)}) collective-permute-start(bf16[48,1536]{1,0:T(8,128)(2,1)S(1)} %bitcast.206), channel_id=1, source_target_pairs={{0,64},{16,80},{32,96},{48,112},{64,0},{80,16},{96,32},{112,48},{1... | collective-permute-start | bytes 442376 | tf_op jit(solution)/shard_map/ppermute | solution.py:351
  34.6 5.5 %collective-permute-start.5 = (bf16[48,1536]{1,0:T(8,128)(2,1)S(1)}, bf16[48,1536]{1,0:T(8,128)(2,1)S(1)}, u32[]{:S(2)}, u32[]{:S(2)}) collective-permute-start(bf16[48,1536]{1,0:T(8,128)(2,1)S(1)} %bitcast.207), channel_id=1, source_target_pairs={{0,96},{16,112},{32,0},{48,16},{64,32},{80,48},{96,64},{112,80},{1... | collective-permute-start | bytes 442376 | tf_op jit(solution)/shard_map/ppermute | solution.py:351
  36.7 6.8 %collective-permute-start.4 = (bf16[48,1536]{1,0:T(8,128)(2,1)S(1)}, bf16[48,1536]{1,0:T(8,128)(2,1)S(1)}, u32[]{:S(2)}, u32[]{:S(2)}) collective-permute-start(bf16[48,1536]{1,0:T(8,128)(2,1)S(1)} %bitcast.208), channel_id=1, source_target_pairs={{0,32},{16,48},{32,64},{48,80},{64,96},{80,112},{96,0},{112,16},{1... | collective-permute-start | bytes 442376 | tf_op jit(solution)/shard_map/ppermute | solution.py:351
  43.5 3.2 %collective-permute-start.7 = (bf16[48,1536]{1,0:T(8,128)(2,1)S(1)}, bf16[48,1536]{1,0:T(8,128)(2,1)S(1)}, u32[]{:S(2)}, u32[]{:S(2)}) collective-permute-start(bf16[48,1536]{1,0:T(8,128)(2,1)S(1)} %bitcast.209), channel_id=1, source_target_pairs={{0,16},{16,0},{32,48},{48,32},{64,80},{80,64},{96,112},{112,96},{1... | collective-permute-start | bytes 442376 | tf_op jit(solution)/shard_map/ppermute | solution.py:38
  45.7 1.4 collective-permute-start.8
  45.7 1.6 collective-permute-start.9
  46.3 2.2 collective-permute-start.10
  70.1 8.7 %collective-permute-start.13 = (bf16[128,1536]{1,0:T(8,128)(2,1)}, bf16[128,1536]{1,0:T(8,128)(2,1)S(1)}, u32[]{:S(2)}, u32[]{:S(2)}) collective-permute-start(bf16[128,1536]{1,0:T(8,128)(2,1)} %get-tuple-element.66), channel_id=1, source_target_pairs={{0,2},{1,3},{2,0},{3,1},{4,6},{5,7},{6,4},{7,5},{8,10},{9,11},{10,... | collective-permute-start | bytes 1179656 | tf_op jit(solution)/shard_map/ppermute | solution.py:34
  73.1 10.2 %collective-permute-start.12 = (bf16[128,1536]{1,0:T(8,128)(2,1)}, bf16[128,1536]{1,0:T(8,128)(2,1)S(1)}, u32[]{:S(2)}, u32[]{:S(2)}) collective-permute-start(bf16[128,1536]{1,0:T(8,128)(2,1)} %get-tuple-element.66), channel_id=1, source_target_pairs={{0,3},{1,0},{2,1},{3,2},{4,7},{5,4},{6,5},{7,6},{8,11},{9,8},{10,9... | collective-permute-start | bytes 1179656 | tf_op jit(solution)/shard_map/ppermute | solution.py:34
  73.9 9.3 %collective-permute-start.11 = (bf16[128,1536]{1,0:T(8,128)(2,1)}, bf16[128,1536]{1,0:T(8,128)(2,1)S(1)}, u32[]{:S(2)}, u32[]{:S(2)}) collective-permute-start(bf16[128,1536]{1,0:T(8,128)(2,1)} %get-tuple-element.66), channel_id=1, source_target_pairs={{0,1},{1,2},{2,3},{3,0},{4,5},{5,6},{6,7},{7,4},{8,9},{9,10},{10,1... | collective-permute-start | bytes 1179656 | tf_op jit(solution)/shard_map/ppermute | solution.py:34
  83.3 16.3 %collective-permute-start.15 = (bf16[2,128,1536]{2,1,0:T(8,128)(2,1)S(1)}, bf16[2,128,1536]{2,1,0:T(8,128)(2,1)S(1)}, u32[]{:S(2)}, u32[]{:S(2)}) collective-permute-start(bf16[2,128,1536]{2,1,0:T(8,128)(2,1)S(1)} %pad_maximum_fusion.1), channel_id=1, source_target_pairs={{0,12},{1,13},{2,14},{3,15},{4,0},{5,1},{6,2},{7,3},{8,4},{9,5},{1... | collective-permute-start | bytes 2359304 | tf_op jit(solution)/shard_map/ppermute | solution.py:34
  85.9 13.8 %collective-permute-start.14 = (bf16[2,128,1536]{2,1,0:T(8,128)(2,1)S(1)}, bf16[2,128,1536]{2,1,0:T(8,128)(2,1)S(1)}, u32[]{:S(2)}, u32[]{:S(2)}) collective-permute-start(bf16[2,128,1536]{2,1,0:T(8,128)(2,1)S(1)} %pad_maximum_fusion), channel_id=1, source_target_pairs={{0,4},{1,5},{2,6},{3,7},{4,8},{5,9},{6,10},{7,11},{8,12},{9,13},{1... | collective-permute-start | bytes 2359304 | tf_op jit(solution)/shard_map/ppermute | solution.py:34
  86.0 20.7 %collective-permute-start.16 = (bf16[2,128,1536]{2,1,0:T(8,128)(2,1)S(1)}, bf16[2,128,1536]{2,1,0:T(8,128)(2,1)S(1)}, u32[]{:S(2)}, u32[]{:S(2)}) collective-permute-start(bf16[2,128,1536]{2,1,0:T(8,128)(2,1)S(1)} %pad_maximum_fusion.1), channel_id=1, source_target_pairs={{0,4},{1,5},{2,6},{3,7},{4,8},{5,9},{6,10},{7,11},{8,12},{9,13},{1... | collective-permute-start | bytes 2359304 | tf_op jit(solution)/shard_map/ppermute | solution.py:34
  86.3 20.4 %collective-permute-start.17 = (bf16[2,128,1536]{2,1,0:T(8,128)(2,1)S(1)}, bf16[2,128,1536]{2,1,0:T(8,128)(2,1)S(1)}, u32[]{:S(2)}, u32[]{:S(2)}) collective-permute-start(bf16[2,128,1536]{2,1,0:T(8,128)(2,1)S(1)} %pad_maximum_fusion), channel_id=1, source_target_pairs={{0,12},{1,13},{2,14},{3,15},{4,0},{5,1},{6,2},{7,3},{8,4},{9,5},{1... | collective-permute-start | bytes 2359304 | tf_op jit(solution)/shard_map/ppermute | solution.py:34
  106.7 12.3 %collective-permute-start.18 = (bf16[2,128,1536]{2,1,0:T(8,128)(2,1)S(1)}, bf16[2,128,1536]{2,1,0:T(8,128)(2,1)S(1)}, u32[]{:S(2)}, u32[]{:S(2)}) collective-permute-start(bf16[2,128,1536]{2,1,0:T(8,128)(2,1)S(1)} %collective-permute-done.14), channel_id=1, source_target_pairs={{0,4},{1,5},{2,6},{3,7},{4,8},{5,9},{6,10},{7,11},{8,12},{9,13},{1... | collective-permute-start | bytes 2359304 | tf_op jit(solution)/shard_map/ppermute | solution.py:34
  106.7 12.3 %collective-permute-start.19 = (bf16[2,128,1536]{2,1,0:T(8,128)(2,1)S(1)}, bf16[2,128,1536]{2,1,0:T(8,128)(2,1)S(1)}, u32[]{:S(2)}, u32[]{:S(2)}) collective-permute-start(bf16[2,128,1536]{2,1,0:T(8,128)(2,1)S(1)} %collective-permute-done.15), channel_id=1, source_target_pairs={{0,12},{1,13},{2,14},{3,15},{4,0},{5,1},{6,2},{7,3},{8,4},{9,5},{1... | collective-permute-start | bytes 2359304 | tf_op jit(solution)/shard_map/ppermute | solution.py:34
  123.6 11.9 %collective-permute-start.23 = (bf16[2,128,1536]{2,1,0:T(8,128)(2,1)S(1)}, bf16[2,128,1536]{2,1,0:T(8,128)(2,1)S(1)}, u32[]{:S(2)}, u32[]{:S(2)}) collective-permute-start(bf16[2,128,1536]{2,1,0:T(8,128)(2,1)S(1)} %bitcast.193), channel_id=1, source_target_pairs={{0,12},{1,13},{2,14},{3,15},{4,0},{5,1},{6,2},{7,3},{8,4},{9,5},{1... | collective-permute-start | bytes 2359304 | tf_op jit(solution)/shard_map/ppermute | solution.py:34
  126.6 12.3 %collective-permute-start.22 = (bf16[2,128,1536]{2,1,0:T(8,128)(2,1)S(1)}, bf16[2,128,1536]{2,1,0:T(8,128)(2,1)S(1)}, u32[]{:S(2)}, u32[]{:S(2)}) collective-permute-start(bf16[2,128,1536]{2,1,0:T(8,128)(2,1)S(1)} %bitcast.192), channel_id=1, source_target_pairs={{0,4},{1,5},{2,6},{3,7},{4,8},{5,9},{6,10},{7,11},{8,12},{9,13},{1... | collective-permute-start | bytes 2359304 | tf_op jit(solution)/shard_map/ppermute | solution.py:34
  126.6 17.4 %collective-permute-start.20 = (bf16[2,128,1536]{2,1,0:T(8,128)(2,1)S(1)}, bf16[2,128,1536]{2,1,0:T(8,128)(2,1)S(1)}, u32[]{:S(2)}, u32[]{:S(2)}) collective-permute-start(bf16[2,128,1536]{2,1,0:T(8,128)(2,1)S(1)} %bitcast.185), channel_id=1, source_target_pairs={{0,12},{1,13},{2,14},{3,15},{4,0},{5,1},{6,2},{7,3},{8,4},{9,5},{1... | collective-permute-start | bytes 2359304 | tf_op jit(solution)/shard_map/ppermute | solution.py:34
  129.3 18.1 %collective-permute-start.21 = (bf16[2,128,1536]{2,1,0:T(8,128)(2,1)S(1)}, bf16[2,128,1536]{2,1,0:T(8,128)(2,1)S(1)}, u32[]{:S(2)}, u32[]{:S(2)}) collective-permute-start(bf16[2,128,1536]{2,1,0:T(8,128)(2,1)S(1)} %bitcast.184), channel_id=1, source_target_pairs={{0,4},{1,5},{2,6},{3,7},{4,8},{5,9},{6,10},{7,11},{8,12},{9,13},{1... | collective-permute-start | bytes 2359304 | tf_op jit(solution)/shard_map/ppermute | solution.py:34
  139.1 16.7 %collective-permute-start.25 = (bf16[2,128,1536]{2,1,0:T(8,128)(2,1)S(1)}, bf16[2,128,1536]{2,1,0:T(8,128)(2,1)S(1)}, u32[]{:S(2)}, u32[]{:S(2)}) collective-permute-start(bf16[2,128,1536]{2,1,0:T(8,128)(2,1)S(1)} %add_convert_fusion.1), channel_id=1, source_target_pairs={{0,4},{1,5},{2,6},{3,7},{4,8},{5,9},{6,10},{7,11},{8,12},{9,13},{1... | collective-permute-start | bytes 2359304 | tf_op jit(solution)/shard_map/ppermute | solution.py:34
  139.4 16.4 %collective-permute-start.24 = (bf16[2,128,1536]{2,1,0:T(8,128)(2,1)S(1)}, bf16[2,128,1536]{2,1,0:T(8,128)(2,1)S(1)}, u32[]{:S(2)}, u32[]{:S(2)}) collective-permute-start(bf16[2,128,1536]{2,1,0:T(8,128)(2,1)S(1)} %add_convert_fusion.2), channel_id=1, source_target_pairs={{0,12},{1,13},{2,14},{3,15},{4,0},{5,1},{6,2},{7,3},{8,4},{9,5},{1... | collective-permute-start | bytes 2359304 | tf_op jit(solution)/shard_map/ppermute | solution.py:34
  156.5 11.1 %collective-permute-start.27 = (bf16[128,1536]{1,0:T(8,128)(2,1)S(1)}, bf16[128,1536]{1,0:T(8,128)(2,1)S(1)}, u32[]{:S(2)}, u32[]{:S(2)}) collective-permute-start(bf16[128,1536]{1,0:T(8,128)(2,1)S(1)} %fusion.6), channel_id=1, source_target_pairs={{0,3},{1,0},{2,1},{3,2},{4,7},{5,4},{6,5},{7,6},{8,11},{9,8},{10,9... | collective-permute-start | bytes 1179656 | tf_op jit(solution)/shard_map/ppermute | solution.py:34
  158.6 8.9 %collective-permute-start.28 = (bf16[128,1536]{1,0:T(8,128)(2,1)S(1)}, bf16[128,1536]{1,0:T(8,128)(2,1)S(1)}, u32[]{:S(2)}, u32[]{:S(2)}) collective-permute-start(bf16[128,1536]{1,0:T(8,128)(2,1)S(1)} %get-tuple-element.108), channel_id=1, source_target_pairs={{0,2},{1,3},{2,0},{3,1},{4,6},{5,7},{6,4},{7,5},{8,10},{9,11},{10,... | collective-permute-start | bytes 1179656 | tf_op jit(solution)/shard_map/ppermute | solution.py:34
  158.6 12.3 %collective-permute-start.26 = (bf16[128,1536]{1,0:T(8,128)(2,1)S(1)}, bf16[128,1536]{1,0:T(8,128)(2,1)S(1)}, u32[]{:S(2)}, u32[]{:S(2)}) collective-permute-start(bf16[128,1536]{1,0:T(8,128)(2,1)S(1)} %get-tuple-element.109), channel_id=1, source_target_pairs={{0,1},{1,2},{2,3},{3,0},{4,5},{5,6},{6,7},{7,4},{8,9},{9,10},{10,1... | collective-permute-start | bytes 1179656 | tf_op jit(solution)/shard_map/ppermute | solution.py:34
  171.2 33.7 %copy-start.5 = (bf16[128,1536]{1,0:T(8,128)(2,1)}, bf16[128,1536]{1,0:T(8,128)(2,1)S(1)}, u32[]{:S(2)}) copy-start(bf16[128,1536]{1,0:T(8,128)(2,1)S(1)} %fusion.5) | copy-start | bytes 1179652
  171.2 33.3 %copy-start.6 = (bf16[1536,384]{1,0:T(8,128)(2,1)S(1)}, bf16[1536,384]{1,0:T(8,128)(2,1)}, u32[]{:S(2)}) copy-start(bf16[1536,384]{1,0:T(8,128)(2,1)} %param.40) | copy-start | bytes 3538948
  (24 other events, 218.4 us)

commit v6 on v5

--- a/solution.py
+++ b/solution.py
@@ -85,10 +85,10 @@
         return jnp.where(keep, moved, 0.0).astype(BF)
 
     lane = lax.broadcasted_iota(jnp.int32, (count, 128), 1)
-    lower = (lane & 63) < 32
     down_rows = lax.broadcasted_iota(jnp.int32, (count, 1), 0)
 
     def rope(u, cos_t, sin_t):
+        lower = (lax.broadcasted_iota(jnp.int32, u.shape, 1) & 63) < 32
         turned = jnp.where(lower, pltpu.roll(u, 96, 1), pltpu.roll(u, 32, 1))
         return u * cos_t + turned * sin_t
 
@@ -96,8 +96,10 @@
     loads[1].wait()
 
     def key_block(b, carry):
-        at = pl.ds(pl.multiple_of(b * count, count), count)
-        docs = document(block_start(b) + down_rows)
+        size = 5 * count // 2
+        at = pl.ds(pl.multiple_of(b * size, 16), size)
+        row = b * size + lax.broadcasted_iota(jnp.int32, (size, 1), 0)
+        docs = document(block_start(row >> 7) + (row & 127))
         rows = xn[at, :]
         z = dot_t(rows, ad[...])
         keys = jnp.dot(rows, wk[...], preferred_element_type=F32) + jnp.dot(
@@ -112,7 +114,7 @@
                 keys[:, 128 * c:128 * c + 128], cos_t, sin_t).astype(BF)
         return carry
 
-    lax.fori_loop(0, 5, key_block, 0)
+    lax.fori_loop(0, 2, key_block, 0)
     own_index = me * count + down_rows
     docs = document(own_index)
     own = xn[0:count, :]
@@ -169,10 +171,17 @@
     loads[3].wait()
     attended = att[...]
     zo = low(dot_t(attended, ad[...]), 4, 10, docs)
-    mixed = (tok[0][...].astype(F32) + jnp.dot(attended, wo[...], preferred_element_type=F32)
-             + jnp.dot(zo, ad[...], preferred_element_type=F32)).astype(BF)
-    mixed_out[...] = mixed
-    moe_out[...] = norm(mixed.astype(F32), gain_moe[...])
+
+    def out_block(c, carry):
+        at = pl.ds(pl.multiple_of(c * 512, 512), 512)
+        mixed_out[:, at] = (
+            tok[0][:, at].astype(F32)
+            + jnp.dot(attended, wo[:, at], preferred_element_type=F32)
+            + jnp.dot(zo, ad[:, at], preferred_element_type=F32)).astype(BF)
+        return carry
+
+    lax.fori_loop(0, 3, out_block, 0)
+    moe_out[...] = norm(mixed_out[...].astype(F32), gain_moe[...])
 
 
 def attention(tok, adapt, place, gain, gain_moe, cosine, sine, wq, wk, wv, wo):
@@ -201,7 +210,7 @@
     )(*tok, *adapt, place, gain, gain_moe, cosine, sine, wq, wk, wv, wo)
 
 
-def expert_kernel(p0, p1, first, table, gate, up, down, out0, out1, xe, ho, scale):
+def expert_kernel(p0, p1, first, table, gate, up, down, out0, out1, last, xe, ho, scale):
     odd, part = first[0], first[1]
     row = lax.broadcasted_iota(jnp.int32, (256, 256), 0)
     col = lax.broadcasted_iota(jnp.int32, (256, 256), 1)
@@ -248,8 +257,14 @@
     ffn(2, 4 - 4 * odd, 1)
     for i, out in enumerate((out0, out1)):
         rows = jnp.concatenate([ho[e, i * 2 * CAP:(i + 1) * 2 * CAP, :] for e in range(3)])
-        out[...] = lax.dot_general(hots[i], rows, (((0,), (0,)), ((), ())),
-                                   preferred_element_type=F32).astype(BF)
+        total = lax.dot_general(hots[i], rows, (((0,), (0,)), ((), ())),
+                                preferred_element_type=F32).astype(BF)
+        out[...] = total
+        marks = table[part, i][3:6]
+        left = lax.broadcasted_iota(jnp.int32, marks.shape, 1) < 128
+        marks = jnp.concatenate([jnp.where(left, marks, 0.0), jnp.where(left, 0.0, marks),
+                                 jnp.zeros((2, 256), F32)]).astype(BF)
+        last[i] = jnp.dot(marks, total, preferred_element_type=F32).astype(BF)
 
 
 def experts(pieces, first, table, gate, up, down):
@@ -257,11 +272,11 @@
     shape = pieces[0].shape
     vm = pl.BlockSpec(memory_space=pltpu.VMEM)
     piece = jax.ShapeDtypeStruct((256, width), BF)
-    outs = pl.pallas_call(
+    first_out, second_out, last = pl.pallas_call(
         expert_kernel,
-        out_shape=(piece, piece),
+        out_shape=(piece, piece, jax.ShapeDtypeStruct((2, 8, width), BF)),
         in_specs=[vm, vm, pl.BlockSpec(memory_space=pltpu.SMEM), vm, vm, vm, vm],
-        out_specs=(vm, vm),
+        out_specs=(vm, vm, vm),
         scratch_shapes=[
             pltpu.VMEM((3, 4 * CAP, width), BF), pltpu.VMEM((3, 4 * CAP, width), BF),
             pltpu.VMEM((3, 4 * CAP, 1), F32),
@@ -272,7 +287,7 @@
         name="expert_block",
     )(*[rows.reshape(256, width) for rows in pieces], first, table, gate, up,
       down.reshape(5 * 256, width))
-    return [rows.reshape(shape) for rows in outs]
+    return first_out.reshape(shape), second_out.reshape(shape), last
 
 
 def rms_scaled(features, scales):
@@ -307,9 +322,13 @@
     thin = lax.dynamic_slice_in_dim(adapter_up_key_value[:, 0], 2 * me, 2, 1)
     thin = jnp.concatenate([thin[0], thin[1], jnp.zeros((2, width - 1024), BF)], axis=1)
     maps = jnp.concatenate([downs, ups, thin], axis=0)
+    ends = jnp.cumsum(lengths[0])
+    marks = (ends[:, None] - 1 == me * count + jnp.arange(count, dtype=jnp.int32)[None, :])
+    mark_row = jnp.concatenate([marks.reshape(1, 3 * count).astype(BF),
+                                jnp.zeros((1, width - 3 * count), BF)], axis=1)
     payload = jnp.concatenate(
         [jnp.broadcast_to(maps[None], (16, 14, width)), route_rows[:, None, :],
-         jnp.zeros((16, 1, width), BF)], axis=1)
+         jnp.broadcast_to(mark_row[None], (16, 1, width))], axis=1)
     payload, own = lax.optimization_barrier((payload, own))
     held = lax.all_to_all(payload, "grp", 0, 0, tiled=True)
     back1 = lax.ppermute(own, "seq", [(s, s + 2) for s in range(6)])
@@ -319,7 +338,6 @@
            partner(jnp.where(odd_core, back2, back1))]
 
     lens = lengths[0]
-    ends = jnp.cumsum(lens)
     starts = ends - lens
     blocks = me - jnp.array([0, 2, 4, 1, 3], jnp.int32)
     row = jnp.arange(count, dtype=jnp.int32)
@@ -357,9 +375,12 @@
     source = jnp.where(me % 2 == 0, second * 4 + first, first * 4 + second).reshape(8, 2)
     source = jnp.concatenate([source[:3], source[5:6], source[3:5], source[6:]]).reshape(16)
     order = (source[:, None] == jnp.arange(16, dtype=jnp.int32)[None, :]).astype(F32)
-    route_in = jnp.dot(order, held[:, 14, :].astype(F32), precision=lax.Precision.HIGHEST)
-    route_in = (route_in[:, :3 * count] + route_in[:, 3 * count:6 * count]).reshape(8, 2, 3, count)
-    route_in = jnp.concatenate([route_in, jnp.zeros((8, 2, 5, count), F32)], axis=2)
+    route_in = jnp.concatenate(
+        [held[:, 14, :3 * count].astype(F32) + held[:, 14, 3 * count:6 * count].astype(F32),
+         held[:, 15, :3 * count].astype(F32)], axis=1)
+    route_in = jnp.dot(order, route_in, precision=lax.Precision.HIGHEST)
+    route_in = route_in.reshape(8, 2, 6, count)
+    route_in = jnp.concatenate([route_in, jnp.zeros((8, 2, 2, count), F32)], axis=2)
     route_in = route_in.transpose(0, 2, 1, 3).reshape(4, 2, 8, 2 * count)
     odd = (grp % 2).astype(jnp.int32)
     weights = (gate_weight, up_weight, down_weight)
@@ -377,19 +398,19 @@
     own_lo, own_hi = jnp.stack([moe_in, line[0]]), jnp.stack([line[1], line[2]])
     minus_lo, plus_hi = shift(own_lo, 1, 1), shift(own_hi, 1, -1)
     minus_hi, plus_lo = shift(own_hi, 1, 1), shift(own_lo, 1, -1)
-    own_lo, own_hi = share([own_lo, own_hi], 0)
+    own_lo, own_hi, last_own = share([own_lo, own_hi], 0)
     minus_lo, plus_hi, own_lo, own_hi = lax.optimization_barrier(
         (minus_lo, plus_hi, own_lo, own_hi))
-    first_lo, first_hi = share([minus_lo, plus_hi], 1)
-    minus_lo, plus_hi, minus_hi, plus_lo, first_lo, first_hi = lax.optimization_barrier(
-        (minus_lo, plus_hi, minus_hi, plus_lo, first_lo, first_hi))
     far_lo, far_hi = shift(minus_lo, 1, 1), shift(plus_hi, 1, -1)
-    minus_hi, plus_lo = share([minus_hi, plus_lo], 2)
+    first_lo, first_hi, last_first = share([minus_lo, plus_hi], 1)
+    minus_hi, plus_lo, first_lo, first_hi = lax.optimization_barrier(
+        (minus_hi, plus_lo, first_lo, first_hi))
+    minus_hi, plus_lo, last_second = share([minus_hi, plus_lo], 2)
     minus_lo, plus_hi, minus_hi, plus_lo, far_lo, far_hi = lax.optimization_barrier(
         (first_lo, first_hi, minus_hi, plus_lo, far_lo, far_hi))
 
     minus_lo, plus_hi = shift(minus_lo, 1, -1), shift(plus_hi, 1, 1)
-    far_lo, far_hi = share([far_lo, far_hi], 3)
+    far_lo, far_hi, last_far = share([far_lo, far_hi], 3)
     far_lo, far_hi = lax.optimization_barrier((shift(far_lo, 1, 1), shift(far_hi, 1, -1)))
     plus_lo = shift((wide(plus_lo) + wide(far_lo)).astype(BF), 1, 1)
     minus_hi = shift((wide(minus_hi) + wide(far_hi)).astype(BF), 1, -1)
@@ -403,9 +424,13 @@
     combined = own_lo[0] + wide(line[0]) + wide(line[1]) + wide(line[2])
     hidden_out = (mixed.astype(F32) + combined).astype(BF)
 
-    selector = (ends[:, None] - 1 == row_index[None, :]).astype(BF)
-    last = jnp.dot(selector, hidden_out, preferred_element_type=F32)
-    last = rms_scaled(last, closing_gain)
+    last = jnp.stack([last_own, last_first, last_second, last_far])[:, :, :6]
+    last = jnp.einsum("jg,jr->gr", order.astype(BF), last.reshape(16, 3 * width),
+                      preferred_element_type=F32).astype(BF)
+    last = lax.all_to_all(last.reshape(16, 3, width), "grp", 0, 0, tiled=True)
+    last = jnp.sum(last.astype(F32), axis=0) + jnp.dot(
+        marks.astype(BF), mixed, preferred_element_type=F32)
+    last = rms_scaled(last.astype(BF), closing_gain)
     part = width // 8
     split = last.reshape(3, 8, part).transpose(1, 0, 2)
     mine = lax.all_to_all(split, "seq", 0, 0, tiled=True)

time: 221 us -> 207 us (0.937)
  blocking collectives: 45.7 us -> 14.7 us
  waiting for transfers between devices: 59.1 us -> 36.2 us
  starting transfers between devices: 45.7 us -> 64.2 us
  other arithmetic: 7.78 us -> 17.1 us
  local copies, waits for them, and re-layouts: 13.9 us -> 21.8 us
  matrix products: 1.14 us -> 4.62 us
    ppermute x18, waiting for transfers between devices: 51.3 us -> 18.8 us  [shift(): return lax.ppermute(rows, WHOLE, pairs)]
    all_to_all x2 -> x0, blocking collectives: 32.2 us -> none  [the longest x1 16.8 us: body(): lax.all_to_all(jnp.broadcast_to(mine[None], (128, 3, part)), WHOLE, 0, 0,...]
    all_to_all x0 -> x3, starting transfers between devices: none -> 19.4 us  [the longest x1 8.24 us: body(): mine = lax.all_to_all(split, 'seq', 0, 0, tiled=True)]
    all_to_all x0 -> x3, waiting for transfers between devices: none -> 11.7 us  [the longest x1 4.47 us: body(): last = lax.all_to_all(last.reshape(16, 3, width), 'grp', 0, 0, tiled=True)]
    unnamed x52 -> x70, local copies, waits for them, and re-layouts: 7.59 us -> 11.2 us
    ppermute x18, starting transfers between devices: 23.6 us -> 20.1 us  [shift(): return lax.ppermute(rows, WHOLE, pairs)]
  transfers between devices with their start and end apart: 30 -> 33, of which waited for: 17 -> 14; matrix products, arithmetic and copies ran while one was open for 3% -> 10% of each run, Pallas kernels for 6% -> 7%
where the time goes in v6:
time: 207 us; the launch traced here: 205 us
  starting transfers between devices  64.2 us (31%)
  Pallas kernels  39.3 us (19%)
  waiting for transfers between devices  36.2 us (17%)
  local copies, waits for them, and re-layouts  21.8 us (11%)
  other arithmetic  17.1 us (8%)
  blocking collectives  14.7 us (7%)
  between operations  6.95 us (3%)
  matrix products  4.62 us (2%)
    ppermute x18, starting transfers between devices, shift(): return lax.ppermute(rows, WHOLE, pairs)  20.1 us
    pallas_call x1, Pallas kernels, attention(): pl.pallas_call(attention_kernel, out_shape=(rows, rows), in_specs=[vm] *...  20.1 us
    pallas_call x4, Pallas kernels, experts(): pl.pallas_call(expert_kernel, out_shape=(piece, piece, jax.ShapeDtypeStru...  19.2 us
    ppermute x18, waiting for transfers between devices, shift(): return lax.ppermute(rows, WHOLE, pairs)  18.8 us
    all_to_all x1, blocking collectives, body(): lax.all_to_all(jnp.broadcast_to(stats[None], (128, 128)), WHOLE, 0, 0, ti...  14.7 us
    unnamed x70, local copies, waits for them, and re-layouts  11.2 us
    all_to_all x1, starting transfers between devices, body(): mine = lax.all_to_all(split, 'seq', 0, 0, tiled=True)  8.24 us
    all_to_all x1, starting transfers between devices, body(): held = lax.all_to_all(payload, 'grp', 0, 0, tiled=True)  7.78 us
  transfers between devices with their start and end apart: 33, of which 14 were waited for; matrix products, arithmetic and copies ran while one was open for 10% of the time, Pallas kernels for 7%

profile of v6, /device:TPU:1, one launch (start us, length us, event | category | flops | bytes accessed | tf_op | source)
XLA Modules:
  0.0 205.0 jit_solution(4193034364048332044)
XLA Ops:
  6.0 4.0 %collective-permute-start = (bf16[128,1536]{1,0:T(8,128)(2,1)S(1)}, bf16[128,1536]{1,0:T(8,128)(2,1)S(1)}, u32[]{:S(2)}, u32[]{:S(2)}) collective-permute-start(bf16[128,1536]{1,0:T(8,128)(2,1)S(1)} %bitcast.213), channel_id=1, source_target_pairs={{0,32},{16,48},{32,64},{48,80},{64,96},{80,112},{1,33},{17,49},{33... | collective-permute-start | bytes 1179656 | tf_op jit(solution)/shard_map/ppermute | solution.py:334
  10.0 4.4 %collective-permute-start.1 = (bf16[128,1536]{1,0:T(8,128)(2,1)S(1)}, bf16[128,1536]{1,0:T(8,128)(2,1)S(1)}, u32[]{:S(2)}, u32[]{:S(2)}) collective-permute-start(bf16[128,1536]{1,0:T(8,128)(2,1)S(1)} %bitcast.214), channel_id=1, source_target_pairs={{0,64},{16,80},{32,96},{48,112},{1,65},{17,81},{33,97},{49,113},{2... | collective-permute-start | bytes 1179656 | tf_op jit(solution)/shard_map/ppermute | solution.py:335
  14.4 7.8 %all-to-all-start = ((bf16[16,16,1536]{2,1,0:T(8,128)(2,1)}), bf16[16,16,1536]{2,1,0:T(8,128)(2,1)S(1)}, u32[]{:S(2)}, u32[]{:S(2)}) async-start(bf16[16,16,1536]{2,1,0:T(8,128)(2,1)} %pad_maximum_fusion), calls=%async_computation | async-start | bytes 1572864 | tf_op jit(solution)/shard_map/all_to_all | solution.py:333
  36.0 2.7 %collective-permute-start.5 = (bf16[48,1536]{1,0:T(8,128)(2,1)S(1)}, bf16[48,1536]{1,0:T(8,128)(2,1)S(1)}, u32[]{:S(2)}, u32[]{:S(2)}) collective-permute-start(bf16[48,1536]{1,0:T(8,128)(2,1)S(1)} %bitcast.223), channel_id=1, source_target_pairs={{0,96},{16,112},{32,0},{48,16},{64,32},{80,48},{96,64},{112,80},{1... | collective-permute-start | bytes 442376 | tf_op jit(solution)/shard_map/ppermute | solution.py:369
  42.5 1.8 collective-permute-done.6.refs_8_
  44.3 3.7 %collective-permute-start.10 = (bf16[48,1536]{1,0:T(8,128)(2,1)S(1)}, bf16[48,1536]{1,0:T(8,128)(2,1)S(1)}, u32[]{:S(2)}, u32[]{:S(2)}) collective-permute-start(bf16[48,1536]{1,0:T(8,128)(2,1)S(1)} %collective-permute-done.6.refs_8_), channel_id=1, source_target_pairs={{0,16},{16,0},{32,48},{48,32},{64,80},{80,64},{96,112},{112,96},{1... | collective-permute-start | bytes 442376 | tf_op jit(solution)/shard_map/ppermute | solution.py:38
  50.7 20.1 %attention_block.1 = (bf16[128,1536]{1,0:T(8,128)(2,1)}, bf16[128,1536]{1,0:T(8,128)(2,1)}) custom-call(bf16[128,1536]{1,0:T(8,128)(2,1)} %bitcast.212, bf16[128,1536]{1,0:T(8,128)(2,1)} %copy-done.12, bf16[128,1536]{1,0:T(8,128)(2,1)} %copy-done.13, bf16[128,1536]{1,0:T(8,128)(2,1)} %copy-done.25, bf16[128,1536]{1,0:T(8,128)(2,1)} %collective-permute-done.3.refs_4_, ...), custom_call_target="tpu_custom_call" | custom-call | flops 8589934592 | bytes 20971520 | tf_op jit(solution)/shard_map/attention_block/pallas_call | solution.py:192
  71.2 2.3 %collective-permute-start.12 = (bf16[128,1536]{1,0:T(8,128)(2,1)}, bf16[128,1536]{1,0:T(8,128)(2,1)S(1)}, u32[]{:S(2)}, u32[]{:S(2)}) collective-permute-start(bf16[128,1536]{1,0:T(8,128)(2,1)} %get-tuple-element.68), channel_id=1, source_target_pairs={{0,3},{1,0},{2,1},{3,2},{4,7},{5,4},{6,5},{7,6},{8,11},{9,8},{10,9... | collective-permute-start | bytes 1179656 | tf_op jit(solution)/shard_map/ppermute | solution.py:34
  74.2 4.9 %collective-permute-done.11 = bf16[128,1536]{1,0:T(8,128)(2,1)S(1)} collective-permute-done((bf16[128,1536]{1,0:T(8,128)(2,1)}, bf16[128,1536]{1,0:T(8,128)(2,1)S(1)}, u32[]{:S(2)}, u32[]{:S(2)}) %collective-permute-start.11) | collective-permute-done | bytes 393248 | tf_op jit(solution)/shard_map/ppermute | solution.py:34
  79.2 3.6 %collective-permute-done.12 = bf16[128,1536]{1,0:T(8,128)(2,1)S(1)} collective-permute-done((bf16[128,1536]{1,0:T(8,128)(2,1)}, bf16[128,1536]{1,0:T(8,128)(2,1)S(1)}, u32[]{:S(2)}, u32[]{:S(2)}) %collective-permute-start.12) | collective-permute-done | bytes 393248 | tf_op jit(solution)/shard_map/ppermute | solution.py:34
  85.6 1.9 collective-permute-start.15
  89.0 2.1 %copy-done.2 = bf16[5,1536,256]{2,1,0:T(8,128)(2,1)S(1)} copy-done((bf16[5,1536,256]{2,1,0:T(8,128)(2,1)S(1)}, bf16[5,1536,256]{2,1,0:T(8,128)(2,1)}, u32[]{:S(2)}) %copy-start.2) | copy-done | bytes 3932184
  91.1 2.1 %copy-done.4 = bf16[5,1536,256]{2,1,0:T(8,128)(2,1)S(1)} copy-done((bf16[5,1536,256]{2,1,0:T(8,128)(2,1)S(1)}, bf16[5,1536,256]{2,1,0:T(8,128)(2,1)}, u32[]{:S(2)}) %copy-start.4) | copy-done | bytes 3932184
  93.2 2.1 %copy-done.5 = bf16[5,256,1536]{2,1,0:T(8,128)(2,1)S(1)} copy-done((bf16[5,256,1536]{2,1,0:T(8,128)(2,1)S(1)}, bf16[5,256,1536]{2,1,0:T(8,128)(2,1)}, u32[]{:S(2)}) %copy-start.5) | copy-done | bytes 3932184
  95.4 4.8 %expert_block.4 = (bf16[256,1536]{1,0:T(8,128)(2,1)S(1)}, bf16[256,1536]{1,0:T(8,128)(2,1)S(1)}, bf16[2,8,1536]{2,1,0:T(8,128)(2,1)S(1)}) custom-call(bf16[256,1536]{1,0:T(8,128)(2,1)S(1)} %bitcast.183, bf16[256,1536]{1,0:T(8,128)(2,1)S(1)} %bitcast.184, s32[2]{0:T(128)S(1)} %get-tuple-element.148.first, f32[4,2,8,256]{3,2,1,0:T(8,128)S(1)} %bitcast.189, ...), custom_call_target="tpu_custom_call" | custom-call | flops 7516192768 | bytes 12582912 | tf_op jit(solution)/shard_map/expert_block/pallas_call | solution.py:275
  100.3 2.7 %collective-permute-start.19 = (bf16[2,128,1536]{2,1,0:T(8,128)(2,1)S(1)}, bf16[2,128,1536]{2,1,0:T(8,128)(2,1)S(1)}, u32[]{:S(2)}, u32[]{:S(2)}) collective-permute-start(bf16[2,128,1536]{2,1,0:T(8,128)(2,1)S(1)} %collective-permute-done.15), channel_id=1, source_target_pairs={{0,12},{1,13},{2,14},{3,15},{4,0},{5,1},{6,2},{7,3},{8,4},{9,5},{1... | collective-permute-start | bytes 2359304 | tf_op jit(solution)/shard_map/ppermute | solution.py:34
  102.9 4.8 %expert_block.5 = (bf16[256,1536]{1,0:T(8,128)(2,1)S(1)}, bf16[256,1536]{1,0:T(8,128)(2,1)S(1)}, bf16[2,8,1536]{2,1,0:T(8,128)(2,1)S(1)}) custom-call(bf16[256,1536]{1,0:T(8,128)(2,1)S(1)} %bitcast.205, bf16[256,1536]{1,0:T(8,128)(2,1)S(1)} %bitcast.206, s32[2]{0:T(128)S(1)} %get-tuple-element.149.first, f32[4,2,8,256]{3,2,1,0:T(8,128)S(1)} %bitcast.190, ...), custom_call_target="tpu_custom_call" | custom-call | flops 7516192768 | bytes 12582912 | tf_op jit(solution)/shard_map/expert_block/pallas_call | solution.py:275
  109.5 4.8 %expert_block.6 = (bf16[256,1536]{1,0:T(8,128)(2,1)S(1)}, bf16[256,1536]{1,0:T(8,128)(2,1)S(1)}, bf16[2,8,1536]{2,1,0:T(8,128)(2,1)S(1)}) custom-call(bf16[256,1536]{1,0:T(8,128)(2,1)S(1)} %bitcast.209, bf16[256,1536]{1,0:T(8,128)(2,1)S(1)} %bitcast.207, s32[2]{0:T(128)S(1)} %get-tuple-element.150.first, f32[4,2,8,256]{3,2,1,0:T(8,128)S(1)} %bitcast.191, ...), custom_call_target="tpu_custom_call" | custom-call | flops 7516192768 | bytes 12582912 | tf_op jit(solution)/shard_map/expert_block/pallas_call | solution.py:275
  114.4 4.8 %expert_block.7 = (bf16[256,1536]{1,0:T(8,128)(2,1)S(1)}, bf16[256,1536]{1,0:T(8,128)(2,1)S(1)}, bf16[2,8,1536]{2,1,0:T(8,128)(2,1)S(1)}) custom-call(bf16[256,1536]{1,0:T(8,128)(2,1)S(1)} %bitcast.208, bf16[256,1536]{1,0:T(8,128)(2,1)S(1)} %bitcast.210, s32[2]{0:T(128)S(1)} %get-tuple-element.151.first, f32[4,2,8,256]{3,2,1,0:T(8,128)S(1)} %bitcast.192, ...), custom_call_target="tpu_custom_call" | custom-call | flops 7516192768 | bytes 12582912 | tf_op jit(solution)/shard_map/expert_block/pallas_call | solution.py:275
  123.8 6.0 %all-to-all-start.1 = ((bf16[16,3,1536]{2,1,0:T(4,128)(2,1)}), bf16[16,3,1536]{2,1,0:T(4,128)(2,1)S(1)}, u32[]{:S(2)}, u32[]{:S(2)}) async-start(bf16[16,3,1536]{2,1,0:T(4,128)(2,1)} %reshape.478), calls=%async_computation.1 | async-start | bytes 393216 | tf_op jit(solution)/shard_map/all_to_all | solution.py:430
  132.5 4.5 %all-to-all-done.1 = bf16[16,3,1536]{2,1,0:T(4,128)(2,1)S(1)} async-done(((bf16[16,3,1536]{2,1,0:T(4,128)(2,1)}), bf16[16,3,1536]{2,1,0:T(4,128)(2,1)S(1)}, u32[]{:S(2)}, u32[]{:S(2)}) %all-to-all-start.1) | async-done | bytes 147488 | tf_op jit(solution)/shard_map/all_to_all | solution.py:430
  139.2 8.2 %all-to-all-start.2 = ((bf16[8,3,192]{2,1,0:T(4,128)(2,1)}), bf16[8,3,192]{2,1,0:T(4,128)(2,1)S(1)}, u32[]{:S(2)}, u32[]{:S(2)}) async-start(bf16[8,3,192]{2,1,0:T(4,128)(2,1)} %bitcast.180), calls=%async_computation.2 | async-start | bytes 32768 | tf_op jit(solution)/shard_map/all_to_all | solution.py:436
  148.9 3.2 %all-to-all-done.2 = bf16[8,3,192]{2,1,0:T(4,128)(2,1)S(1)} async-done(((bf16[8,3,192]{2,1,0:T(4,128)(2,1)}), bf16[8,3,192]{2,1,0:T(4,128)(2,1)S(1)}, u32[]{:S(2)}, u32[]{:S(2)}) %all-to-all-start.2) | async-done | bytes 9248 | tf_op jit(solution)/shard_map/all_to_all | solution.py:436
  152.9 5.1 %all-to-all-start.3 = ((bf16[128,3,192]{2,1,0:T(4,128)(2,1)}), bf16[128,3,192]{2,1,0:T(4,128)(2,1)}, u32[]{:S(2)}, u32[]{:S(2)}) async-start(bf16[128,3,192]{2,1,0:T(4,128)(2,1)} %broadcast_in_dim.218), calls=%async_computation.3 | async-start | bytes 524288 | tf_op jit(solution)/shard_map/all_to_all | solution.py:438
  158.1 2.2 %add_convert_fusion.1 = bf16[2,128,1536]{2,1,0:T(8,128)(2,1)} fusion(bf16[2,128,1536]{2,1,0:T(8,128)(2,1)} %collective-permute-done.22, bf16[2,128,1536]{2,1,0:T(8,128)(2,1)S(1)} %bitcast.187), kind=kLoop, calls=%fused_computation.8 | loop fusion | flops 1572864 | bytes 2359296 | tf_op jit(solution)/shard_map/convert_element_type | solution.py:415
  161.8 2.2 %add_convert_fusion.2 = bf16[2,128,1536]{2,1,0:T(8,128)(2,1)} fusion(bf16[2,128,1536]{2,1,0:T(8,128)(2,1)} %collective-permute-done.23, bf16[2,128,1536]{2,1,0:T(8,128)(2,1)S(1)} %bitcast.186), kind=kLoop, calls=%fused_computation.9 | loop fusion | flops 1572864 | bytes 2359296 | tf_op jit(solution)/shard_map/convert_element_type | solution.py:416
  165.3 4.0 %all-to-all-done.3 = bf16[128,3,192]{2,1,0:T(4,128)(2,1)} async-done(((bf16[128,3,192]{2,1,0:T(4,128)(2,1)}), bf16[128,3,192]{2,1,0:T(4,128)(2,1)}, u32[]{:S(2)}, u32[]{:S(2)}) %all-to-all-start.3) | async-done | bytes 147488 | tf_op jit(solution)/shard_map/all_to_all | solution.py:438
  170.7 1.7 fusion.43
  172.7 14.7 %all_to_all.29 = f32[128,1,128]{2,1,0:T(1,128)S(1)} all-to-all(f32[128,1,128]{2,1,0:T(1,128)S(1)} %broadcast_in_dim.220), channel_id=1, replica_groups=mesh['seq'=8,'grp'=16] {'seq','grp'}, dimensions={0} | all-to-all | bytes 131072 | tf_op jit(solution)/shard_map/all_to_all | solution.py:445
  187.9 1.6 convert_add_fusion
  194.4 2.2 %collective-permute-done.27 = bf16[128,1536]{1,0:T(8,128)(2,1)S(1)} collective-permute-done((bf16[128,1536]{1,0:T(8,128)(2,1)S(1)}, bf16[128,1536]{1,0:T(8,128)(2,1)S(1)}, u32[]{:S(2)}, u32[]{:S(2)}) %collective-permute-start.27) | collective-permute-done | bytes 393248 | tf_op jit(solution)/shard_map/ppermute | solution.py:34
  196.6 7.4 %collective-permute-done.26 = bf16[128,1536]{1,0:T(8,128)(2,1)S(1)} collective-permute-done((bf16[128,1536]{1,0:T(8,128)(2,1)S(1)}, bf16[128,1536]{1,0:T(8,128)(2,1)S(1)}, u32[]{:S(2)}, u32[]{:S(2)}) %collective-permute-start.26) | collective-permute-done | bytes 393248 | tf_op jit(solution)/shard_map/ppermute | solution.py:34
  (218 shorter events, 49.6 us)
Async XLA Ops:
  6.0 27.6 %collective-permute-start = (bf16[128,1536]{1,0:T(8,128)(2,1)S(1)}, bf16[128,1536]{1,0:T(8,128)(2,1)S(1)}, u32[]{:S(2)}, u32[]{:S(2)}) collective-permute-start(bf16[128,1536]{1,0:T(8,128)(2,1)S(1)} %bitcast.213), channel_id=1, source_target_pairs={{0,32},{16,48},{32,64},{48,80},{64,96},{80,112},{1,33},{17,49},{33... | collective-permute-start | bytes 1179656 | tf_op jit(solution)/shard_map/ppermute | solution.py:334
  10.0 23.6 %collective-permute-start.1 = (bf16[128,1536]{1,0:T(8,128)(2,1)S(1)}, bf16[128,1536]{1,0:T(8,128)(2,1)S(1)}, u32[]{:S(2)}, u32[]{:S(2)}) collective-permute-start(bf16[128,1536]{1,0:T(8,128)(2,1)S(1)} %bitcast.214), channel_id=1, source_target_pairs={{0,64},{16,80},{32,96},{48,112},{1,65},{17,81},{33,97},{49,113},{2... | collective-permute-start | bytes 1179656 | tf_op jit(solution)/shard_map/ppermute | solution.py:335
  14.4 21.0 %all-to-all-start = ((bf16[16,16,1536]{2,1,0:T(8,128)(2,1)}), bf16[16,16,1536]{2,1,0:T(8,128)(2,1)S(1)}, u32[]{:S(2)}, u32[]{:S(2)}) async-start(bf16[16,16,1536]{2,1,0:T(8,128)(2,1)} %pad_maximum_fusion), calls=%async_computation | async-start | bytes 1572864 | tf_op jit(solution)/shard_map/all_to_all | solution.py:333
  33.7 14.8 %collective-permute-start.2 = (bf16[128,1536]{1,0:T(8,128)(2,1)S(1)}, bf16[128,1536]{1,0:T(8,128)(2,1)S(1)}, u32[]{:S(2)}, u32[]{:S(2)}) collective-permute-start(bf16[128,1536]{1,0:T(8,128)(2,1)S(1)} %get-tuple-element.118), channel_id=1, source_target_pairs={{0,16},{16,0},{32,48},{48,32},{64,80},{80,64},{96,112},{112,96},{1... | collective-permute-start | bytes 1179656 | tf_op jit(solution)/shard_map/ppermute | solution.py:38
  35.3 13.3 %collective-permute-start.3 = (bf16[128,1536]{1,0:T(8,128)(2,1)S(1)}, bf16[128,1536]{1,0:T(8,128)(2,1)}, u32[]{:S(2)}, u32[]{:S(2)}) collective-permute-start(bf16[128,1536]{1,0:T(8,128)(2,1)S(1)} %get-tuple-element.117), channel_id=1, source_target_pairs={{0,16},{16,0},{32,48},{48,32},{64,80},{80,64},{96,112},{112,96},{1... | collective-permute-start | bytes 1179656 | tf_op jit(solution)/shard_map/ppermute | solution.py:38
  35.9 5.3 %collective-permute-start.4 = (bf16[48,1536]{1,0:T(8,128)(2,1)S(1)}, bf16[48,1536]{1,0:T(8,128)(2,1)S(1)}, u32[]{:S(2)}, u32[]{:S(2)}) collective-permute-start(bf16[48,1536]{1,0:T(8,128)(2,1)S(1)} %bitcast.222), channel_id=1, source_target_pairs={{0,32},{16,48},{32,64},{48,80},{64,96},{80,112},{96,0},{112,16},{1... | collective-permute-start | bytes 442376 | tf_op jit(solution)/shard_map/ppermute | solution.py:369
  36.0 6.4 %collective-permute-start.5 = (bf16[48,1536]{1,0:T(8,128)(2,1)S(1)}, bf16[48,1536]{1,0:T(8,128)(2,1)S(1)}, u32[]{:S(2)}, u32[]{:S(2)}) collective-permute-start(bf16[48,1536]{1,0:T(8,128)(2,1)S(1)} %bitcast.223), channel_id=1, source_target_pairs={{0,96},{16,112},{32,0},{48,16},{64,32},{80,48},{96,64},{112,80},{1... | collective-permute-start | bytes 442376 | tf_op jit(solution)/shard_map/ppermute | solution.py:369
  38.7 5.6 %collective-permute-start.6 = (bf16[48,1536]{1,0:T(8,128)(2,1)S(1)}, bf16[48,1536]{1,0:T(8,128)(2,1)S(1)}, u32[]{:S(2)}, u32[]{:S(2)}) collective-permute-start(bf16[48,1536]{1,0:T(8,128)(2,1)S(1)} %bitcast.224), channel_id=1, source_target_pairs={{0,64},{16,80},{32,96},{48,112},{64,0},{80,16},{96,32},{112,48},{1... | collective-permute-start | bytes 442376 | tf_op jit(solution)/shard_map/ppermute | solution.py:369
  44.3 4.7 %collective-permute-start.10 = (bf16[48,1536]{1,0:T(8,128)(2,1)S(1)}, bf16[48,1536]{1,0:T(8,128)(2,1)S(1)}, u32[]{:S(2)}, u32[]{:S(2)}) collective-permute-start(bf16[48,1536]{1,0:T(8,128)(2,1)S(1)} %collective-permute-done.6.refs_8_), channel_id=1, source_target_pairs={{0,16},{16,0},{32,48},{48,32},{64,80},{80,64},{96,112},{112,96},{1... | collective-permute-start | bytes 442376 | tf_op jit(solution)/shard_map/ppermute | solution.py:38
  48.0 1.6 collective-permute-start.8
  48.5 2.2 %collective-permute-start.9 = (bf16[48,1536]{1,0:T(8,128)(2,1)S(1)}, bf16[48,1536]{1,0:T(8,128)(2,1)}, u32[]{:S(2)}, u32[]{:S(2)}) collective-permute-start(bf16[48,1536]{1,0:T(8,128)(2,1)S(1)} %collective-permute-done.5.refs_7_), channel_id=1, source_target_pairs={{0,16},{16,0},{32,48},{48,32},{64,80},{80,64},{96,112},{112,96},{1... | collective-permute-start | bytes 442376 | tf_op jit(solution)/shard_map/ppermute | solution.py:38
  70.8 8.4 %collective-permute-start.11 = (bf16[128,1536]{1,0:T(8,128)(2,1)}, bf16[128,1536]{1,0:T(8,128)(2,1)S(1)}, u32[]{:S(2)}, u32[]{:S(2)}) collective-permute-start(bf16[128,1536]{1,0:T(8,128)(2,1)} %get-tuple-element.68), channel_id=1, source_target_pairs={{0,1},{1,2},{2,3},{3,0},{4,5},{5,6},{6,7},{7,4},{8,9},{9,10},{10,1... | collective-permute-start | bytes 1179656 | tf_op jit(solution)/shard_map/ppermute | solution.py:34
  71.2 11.6 %collective-permute-start.12 = (bf16[128,1536]{1,0:T(8,128)(2,1)}, bf16[128,1536]{1,0:T(8,128)(2,1)S(1)}, u32[]{:S(2)}, u32[]{:S(2)}) collective-permute-start(bf16[128,1536]{1,0:T(8,128)(2,1)} %get-tuple-element.68), channel_id=1, source_target_pairs={{0,3},{1,0},{2,1},{3,2},{4,7},{5,4},{6,5},{7,6},{8,11},{9,8},{10,9... | collective-permute-start | bytes 1179656 | tf_op jit(solution)/shard_map/ppermute | solution.py:34
  73.5 10.0 %collective-permute-start.13 = (bf16[128,1536]{1,0:T(8,128)(2,1)}, bf16[128,1536]{1,0:T(8,128)(2,1)S(1)}, u32[]{:S(2)}, u32[]{:S(2)}) collective-permute-start(bf16[128,1536]{1,0:T(8,128)(2,1)} %get-tuple-element.68), channel_id=1, source_target_pairs={{0,2},{1,3},{2,0},{3,1},{4,6},{5,7},{6,4},{7,5},{8,10},{9,11},{10,... | collective-permute-start | bytes 1179656 | tf_op jit(solution)/shard_map/ppermute | solution.py:34
  84.6 15.6 %collective-permute-start.14 = (bf16[2,128,1536]{2,1,0:T(8,128)(2,1)S(1)}, bf16[2,128,1536]{2,1,0:T(8,128)(2,1)S(1)}, u32[]{:S(2)}, u32[]{:S(2)}) collective-permute-start(bf16[2,128,1536]{2,1,0:T(8,128)(2,1)S(1)} %pad_maximum_fusion.1), channel_id=1, source_target_pairs={{0,4},{1,5},{2,6},{3,7},{4,8},{5,9},{6,10},{7,11},{8,12},{9,13},{1... | collective-permute-start | bytes 2359304 | tf_op jit(solution)/shard_map/ppermute | solution.py:34
  85.6 14.6 %collective-permute-start.15 = (bf16[2,128,1536]{2,1,0:T(8,128)(2,1)S(1)}, bf16[2,128,1536]{2,1,0:T(8,128)(2,1)S(1)}, u32[]{:S(2)}, u32[]{:S(2)}) collective-permute-start(bf16[2,128,1536]{2,1,0:T(8,128)(2,1)S(1)} %pad_maximum_fusion.2), channel_id=1, source_target_pairs={{0,12},{1,13},{2,14},{3,15},{4,0},{5,1},{6,2},{7,3},{8,4},{9,5},{1... | collective-permute-start | bytes 2359304 | tf_op jit(solution)/shard_map/ppermute | solution.py:34
  87.5 22.0 %collective-permute-start.17 = (bf16[2,128,1536]{2,1,0:T(8,128)(2,1)S(1)}, bf16[2,128,1536]{2,1,0:T(8,128)(2,1)S(1)}, u32[]{:S(2)}, u32[]{:S(2)}) collective-permute-start(bf16[2,128,1536]{2,1,0:T(8,128)(2,1)S(1)} %pad_maximum_fusion.1), channel_id=1, source_target_pairs={{0,12},{1,13},{2,14},{3,15},{4,0},{5,1},{6,2},{7,3},{8,4},{9,5},{1... | collective-permute-start | bytes 2359304 | tf_op jit(solution)/shard_map/ppermute | solution.py:34
  88.7 20.8 %collective-permute-start.16 = (bf16[2,128,1536]{2,1,0:T(8,128)(2,1)S(1)}, bf16[2,128,1536]{2,1,0:T(8,128)(2,1)S(1)}, u32[]{:S(2)}, u32[]{:S(2)}) collective-permute-start(bf16[2,128,1536]{2,1,0:T(8,128)(2,1)S(1)} %pad_maximum_fusion.2), channel_id=1, source_target_pairs={{0,4},{1,5},{2,6},{3,7},{4,8},{5,9},{6,10},{7,11},{8,12},{9,13},{1... | collective-permute-start | bytes 2359304 | tf_op jit(solution)/shard_map/ppermute | solution.py:34
  100.2 14.2 %collective-permute-start.18 = (bf16[2,128,1536]{2,1,0:T(8,128)(2,1)S(1)}, bf16[2,128,1536]{2,1,0:T(8,128)(2,1)S(1)}, u32[]{:S(2)}, u32[]{:S(2)}) collective-permute-start(bf16[2,128,1536]{2,1,0:T(8,128)(2,1)S(1)} %collective-permute-done.14), channel_id=1, source_target_pairs={{0,4},{1,5},{2,6},{3,7},{4,8},{5,9},{6,10},{7,11},{8,12},{9,13},{1... | collective-permute-start | bytes 2359304 | tf_op jit(solution)/shard_map/ppermute | solution.py:34
  100.3 14.1 %collective-permute-start.19 = (bf16[2,128,1536]{2,1,0:T(8,128)(2,1)S(1)}, bf16[2,128,1536]{2,1,0:T(8,128)(2,1)S(1)}, u32[]{:S(2)}, u32[]{:S(2)}) collective-permute-start(bf16[2,128,1536]{2,1,0:T(8,128)(2,1)S(1)} %collective-permute-done.15), channel_id=1, source_target_pairs={{0,12},{1,13},{2,14},{3,15},{4,0},{5,1},{6,2},{7,3},{8,4},{9,5},{1... | collective-permute-start | bytes 2359304 | tf_op jit(solution)/shard_map/ppermute | solution.py:34
  123.8 13.2 %all-to-all-start.1 = ((bf16[16,3,1536]{2,1,0:T(4,128)(2,1)}), bf16[16,3,1536]{2,1,0:T(4,128)(2,1)S(1)}, u32[]{:S(2)}, u32[]{:S(2)}) async-start(bf16[16,3,1536]{2,1,0:T(4,128)(2,1)} %reshape.478), calls=%async_computation.1 | async-start | bytes 393216 | tf_op jit(solution)/shard_map/all_to_all | solution.py:430
  129.8 28.3 %collective-permute-start.22 = (bf16[2,128,1536]{2,1,0:T(8,128)(2,1)}, bf16[2,128,1536]{2,1,0:T(8,128)(2,1)}, u32[]{:S(2)}, u32[]{:S(2)}) collective-permute-start(bf16[2,128,1536]{2,1,0:T(8,128)(2,1)} %bitcast.204), channel_id=1, source_target_pairs={{0,4},{1,5},{2,6},{3,7},{4,8},{5,9},{6,10},{7,11},{8,12},{9,13},{1... | collective-permute-start | bytes 2359304 | tf_op jit(solution)/shard_map/ppermute | solution.py:34
  131.1 27.0 %collective-permute-start.23 = (bf16[2,128,1536]{2,1,0:T(8,128)(2,1)}, bf16[2,128,1536]{2,1,0:T(8,128)(2,1)}, u32[]{:S(2)}, u32[]{:S(2)}) collective-permute-start(bf16[2,128,1536]{2,1,0:T(8,128)(2,1)} %bitcast.203), channel_id=1, source_target_pairs={{0,12},{1,13},{2,14},{3,15},{4,0},{5,1},{6,2},{7,3},{8,4},{9,5},{1... | collective-permute-start | bytes 2359304 | tf_op jit(solution)/shard_map/ppermute | solution.py:34
  139.2 12.9 %all-to-all-start.2 = ((bf16[8,3,192]{2,1,0:T(4,128)(2,1)}), bf16[8,3,192]{2,1,0:T(4,128)(2,1)S(1)}, u32[]{:S(2)}, u32[]{:S(2)}) async-start(bf16[8,3,192]{2,1,0:T(4,128)(2,1)} %bitcast.180), calls=%async_computation.2 | async-start | bytes 32768 | tf_op jit(solution)/shard_map/all_to_all | solution.py:436
  147.5 40.4 %collective-permute-start.20 = (bf16[2,128,1536]{2,1,0:T(8,128)(2,1)}, bf16[2,128,1536]{2,1,0:T(8,128)(2,1)}, u32[]{:S(2)}, u32[]{:S(2)}) collective-permute-start(bf16[2,128,1536]{2,1,0:T(8,128)(2,1)} %bitcast.202), channel_id=1, source_target_pairs={{0,12},{1,13},{2,14},{3,15},{4,0},{5,1},{6,2},{7,3},{8,4},{9,5},{1... | collective-permute-start | bytes 2359304 | tf_op jit(solution)/shard_map/ppermute | solution.py:34
  147.5 40.3 %collective-permute-start.21 = (bf16[2,128,1536]{2,1,0:T(8,128)(2,1)}, bf16[2,128,1536]{2,1,0:T(8,128)(2,1)}, u32[]{:S(2)}, u32[]{:S(2)}) collective-permute-start(bf16[2,128,1536]{2,1,0:T(8,128)(2,1)} %bitcast.201), channel_id=1, source_target_pairs={{0,4},{1,5},{2,6},{3,7},{4,8},{5,9},{6,10},{7,11},{8,12},{9,13},{1... | collective-permute-start | bytes 2359304 | tf_op jit(solution)/shard_map/ppermute | solution.py:34
  152.9 16.4 %all-to-all-start.3 = ((bf16[128,3,192]{2,1,0:T(4,128)(2,1)}), bf16[128,3,192]{2,1,0:T(4,128)(2,1)}, u32[]{:S(2)}, u32[]{:S(2)}) async-start(bf16[128,3,192]{2,1,0:T(4,128)(2,1)} %broadcast_in_dim.218), calls=%async_computation.3 | async-start | bytes 524288 | tf_op jit(solution)/shard_map/all_to_all | solution.py:438
  160.3 27.5 %collective-permute-start.25 = (bf16[2,128,1536]{2,1,0:T(8,128)(2,1)}, bf16[2,128,1536]{2,1,0:T(8,128)(2,1)}, u32[]{:S(2)}, u32[]{:S(2)}) collective-permute-start(bf16[2,128,1536]{2,1,0:T(8,128)(2,1)} %add_convert_fusion.1), channel_id=1, source_target_pairs={{0,4},{1,5},{2,6},{3,7},{4,8},{5,9},{6,10},{7,11},{8,12},{9,13},{1... | collective-permute-start | bytes 2359304 | tf_op jit(solution)/shard_map/ppermute | solution.py:34
  164.0 23.9 %collective-permute-start.24 = (bf16[2,128,1536]{2,1,0:T(8,128)(2,1)}, bf16[2,128,1536]{2,1,0:T(8,128)(2,1)S(1)}, u32[]{:S(2)}, u32[]{:S(2)}) collective-permute-start(bf16[2,128,1536]{2,1,0:T(8,128)(2,1)} %add_convert_fusion.2), channel_id=1, source_target_pairs={{0,12},{1,13},{2,14},{3,15},{4,0},{5,1},{6,2},{7,3},{8,4},{9,5},{1... | collective-permute-start | bytes 2359304 | tf_op jit(solution)/shard_map/ppermute | solution.py:34
  189.6 7.0 %collective-permute-start.27 = (bf16[128,1536]{1,0:T(8,128)(2,1)S(1)}, bf16[128,1536]{1,0:T(8,128)(2,1)S(1)}, u32[]{:S(2)}, u32[]{:S(2)}) collective-permute-start(bf16[128,1536]{1,0:T(8,128)(2,1)S(1)} %fusion.9), channel_id=1, source_target_pairs={{0,3},{1,0},{2,1},{3,2},{4,7},{5,4},{6,5},{7,6},{8,11},{9,8},{10,9... | collective-permute-start | bytes 1179656 | tf_op jit(solution)/shard_map/ppermute | solution.py:34
  191.6 12.4 %collective-permute-start.26 = (bf16[128,1536]{1,0:T(8,128)(2,1)S(1)}, bf16[128,1536]{1,0:T(8,128)(2,1)S(1)}, u32[]{:S(2)}, u32[]{:S(2)}) collective-permute-start(bf16[128,1536]{1,0:T(8,128)(2,1)S(1)} %get-tuple-element.113), channel_id=1, source_target_pairs={{0,1},{1,2},{2,3},{3,0},{4,5},{5,6},{6,7},{7,4},{8,9},{9,10},{10,1... | collective-permute-start | bytes 1179656 | tf_op jit(solution)/shard_map/ppermute | solution.py:34
  192.7 11.3 %collective-permute-start.28 = (bf16[128,1536]{1,0:T(8,128)(2,1)S(1)}, bf16[128,1536]{1,0:T(8,128)(2,1)S(1)}, u32[]{:S(2)}, u32[]{:S(2)}) collective-permute-start(bf16[128,1536]{1,0:T(8,128)(2,1)S(1)} %get-tuple-element.112), channel_id=1, source_target_pairs={{0,2},{1,3},{2,0},{3,1},{4,6},{5,7},{6,4},{7,5},{8,10},{9,11},{10,... | collective-permute-start | bytes 1179656 | tf_op jit(solution)/shard_map/ppermute | solution.py:34
  (35 other events, 287.5 us)

commit v7 on v6

--- a/solution.py
+++ b/solution.py
@@ -55,7 +55,7 @@
     tok = refs[0:5]
     adapt = refs[5:13]
     (place, gain, gain_moe, cosine, sine, wq_hbm, wk_hbm, wv_hbm, wo_hbm, mixed_out, moe_out,
-     wq, wk, wv, wo, xn, ad, qbuf, kbuf, vbuf, att, score, prob, sems) = refs[13:]
+     wq, wk, wv, wo, xn, ad, qbuf, kbuf, vbuf, att, score, prob, total, sems) = refs[13:]
     loads = [pltpu.make_async_copy(src, dst, sems.at[i]) for i, (src, dst) in enumerate(
         [(wk_hbm, wk), (wv_hbm, wv), (wq_hbm, wq), (wo_hbm, wo)])]
     for load in loads:
@@ -149,18 +149,21 @@
     def pair(j, carry):
         kv = pl.ds(pl.multiple_of(j * 128, 128), 128)
         score[...] = dot_t(qbuf[j], kbuf[:, kv])
-        totals = []
-        for h in range(6):
-            at = slice(count * h, count * h + count)
+
+        def soften(h, carry):
+            at = pl.ds(pl.multiple_of(h * count, count), count)
             s = score[at, :] + bias
             top = jnp.max(s, axis=-1, keepdims=True)
             w = jnp.exp(s - top)
-            totals.append(jnp.sum(w, axis=-1, keepdims=True))
+            total[at, :] = jnp.sum(w, axis=-1, keepdims=True)
             prob[at, :] = w.astype(BF)
-        out = jnp.dot(prob[...], vbuf[:, kv], preferred_element_type=F32)
+            return carry
+
+        lax.fori_loop(0, 6, soften, 0)
+        out = jnp.dot(prob[...], vbuf[:, kv], preferred_element_type=F32) / total[...]
         results = []
         for h in range(6):
-            o = out[count * h:count * h + count] / totals[h]
+            o = out[count * h:count * h + count]
             results.append(pltpu.roll(o, 64, 1) if (h % 2 == 0) != (h < 3) else o)
         for t in range(3):
             att[:, pl.ds(pl.multiple_of(j * 384 + 128 * t, 128), 128)] = jnp.where(
@@ -201,7 +204,8 @@
             pltpu.VMEM((384, width), BF), pltpu.VMEM((4, 6 * count, 128), BF),
             pltpu.VMEM((5 * count, 512), BF), pltpu.VMEM((5 * count, 512), BF),
             pltpu.VMEM((count, width), BF), pltpu.VMEM((6 * count, 5 * count), F32),
-            pltpu.VMEM((6 * count, 5 * count), BF), pltpu.SemaphoreType.DMA((4,)),
+            pltpu.VMEM((6 * count, 5 * count), BF), pltpu.VMEM((6 * count, 1), F32),
+            pltpu.SemaphoreType.DMA((4,)),
         ],
         compiler_params=pltpu.CompilerParams(vmem_limit_bytes=ATTENTION_VMEM),
         cost_estimate=pl.CostEstimate(flops=8 << 30, transcendentals=0,
@@ -245,9 +249,16 @@
             u = jnp.dot(rows, up[half + h], preferred_element_type=F32)
             hidden.append((g / (1.0 + jnp.exp(-g)) * u).astype(BF))
         hidden = jnp.concatenate(hidden, axis=1)
-        maps = down[pl.ds(pl.multiple_of(256 * half, 256), 256 * count), :]
-        out = jnp.dot(hidden, maps, preferred_element_type=F32)
-        ho[e] = (out * scale[e]).astype(BF)
+        depth = pl.ds(pl.multiple_of(256 * half, 256), 256 * count)
+        given = scale[e]
+
+        def columns(c, carry):
+            at = pl.ds(pl.multiple_of(c * 512, 512), 512)
+            out = jnp.dot(hidden, down[depth, at], preferred_element_type=F32)
+            ho[e, :, at] = (out * given).astype(BF)
+            return carry
+
+        lax.fori_loop(0, 3, columns, 0)
 
     def whole(e, carry):
         ffn(e, odd + 2 * e, 2)
@@ -411,37 +422,40 @@
 
     minus_lo, plus_hi = shift(minus_lo, 1, -1), shift(plus_hi, 1, 1)
     far_lo, far_hi, last_far = share([far_lo, far_hi], 3)
-    far_lo, far_hi = lax.optimization_barrier((shift(far_lo, 1, 1), shift(far_hi, 1, -1)))
-    plus_lo = shift((wide(plus_lo) + wide(far_lo)).astype(BF), 1, 1)
-    minus_hi = shift((wide(minus_hi) + wide(far_hi)).astype(BF), 1, -1)
-    minus_lo, plus_hi, minus_hi, plus_lo = lax.optimization_barrier(
-        (minus_lo, plus_hi, minus_hi, plus_lo))
-    own_lo = wide(own_lo) + wide(plus_lo) + wide(minus_lo)
-    own_hi = wide(own_hi) + wide(plus_hi) + wide(minus_hi)
-    line = lax.optimization_barrier(
-        [shift(own_hi[0].astype(BF), 0, 1), shift(own_lo[1].astype(BF), 0, -1),
-         shift(own_hi[1].astype(BF), 0, 2)])
-    combined = own_lo[0] + wide(line[0]) + wide(line[1]) + wide(line[2])
-    hidden_out = (mixed.astype(F32) + combined).astype(BF)
-
+    columns = width // 8
     last = jnp.stack([last_own, last_first, last_second, last_far])[:, :, :6]
     last = jnp.einsum("jg,jr->gr", order.astype(BF), last.reshape(16, 3 * width),
                       preferred_element_type=F32).astype(BF)
-    last = lax.all_to_all(last.reshape(16, 3, width), "grp", 0, 0, tiled=True)
-    last = jnp.sum(last.astype(F32), axis=0) + jnp.dot(
-        marks.astype(BF), mixed, preferred_element_type=F32)
-    last = rms_scaled(last.astype(BF), closing_gain)
-    part = width // 8
-    split = last.reshape(3, 8, part).transpose(1, 0, 2)
-    mine = lax.all_to_all(split, "seq", 0, 0, tiled=True)
-    mine = jnp.sum(mine.astype(F32), axis=0).astype(BF)
-    everyone = lax.all_to_all(jnp.broadcast_to(mine[None], (128, 3, part)), WHOLE, 0, 0,
+    last = last.reshape(16, 3, 8, columns).transpose(2, 0, 1, 3)
+    rows = jnp.dot(marks.astype(BF), mixed, preferred_element_type=F32).astype(BF)
+    rows = rows.reshape(3, 8, columns).transpose(1, 0, 2)[:, None]
+    here = (jnp.arange(16, dtype=jnp.int32) == grp)[None, :, None, None]
+    shares = jnp.concatenate([last, jnp.where(here, rows, 0)], axis=2)
+    shares = shares.reshape(128, 6, columns)
+    far_lo, far_hi, shares = lax.optimization_barrier(
+        (shift(far_lo, 1, 1), shift(far_hi, 1, -1), shares))
+    plus_lo = shift((wide(plus_lo) + wide(far_lo)).astype(BF), 1, 1)
+    minus_hi = shift((wide(minus_hi) + wide(far_hi)).astype(BF), 1, -1)
+    minus_lo, plus_hi, minus_hi, plus_lo, shares = lax.optimization_barrier(
+        (minus_lo, plus_hi, minus_hi, plus_lo, lax.all_to_all(shares, WHOLE, 0, 0, tiled=True)))
+    own_lo = wide(own_lo) + wide(plus_lo) + wide(minus_lo)
+    own_hi = wide(own_hi) + wide(plus_hi) + wide(minus_hi)
+    line = [shift(own_hi[0].astype(BF), 0, 1), shift(own_lo[1].astype(BF), 0, -1),
+            shift(own_hi[1].astype(BF), 0, 2)]
+
+    mine = jnp.sum(shares.astype(F32), axis=0)
+    mine = (mine[:3] + mine[3:]).astype(BF)
+    everyone = lax.all_to_all(jnp.broadcast_to(mine[None], (128, 3, columns)), WHOLE, 0, 0,
                               tiled=True)
-    final_rows = everyone.reshape(8, 48, part).transpose(1, 0, 2).reshape(48, width)
+    final_rows = everyone.reshape(8, 48, columns).transpose(1, 0, 2).reshape(48, width)
+    final_rows = rms_scaled(final_rows, closing_gain)
     logits = jnp.dot(final_rows, vocab_projection, preferred_element_type=F32)
     top = jnp.max(logits, axis=1)
     mass = jnp.sum(jnp.exp(logits - top[:, None]), axis=1)
     stats = jnp.concatenate([top, mass, jnp.zeros((32,), F32)])
+    line, stats = lax.optimization_barrier((line, stats))
+    combined = own_lo[0] + wide(line[0]) + wide(line[1]) + wide(line[2])
+    hidden_out = (mixed.astype(F32) + combined).astype(BF)
     stats = lax.all_to_all(jnp.broadcast_to(stats[None], (128, 128)), WHOLE, 0, 0, tiled=True)
     tops = stats[:, :48]
     peak = jnp.max(tops, axis=0)

time: 207 us -> 223 us (1.077)
  blocking collectives: 14.7 us -> 0 us
  Pallas kernels: 39.3 us -> 50.7 us
  waiting for transfers between devices: 36.2 us -> 42.8 us
  starting transfers between devices: 64.2 us -> 70.7 us
  other arithmetic: 17.1 us -> 22.5 us
    all_to_all x1 -> x0, blocking collectives: 14.7 us -> none  [body(): lax.all_to_all(jnp.broadcast_to(stats[None], (128, 128)), WHOLE, 0, 0, ti...]
    all_to_all x3, waiting for transfers between devices: 11.7 us -> 23.1 us  [the longest x1 14.1 us: body(): lax.all_to_all(shares, WHOLE, 0, 0, tiled=True)]
    pallas_call x4, Pallas kernels: 19.2 us -> 26.4 us  [experts(): pl.pallas_call(expert_kernel, out_shape=(piece, piece, jax.ShapeDtypeStru...]
    ppermute x18, waiting for transfers between devices: 18.8 us -> 14.1 us  [shift(): return lax.ppermute(rows, WHOLE, pairs)]
    all_to_all x3, starting transfers between devices: 19.4 us -> 23.6 us  [the longest x1 10.9 us: body(): lax.all_to_all(shares, WHOLE, 0, 0, tiled=True)]
    pallas_call x1, Pallas kernels: 20.1 us -> 24.3 us  [attention(): pl.pallas_call(attention_kernel, out_shape=(rows, rows), in_specs=[vm] *...]
    unnamed x70 -> x76, local copies, waits for them, and re-layouts: 11.2 us -> 8.11 us
    ppermute x18, starting transfers between devices: 20.1 us -> 22.7 us  [shift(): return lax.ppermute(rows, WHOLE, pairs)]
  transfers between devices with their start and end apart: 33 -> 33, of which waited for: 14 -> 14; matrix products, arithmetic and copies ran while one was open for 10% -> 15% of each run, Pallas kernels for 7% -> 9%
where the time goes in v7:
time: 223 us; the launch traced here: 222 us
  starting transfers between devices  70.7 us (32%)
  Pallas kernels  50.7 us (23%)
  waiting for transfers between devices  42.8 us (19%)
  local copies, waits for them, and re-layouts  24 us (11%)
  other arithmetic  22.5 us (10%)
  between operations  7.31 us (3%)
  matrix products  3.93 us (2%)
    pallas_call x4, Pallas kernels, experts(): pl.pallas_call(expert_kernel, out_shape=(piece, piece, jax.ShapeDtypeStru...  26.4 us
    pallas_call x1, Pallas kernels, attention(): pl.pallas_call(attention_kernel, out_shape=(rows, rows), in_specs=[vm] *...  24.3 us
    ppermute x18, starting transfers between devices, shift(): return lax.ppermute(rows, WHOLE, pairs)  22.7 us
    ppermute x18, waiting for transfers between devices, shift(): return lax.ppermute(rows, WHOLE, pairs)  14.1 us
    all_to_all x1, waiting for transfers between devices, body(): lax.all_to_all(shares, WHOLE, 0, 0, tiled=True)  14.1 us
    all_to_all x1, starting transfers between devices, body(): lax.all_to_all(shares, WHOLE, 0, 0, tiled=True)  10.9 us
    unnamed x76, local copies, waits for them, and re-layouts  8.11 us
    all_to_all x1, starting transfers between devices, body(): held = lax.all_to_all(payload, 'grp', 0, 0, tiled=True)  7.78 us
  transfers between devices with their start and end apart: 33, of which 14 were waited for; matrix products, arithmetic and copies ran while one was open for 15% of the time, Pallas kernels for 9%

profile of v7, /device:TPU:1, one launch (start us, length us, event | category | flops | bytes accessed | tf_op | source)
XLA Modules:
  0.0 222.0 jit_solution(1666868752205101618)
XLA Ops:
  6.5 4.0 %collective-permute-start = (bf16[128,1536]{1,0:T(8,128)(2,1)S(1)}, bf16[128,1536]{1,0:T(8,128)(2,1)S(1)}, u32[]{:S(2)}, u32[]{:S(2)}) collective-permute-start(bf16[128,1536]{1,0:T(8,128)(2,1)S(1)} %bitcast.212), channel_id=1, source_target_pairs={{0,32},{16,48},{32,64},{48,80},{64,96},{80,112},{1,33},{17,49},{33... | collective-permute-start | bytes 1179656 | tf_op jit(solution)/shard_map/ppermute | solution.py:345
  10.5 4.4 %collective-permute-start.1 = (bf16[128,1536]{1,0:T(8,128)(2,1)S(1)}, bf16[128,1536]{1,0:T(8,128)(2,1)S(1)}, u32[]{:S(2)}, u32[]{:S(2)}) collective-permute-start(bf16[128,1536]{1,0:T(8,128)(2,1)S(1)} %bitcast.213), channel_id=1, source_target_pairs={{0,64},{16,80},{32,96},{48,112},{1,65},{17,81},{33,97},{49,113},{2... | collective-permute-start | bytes 1179656 | tf_op jit(solution)/shard_map/ppermute | solution.py:346
  14.8 7.8 %all-to-all-start = ((bf16[16,16,1536]{2,1,0:T(8,128)(2,1)}), bf16[16,16,1536]{2,1,0:T(8,128)(2,1)S(1)}, u32[]{:S(2)}, u32[]{:S(2)}) async-start(bf16[16,16,1536]{2,1,0:T(8,128)(2,1)} %pad_maximum_fusion), calls=%async_computation | async-start | bytes 1572864 | tf_op jit(solution)/shard_map/all_to_all | solution.py:344
  36.9 2.7 %collective-permute-start.5 = (bf16[48,1536]{1,0:T(8,128)(2,1)S(1)}, bf16[48,1536]{1,0:T(8,128)(2,1)S(1)}, u32[]{:S(2)}, u32[]{:S(2)}) collective-permute-start(bf16[48,1536]{1,0:T(8,128)(2,1)S(1)} %bitcast.222), channel_id=1, source_target_pairs={{0,96},{16,112},{32,0},{48,16},{64,32},{80,48},{96,64},{112,80},{1... | collective-permute-start | bytes 442376 | tf_op jit(solution)/shard_map/ppermute | solution.py:380
  43.4 1.8 collective-permute-done.6.refs_8_
  45.2 3.2 %collective-permute-start.10 = (bf16[48,1536]{1,0:T(8,128)(2,1)S(1)}, bf16[48,1536]{1,0:T(8,128)(2,1)S(1)}, u32[]{:S(2)}, u32[]{:S(2)}) collective-permute-start(bf16[48,1536]{1,0:T(8,128)(2,1)S(1)} %collective-permute-done.6.refs_8_), channel_id=1, source_target_pairs={{0,16},{16,0},{32,48},{48,32},{64,80},{80,64},{96,112},{112,96},{1... | collective-permute-start | bytes 442376 | tf_op jit(solution)/shard_map/ppermute | solution.py:38
  51.2 24.3 %attention_block.1 = (bf16[128,1536]{1,0:T(8,128)(2,1)}, bf16[128,1536]{1,0:T(8,128)(2,1)}) custom-call(bf16[128,1536]{1,0:T(8,128)(2,1)} %bitcast.211, bf16[128,1536]{1,0:T(8,128)(2,1)} %copy-done.15, bf16[128,1536]{1,0:T(8,128)(2,1)} %copy-done.16, bf16[128,1536]{1,0:T(8,128)(2,1)} %copy-done.28, bf16[128,1536]{1,0:T(8,128)(2,1)} %collective-permute-done.3.refs_4_, ...), custom_call_target="tpu_custom_call" | custom-call | flops 8589934592 | bytes 20971520 | tf_op jit(solution)/shard_map/attention_block/pallas_call | solution.py:195
  76.3 1.9 collective-permute-start.12
  80.1 3.8 %collective-permute-done.11 = bf16[128,1536]{1,0:T(8,128)(2,1)S(1)} collective-permute-done((bf16[128,1536]{1,0:T(8,128)(2,1)}, bf16[128,1536]{1,0:T(8,128)(2,1)S(1)}, u32[]{:S(2)}, u32[]{:S(2)}) %collective-permute-start.11) | collective-permute-done | bytes 393248 | tf_op jit(solution)/shard_map/ppermute | solution.py:34
  83.9 3.6 %collective-permute-done.12 = bf16[128,1536]{1,0:T(8,128)(2,1)S(1)} collective-permute-done((bf16[128,1536]{1,0:T(8,128)(2,1)}, bf16[128,1536]{1,0:T(8,128)(2,1)S(1)}, u32[]{:S(2)}, u32[]{:S(2)}) %collective-permute-start.12) | collective-permute-done | bytes 393248 | tf_op jit(solution)/shard_map/ppermute | solution.py:34
  90.8 1.9 collective-permute-start.15
  94.4 2.1 copy-done.4
  96.5 2.1 copy-done.6
  98.7 2.1 copy-done.7
  100.8 6.2 %expert_block.4 = (bf16[256,1536]{1,0:T(8,128)(2,1)S(1)}, bf16[256,1536]{1,0:T(8,128)(2,1)S(1)}, bf16[2,8,1536]{2,1,0:T(8,128)(2,1)S(1)}) custom-call(bf16[256,1536]{1,0:T(8,128)(2,1)S(1)} %bitcast.184, bf16[256,1536]{1,0:T(8,128)(2,1)S(1)} %bitcast.185, s32[2]{0:T(128)S(1)} %get-tuple-element.152.first, f32[4,2,8,256]{3,2,1,0:T(8,128)S(1)} %bitcast.190, ...), custom_call_target="tpu_custom_call" | custom-call | flops 7516192768 | bytes 12582912 | tf_op jit(solution)/shard_map/expert_block/pallas_call | solution.py:286
  107.1 2.7 %collective-permute-start.19 = (bf16[2,128,1536]{2,1,0:T(8,128)(2,1)}, bf16[2,128,1536]{2,1,0:T(8,128)(2,1)S(1)}, u32[]{:S(2)}, u32[]{:S(2)}) collective-permute-start(bf16[2,128,1536]{2,1,0:T(8,128)(2,1)} %collective-permute-done.15), channel_id=1, source_target_pairs={{0,12},{1,13},{2,14},{3,15},{4,0},{5,1},{6,2},{7,3},{8,4},{9,5},{1... | collective-permute-start | bytes 2359304 | tf_op jit(solution)/shard_map/ppermute | solution.py:34
  109.7 7.0 %expert_block.5 = (bf16[256,1536]{1,0:T(8,128)(2,1)S(1)}, bf16[256,1536]{1,0:T(8,128)(2,1)S(1)}, bf16[2,8,1536]{2,1,0:T(8,128)(2,1)S(1)}) custom-call(bf16[256,1536]{1,0:T(8,128)(2,1)} %bitcast.49.p0, bf16[256,1536]{1,0:T(8,128)(2,1)} %bitcast.50.p1, s32[2]{0:T(128)S(1)} %get-tuple-element.153.first, f32[4,2,8,256]{3,2,1,0:T(8,128)S(1)} %bitcast.191, ...), custom_call_target="tpu_custom_call" | custom-call | flops 7516192768 | bytes 12582912 | tf_op jit(solution)/shard_map/expert_block/pallas_call | solution.py:286
  116.8 6.2 %expert_block.6 = (bf16[256,1536]{1,0:T(8,128)(2,1)S(1)}, bf16[256,1536]{1,0:T(8,128)(2,1)S(1)}, bf16[2,8,1536]{2,1,0:T(8,128)(2,1)S(1)}) custom-call(bf16[256,1536]{1,0:T(8,128)(2,1)S(1)} %bitcast.206, bf16[256,1536]{1,0:T(8,128)(2,1)S(1)} %bitcast.204, s32[2]{0:T(128)S(1)} %copy-done.3, f32[4,2,8,256]{3,2,1,0:T(8,128)S(1)} %bitcast.192, ...), custom_call_target="tpu_custom_call" | custom-call | flops 7516192768 | bytes 12582912 | tf_op jit(solution)/shard_map/expert_block/pallas_call | solution.py:286
  123.1 7.0 %expert_block.7 = (bf16[256,1536]{1,0:T(8,128)(2,1)}, bf16[256,1536]{1,0:T(8,128)(2,1)}, bf16[2,8,1536]{2,1,0:T(8,128)(2,1)S(1)}) custom-call(bf16[256,1536]{1,0:T(8,128)(2,1)S(1)} %bitcast.205, bf16[256,1536]{1,0:T(8,128)(2,1)S(1)} %bitcast.207, s32[2]{0:T(128)S(1)} %copy-done.2, f32[4,2,8,256]{3,2,1,0:T(8,128)S(1)} %bitcast.193, ...), custom_call_target="tpu_custom_call" | custom-call | flops 7516192768 | bytes 12582912 | tf_op jit(solution)/shard_map/expert_block/pallas_call | solution.py:286
  130.1 2.7 %collective-permute-start.23 = (bf16[2,128,1536]{2,1,0:T(8,128)(2,1)}, bf16[2,128,1536]{2,1,0:T(8,128)(2,1)}, u32[]{:S(2)}, u32[]{:S(2)}) collective-permute-start(bf16[2,128,1536]{2,1,0:T(8,128)(2,1)} %bitcast.60), channel_id=1, source_target_pairs={{0,12},{1,13},{2,14},{3,15},{4,0},{5,1},{6,2},{7,3},{8,4},{9,5},{1... | collective-permute-start | bytes 2359304 | tf_op jit(solution)/shard_map/ppermute | solution.py:34
  136.8 1.8 reshape.489
  142.8 2.2 add_convert_fusion.1
  145.0 2.2 %add_convert_fusion.2 = bf16[2,128,1536]{2,1,0:T(8,128)(2,1)} fusion(bf16[2,128,1536]{2,1,0:T(8,128)(2,1)} %collective-permute-done.23, bf16[2,128,1536]{2,1,0:T(8,128)(2,1)S(1)} %bitcast.187), kind=kLoop, calls=%fused_computation.7 | loop fusion | flops 1572864 | bytes 2359296 | tf_op jit(solution)/shard_map/convert_element_type | solution.py:438
  147.2 2.7 %collective-permute-start.24 = (bf16[2,128,1536]{2,1,0:T(8,128)(2,1)}, bf16[2,128,1536]{2,1,0:T(8,128)(2,1)S(1)}, u32[]{:S(2)}, u32[]{:S(2)}) collective-permute-start(bf16[2,128,1536]{2,1,0:T(8,128)(2,1)} %add_convert_fusion.2), channel_id=1, source_target_pairs={{0,12},{1,13},{2,14},{3,15},{4,0},{5,1},{6,2},{7,3},{8,4},{9,5},{1... | collective-permute-start | bytes 2359304 | tf_op jit(solution)/shard_map/ppermute | solution.py:34
  150.9 10.9 %all-to-all-start.1 = ((bf16[128,6,192]{2,1,0:T(8,128)(2,1)}), bf16[128,6,192]{2,1,0:T(8,128)(2,1)S(1)}, u32[]{:S(2)}, u32[]{:S(2)}) async-start(bf16[128,6,192]{2,1,0:T(8,128)(2,1)} %copy.85), calls=%async_computation.1 | async-start | bytes 1048576 | tf_op jit(solution)/shard_map/all_to_all | solution.py:440
  161.8 14.1 %all-to-all-done.1 = bf16[128,6,192]{2,1,0:T(8,128)(2,1)S(1)} async-done(((bf16[128,6,192]{2,1,0:T(8,128)(2,1)}), bf16[128,6,192]{2,1,0:T(8,128)(2,1)S(1)}, u32[]{:S(2)}, u32[]{:S(2)}) %all-to-all-start.1) | async-done | bytes 294944 | tf_op jit(solution)/shard_map/all_to_all | solution.py:440
  176.9 5.0 %all-to-all-start.2 = ((bf16[128,3,192]{2,1,0:T(4,128)(2,1)}), bf16[128,3,192]{2,1,0:T(4,128)(2,1)}, u32[]{:S(2)}, u32[]{:S(2)}) async-start(bf16[128,3,192]{2,1,0:T(4,128)(2,1)} %broadcast_in_dim.242), calls=%async_computation.2 | async-start | bytes 524288 | tf_op jit(solution)/shard_map/all_to_all | solution.py:448
  184.4 3.4 %collective-permute-start.27 = (bf16[128,1536]{1,0:T(8,128)(2,1)}, bf16[128,1536]{1,0:T(8,128)(2,1)}, u32[]{:S(2)}, u32[]{:S(2)}) collective-permute-start(bf16[128,1536]{1,0:T(8,128)(2,1)} %fusion.7), channel_id=1, source_target_pairs={{0,3},{1,0},{2,1},{3,2},{4,7},{5,4},{6,5},{7,6},{8,11},{9,8},{10,9... | collective-permute-start | bytes 1179656 | tf_op jit(solution)/shard_map/ppermute | solution.py:34
  197.9 4.8 %collective-permute-done.26 = bf16[128,1536]{1,0:T(8,128)(2,1)S(1)} collective-permute-done((bf16[128,1536]{1,0:T(8,128)(2,1)}, bf16[128,1536]{1,0:T(8,128)(2,1)S(1)}, u32[]{:S(2)}, u32[]{:S(2)}) %collective-permute-start.26) | collective-permute-done | bytes 393248 | tf_op jit(solution)/shard_map/ppermute | solution.py:34
  203.4 7.7 %all-to-all-start.3 = ((f32[128,1,128]{2,1,0:T(1,128)}), f32[128,1,128]{2,1,0:T(1,128)S(1)}, u32[]{:S(2)}, u32[]{:S(2)}) async-start(f32[128,1,128]{2,1,0:T(1,128)} %broadcast_in_dim.245), calls=%async_computation.3 | async-start | bytes 131072 | tf_op jit(solution)/shard_map/all_to_all | solution.py:459
  211.1 2.1 fusion.6
  213.2 7.6 %all-to-all-done.3 = f32[128,1,128]{2,1,0:T(1,128)S(1)} async-done(((f32[128,1,128]{2,1,0:T(1,128)}), f32[128,1,128]{2,1,0:T(1,128)S(1)}, u32[]{:S(2)}, u32[]{:S(2)}) %all-to-all-start.3) | async-done | bytes 65568 | tf_op jit(solution)/shard_map/all_to_all | solution.py:459
  (229 shorter events, 52.9 us)
Async XLA Ops:
  6.5 28.0 %collective-permute-start = (bf16[128,1536]{1,0:T(8,128)(2,1)S(1)}, bf16[128,1536]{1,0:T(8,128)(2,1)S(1)}, u32[]{:S(2)}, u32[]{:S(2)}) collective-permute-start(bf16[128,1536]{1,0:T(8,128)(2,1)S(1)} %bitcast.212), channel_id=1, source_target_pairs={{0,32},{16,48},{32,64},{48,80},{64,96},{80,112},{1,33},{17,49},{33... | collective-permute-start | bytes 1179656 | tf_op jit(solution)/shard_map/ppermute | solution.py:345
  10.5 24.0 %collective-permute-start.1 = (bf16[128,1536]{1,0:T(8,128)(2,1)S(1)}, bf16[128,1536]{1,0:T(8,128)(2,1)S(1)}, u32[]{:S(2)}, u32[]{:S(2)}) collective-permute-start(bf16[128,1536]{1,0:T(8,128)(2,1)S(1)} %bitcast.213), channel_id=1, source_target_pairs={{0,64},{16,80},{32,96},{48,112},{1,65},{17,81},{33,97},{49,113},{2... | collective-permute-start | bytes 1179656 | tf_op jit(solution)/shard_map/ppermute | solution.py:346
  14.8 21.4 %all-to-all-start = ((bf16[16,16,1536]{2,1,0:T(8,128)(2,1)}), bf16[16,16,1536]{2,1,0:T(8,128)(2,1)S(1)}, u32[]{:S(2)}, u32[]{:S(2)}) async-start(bf16[16,16,1536]{2,1,0:T(8,128)(2,1)} %pad_maximum_fusion), calls=%async_computation | async-start | bytes 1572864 | tf_op jit(solution)/shard_map/all_to_all | solution.py:344
  34.6 14.4 %collective-permute-start.2 = (bf16[128,1536]{1,0:T(8,128)(2,1)S(1)}, bf16[128,1536]{1,0:T(8,128)(2,1)S(1)}, u32[]{:S(2)}, u32[]{:S(2)}) collective-permute-start(bf16[128,1536]{1,0:T(8,128)(2,1)S(1)} %get-tuple-element.124), channel_id=1, source_target_pairs={{0,16},{16,0},{32,48},{48,32},{64,80},{80,64},{96,112},{112,96},{1... | collective-permute-start | bytes 1179656 | tf_op jit(solution)/shard_map/ppermute | solution.py:38
  36.2 12.9 %collective-permute-start.3 = (bf16[128,1536]{1,0:T(8,128)(2,1)S(1)}, bf16[128,1536]{1,0:T(8,128)(2,1)}, u32[]{:S(2)}, u32[]{:S(2)}) collective-permute-start(bf16[128,1536]{1,0:T(8,128)(2,1)S(1)} %get-tuple-element.123), channel_id=1, source_target_pairs={{0,16},{16,0},{32,48},{48,32},{64,80},{80,64},{96,112},{112,96},{1... | collective-permute-start | bytes 1179656 | tf_op jit(solution)/shard_map/ppermute | solution.py:38
  36.8 5.3 %collective-permute-start.4 = (bf16[48,1536]{1,0:T(8,128)(2,1)S(1)}, bf16[48,1536]{1,0:T(8,128)(2,1)S(1)}, u32[]{:S(2)}, u32[]{:S(2)}) collective-permute-start(bf16[48,1536]{1,0:T(8,128)(2,1)S(1)} %bitcast.221), channel_id=1, source_target_pairs={{0,32},{16,48},{32,64},{48,80},{64,96},{80,112},{96,0},{112,16},{1... | collective-permute-start | bytes 442376 | tf_op jit(solution)/shard_map/ppermute | solution.py:380
  36.9 6.5 %collective-permute-start.5 = (bf16[48,1536]{1,0:T(8,128)(2,1)S(1)}, bf16[48,1536]{1,0:T(8,128)(2,1)S(1)}, u32[]{:S(2)}, u32[]{:S(2)}) collective-permute-start(bf16[48,1536]{1,0:T(8,128)(2,1)S(1)} %bitcast.222), channel_id=1, source_target_pairs={{0,96},{16,112},{32,0},{48,16},{64,32},{80,48},{96,64},{112,80},{1... | collective-permute-start | bytes 442376 | tf_op jit(solution)/shard_map/ppermute | solution.py:380
  39.6 5.6 %collective-permute-start.6 = (bf16[48,1536]{1,0:T(8,128)(2,1)S(1)}, bf16[48,1536]{1,0:T(8,128)(2,1)S(1)}, u32[]{:S(2)}, u32[]{:S(2)}) collective-permute-start(bf16[48,1536]{1,0:T(8,128)(2,1)S(1)} %bitcast.223), channel_id=1, source_target_pairs={{0,64},{16,80},{32,96},{48,112},{64,0},{80,16},{96,32},{112,48},{1... | collective-permute-start | bytes 442376 | tf_op jit(solution)/shard_map/ppermute | solution.py:380
  45.2 4.3 %collective-permute-start.10 = (bf16[48,1536]{1,0:T(8,128)(2,1)S(1)}, bf16[48,1536]{1,0:T(8,128)(2,1)S(1)}, u32[]{:S(2)}, u32[]{:S(2)}) collective-permute-start(bf16[48,1536]{1,0:T(8,128)(2,1)S(1)} %collective-permute-done.6.refs_8_), channel_id=1, source_target_pairs={{0,16},{16,0},{32,48},{48,32},{64,80},{80,64},{96,112},{112,96},{1... | collective-permute-start | bytes 442376 | tf_op jit(solution)/shard_map/ppermute | solution.py:38
  48.4 1.6 collective-permute-start.8
  49.0 2.2 collective-permute-start.9
  75.4 8.4 %collective-permute-start.11 = (bf16[128,1536]{1,0:T(8,128)(2,1)}, bf16[128,1536]{1,0:T(8,128)(2,1)S(1)}, u32[]{:S(2)}, u32[]{:S(2)}) collective-permute-start(bf16[128,1536]{1,0:T(8,128)(2,1)} %get-tuple-element.71), channel_id=1, source_target_pairs={{0,1},{1,2},{2,3},{3,0},{4,5},{5,6},{6,7},{7,4},{8,9},{9,10},{10,1... | collective-permute-start | bytes 1179656 | tf_op jit(solution)/shard_map/ppermute | solution.py:34
  76.3 11.1 %collective-permute-start.12 = (bf16[128,1536]{1,0:T(8,128)(2,1)}, bf16[128,1536]{1,0:T(8,128)(2,1)S(1)}, u32[]{:S(2)}, u32[]{:S(2)}) collective-permute-start(bf16[128,1536]{1,0:T(8,128)(2,1)} %get-tuple-element.71), channel_id=1, source_target_pairs={{0,3},{1,0},{2,1},{3,2},{4,7},{5,4},{6,5},{7,6},{8,11},{9,8},{10,9... | collective-permute-start | bytes 1179656 | tf_op jit(solution)/shard_map/ppermute | solution.py:34
  78.2 10.4 %collective-permute-start.13 = (bf16[128,1536]{1,0:T(8,128)(2,1)}, bf16[128,1536]{1,0:T(8,128)(2,1)S(1)}, u32[]{:S(2)}, u32[]{:S(2)}) collective-permute-start(bf16[128,1536]{1,0:T(8,128)(2,1)} %get-tuple-element.71), channel_id=1, source_target_pairs={{0,2},{1,3},{2,0},{3,1},{4,6},{5,7},{6,4},{7,5},{8,10},{9,11},{10,... | collective-permute-start | bytes 1179656 | tf_op jit(solution)/shard_map/ppermute | solution.py:34
  89.7 17.2 %collective-permute-start.14 = (bf16[2,128,1536]{2,1,0:T(8,128)(2,1)S(1)}, bf16[2,128,1536]{2,1,0:T(8,128)(2,1)}, u32[]{:S(2)}, u32[]{:S(2)}) collective-permute-start(bf16[2,128,1536]{2,1,0:T(8,128)(2,1)S(1)} %pad_maximum_fusion.1), channel_id=1, source_target_pairs={{0,4},{1,5},{2,6},{3,7},{4,8},{5,9},{6,10},{7,11},{8,12},{9,13},{1... | collective-permute-start | bytes 2359304 | tf_op jit(solution)/shard_map/ppermute | solution.py:34
  90.8 16.2 %collective-permute-start.15 = (bf16[2,128,1536]{2,1,0:T(8,128)(2,1)S(1)}, bf16[2,128,1536]{2,1,0:T(8,128)(2,1)}, u32[]{:S(2)}, u32[]{:S(2)}) collective-permute-start(bf16[2,128,1536]{2,1,0:T(8,128)(2,1)S(1)} %pad_maximum_fusion.2), channel_id=1, source_target_pairs={{0,12},{1,13},{2,14},{3,15},{4,0},{5,1},{6,2},{7,3},{8,4},{9,5},{1... | collective-permute-start | bytes 2359304 | tf_op jit(solution)/shard_map/ppermute | solution.py:34
  92.9 23.9 %collective-permute-start.17 = (bf16[2,128,1536]{2,1,0:T(8,128)(2,1)S(1)}, bf16[2,128,1536]{2,1,0:T(8,128)(2,1)S(1)}, u32[]{:S(2)}, u32[]{:S(2)}) collective-permute-start(bf16[2,128,1536]{2,1,0:T(8,128)(2,1)S(1)} %pad_maximum_fusion.1), channel_id=1, source_target_pairs={{0,12},{1,13},{2,14},{3,15},{4,0},{5,1},{6,2},{7,3},{8,4},{9,5},{1... | collective-permute-start | bytes 2359304 | tf_op jit(solution)/shard_map/ppermute | solution.py:34
  94.1 22.7 %collective-permute-start.16 = (bf16[2,128,1536]{2,1,0:T(8,128)(2,1)S(1)}, bf16[2,128,1536]{2,1,0:T(8,128)(2,1)S(1)}, u32[]{:S(2)}, u32[]{:S(2)}) collective-permute-start(bf16[2,128,1536]{2,1,0:T(8,128)(2,1)S(1)} %pad_maximum_fusion.2), channel_id=1, source_target_pairs={{0,4},{1,5},{2,6},{3,7},{4,8},{5,9},{6,10},{7,11},{8,12},{9,13},{1... | collective-permute-start | bytes 2359304 | tf_op jit(solution)/shard_map/ppermute | solution.py:34
  107.0 16.1 %collective-permute-start.18 = (bf16[2,128,1536]{2,1,0:T(8,128)(2,1)}, bf16[2,128,1536]{2,1,0:T(8,128)(2,1)S(1)}, u32[]{:S(2)}, u32[]{:S(2)}) collective-permute-start(bf16[2,128,1536]{2,1,0:T(8,128)(2,1)} %collective-permute-done.14), channel_id=1, source_target_pairs={{0,4},{1,5},{2,6},{3,7},{4,8},{5,9},{6,10},{7,11},{8,12},{9,13},{1... | collective-permute-start | bytes 2359304 | tf_op jit(solution)/shard_map/ppermute | solution.py:34
  107.1 16.0 %collective-permute-start.19 = (bf16[2,128,1536]{2,1,0:T(8,128)(2,1)}, bf16[2,128,1536]{2,1,0:T(8,128)(2,1)S(1)}, u32[]{:S(2)}, u32[]{:S(2)}) collective-permute-start(bf16[2,128,1536]{2,1,0:T(8,128)(2,1)} %collective-permute-done.15), channel_id=1, source_target_pairs={{0,12},{1,13},{2,14},{3,15},{4,0},{5,1},{6,2},{7,3},{8,4},{9,5},{1... | collective-permute-start | bytes 2359304 | tf_op jit(solution)/shard_map/ppermute | solution.py:34
  130.1 12.7 %collective-permute-start.22 = (bf16[2,128,1536]{2,1,0:T(8,128)(2,1)}, bf16[2,128,1536]{2,1,0:T(8,128)(2,1)}, u32[]{:S(2)}, u32[]{:S(2)}) collective-permute-start(bf16[2,128,1536]{2,1,0:T(8,128)(2,1)} %bitcast.59), channel_id=1, source_target_pairs={{0,4},{1,5},{2,6},{3,7},{4,8},{5,9},{6,10},{7,11},{8,12},{9,13},{1... | collective-permute-start | bytes 2359304 | tf_op jit(solution)/shard_map/ppermute | solution.py:34
  130.1 12.7 %collective-permute-start.23 = (bf16[2,128,1536]{2,1,0:T(8,128)(2,1)}, bf16[2,128,1536]{2,1,0:T(8,128)(2,1)}, u32[]{:S(2)}, u32[]{:S(2)}) collective-permute-start(bf16[2,128,1536]{2,1,0:T(8,128)(2,1)} %bitcast.60), channel_id=1, source_target_pairs={{0,12},{1,13},{2,14},{3,15},{4,0},{5,1},{6,2},{7,3},{8,4},{9,5},{1... | collective-permute-start | bytes 2359304 | tf_op jit(solution)/shard_map/ppermute | solution.py:34
  139.6 22.2 %collective-permute-start.20 = (bf16[2,128,1536]{2,1,0:T(8,128)(2,1)}, bf16[2,128,1536]{2,1,0:T(8,128)(2,1)}, u32[]{:S(2)}, u32[]{:S(2)}) collective-permute-start(bf16[2,128,1536]{2,1,0:T(8,128)(2,1)} %bitcast.203), channel_id=1, source_target_pairs={{0,12},{1,13},{2,14},{3,15},{4,0},{5,1},{6,2},{7,3},{8,4},{9,5},{1... | collective-permute-start | bytes 2359304 | tf_op jit(solution)/shard_map/ppermute | solution.py:34
  139.6 22.2 %collective-permute-start.21 = (bf16[2,128,1536]{2,1,0:T(8,128)(2,1)}, bf16[2,128,1536]{2,1,0:T(8,128)(2,1)}, u32[]{:S(2)}, u32[]{:S(2)}) collective-permute-start(bf16[2,128,1536]{2,1,0:T(8,128)(2,1)} %bitcast.202), channel_id=1, source_target_pairs={{0,4},{1,5},{2,6},{3,7},{4,8},{5,9},{6,10},{7,11},{8,12},{9,13},{1... | collective-permute-start | bytes 2359304 | tf_op jit(solution)/shard_map/ppermute | solution.py:34
  145.0 30.9 %collective-permute-start.25 = (bf16[2,128,1536]{2,1,0:T(8,128)(2,1)}, bf16[2,128,1536]{2,1,0:T(8,128)(2,1)}, u32[]{:S(2)}, u32[]{:S(2)}) collective-permute-start(bf16[2,128,1536]{2,1,0:T(8,128)(2,1)} %add_convert_fusion.1), channel_id=1, source_target_pairs={{0,4},{1,5},{2,6},{3,7},{4,8},{5,9},{6,10},{7,11},{8,12},{9,13},{1... | collective-permute-start | bytes 2359304 | tf_op jit(solution)/shard_map/ppermute | solution.py:34
  147.2 28.7 %collective-permute-start.24 = (bf16[2,128,1536]{2,1,0:T(8,128)(2,1)}, bf16[2,128,1536]{2,1,0:T(8,128)(2,1)S(1)}, u32[]{:S(2)}, u32[]{:S(2)}) collective-permute-start(bf16[2,128,1536]{2,1,0:T(8,128)(2,1)} %add_convert_fusion.2), channel_id=1, source_target_pairs={{0,12},{1,13},{2,14},{3,15},{4,0},{5,1},{6,2},{7,3},{8,4},{9,5},{1... | collective-permute-start | bytes 2359304 | tf_op jit(solution)/shard_map/ppermute | solution.py:34
  150.9 25.0 %all-to-all-start.1 = ((bf16[128,6,192]{2,1,0:T(8,128)(2,1)}), bf16[128,6,192]{2,1,0:T(8,128)(2,1)S(1)}, u32[]{:S(2)}, u32[]{:S(2)}) async-start(bf16[128,6,192]{2,1,0:T(8,128)(2,1)} %copy.85), calls=%async_computation.1 | async-start | bytes 1048576 | tf_op jit(solution)/shard_map/all_to_all | solution.py:440
  176.9 16.2 %all-to-all-start.2 = ((bf16[128,3,192]{2,1,0:T(4,128)(2,1)}), bf16[128,3,192]{2,1,0:T(4,128)(2,1)}, u32[]{:S(2)}, u32[]{:S(2)}) async-start(bf16[128,3,192]{2,1,0:T(4,128)(2,1)} %broadcast_in_dim.242), calls=%async_computation.2 | async-start | bytes 524288 | tf_op jit(solution)/shard_map/all_to_all | solution.py:448
  184.4 13.5 %collective-permute-start.27 = (bf16[128,1536]{1,0:T(8,128)(2,1)}, bf16[128,1536]{1,0:T(8,128)(2,1)}, u32[]{:S(2)}, u32[]{:S(2)}) collective-permute-start(bf16[128,1536]{1,0:T(8,128)(2,1)} %fusion.7), channel_id=1, source_target_pairs={{0,3},{1,0},{2,1},{3,2},{4,7},{5,4},{6,5},{7,6},{8,11},{9,8},{10,9... | collective-permute-start | bytes 1179656 | tf_op jit(solution)/shard_map/ppermute | solution.py:34
  190.2 12.6 %collective-permute-start.26 = (bf16[128,1536]{1,0:T(8,128)(2,1)}, bf16[128,1536]{1,0:T(8,128)(2,1)S(1)}, u32[]{:S(2)}, u32[]{:S(2)}) collective-permute-start(bf16[128,1536]{1,0:T(8,128)(2,1)} %get-tuple-element.119), channel_id=1, source_target_pairs={{0,1},{1,2},{2,3},{3,0},{4,5},{5,6},{6,7},{7,4},{8,9},{9,10},{10,1... | collective-permute-start | bytes 1179656 | tf_op jit(solution)/shard_map/ppermute | solution.py:34
  190.2 12.6 %collective-permute-start.28 = (bf16[128,1536]{1,0:T(8,128)(2,1)}, bf16[128,1536]{1,0:T(8,128)(2,1)}, u32[]{:S(2)}, u32[]{:S(2)}) collective-permute-start(bf16[128,1536]{1,0:T(8,128)(2,1)} %get-tuple-element.118), channel_id=1, source_target_pairs={{0,2},{1,3},{2,0},{3,1},{4,6},{5,7},{6,4},{7,5},{8,10},{9,11},{10,... | collective-permute-start | bytes 1179656 | tf_op jit(solution)/shard_map/ppermute | solution.py:34
  203.4 17.4 %all-to-all-start.3 = ((f32[128,1,128]{2,1,0:T(1,128)}), f32[128,1,128]{2,1,0:T(1,128)S(1)}, u32[]{:S(2)}, u32[]{:S(2)}) async-start(f32[128,1,128]{2,1,0:T(1,128)} %broadcast_in_dim.245), calls=%async_computation.3 | async-start | bytes 131072 | tf_op jit(solution)/shard_map/all_to_all | solution.py:459
  (38 other events, 279.3 us)

commit v8 on v6

--- a/solution.py
+++ b/solution.py
@@ -411,18 +411,11 @@
 
     minus_lo, plus_hi = shift(minus_lo, 1, -1), shift(plus_hi, 1, 1)
     far_lo, far_hi, last_far = share([far_lo, far_hi], 3)
+    minus_lo, plus_hi, far_lo, far_hi, last_far = lax.optimization_barrier(
+        (minus_lo, plus_hi, far_lo, far_hi, last_far))
     far_lo, far_hi = lax.optimization_barrier((shift(far_lo, 1, 1), shift(far_hi, 1, -1)))
-    plus_lo = shift((wide(plus_lo) + wide(far_lo)).astype(BF), 1, 1)
-    minus_hi = shift((wide(minus_hi) + wide(far_hi)).astype(BF), 1, -1)
-    minus_lo, plus_hi, minus_hi, plus_lo = lax.optimization_barrier(
-        (minus_lo, plus_hi, minus_hi, plus_lo))
-    own_lo = wide(own_lo) + wide(plus_lo) + wide(minus_lo)
-    own_hi = wide(own_hi) + wide(plus_hi) + wide(minus_hi)
-    line = lax.optimization_barrier(
-        [shift(own_hi[0].astype(BF), 0, 1), shift(own_lo[1].astype(BF), 0, -1),
-         shift(own_hi[1].astype(BF), 0, 2)])
-    combined = own_lo[0] + wide(line[0]) + wide(line[1]) + wide(line[2])
-    hidden_out = (mixed.astype(F32) + combined).astype(BF)
+    plus_lo = (wide(plus_lo) + wide(far_lo)).astype(BF)
+    minus_hi = (wide(minus_hi) + wide(far_hi)).astype(BF)
 
     last = jnp.stack([last_own, last_first, last_second, last_far])[:, :, :6]
     last = jnp.einsum("jg,jr->gr", order.astype(BF), last.reshape(16, 3 * width),
@@ -435,6 +428,7 @@
     split = last.reshape(3, 8, part).transpose(1, 0, 2)
     mine = lax.all_to_all(split, "seq", 0, 0, tiled=True)
     mine = jnp.sum(mine.astype(F32), axis=0).astype(BF)
+    plus_lo, minus_hi, mine = lax.optimization_barrier((plus_lo, minus_hi, mine))
     everyone = lax.all_to_all(jnp.broadcast_to(mine[None], (128, 3, part)), WHOLE, 0, 0,
                               tiled=True)
     final_rows = everyone.reshape(8, 48, part).transpose(1, 0, 2).reshape(48, width)
@@ -442,6 +436,15 @@
     top = jnp.max(logits, axis=1)
     mass = jnp.sum(jnp.exp(logits - top[:, None]), axis=1)
     stats = jnp.concatenate([top, mass, jnp.zeros((32,), F32)])
+    plus_lo, minus_hi = shift(plus_lo, 1, 1), shift(minus_hi, 1, -1)
+    own_lo = wide(own_lo) + wide(plus_lo) + wide(minus_lo)
+    own_hi = wide(own_hi) + wide(plus_hi) + wide(minus_hi)
+    line = [own_hi[0].astype(BF), own_lo[1].astype(BF), own_hi[1].astype(BF)]
+    line, stats = lax.optimization_barrier((line, stats))
+    line = lax.optimization_barrier(
+        [shift(line[0], 0, 1), shift(line[1], 0, -1), shift(line[2], 0, 2)])
+    combined = own_lo[0] + wide(line[0]) + wide(line[1]) + wide(line[2])
+    hidden_out = (mixed.astype(F32) + combined).astype(BF)
     stats = lax.all_to_all(jnp.broadcast_to(stats[None], (128, 128)), WHOLE, 0, 0, tiled=True)
     tops = stats[:, :48]
     peak = jnp.max(tops, axis=0)

time: 207 us -> 215 us (1.039)
  waiting for transfers between devices: 36.2 us -> 44.1 us
    all_to_all x1, waiting for transfers between devices: 3.98 us -> 8.73 us  [body(): lax.all_to_all(jnp.broadcast_to(mine[None], (128, 3, part)), WHOLE, 0, 0,...]
    ppermute x18, starting transfers between devices: 20.1 us -> 24.3 us  [shift(): return lax.ppermute(rows, WHOLE, pairs)]
    all_to_all x1, starting transfers between devices: 5.98 us -> 3.52 us  [body(): last = lax.all_to_all(last.reshape(16, 3, width), 'grp', 0, 0, tiled=True)]
    unnamed x70 -> x78, local copies, waits for them, and re-layouts: 11.2 us -> 10.7 us
  transfers between devices with their start and end apart: 33 -> 33, of which waited for: 14 -> 17; matrix products, arithmetic and copies ran while one was open for 10% -> 7% of each run, Pallas kernels for 7% -> 9%
where the time goes in v8:
time: 215 us; the launch traced here: 214 us
  starting transfers between devices  65.5 us (30%)
  waiting for transfers between devices  44.1 us (21%)
  Pallas kernels  39.3 us (18%)
  local copies, waits for them, and re-layouts  22.1 us (10%)
  other arithmetic  17.9 us (8%)
  blocking collectives  14.2 us (7%)
  between operations  7.32 us (3%)
  matrix products  3.34 us (2%)
    ppermute x18, starting transfers between devices, shift(): return lax.ppermute(rows, WHOLE, pairs)  24.3 us
    ppermute x18, waiting for transfers between devices, shift(): return lax.ppermute(rows, WHOLE, pairs)  20.4 us
    pallas_call x1, Pallas kernels, attention(): pl.pallas_call(attention_kernel, out_shape=(rows, rows), in_specs=[vm] *...  20 us
    pallas_call x4, Pallas kernels, experts(): pl.pallas_call(expert_kernel, out_shape=(piece, piece, jax.ShapeDtypeStru...  19.2 us
    all_to_all x1, blocking collectives, body(): mine = lax.all_to_all(split, 'seq', 0, 0, tiled=True)  14.2 us
    unnamed x78, local copies, waits for them, and re-layouts  10.7 us
    all_to_all x1, waiting for transfers between devices, body(): lax.all_to_all(jnp.broadcast_to(mine[None], (128, 3, part)), WHOLE, 0, 0,...  8.73 us
    all_to_all x1, starting transfers between devices, body(): lax.all_to_all(jnp.broadcast_to(stats[None], (128, 128)), WHOLE, 0, 0, ti...  8.15 us
  transfers between devices with their start and end apart: 33, of which 17 were waited for; matrix products, arithmetic and copies ran while one was open for 7% of the time, Pallas kernels for 9%

profile of v8, /device:TPU:1, one launch (start us, length us, event | category | flops | bytes accessed | tf_op | source)
XLA Modules:
  0.0 213.8 jit_solution(297232703458300930)
XLA Ops:
  6.0 4.0 %collective-permute-start = (bf16[128,1536]{1,0:T(8,128)(2,1)S(1)}, bf16[128,1536]{1,0:T(8,128)(2,1)S(1)}, u32[]{:S(2)}, u32[]{:S(2)}) collective-permute-start(bf16[128,1536]{1,0:T(8,128)(2,1)S(1)} %bitcast.213), channel_id=1, source_target_pairs={{0,32},{16,48},{32,64},{48,80},{64,96},{80,112},{1,33},{17,49},{33... | collective-permute-start | bytes 1179656 | tf_op jit(solution)/shard_map/ppermute | solution.py:334
  10.0 4.4 %collective-permute-start.1 = (bf16[128,1536]{1,0:T(8,128)(2,1)S(1)}, bf16[128,1536]{1,0:T(8,128)(2,1)S(1)}, u32[]{:S(2)}, u32[]{:S(2)}) collective-permute-start(bf16[128,1536]{1,0:T(8,128)(2,1)S(1)} %bitcast.214), channel_id=1, source_target_pairs={{0,64},{16,80},{32,96},{48,112},{1,65},{17,81},{33,97},{49,113},{2... | collective-permute-start | bytes 1179656 | tf_op jit(solution)/shard_map/ppermute | solution.py:335
  14.4 7.8 %all-to-all-start = ((bf16[16,16,1536]{2,1,0:T(8,128)(2,1)}), bf16[16,16,1536]{2,1,0:T(8,128)(2,1)S(1)}, u32[]{:S(2)}, u32[]{:S(2)}) async-start(bf16[16,16,1536]{2,1,0:T(8,128)(2,1)} %pad_maximum_fusion), calls=%async_computation | async-start | bytes 1572864 | tf_op jit(solution)/shard_map/all_to_all | solution.py:333
  36.5 2.7 %collective-permute-start.5 = (bf16[48,1536]{1,0:T(8,128)(2,1)S(1)}, bf16[48,1536]{1,0:T(8,128)(2,1)S(1)}, u32[]{:S(2)}, u32[]{:S(2)}) collective-permute-start(bf16[48,1536]{1,0:T(8,128)(2,1)S(1)} %bitcast.223), channel_id=1, source_target_pairs={{0,96},{16,112},{32,0},{48,16},{64,32},{80,48},{96,64},{112,80},{1... | collective-permute-start | bytes 442376 | tf_op jit(solution)/shard_map/ppermute | solution.py:369
  44.8 3.2 %collective-permute-start.10 = (bf16[48,1536]{1,0:T(8,128)(2,1)S(1)}, bf16[48,1536]{1,0:T(8,128)(2,1)S(1)}, u32[]{:S(2)}, u32[]{:S(2)}) collective-permute-start(bf16[48,1536]{1,0:T(8,128)(2,1)S(1)} %collective-permute-done.6.refs_8_), channel_id=1, source_target_pairs={{0,16},{16,0},{32,48},{48,32},{64,80},{80,64},{96,112},{112,96},{1... | collective-permute-start | bytes 442376 | tf_op jit(solution)/shard_map/ppermute | solution.py:38
  50.7 20.0 %attention_block.1 = (bf16[128,1536]{1,0:T(8,128)(2,1)}, bf16[128,1536]{1,0:T(8,128)(2,1)}) custom-call(bf16[128,1536]{1,0:T(8,128)(2,1)} %bitcast.212, bf16[128,1536]{1,0:T(8,128)(2,1)} %copy-done.16, bf16[128,1536]{1,0:T(8,128)(2,1)} %copy-done.17, bf16[128,1536]{1,0:T(8,128)(2,1)} %copy-done.29, bf16[128,1536]{1,0:T(8,128)(2,1)} %collective-permute-done.3.refs_4_, ...), custom_call_target="tpu_custom_call" | custom-call | flops 8589934592 | bytes 20971520 | tf_op jit(solution)/shard_map/attention_block/pallas_call | solution.py:192
  74.7 4.5 %collective-permute-done.11 = bf16[128,1536]{1,0:T(8,128)(2,1)S(1)} collective-permute-done((bf16[128,1536]{1,0:T(8,128)(2,1)}, bf16[128,1536]{1,0:T(8,128)(2,1)S(1)}, u32[]{:S(2)}, u32[]{:S(2)}) %collective-permute-start.11) | collective-permute-done | bytes 393248 | tf_op jit(solution)/shard_map/ppermute | solution.py:34
  79.2 3.6 %collective-permute-done.12 = bf16[128,1536]{1,0:T(8,128)(2,1)S(1)} collective-permute-done((bf16[128,1536]{1,0:T(8,128)(2,1)}, bf16[128,1536]{1,0:T(8,128)(2,1)S(1)}, u32[]{:S(2)}, u32[]{:S(2)}) %collective-permute-start.12) | collective-permute-done | bytes 393248 | tf_op jit(solution)/shard_map/ppermute | solution.py:34
  86.1 1.9 collective-permute-start.15
  89.5 2.1 copy-done.2
  91.6 2.1 copy-done.4
  93.7 2.1 copy-done.5
  95.8 4.8 %expert_block.4 = (bf16[256,1536]{1,0:T(8,128)(2,1)S(1)}, bf16[256,1536]{1,0:T(8,128)(2,1)S(1)}, bf16[2,8,1536]{2,1,0:T(8,128)(2,1)S(1)}) custom-call(bf16[256,1536]{1,0:T(8,128)(2,1)S(1)} %bitcast.183, bf16[256,1536]{1,0:T(8,128)(2,1)S(1)} %bitcast.184, s32[2]{0:T(128)S(1)} %get-tuple-element.164.first, f32[4,2,8,256]{3,2,1,0:T(8,128)S(1)} %bitcast.189, ...), custom_call_target="tpu_custom_call" | custom-call | flops 7516192768 | bytes 12582912 | tf_op jit(solution)/shard_map/expert_block/pallas_call | solution.py:275
  100.7 2.7 %collective-permute-start.19 = (bf16[2,128,1536]{2,1,0:T(8,128)(2,1)S(1)}, bf16[2,128,1536]{2,1,0:T(8,128)(2,1)S(1)}, u32[]{:S(2)}, u32[]{:S(2)}) collective-permute-start(bf16[2,128,1536]{2,1,0:T(8,128)(2,1)S(1)} %collective-permute-done.15), channel_id=1, source_target_pairs={{0,12},{1,13},{2,14},{3,15},{4,0},{5,1},{6,2},{7,3},{8,4},{9,5},{1... | collective-permute-start | bytes 2359304 | tf_op jit(solution)/shard_map/ppermute | solution.py:34
  103.4 4.8 %expert_block.5 = (bf16[256,1536]{1,0:T(8,128)(2,1)S(1)}, bf16[256,1536]{1,0:T(8,128)(2,1)S(1)}, bf16[2,8,1536]{2,1,0:T(8,128)(2,1)S(1)}) custom-call(bf16[256,1536]{1,0:T(8,128)(2,1)S(1)} %bitcast.203, bf16[256,1536]{1,0:T(8,128)(2,1)S(1)} %bitcast.204, s32[2]{0:T(128)S(1)} %get-tuple-element.165.first, f32[4,2,8,256]{3,2,1,0:T(8,128)S(1)} %bitcast.190, ...), custom_call_target="tpu_custom_call" | custom-call | flops 7516192768 | bytes 12582912 | tf_op jit(solution)/shard_map/expert_block/pallas_call | solution.py:275
  108.2 4.8 %expert_block.6 = (bf16[256,1536]{1,0:T(8,128)(2,1)S(1)}, bf16[256,1536]{1,0:T(8,128)(2,1)S(1)}, bf16[2,8,1536]{2,1,0:T(8,128)(2,1)S(1)}) custom-call(bf16[256,1536]{1,0:T(8,128)(2,1)S(1)} %bitcast.210, bf16[256,1536]{1,0:T(8,128)(2,1)S(1)} %bitcast.209, s32[2]{0:T(128)S(1)} %get-tuple-element.166.first, f32[4,2,8,256]{3,2,1,0:T(8,128)S(1)} %bitcast.191, ...), custom_call_target="tpu_custom_call" | custom-call | flops 7516192768 | bytes 12582912 | tf_op jit(solution)/shard_map/expert_block/pallas_call | solution.py:275
  114.3 2.8 %collective-permute-start.20 = (bf16[2,128,1536]{2,1,0:T(8,128)(2,1)S(1)}, bf16[2,128,1536]{2,1,0:T(8,128)(2,1)S(1)}, u32[]{:S(2)}, u32[]{:S(2)}) collective-permute-start(bf16[2,128,1536]{2,1,0:T(8,128)(2,1)S(1)} %bitcast.208), channel_id=1, source_target_pairs={{0,12},{1,13},{2,14},{3,15},{4,0},{5,1},{6,2},{7,3},{8,4},{9,5},{1... | collective-permute-start | bytes 2359304 | tf_op jit(solution)/shard_map/ppermute | solution.py:34
  117.2 4.8 %expert_block.7 = (bf16[256,1536]{1,0:T(8,128)(2,1)S(1)}, bf16[256,1536]{1,0:T(8,128)(2,1)S(1)}, bf16[2,8,1536]{2,1,0:T(8,128)(2,1)S(1)}) custom-call(bf16[256,1536]{1,0:T(8,128)(2,1)S(1)} %bitcast.205, bf16[256,1536]{1,0:T(8,128)(2,1)S(1)} %bitcast.207, s32[2]{0:T(128)S(1)} %get-tuple-element.167.first, f32[4,2,8,256]{3,2,1,0:T(8,128)S(1)} %bitcast.192, ...), custom_call_target="tpu_custom_call" | custom-call | flops 7516192768 | bytes 12582912 | tf_op jit(solution)/shard_map/expert_block/pallas_call | solution.py:275
  123.8 2.3 %collective-permute-done.20 = bf16[2,128,1536]{2,1,0:T(8,128)(2,1)S(1)} collective-permute-done((bf16[2,128,1536]{2,1,0:T(8,128)(2,1)S(1)}, bf16[2,128,1536]{2,1,0:T(8,128)(2,1)S(1)}, u32[]{:S(2)}, u32[]{:S(2)}) %collective-permute-start.20) | collective-permute-done | bytes 786464 | tf_op jit(solution)/shard_map/ppermute | solution.py:34
  126.1 3.4 %collective-permute-done.21 = bf16[2,128,1536]{2,1,0:T(8,128)(2,1)S(1)} collective-permute-done((bf16[2,128,1536]{2,1,0:T(8,128)(2,1)S(1)}, bf16[2,128,1536]{2,1,0:T(8,128)(2,1)S(1)}, u32[]{:S(2)}, u32[]{:S(2)}) %collective-permute-start.21) | collective-permute-done | bytes 786464 | tf_op jit(solution)/shard_map/ppermute | solution.py:34
  133.2 3.5 %all-to-all-start.1 = ((bf16[16,3,1536]{2,1,0:T(4,128)(2,1)}), bf16[16,3,1536]{2,1,0:T(4,128)(2,1)S(1)}, u32[]{:S(2)}, u32[]{:S(2)}) async-start(bf16[16,3,1536]{2,1,0:T(4,128)(2,1)} %reshape.478), calls=%async_computation.1 | async-start | bytes 393216 | tf_op jit(solution)/shard_map/all_to_all | solution.py:423
  139.5 4.4 %all-to-all-done.1 = bf16[16,3,1536]{2,1,0:T(4,128)(2,1)S(1)} async-done(((bf16[16,3,1536]{2,1,0:T(4,128)(2,1)}), bf16[16,3,1536]{2,1,0:T(4,128)(2,1)S(1)}, u32[]{:S(2)}, u32[]{:S(2)}) %all-to-all-start.1) | async-done | bytes 147488 | tf_op jit(solution)/shard_map/all_to_all | solution.py:423
  145.5 14.2 %all_to_all.29 = bf16[8,3,192]{2,1,0:T(4,128)(2,1)S(1)} all-to-all(bf16[8,3,192]{2,1,0:T(4,128)(2,1)S(1)} %bitcast.228), channel_id=1, replica_groups=mesh['seq'=8,'grp'=16] {'seq'}, dimensions={0} | all-to-all | bytes 18432 | tf_op jit(solution)/shard_map/all_to_all | solution.py:429
  159.8 2.2 %add_convert_fusion.1 = bf16[2,128,1536]{2,1,0:T(8,128)(2,1)} fusion(bf16[2,128,1536]{2,1,0:T(8,128)(2,1)} %collective-permute-done.23, bf16[2,128,1536]{2,1,0:T(8,128)(2,1)S(1)} %bitcast.187), kind=kLoop, calls=%fused_computation.8 | loop fusion | flops 1572864 | bytes 2359296 | tf_op jit(solution)/shard_map/convert_element_type | solution.py:418
  162.0 2.2 %add_convert_fusion.2 = bf16[2,128,1536]{2,1,0:T(8,128)(2,1)} fusion(bf16[2,128,1536]{2,1,0:T(8,128)(2,1)} %collective-permute-done.22, bf16[2,128,1536]{2,1,0:T(8,128)(2,1)S(1)} %bitcast.186), kind=kLoop, calls=%fused_computation.9 | loop fusion | flops 1572864 | bytes 2359296 | tf_op jit(solution)/shard_map/convert_element_type | solution.py:417
  165.3 5.2 %all-to-all-start.3 = ((bf16[128,3,192]{2,1,0:T(4,128)(2,1)}), bf16[128,3,192]{2,1,0:T(4,128)(2,1)S(1)}, u32[]{:S(2)}, u32[]{:S(2)}) async-start(bf16[128,3,192]{2,1,0:T(4,128)(2,1)} %broadcast_in_dim.217), calls=%async_computation.3 | async-start | bytes 524288 | tf_op jit(solution)/shard_map/all_to_all | solution.py:432
  170.5 2.7 %collective-permute-start.25 = (bf16[2,128,1536]{2,1,0:T(8,128)(2,1)}, bf16[2,128,1536]{2,1,0:T(8,128)(2,1)}, u32[]{:S(2)}, u32[]{:S(2)}) collective-permute-start(bf16[2,128,1536]{2,1,0:T(8,128)(2,1)} %add_convert_fusion.1), channel_id=1, source_target_pairs={{0,12},{1,13},{2,14},{3,15},{4,0},{5,1},{6,2},{7,3},{8,4},{9,5},{1... | collective-permute-start | bytes 2359304 | tf_op jit(solution)/shard_map/ppermute | solution.py:34
  173.2 8.7 %all-to-all-done.3 = bf16[128,3,192]{2,1,0:T(4,128)(2,1)S(1)} async-done(((bf16[128,3,192]{2,1,0:T(4,128)(2,1)}), bf16[128,3,192]{2,1,0:T(4,128)(2,1)S(1)}, u32[]{:S(2)}, u32[]{:S(2)}) %all-to-all-start.3) | async-done | bytes 147488 | tf_op jit(solution)/shard_map/all_to_all | solution.py:432
  188.7 8.1 %all-to-all-start.4 = ((f32[128,1,128]{2,1,0:T(1,128)}), f32[128,1,128]{2,1,0:T(1,128)S(1)}, u32[]{:S(2)}, u32[]{:S(2)}) async-start(f32[128,1,128]{2,1,0:T(1,128)} %broadcast_in_dim.220), calls=%async_computation.4 | async-start | bytes 131072 | tf_op jit(solution)/shard_map/all_to_all | solution.py:448
  201.7 4.9 %all-to-all-done.4 = f32[128,1,128]{2,1,0:T(1,128)S(1)} async-done(((f32[128,1,128]{2,1,0:T(1,128)}), f32[128,1,128]{2,1,0:T(1,128)S(1)}, u32[]{:S(2)}, u32[]{:S(2)}) %all-to-all-start.4) | async-done | bytes 65568 | tf_op jit(solution)/shard_map/all_to_all | solution.py:448
  209.6 2.3 %collective-permute-done.28 = bf16[128,1536]{1,0:T(8,128)(2,1)} collective-permute-done((bf16[128,1536]{1,0:T(8,128)(2,1)}, bf16[128,1536]{1,0:T(8,128)(2,1)}, u32[]{:S(2)}, u32[]{:S(2)}) %collective-permute-start.28) | collective-permute-done | bytes 393248 | tf_op jit(solution)/shard_map/ppermute | solution.py:34
  211.8 2.0 fusion.8
  (226 shorter events, 57.3 us)
Async XLA Ops:
  6.0 28.0 %collective-permute-start = (bf16[128,1536]{1,0:T(8,128)(2,1)S(1)}, bf16[128,1536]{1,0:T(8,128)(2,1)S(1)}, u32[]{:S(2)}, u32[]{:S(2)}) collective-permute-start(bf16[128,1536]{1,0:T(8,128)(2,1)S(1)} %bitcast.213), channel_id=1, source_target_pairs={{0,32},{16,48},{32,64},{48,80},{64,96},{80,112},{1,33},{17,49},{33... | collective-permute-start | bytes 1179656 | tf_op jit(solution)/shard_map/ppermute | solution.py:334
  10.0 24.1 %collective-permute-start.1 = (bf16[128,1536]{1,0:T(8,128)(2,1)S(1)}, bf16[128,1536]{1,0:T(8,128)(2,1)S(1)}, u32[]{:S(2)}, u32[]{:S(2)}) collective-permute-start(bf16[128,1536]{1,0:T(8,128)(2,1)S(1)} %bitcast.214), channel_id=1, source_target_pairs={{0,64},{16,80},{32,96},{48,112},{1,65},{17,81},{33,97},{49,113},{2... | collective-permute-start | bytes 1179656 | tf_op jit(solution)/shard_map/ppermute | solution.py:335
  14.4 21.5 %all-to-all-start = ((bf16[16,16,1536]{2,1,0:T(8,128)(2,1)}), bf16[16,16,1536]{2,1,0:T(8,128)(2,1)S(1)}, u32[]{:S(2)}, u32[]{:S(2)}) async-start(bf16[16,16,1536]{2,1,0:T(8,128)(2,1)} %pad_maximum_fusion), calls=%async_computation | async-start | bytes 1572864 | tf_op jit(solution)/shard_map/all_to_all | solution.py:333
  34.2 14.3 %collective-permute-start.2 = (bf16[128,1536]{1,0:T(8,128)(2,1)S(1)}, bf16[128,1536]{1,0:T(8,128)(2,1)S(1)}, u32[]{:S(2)}, u32[]{:S(2)}) collective-permute-start(bf16[128,1536]{1,0:T(8,128)(2,1)S(1)} %get-tuple-element.134), channel_id=1, source_target_pairs={{0,16},{16,0},{32,48},{48,32},{64,80},{80,64},{96,112},{112,96},{1... | collective-permute-start | bytes 1179656 | tf_op jit(solution)/shard_map/ppermute | solution.py:38
  35.8 12.8 %collective-permute-start.3 = (bf16[128,1536]{1,0:T(8,128)(2,1)S(1)}, bf16[128,1536]{1,0:T(8,128)(2,1)}, u32[]{:S(2)}, u32[]{:S(2)}) collective-permute-start(bf16[128,1536]{1,0:T(8,128)(2,1)S(1)} %get-tuple-element.133), channel_id=1, source_target_pairs={{0,16},{16,0},{32,48},{48,32},{64,80},{80,64},{96,112},{112,96},{1... | collective-permute-start | bytes 1179656 | tf_op jit(solution)/shard_map/ppermute | solution.py:38
  36.4 5.3 %collective-permute-start.4 = (bf16[48,1536]{1,0:T(8,128)(2,1)S(1)}, bf16[48,1536]{1,0:T(8,128)(2,1)S(1)}, u32[]{:S(2)}, u32[]{:S(2)}) collective-permute-start(bf16[48,1536]{1,0:T(8,128)(2,1)S(1)} %bitcast.222), channel_id=1, source_target_pairs={{0,32},{16,48},{32,64},{48,80},{64,96},{80,112},{96,0},{112,16},{1... | collective-permute-start | bytes 442376 | tf_op jit(solution)/shard_map/ppermute | solution.py:369
  36.5 6.4 %collective-permute-start.5 = (bf16[48,1536]{1,0:T(8,128)(2,1)S(1)}, bf16[48,1536]{1,0:T(8,128)(2,1)S(1)}, u32[]{:S(2)}, u32[]{:S(2)}) collective-permute-start(bf16[48,1536]{1,0:T(8,128)(2,1)S(1)} %bitcast.223), channel_id=1, source_target_pairs={{0,96},{16,112},{32,0},{48,16},{64,32},{80,48},{96,64},{112,80},{1... | collective-permute-start | bytes 442376 | tf_op jit(solution)/shard_map/ppermute | solution.py:369
  39.2 5.6 %collective-permute-start.6 = (bf16[48,1536]{1,0:T(8,128)(2,1)S(1)}, bf16[48,1536]{1,0:T(8,128)(2,1)S(1)}, u32[]{:S(2)}, u32[]{:S(2)}) collective-permute-start(bf16[48,1536]{1,0:T(8,128)(2,1)S(1)} %bitcast.224), channel_id=1, source_target_pairs={{0,64},{16,80},{32,96},{48,112},{64,0},{80,16},{96,32},{112,48},{1... | collective-permute-start | bytes 442376 | tf_op jit(solution)/shard_map/ppermute | solution.py:369
  44.8 4.2 %collective-permute-start.10 = (bf16[48,1536]{1,0:T(8,128)(2,1)S(1)}, bf16[48,1536]{1,0:T(8,128)(2,1)S(1)}, u32[]{:S(2)}, u32[]{:S(2)}) collective-permute-start(bf16[48,1536]{1,0:T(8,128)(2,1)S(1)} %collective-permute-done.6.refs_8_), channel_id=1, source_target_pairs={{0,16},{16,0},{32,48},{48,32},{64,80},{80,64},{96,112},{112,96},{1... | collective-permute-start | bytes 442376 | tf_op jit(solution)/shard_map/ppermute | solution.py:38
  48.0 1.6 collective-permute-start.8
  48.5 2.2 %collective-permute-start.9 = (bf16[48,1536]{1,0:T(8,128)(2,1)S(1)}, bf16[48,1536]{1,0:T(8,128)(2,1)}, u32[]{:S(2)}, u32[]{:S(2)}) collective-permute-start(bf16[48,1536]{1,0:T(8,128)(2,1)S(1)} %collective-permute-done.5.refs_7_), channel_id=1, source_target_pairs={{0,16},{16,0},{32,48},{48,32},{64,80},{80,64},{96,112},{112,96},{1... | collective-permute-start | bytes 442376 | tf_op jit(solution)/shard_map/ppermute | solution.py:38
  70.8 8.4 %collective-permute-start.11 = (bf16[128,1536]{1,0:T(8,128)(2,1)}, bf16[128,1536]{1,0:T(8,128)(2,1)S(1)}, u32[]{:S(2)}, u32[]{:S(2)}) collective-permute-start(bf16[128,1536]{1,0:T(8,128)(2,1)} %get-tuple-element.76), channel_id=1, source_target_pairs={{0,1},{1,2},{2,3},{3,0},{4,5},{5,6},{6,7},{7,4},{8,9},{9,10},{10,1... | collective-permute-start | bytes 1179656 | tf_op jit(solution)/shard_map/ppermute | solution.py:34
  71.7 11.1 %collective-permute-start.12 = (bf16[128,1536]{1,0:T(8,128)(2,1)}, bf16[128,1536]{1,0:T(8,128)(2,1)S(1)}, u32[]{:S(2)}, u32[]{:S(2)}) collective-permute-start(bf16[128,1536]{1,0:T(8,128)(2,1)} %get-tuple-element.76), channel_id=1, source_target_pairs={{0,3},{1,0},{2,1},{3,2},{4,7},{5,4},{6,5},{7,6},{8,11},{9,8},{10,9... | collective-permute-start | bytes 1179656 | tf_op jit(solution)/shard_map/ppermute | solution.py:34
  73.5 10.4 %collective-permute-start.13 = (bf16[128,1536]{1,0:T(8,128)(2,1)}, bf16[128,1536]{1,0:T(8,128)(2,1)S(1)}, u32[]{:S(2)}, u32[]{:S(2)}) collective-permute-start(bf16[128,1536]{1,0:T(8,128)(2,1)} %get-tuple-element.76), channel_id=1, source_target_pairs={{0,2},{1,3},{2,0},{3,1},{4,6},{5,7},{6,4},{7,5},{8,10},{9,11},{10,... | collective-permute-start | bytes 1179656 | tf_op jit(solution)/shard_map/ppermute | solution.py:34
  85.1 15.6 %collective-permute-start.14 = (bf16[2,128,1536]{2,1,0:T(8,128)(2,1)S(1)}, bf16[2,128,1536]{2,1,0:T(8,128)(2,1)S(1)}, u32[]{:S(2)}, u32[]{:S(2)}) collective-permute-start(bf16[2,128,1536]{2,1,0:T(8,128)(2,1)S(1)} %pad_maximum_fusion.1), channel_id=1, source_target_pairs={{0,4},{1,5},{2,6},{3,7},{4,8},{5,9},{6,10},{7,11},{8,12},{9,13},{1... | collective-permute-start | bytes 2359304 | tf_op jit(solution)/shard_map/ppermute | solution.py:34
  86.1 14.6 %collective-permute-start.15 = (bf16[2,128,1536]{2,1,0:T(8,128)(2,1)S(1)}, bf16[2,128,1536]{2,1,0:T(8,128)(2,1)S(1)}, u32[]{:S(2)}, u32[]{:S(2)}) collective-permute-start(bf16[2,128,1536]{2,1,0:T(8,128)(2,1)S(1)} %pad_maximum_fusion.2), channel_id=1, source_target_pairs={{0,12},{1,13},{2,14},{3,15},{4,0},{5,1},{6,2},{7,3},{8,4},{9,5},{1... | collective-permute-start | bytes 2359304 | tf_op jit(solution)/shard_map/ppermute | solution.py:34
  88.0 20.2 %collective-permute-start.17 = (bf16[2,128,1536]{2,1,0:T(8,128)(2,1)S(1)}, bf16[2,128,1536]{2,1,0:T(8,128)(2,1)S(1)}, u32[]{:S(2)}, u32[]{:S(2)}) collective-permute-start(bf16[2,128,1536]{2,1,0:T(8,128)(2,1)S(1)} %pad_maximum_fusion.1), channel_id=1, source_target_pairs={{0,12},{1,13},{2,14},{3,15},{4,0},{5,1},{6,2},{7,3},{8,4},{9,5},{1... | collective-permute-start | bytes 2359304 | tf_op jit(solution)/shard_map/ppermute | solution.py:34
  89.2 19.0 %collective-permute-start.16 = (bf16[2,128,1536]{2,1,0:T(8,128)(2,1)S(1)}, bf16[2,128,1536]{2,1,0:T(8,128)(2,1)S(1)}, u32[]{:S(2)}, u32[]{:S(2)}) collective-permute-start(bf16[2,128,1536]{2,1,0:T(8,128)(2,1)S(1)} %pad_maximum_fusion.2), channel_id=1, source_target_pairs={{0,4},{1,5},{2,6},{3,7},{4,8},{5,9},{6,10},{7,11},{8,12},{9,13},{1... | collective-permute-start | bytes 2359304 | tf_op jit(solution)/shard_map/ppermute | solution.py:34
  100.6 13.7 %collective-permute-start.18 = (bf16[2,128,1536]{2,1,0:T(8,128)(2,1)S(1)}, bf16[2,128,1536]{2,1,0:T(8,128)(2,1)S(1)}, u32[]{:S(2)}, u32[]{:S(2)}) collective-permute-start(bf16[2,128,1536]{2,1,0:T(8,128)(2,1)S(1)} %collective-permute-done.14), channel_id=1, source_target_pairs={{0,4},{1,5},{2,6},{3,7},{4,8},{5,9},{6,10},{7,11},{8,12},{9,13},{1... | collective-permute-start | bytes 2359304 | tf_op jit(solution)/shard_map/ppermute | solution.py:34
  100.7 13.6 %collective-permute-start.19 = (bf16[2,128,1536]{2,1,0:T(8,128)(2,1)S(1)}, bf16[2,128,1536]{2,1,0:T(8,128)(2,1)S(1)}, u32[]{:S(2)}, u32[]{:S(2)}) collective-permute-start(bf16[2,128,1536]{2,1,0:T(8,128)(2,1)S(1)} %collective-permute-done.15), channel_id=1, source_target_pairs={{0,12},{1,13},{2,14},{3,15},{4,0},{5,1},{6,2},{7,3},{8,4},{9,5},{1... | collective-permute-start | bytes 2359304 | tf_op jit(solution)/shard_map/ppermute | solution.py:34
  114.3 11.8 %collective-permute-start.20 = (bf16[2,128,1536]{2,1,0:T(8,128)(2,1)S(1)}, bf16[2,128,1536]{2,1,0:T(8,128)(2,1)S(1)}, u32[]{:S(2)}, u32[]{:S(2)}) collective-permute-start(bf16[2,128,1536]{2,1,0:T(8,128)(2,1)S(1)} %bitcast.208), channel_id=1, source_target_pairs={{0,12},{1,13},{2,14},{3,15},{4,0},{5,1},{6,2},{7,3},{8,4},{9,5},{1... | collective-permute-start | bytes 2359304 | tf_op jit(solution)/shard_map/ppermute | solution.py:34
  117.1 12.3 %collective-permute-start.21 = (bf16[2,128,1536]{2,1,0:T(8,128)(2,1)S(1)}, bf16[2,128,1536]{2,1,0:T(8,128)(2,1)S(1)}, u32[]{:S(2)}, u32[]{:S(2)}) collective-permute-start(bf16[2,128,1536]{2,1,0:T(8,128)(2,1)S(1)} %bitcast.206), channel_id=1, source_target_pairs={{0,4},{1,5},{2,6},{3,7},{4,8},{5,9},{6,10},{7,11},{8,12},{9,13},{1... | collective-permute-start | bytes 2359304 | tf_op jit(solution)/shard_map/ppermute | solution.py:34
  133.2 10.7 %all-to-all-start.1 = ((bf16[16,3,1536]{2,1,0:T(4,128)(2,1)}), bf16[16,3,1536]{2,1,0:T(4,128)(2,1)S(1)}, u32[]{:S(2)}, u32[]{:S(2)}) async-start(bf16[16,3,1536]{2,1,0:T(4,128)(2,1)} %reshape.478), calls=%async_computation.1 | async-start | bytes 393216 | tf_op jit(solution)/shard_map/all_to_all | solution.py:423
  136.7 23.1 %collective-permute-start.22 = (bf16[2,128,1536]{2,1,0:T(8,128)(2,1)}, bf16[2,128,1536]{2,1,0:T(8,128)(2,1)}, u32[]{:S(2)}, u32[]{:S(2)}) collective-permute-start(bf16[2,128,1536]{2,1,0:T(8,128)(2,1)} %bitcast.202), channel_id=1, source_target_pairs={{0,4},{1,5},{2,6},{3,7},{4,8},{5,9},{6,10},{7,11},{8,12},{9,13},{1... | collective-permute-start | bytes 2359304 | tf_op jit(solution)/shard_map/ppermute | solution.py:34
  138.1 21.7 %collective-permute-start.23 = (bf16[2,128,1536]{2,1,0:T(8,128)(2,1)}, bf16[2,128,1536]{2,1,0:T(8,128)(2,1)}, u32[]{:S(2)}, u32[]{:S(2)}) collective-permute-start(bf16[2,128,1536]{2,1,0:T(8,128)(2,1)} %bitcast.201), channel_id=1, source_target_pairs={{0,12},{1,13},{2,14},{3,15},{4,0},{5,1},{6,2},{7,3},{8,4},{9,5},{1... | collective-permute-start | bytes 2359304 | tf_op jit(solution)/shard_map/ppermute | solution.py:34
  164.2 18.9 %collective-permute-start.24 = (bf16[2,128,1536]{2,1,0:T(8,128)(2,1)}, bf16[2,128,1536]{2,1,0:T(8,128)(2,1)}, u32[]{:S(2)}, u32[]{:S(2)}) collective-permute-start(bf16[2,128,1536]{2,1,0:T(8,128)(2,1)} %add_convert_fusion.2), channel_id=1, source_target_pairs={{0,4},{1,5},{2,6},{3,7},{4,8},{5,9},{6,10},{7,11},{8,12},{9,13},{1... | collective-permute-start | bytes 2359304 | tf_op jit(solution)/shard_map/ppermute | solution.py:34
  165.3 16.7 %all-to-all-start.3 = ((bf16[128,3,192]{2,1,0:T(4,128)(2,1)}), bf16[128,3,192]{2,1,0:T(4,128)(2,1)S(1)}, u32[]{:S(2)}, u32[]{:S(2)}) async-start(bf16[128,3,192]{2,1,0:T(4,128)(2,1)} %broadcast_in_dim.217), calls=%async_computation.3 | async-start | bytes 524288 | tf_op jit(solution)/shard_map/all_to_all | solution.py:432
  170.5 15.2 %collective-permute-start.25 = (bf16[2,128,1536]{2,1,0:T(8,128)(2,1)}, bf16[2,128,1536]{2,1,0:T(8,128)(2,1)}, u32[]{:S(2)}, u32[]{:S(2)}) collective-permute-start(bf16[2,128,1536]{2,1,0:T(8,128)(2,1)} %add_convert_fusion.1), channel_id=1, source_target_pairs={{0,12},{1,13},{2,14},{3,15},{4,0},{5,1},{6,2},{7,3},{8,4},{9,5},{1... | collective-permute-start | bytes 2359304 | tf_op jit(solution)/shard_map/ppermute | solution.py:34
  188.7 17.9 %all-to-all-start.4 = ((f32[128,1,128]{2,1,0:T(1,128)}), f32[128,1,128]{2,1,0:T(1,128)S(1)}, u32[]{:S(2)}, u32[]{:S(2)}) async-start(f32[128,1,128]{2,1,0:T(1,128)} %broadcast_in_dim.220), calls=%async_computation.4 | async-start | bytes 131072 | tf_op jit(solution)/shard_map/all_to_all | solution.py:448
  196.9 10.8 %collective-permute-start.26 = (bf16[128,1536]{1,0:T(8,128)(2,1)}, bf16[128,1536]{1,0:T(8,128)(2,1)S(1)}, u32[]{:S(2)}, u32[]{:S(2)}) collective-permute-start(bf16[128,1536]{1,0:T(8,128)(2,1)} %get-tuple-element.117), channel_id=1, source_target_pairs={{0,1},{1,2},{2,3},{3,0},{4,5},{5,6},{6,7},{7,4},{8,9},{9,10},{10,1... | collective-permute-start | bytes 1179656 | tf_op jit(solution)/shard_map/ppermute | solution.py:34
  198.5 11.1 %collective-permute-start.27 = (bf16[128,1536]{1,0:T(8,128)(2,1)S(1)}, bf16[128,1536]{1,0:T(8,128)(2,1)S(1)}, u32[]{:S(2)}, u32[]{:S(2)}) collective-permute-start(bf16[128,1536]{1,0:T(8,128)(2,1)S(1)} %copy-done.14), channel_id=1, source_target_pairs={{0,3},{1,0},{2,1},{3,2},{4,7},{5,4},{6,5},{7,6},{8,11},{9,8},{10,9... | collective-permute-start | bytes 1179656 | tf_op jit(solution)/shard_map/ppermute | solution.py:34
  200.3 11.5 %collective-permute-start.28 = (bf16[128,1536]{1,0:T(8,128)(2,1)}, bf16[128,1536]{1,0:T(8,128)(2,1)}, u32[]{:S(2)}, u32[]{:S(2)}) collective-permute-start(bf16[128,1536]{1,0:T(8,128)(2,1)} %get-tuple-element.119), channel_id=1, source_target_pairs={{0,2},{1,3},{2,0},{3,1},{4,6},{5,7},{6,4},{7,5},{8,10},{9,11},{10,... | collective-permute-start | bytes 1179656 | tf_op jit(solution)/shard_map/ppermute | solution.py:34
  (39 other events, 354.8 us)

commit v9 on v6

--- a/solution.py
+++ b/solution.py
@@ -383,9 +383,16 @@
     route_in = jnp.concatenate([route_in, jnp.zeros((8, 2, 2, count), F32)], axis=2)
     route_in = route_in.transpose(0, 2, 1, 3).reshape(4, 2, 8, 2 * count)
     odd = (grp % 2).astype(jnp.int32)
+    slot = jnp.arange(8, dtype=jnp.int32)
+    which = (slot[None, :] % 3 == jnp.arange(3, dtype=jnp.int32)[:, None]) & (slot[None, :] < 6)
+    pairs = order.reshape(8, 2, 16)
+    chosen = jnp.where((slot < 3)[None, None, :], pairs[:, 0].T[:, :, None],
+                       pairs[:, 1].T[:, :, None])
+    spread = jnp.where(which[None, :, None, :], chosen[:, None], 0.0)
+    spread = spread.reshape(48, 64).astype(BF)
     weights = (gate_weight, up_weight, down_weight)
 
-    turn, route_in = lax.optimization_barrier((turn, route_in))
+    turn, route_in, spread = lax.optimization_barrier((turn, route_in, spread))
     adapt = turn + [partner(piece) for piece in turn]
     mixed, moe_in = attention(tok, adapt, place, gain, gain_moe, cosine, sine, query_weight,
                               key_weight, value_weight, output_weight)
@@ -424,9 +431,9 @@
     combined = own_lo[0] + wide(line[0]) + wide(line[1]) + wide(line[2])
     hidden_out = (mixed.astype(F32) + combined).astype(BF)
 
-    last = jnp.stack([last_own, last_first, last_second, last_far])[:, :, :6]
-    last = jnp.einsum("jg,jr->gr", order.astype(BF), last.reshape(16, 3 * width),
-                      preferred_element_type=F32).astype(BF)
+    last = jnp.concatenate([piece.reshape(16, width) for piece in (
+        last_own, last_first, last_second, last_far)])
+    last = jnp.dot(spread, last, preferred_element_type=F32).astype(BF)
     last = lax.all_to_all(last.reshape(16, 3, width), "grp", 0, 0, tiled=True)
     last = jnp.sum(last.astype(F32), axis=0) + jnp.dot(
         marks.astype(BF), mixed, preferred_element_type=F32)

time: 207 us -> 206 us (level)
  transfers between devices with their start and end apart: 33 -> 33, of which waited for: 14 -> 14; matrix products, arithmetic and copies ran while one was open for 10% -> 11% of each run, Pallas kernels for 7% -> 7%
where the time goes in v9:
time: 206 us; the launch traced here: 204 us
  starting transfers between devices  64.3 us (31%)
  Pallas kernels  39.3 us (19%)
  waiting for transfers between devices  36.2 us (18%)
  local copies, waits for them, and re-layouts  21.9 us (11%)
  other arithmetic  17.3 us (8%)
  blocking collectives  14.7 us (7%)
  between operations  7.16 us (3%)
  matrix products  3.6 us (2%)
    ppermute x18, starting transfers between devices, shift(): return lax.ppermute(rows, WHOLE, pairs)  21.5 us
    pallas_call x1, Pallas kernels, attention(): pl.pallas_call(attention_kernel, out_shape=(rows, rows), in_specs=[vm] *...  20 us
    pallas_call x4, Pallas kernels, experts(): pl.pallas_call(expert_kernel, out_shape=(piece, piece, jax.ShapeDtypeStru...  19.2 us
    ppermute x18, waiting for transfers between devices, shift(): return lax.ppermute(rows, WHOLE, pairs)  18.8 us
    all_to_all x1, blocking collectives, body(): lax.all_to_all(jnp.broadcast_to(stats[None], (128, 128)), WHOLE, 0, 0, ti...  14.7 us
    unnamed x70, local copies, waits for them, and re-layouts  11.2 us
    all_to_all x1, starting transfers between devices, body(): mine = lax.all_to_all(split, 'seq', 0, 0, tiled=True)  9.02 us
    all_to_all x1, starting transfers between devices, body(): held = lax.all_to_all(payload, 'grp', 0, 0, tiled=True)  7.78 us
  transfers between devices with their start and end apart: 33, of which 14 were waited for; matrix products, arithmetic and copies ran while one was open for 11% of the time, Pallas kernels for 7%

profile of v9, /device:TPU:1, one launch (start us, length us, event | category | flops | bytes accessed | tf_op | source)
XLA Modules:
  0.0 204.5 jit_solution(2817143984458455551)
XLA Ops:
  6.0 4.1 %collective-permute-start = (bf16[128,1536]{1,0:T(8,128)(2,1)S(1)}, bf16[128,1536]{1,0:T(8,128)(2,1)S(1)}, u32[]{:S(2)}, u32[]{:S(2)}) collective-permute-start(bf16[128,1536]{1,0:T(8,128)(2,1)S(1)} %bitcast.223), channel_id=1, source_target_pairs={{0,32},{16,48},{32,64},{48,80},{64,96},{80,112},{1,33},{17,49},{33... | collective-permute-start | bytes 1179656 | tf_op jit(solution)/shard_map/ppermute | solution.py:334
  10.1 4.4 %collective-permute-start.1 = (bf16[128,1536]{1,0:T(8,128)(2,1)S(1)}, bf16[128,1536]{1,0:T(8,128)(2,1)S(1)}, u32[]{:S(2)}, u32[]{:S(2)}) collective-permute-start(bf16[128,1536]{1,0:T(8,128)(2,1)S(1)} %bitcast.224), channel_id=1, source_target_pairs={{0,64},{16,80},{32,96},{48,112},{1,65},{17,81},{33,97},{49,113},{2... | collective-permute-start | bytes 1179656 | tf_op jit(solution)/shard_map/ppermute | solution.py:335
  14.5 7.8 %all-to-all-start = ((bf16[16,16,1536]{2,1,0:T(8,128)(2,1)}), bf16[16,16,1536]{2,1,0:T(8,128)(2,1)S(1)}, u32[]{:S(2)}, u32[]{:S(2)}) async-start(bf16[16,16,1536]{2,1,0:T(8,128)(2,1)} %pad_maximum_fusion), calls=%async_computation | async-start | bytes 1572864 | tf_op jit(solution)/shard_map/all_to_all | solution.py:333
  37.4 2.7 %collective-permute-start.5 = (bf16[48,1536]{1,0:T(8,128)(2,1)S(1)}, bf16[48,1536]{1,0:T(8,128)(2,1)S(1)}, u32[]{:S(2)}, u32[]{:S(2)}) collective-permute-start(bf16[48,1536]{1,0:T(8,128)(2,1)S(1)} %bitcast.233), channel_id=1, source_target_pairs={{0,96},{16,112},{32,0},{48,16},{64,32},{80,48},{96,64},{112,80},{1... | collective-permute-start | bytes 442376 | tf_op jit(solution)/shard_map/ppermute | solution.py:369
  40.9 2.2 %collective-permute-done.4.refs_6_ = bf16[48,1536]{1,0:T(8,128)(2,1)S(1)} collective-permute-done((bf16[48,1536]{1,0:T(8,128)(2,1)S(1)}, bf16[48,1536]{1,0:T(8,128)(2,1)S(1)}, u32[]{:S(2)}, u32[]{:S(2)}) %collective-permute-start.4) | collective-permute-done | bytes 147488 | tf_op jit(solution)/shard_map/ppermute | solution.py:369
  43.8 1.8 collective-permute-done.6.refs_8_
  45.6 2.4 %collective-permute-start.10 = (bf16[48,1536]{1,0:T(8,128)(2,1)S(1)}, bf16[48,1536]{1,0:T(8,128)(2,1)S(1)}, u32[]{:S(2)}, u32[]{:S(2)}) collective-permute-start(bf16[48,1536]{1,0:T(8,128)(2,1)S(1)} %collective-permute-done.6.refs_8_), channel_id=1, source_target_pairs={{0,16},{16,0},{32,48},{48,32},{64,80},{80,64},{96,112},{112,96},{1... | collective-permute-start | bytes 442376 | tf_op jit(solution)/shard_map/ppermute | solution.py:38
  50.8 20.0 %attention_block.1 = (bf16[128,1536]{1,0:T(8,128)(2,1)}, bf16[128,1536]{1,0:T(8,128)(2,1)}) custom-call(bf16[128,1536]{1,0:T(8,128)(2,1)} %bitcast.222, bf16[128,1536]{1,0:T(8,128)(2,1)} %copy-done.12, bf16[128,1536]{1,0:T(8,128)(2,1)} %copy-done.13, bf16[128,1536]{1,0:T(8,128)(2,1)} %copy-done.25, bf16[128,1536]{1,0:T(8,128)(2,1)} %collective-permute-done.3.refs_4_, ...), custom_call_target="tpu_custom_call" | custom-call | flops 8589934592 | bytes 20971520 | tf_op jit(solution)/shard_map/attention_block/pallas_call | solution.py:192
  70.8 1.9 collective-permute-start.11
  75.7 3.8 %collective-permute-done.11 = bf16[128,1536]{1,0:T(8,128)(2,1)S(1)} collective-permute-done((bf16[128,1536]{1,0:T(8,128)(2,1)}, bf16[128,1536]{1,0:T(8,128)(2,1)S(1)}, u32[]{:S(2)}, u32[]{:S(2)}) %collective-permute-start.11) | collective-permute-done | bytes 393248 | tf_op jit(solution)/shard_map/ppermute | solution.py:34
  79.8 5.1 %collective-permute-done.13 = bf16[128,1536]{1,0:T(8,128)(2,1)S(1)} collective-permute-done((bf16[128,1536]{1,0:T(8,128)(2,1)}, bf16[128,1536]{1,0:T(8,128)(2,1)S(1)}, u32[]{:S(2)}, u32[]{:S(2)}) %collective-permute-start.13) | collective-permute-done | bytes 393248 | tf_op jit(solution)/shard_map/ppermute | solution.py:34
  87.1 1.9 collective-permute-start.15
  90.5 2.1 %copy-done.2 = bf16[5,1536,256]{2,1,0:T(8,128)(2,1)S(1)} copy-done((bf16[5,1536,256]{2,1,0:T(8,128)(2,1)S(1)}, bf16[5,1536,256]{2,1,0:T(8,128)(2,1)}, u32[]{:S(2)}) %copy-start.2) | copy-done | bytes 3932184
  92.6 2.1 %copy-done.4 = bf16[5,1536,256]{2,1,0:T(8,128)(2,1)S(1)} copy-done((bf16[5,1536,256]{2,1,0:T(8,128)(2,1)S(1)}, bf16[5,1536,256]{2,1,0:T(8,128)(2,1)}, u32[]{:S(2)}) %copy-start.4) | copy-done | bytes 3932184
  94.7 2.1 %copy-done.5 = bf16[5,256,1536]{2,1,0:T(8,128)(2,1)S(1)} copy-done((bf16[5,256,1536]{2,1,0:T(8,128)(2,1)S(1)}, bf16[5,256,1536]{2,1,0:T(8,128)(2,1)}, u32[]{:S(2)}) %copy-start.5) | copy-done | bytes 3932184
  96.9 4.8 %expert_block.4 = (bf16[256,1536]{1,0:T(8,128)(2,1)S(1)}, bf16[256,1536]{1,0:T(8,128)(2,1)S(1)}, bf16[2,8,1536]{2,1,0:T(8,128)(2,1)S(1)}) custom-call(bf16[256,1536]{1,0:T(8,128)(2,1)S(1)} %bitcast.193, bf16[256,1536]{1,0:T(8,128)(2,1)S(1)} %bitcast.194, s32[2]{0:T(128)S(1)} %get-tuple-element.152.first, f32[4,2,8,256]{3,2,1,0:T(8,128)S(1)} %bitcast.199, ...), custom_call_target="tpu_custom_call" | custom-call | flops 7516192768 | bytes 12582912 | tf_op jit(solution)/shard_map/expert_block/pallas_call | solution.py:275
  101.8 2.7 %collective-permute-start.19 = (bf16[2,128,1536]{2,1,0:T(8,128)(2,1)S(1)}, bf16[2,128,1536]{2,1,0:T(8,128)(2,1)S(1)}, u32[]{:S(2)}, u32[]{:S(2)}) collective-permute-start(bf16[2,128,1536]{2,1,0:T(8,128)(2,1)S(1)} %collective-permute-done.15), channel_id=1, source_target_pairs={{0,12},{1,13},{2,14},{3,15},{4,0},{5,1},{6,2},{7,3},{8,4},{9,5},{1... | collective-permute-start | bytes 2359304 | tf_op jit(solution)/shard_map/ppermute | solution.py:34
  104.4 4.8 %expert_block.5 = (bf16[256,1536]{1,0:T(8,128)(2,1)S(1)}, bf16[256,1536]{1,0:T(8,128)(2,1)S(1)}, bf16[2,8,1536]{2,1,0:T(8,128)(2,1)S(1)}) custom-call(bf16[256,1536]{1,0:T(8,128)(2,1)S(1)} %bitcast.211, bf16[256,1536]{1,0:T(8,128)(2,1)S(1)} %bitcast.212, s32[2]{0:T(128)S(1)} %get-tuple-element.153.first, f32[4,2,8,256]{3,2,1,0:T(8,128)S(1)} %bitcast.200, ...), custom_call_target="tpu_custom_call" | custom-call | flops 7516192768 | bytes 12582912 | tf_op jit(solution)/shard_map/expert_block/pallas_call | solution.py:275
  111.0 4.8 %expert_block.6 = (bf16[256,1536]{1,0:T(8,128)(2,1)S(1)}, bf16[256,1536]{1,0:T(8,128)(2,1)S(1)}, bf16[2,8,1536]{2,1,0:T(8,128)(2,1)S(1)}) custom-call(bf16[256,1536]{1,0:T(8,128)(2,1)S(1)} %bitcast.215, bf16[256,1536]{1,0:T(8,128)(2,1)S(1)} %bitcast.213, s32[2]{0:T(128)S(1)} %get-tuple-element.154.first, f32[4,2,8,256]{3,2,1,0:T(8,128)S(1)} %bitcast.201, ...), custom_call_target="tpu_custom_call" | custom-call | flops 7516192768 | bytes 12582912 | tf_op jit(solution)/shard_map/expert_block/pallas_call | solution.py:275
  115.9 4.8 %expert_block.7 = (bf16[256,1536]{1,0:T(8,128)(2,1)S(1)}, bf16[256,1536]{1,0:T(8,128)(2,1)S(1)}, bf16[2,8,1536]{2,1,0:T(8,128)(2,1)S(1)}) custom-call(bf16[256,1536]{1,0:T(8,128)(2,1)S(1)} %bitcast.214, bf16[256,1536]{1,0:T(8,128)(2,1)S(1)} %bitcast.216, s32[2]{0:T(128)S(1)} %get-tuple-element.155.first, f32[4,2,8,256]{3,2,1,0:T(8,128)S(1)} %bitcast.202, ...), custom_call_target="tpu_custom_call" | custom-call | flops 7516192768 | bytes 12582912 | tf_op jit(solution)/shard_map/expert_block/pallas_call | solution.py:275
  123.5 4.9 %all-to-all-start.1 = ((bf16[16,3,1536]{2,1,0:T(4,128)(2,1)}), bf16[16,3,1536]{2,1,0:T(4,128)(2,1)S(1)}, u32[]{:S(2)}, u32[]{:S(2)}) async-start(bf16[16,3,1536]{2,1,0:T(4,128)(2,1)} %reshape.569), calls=%async_computation.1 | async-start | bytes 393216 | tf_op jit(solution)/shard_map/all_to_all | solution.py:437
  131.2 4.6 %all-to-all-done.1 = bf16[16,3,1536]{2,1,0:T(4,128)(2,1)S(1)} async-done(((bf16[16,3,1536]{2,1,0:T(4,128)(2,1)}), bf16[16,3,1536]{2,1,0:T(4,128)(2,1)S(1)}, u32[]{:S(2)}, u32[]{:S(2)}) %all-to-all-start.1) | async-done | bytes 147488 | tf_op jit(solution)/shard_map/all_to_all | solution.py:437
  138.0 9.0 %all-to-all-start.2 = ((bf16[8,3,192]{2,1,0:T(4,128)(2,1)}), bf16[8,3,192]{2,1,0:T(4,128)(2,1)S(1)}, u32[]{:S(2)}, u32[]{:S(2)}) async-start(bf16[8,3,192]{2,1,0:T(4,128)(2,1)} %bitcast.190), calls=%async_computation.2 | async-start | bytes 32768 | tf_op jit(solution)/shard_map/all_to_all | solution.py:443
  148.5 3.2 %all-to-all-done.2 = bf16[8,3,192]{2,1,0:T(4,128)(2,1)S(1)} async-done(((bf16[8,3,192]{2,1,0:T(4,128)(2,1)}), bf16[8,3,192]{2,1,0:T(4,128)(2,1)S(1)}, u32[]{:S(2)}, u32[]{:S(2)}) %all-to-all-start.2) | async-done | bytes 9248 | tf_op jit(solution)/shard_map/all_to_all | solution.py:443
  152.4 5.1 %all-to-all-start.3 = ((bf16[128,3,192]{2,1,0:T(4,128)(2,1)}), bf16[128,3,192]{2,1,0:T(4,128)(2,1)}, u32[]{:S(2)}, u32[]{:S(2)}) async-start(bf16[128,3,192]{2,1,0:T(4,128)(2,1)} %broadcast_in_dim.276), calls=%async_computation.3 | async-start | bytes 524288 | tf_op jit(solution)/shard_map/all_to_all | solution.py:445
  157.6 2.2 %add_convert_fusion.1 = bf16[2,128,1536]{2,1,0:T(8,128)(2,1)} fusion(bf16[2,128,1536]{2,1,0:T(8,128)(2,1)} %collective-permute-done.22, bf16[2,128,1536]{2,1,0:T(8,128)(2,1)S(1)} %bitcast.197), kind=kLoop, calls=%fused_computation.8 | loop fusion | flops 1572864 | bytes 2359296 | tf_op jit(solution)/shard_map/convert_element_type | solution.py:422
  161.3 2.2 %add_convert_fusion.2 = bf16[2,128,1536]{2,1,0:T(8,128)(2,1)} fusion(bf16[2,128,1536]{2,1,0:T(8,128)(2,1)} %collective-permute-done.23, bf16[2,128,1536]{2,1,0:T(8,128)(2,1)S(1)} %bitcast.196), kind=kLoop, calls=%fused_computation.9 | loop fusion | flops 1572864 | bytes 2359296 | tf_op jit(solution)/shard_map/convert_element_type | solution.py:423
  164.9 4.0 %all-to-all-done.3 = bf16[128,3,192]{2,1,0:T(4,128)(2,1)} async-done(((bf16[128,3,192]{2,1,0:T(4,128)(2,1)}), bf16[128,3,192]{2,1,0:T(4,128)(2,1)}, u32[]{:S(2)}, u32[]{:S(2)}) %all-to-all-start.3) | async-done | bytes 147488 | tf_op jit(solution)/shard_map/all_to_all | solution.py:445
  170.2 1.7 fusion.52
  172.2 14.7 %all_to_all.29 = f32[128,1,128]{2,1,0:T(1,128)S(1)} all-to-all(f32[128,1,128]{2,1,0:T(1,128)S(1)} %broadcast_in_dim.278), channel_id=1, replica_groups=mesh['seq'=8,'grp'=16] {'seq','grp'}, dimensions={0} | all-to-all | bytes 131072 | tf_op jit(solution)/shard_map/all_to_all | solution.py:452
  193.9 2.2 %collective-permute-done.27 = bf16[128,1536]{1,0:T(8,128)(2,1)S(1)} collective-permute-done((bf16[128,1536]{1,0:T(8,128)(2,1)S(1)}, bf16[128,1536]{1,0:T(8,128)(2,1)S(1)}, u32[]{:S(2)}, u32[]{:S(2)}) %collective-permute-start.27) | collective-permute-done | bytes 393248 | tf_op jit(solution)/shard_map/ppermute | solution.py:34
  196.1 7.4 %collective-permute-done.26 = bf16[128,1536]{1,0:T(8,128)(2,1)S(1)} collective-permute-done((bf16[128,1536]{1,0:T(8,128)(2,1)S(1)}, bf16[128,1536]{1,0:T(8,128)(2,1)S(1)}, u32[]{:S(2)}, u32[]{:S(2)}) %collective-permute-start.26) | collective-permute-done | bytes 393248 | tf_op jit(solution)/shard_map/ppermute | solution.py:34
  (227 shorter events, 49.8 us)
Async XLA Ops:
  6.0 28.9 %collective-permute-start = (bf16[128,1536]{1,0:T(8,128)(2,1)S(1)}, bf16[128,1536]{1,0:T(8,128)(2,1)S(1)}, u32[]{:S(2)}, u32[]{:S(2)}) collective-permute-start(bf16[128,1536]{1,0:T(8,128)(2,1)S(1)} %bitcast.223), channel_id=1, source_target_pairs={{0,32},{16,48},{32,64},{48,80},{64,96},{80,112},{1,33},{17,49},{33... | collective-permute-start | bytes 1179656 | tf_op jit(solution)/shard_map/ppermute | solution.py:334
  10.1 24.9 %collective-permute-start.1 = (bf16[128,1536]{1,0:T(8,128)(2,1)S(1)}, bf16[128,1536]{1,0:T(8,128)(2,1)S(1)}, u32[]{:S(2)}, u32[]{:S(2)}) collective-permute-start(bf16[128,1536]{1,0:T(8,128)(2,1)S(1)} %bitcast.224), channel_id=1, source_target_pairs={{0,64},{16,80},{32,96},{48,112},{1,65},{17,81},{33,97},{49,113},{2... | collective-permute-start | bytes 1179656 | tf_op jit(solution)/shard_map/ppermute | solution.py:335
  14.5 22.2 %all-to-all-start = ((bf16[16,16,1536]{2,1,0:T(8,128)(2,1)}), bf16[16,16,1536]{2,1,0:T(8,128)(2,1)S(1)}, u32[]{:S(2)}, u32[]{:S(2)}) async-start(bf16[16,16,1536]{2,1,0:T(8,128)(2,1)} %pad_maximum_fusion), calls=%async_computation | async-start | bytes 1572864 | tf_op jit(solution)/shard_map/all_to_all | solution.py:333
  35.0 13.6 %collective-permute-start.2 = (bf16[128,1536]{1,0:T(8,128)(2,1)S(1)}, bf16[128,1536]{1,0:T(8,128)(2,1)S(1)}, u32[]{:S(2)}, u32[]{:S(2)}) collective-permute-start(bf16[128,1536]{1,0:T(8,128)(2,1)S(1)} %get-tuple-element.120), channel_id=1, source_target_pairs={{0,16},{16,0},{32,48},{48,32},{64,80},{80,64},{96,112},{112,96},{1... | collective-permute-start | bytes 1179656 | tf_op jit(solution)/shard_map/ppermute | solution.py:38
  36.6 12.1 %collective-permute-start.3 = (bf16[128,1536]{1,0:T(8,128)(2,1)S(1)}, bf16[128,1536]{1,0:T(8,128)(2,1)}, u32[]{:S(2)}, u32[]{:S(2)}) collective-permute-start(bf16[128,1536]{1,0:T(8,128)(2,1)S(1)} %get-tuple-element.119), channel_id=1, source_target_pairs={{0,16},{16,0},{32,48},{48,32},{64,80},{80,64},{96,112},{112,96},{1... | collective-permute-start | bytes 1179656 | tf_op jit(solution)/shard_map/ppermute | solution.py:38
  37.3 5.8 %collective-permute-start.4 = (bf16[48,1536]{1,0:T(8,128)(2,1)S(1)}, bf16[48,1536]{1,0:T(8,128)(2,1)S(1)}, u32[]{:S(2)}, u32[]{:S(2)}) collective-permute-start(bf16[48,1536]{1,0:T(8,128)(2,1)S(1)} %bitcast.232), channel_id=1, source_target_pairs={{0,32},{16,48},{32,64},{48,80},{64,96},{80,112},{96,0},{112,16},{1... | collective-permute-start | bytes 442376 | tf_op jit(solution)/shard_map/ppermute | solution.py:369
  37.4 6.5 %collective-permute-start.5 = (bf16[48,1536]{1,0:T(8,128)(2,1)S(1)}, bf16[48,1536]{1,0:T(8,128)(2,1)S(1)}, u32[]{:S(2)}, u32[]{:S(2)}) collective-permute-start(bf16[48,1536]{1,0:T(8,128)(2,1)S(1)} %bitcast.233), channel_id=1, source_target_pairs={{0,96},{16,112},{32,0},{48,16},{64,32},{80,48},{96,64},{112,80},{1... | collective-permute-start | bytes 442376 | tf_op jit(solution)/shard_map/ppermute | solution.py:369
  40.0 5.6 %collective-permute-start.6 = (bf16[48,1536]{1,0:T(8,128)(2,1)S(1)}, bf16[48,1536]{1,0:T(8,128)(2,1)S(1)}, u32[]{:S(2)}, u32[]{:S(2)}) collective-permute-start(bf16[48,1536]{1,0:T(8,128)(2,1)S(1)} %bitcast.234), channel_id=1, source_target_pairs={{0,64},{16,80},{32,96},{48,112},{64,0},{80,16},{96,32},{112,48},{1... | collective-permute-start | bytes 442376 | tf_op jit(solution)/shard_map/ppermute | solution.py:369
  45.6 3.5 %collective-permute-start.10 = (bf16[48,1536]{1,0:T(8,128)(2,1)S(1)}, bf16[48,1536]{1,0:T(8,128)(2,1)S(1)}, u32[]{:S(2)}, u32[]{:S(2)}) collective-permute-start(bf16[48,1536]{1,0:T(8,128)(2,1)S(1)} %collective-permute-done.6.refs_8_), channel_id=1, source_target_pairs={{0,16},{16,0},{32,48},{48,32},{64,80},{80,64},{96,112},{112,96},{1... | collective-permute-start | bytes 442376 | tf_op jit(solution)/shard_map/ppermute | solution.py:38
  48.1 1.6 collective-permute-start.8
  48.6 2.2 %collective-permute-start.9 = (bf16[48,1536]{1,0:T(8,128)(2,1)S(1)}, bf16[48,1536]{1,0:T(8,128)(2,1)}, u32[]{:S(2)}, u32[]{:S(2)}) collective-permute-start(bf16[48,1536]{1,0:T(8,128)(2,1)S(1)} %collective-permute-done.5.refs_7_), channel_id=1, source_target_pairs={{0,16},{16,0},{32,48},{48,32},{64,80},{80,64},{96,112},{112,96},{1... | collective-permute-start | bytes 442376 | tf_op jit(solution)/shard_map/ppermute | solution.py:38
  70.8 8.8 %collective-permute-start.11 = (bf16[128,1536]{1,0:T(8,128)(2,1)}, bf16[128,1536]{1,0:T(8,128)(2,1)S(1)}, u32[]{:S(2)}, u32[]{:S(2)}) collective-permute-start(bf16[128,1536]{1,0:T(8,128)(2,1)} %get-tuple-element.69), channel_id=1, source_target_pairs={{0,1},{1,2},{2,3},{3,0},{4,5},{5,6},{6,7},{7,4},{8,9},{9,10},{10,1... | collective-permute-start | bytes 1179656 | tf_op jit(solution)/shard_map/ppermute | solution.py:34
  72.7 7.1 %collective-permute-start.12 = (bf16[128,1536]{1,0:T(8,128)(2,1)}, bf16[128,1536]{1,0:T(8,128)(2,1)S(1)}, u32[]{:S(2)}, u32[]{:S(2)}) collective-permute-start(bf16[128,1536]{1,0:T(8,128)(2,1)} %get-tuple-element.69), channel_id=1, source_target_pairs={{0,3},{1,0},{2,1},{3,2},{4,7},{5,4},{6,5},{7,6},{8,11},{9,8},{10,9... | collective-permute-start | bytes 1179656 | tf_op jit(solution)/shard_map/ppermute | solution.py:34
  74.0 11.0 %collective-permute-start.13 = (bf16[128,1536]{1,0:T(8,128)(2,1)}, bf16[128,1536]{1,0:T(8,128)(2,1)S(1)}, u32[]{:S(2)}, u32[]{:S(2)}) collective-permute-start(bf16[128,1536]{1,0:T(8,128)(2,1)} %get-tuple-element.69), channel_id=1, source_target_pairs={{0,2},{1,3},{2,0},{3,1},{4,6},{5,7},{6,4},{7,5},{8,10},{9,11},{10,... | collective-permute-start | bytes 1179656 | tf_op jit(solution)/shard_map/ppermute | solution.py:34
  86.1 15.6 %collective-permute-start.14 = (bf16[2,128,1536]{2,1,0:T(8,128)(2,1)S(1)}, bf16[2,128,1536]{2,1,0:T(8,128)(2,1)S(1)}, u32[]{:S(2)}, u32[]{:S(2)}) collective-permute-start(bf16[2,128,1536]{2,1,0:T(8,128)(2,1)S(1)} %pad_maximum_fusion.1), channel_id=1, source_target_pairs={{0,4},{1,5},{2,6},{3,7},{4,8},{5,9},{6,10},{7,11},{8,12},{9,13},{1... | collective-permute-start | bytes 2359304 | tf_op jit(solution)/shard_map/ppermute | solution.py:34
  87.1 14.6 %collective-permute-start.15 = (bf16[2,128,1536]{2,1,0:T(8,128)(2,1)S(1)}, bf16[2,128,1536]{2,1,0:T(8,128)(2,1)S(1)}, u32[]{:S(2)}, u32[]{:S(2)}) collective-permute-start(bf16[2,128,1536]{2,1,0:T(8,128)(2,1)S(1)} %pad_maximum_fusion.2), channel_id=1, source_target_pairs={{0,12},{1,13},{2,14},{3,15},{4,0},{5,1},{6,2},{7,3},{8,4},{9,5},{1... | collective-permute-start | bytes 2359304 | tf_op jit(solution)/shard_map/ppermute | solution.py:34
  89.0 22.0 %collective-permute-start.17 = (bf16[2,128,1536]{2,1,0:T(8,128)(2,1)S(1)}, bf16[2,128,1536]{2,1,0:T(8,128)(2,1)S(1)}, u32[]{:S(2)}, u32[]{:S(2)}) collective-permute-start(bf16[2,128,1536]{2,1,0:T(8,128)(2,1)S(1)} %pad_maximum_fusion.1), channel_id=1, source_target_pairs={{0,12},{1,13},{2,14},{3,15},{4,0},{5,1},{6,2},{7,3},{8,4},{9,5},{1... | collective-permute-start | bytes 2359304 | tf_op jit(solution)/shard_map/ppermute | solution.py:34
  90.2 20.8 %collective-permute-start.16 = (bf16[2,128,1536]{2,1,0:T(8,128)(2,1)S(1)}, bf16[2,128,1536]{2,1,0:T(8,128)(2,1)S(1)}, u32[]{:S(2)}, u32[]{:S(2)}) collective-permute-start(bf16[2,128,1536]{2,1,0:T(8,128)(2,1)S(1)} %pad_maximum_fusion.2), channel_id=1, source_target_pairs={{0,4},{1,5},{2,6},{3,7},{4,8},{5,9},{6,10},{7,11},{8,12},{9,13},{1... | collective-permute-start | bytes 2359304 | tf_op jit(solution)/shard_map/ppermute | solution.py:34
  101.7 14.2 %collective-permute-start.18 = (bf16[2,128,1536]{2,1,0:T(8,128)(2,1)S(1)}, bf16[2,128,1536]{2,1,0:T(8,128)(2,1)S(1)}, u32[]{:S(2)}, u32[]{:S(2)}) collective-permute-start(bf16[2,128,1536]{2,1,0:T(8,128)(2,1)S(1)} %collective-permute-done.14), channel_id=1, source_target_pairs={{0,4},{1,5},{2,6},{3,7},{4,8},{5,9},{6,10},{7,11},{8,12},{9,13},{1... | collective-permute-start | bytes 2359304 | tf_op jit(solution)/shard_map/ppermute | solution.py:34
  101.8 14.1 %collective-permute-start.19 = (bf16[2,128,1536]{2,1,0:T(8,128)(2,1)S(1)}, bf16[2,128,1536]{2,1,0:T(8,128)(2,1)S(1)}, u32[]{:S(2)}, u32[]{:S(2)}) collective-permute-start(bf16[2,128,1536]{2,1,0:T(8,128)(2,1)S(1)} %collective-permute-done.15), channel_id=1, source_target_pairs={{0,12},{1,13},{2,14},{3,15},{4,0},{5,1},{6,2},{7,3},{8,4},{9,5},{1... | collective-permute-start | bytes 2359304 | tf_op jit(solution)/shard_map/ppermute | solution.py:34
  123.5 12.2 %all-to-all-start.1 = ((bf16[16,3,1536]{2,1,0:T(4,128)(2,1)}), bf16[16,3,1536]{2,1,0:T(4,128)(2,1)S(1)}, u32[]{:S(2)}, u32[]{:S(2)}) async-start(bf16[16,3,1536]{2,1,0:T(4,128)(2,1)} %reshape.569), calls=%async_computation.1 | async-start | bytes 393216 | tf_op jit(solution)/shard_map/all_to_all | solution.py:437
  128.4 29.2 %collective-permute-start.22 = (bf16[2,128,1536]{2,1,0:T(8,128)(2,1)}, bf16[2,128,1536]{2,1,0:T(8,128)(2,1)}, u32[]{:S(2)}, u32[]{:S(2)}) collective-permute-start(bf16[2,128,1536]{2,1,0:T(8,128)(2,1)} %bitcast.210), channel_id=1, source_target_pairs={{0,4},{1,5},{2,6},{3,7},{4,8},{5,9},{6,10},{7,11},{8,12},{9,13},{1... | collective-permute-start | bytes 2359304 | tf_op jit(solution)/shard_map/ppermute | solution.py:34
  129.8 27.8 %collective-permute-start.23 = (bf16[2,128,1536]{2,1,0:T(8,128)(2,1)}, bf16[2,128,1536]{2,1,0:T(8,128)(2,1)}, u32[]{:S(2)}, u32[]{:S(2)}) collective-permute-start(bf16[2,128,1536]{2,1,0:T(8,128)(2,1)} %bitcast.209), channel_id=1, source_target_pairs={{0,12},{1,13},{2,14},{3,15},{4,0},{5,1},{6,2},{7,3},{8,4},{9,5},{1... | collective-permute-start | bytes 2359304 | tf_op jit(solution)/shard_map/ppermute | solution.py:34
  138.0 13.7 %all-to-all-start.2 = ((bf16[8,3,192]{2,1,0:T(4,128)(2,1)}), bf16[8,3,192]{2,1,0:T(4,128)(2,1)S(1)}, u32[]{:S(2)}, u32[]{:S(2)}) async-start(bf16[8,3,192]{2,1,0:T(4,128)(2,1)} %bitcast.190), calls=%async_computation.2 | async-start | bytes 32768 | tf_op jit(solution)/shard_map/all_to_all | solution.py:443
  147.0 40.4 %collective-permute-start.20 = (bf16[2,128,1536]{2,1,0:T(8,128)(2,1)}, bf16[2,128,1536]{2,1,0:T(8,128)(2,1)}, u32[]{:S(2)}, u32[]{:S(2)}) collective-permute-start(bf16[2,128,1536]{2,1,0:T(8,128)(2,1)} %bitcast.208), channel_id=1, source_target_pairs={{0,12},{1,13},{2,14},{3,15},{4,0},{5,1},{6,2},{7,3},{8,4},{9,5},{1... | collective-permute-start | bytes 2359304 | tf_op jit(solution)/shard_map/ppermute | solution.py:34
  147.0 40.3 %collective-permute-start.21 = (bf16[2,128,1536]{2,1,0:T(8,128)(2,1)}, bf16[2,128,1536]{2,1,0:T(8,128)(2,1)}, u32[]{:S(2)}, u32[]{:S(2)}) collective-permute-start(bf16[2,128,1536]{2,1,0:T(8,128)(2,1)} %bitcast.207), channel_id=1, source_target_pairs={{0,4},{1,5},{2,6},{3,7},{4,8},{5,9},{6,10},{7,11},{8,12},{9,13},{1... | collective-permute-start | bytes 2359304 | tf_op jit(solution)/shard_map/ppermute | solution.py:34
  152.4 16.4 %all-to-all-start.3 = ((bf16[128,3,192]{2,1,0:T(4,128)(2,1)}), bf16[128,3,192]{2,1,0:T(4,128)(2,1)}, u32[]{:S(2)}, u32[]{:S(2)}) async-start(bf16[128,3,192]{2,1,0:T(4,128)(2,1)} %broadcast_in_dim.276), calls=%async_computation.3 | async-start | bytes 524288 | tf_op jit(solution)/shard_map/all_to_all | solution.py:445
  159.8 27.5 %collective-permute-start.25 = (bf16[2,128,1536]{2,1,0:T(8,128)(2,1)}, bf16[2,128,1536]{2,1,0:T(8,128)(2,1)}, u32[]{:S(2)}, u32[]{:S(2)}) collective-permute-start(bf16[2,128,1536]{2,1,0:T(8,128)(2,1)} %add_convert_fusion.1), channel_id=1, source_target_pairs={{0,4},{1,5},{2,6},{3,7},{4,8},{5,9},{6,10},{7,11},{8,12},{9,13},{1... | collective-permute-start | bytes 2359304 | tf_op jit(solution)/shard_map/ppermute | solution.py:34
  163.5 23.9 %collective-permute-start.24 = (bf16[2,128,1536]{2,1,0:T(8,128)(2,1)}, bf16[2,128,1536]{2,1,0:T(8,128)(2,1)S(1)}, u32[]{:S(2)}, u32[]{:S(2)}) collective-permute-start(bf16[2,128,1536]{2,1,0:T(8,128)(2,1)} %add_convert_fusion.2), channel_id=1, source_target_pairs={{0,12},{1,13},{2,14},{3,15},{4,0},{5,1},{6,2},{7,3},{8,4},{9,5},{1... | collective-permute-start | bytes 2359304 | tf_op jit(solution)/shard_map/ppermute | solution.py:34
  189.1 7.0 %collective-permute-start.27 = (bf16[128,1536]{1,0:T(8,128)(2,1)S(1)}, bf16[128,1536]{1,0:T(8,128)(2,1)S(1)}, u32[]{:S(2)}, u32[]{:S(2)}) collective-permute-start(bf16[128,1536]{1,0:T(8,128)(2,1)S(1)} %fusion.9), channel_id=1, source_target_pairs={{0,3},{1,0},{2,1},{3,2},{4,7},{5,4},{6,5},{7,6},{8,11},{9,8},{10,9... | collective-permute-start | bytes 1179656 | tf_op jit(solution)/shard_map/ppermute | solution.py:34
  191.1 12.4 %collective-permute-start.26 = (bf16[128,1536]{1,0:T(8,128)(2,1)S(1)}, bf16[128,1536]{1,0:T(8,128)(2,1)S(1)}, u32[]{:S(2)}, u32[]{:S(2)}) collective-permute-start(bf16[128,1536]{1,0:T(8,128)(2,1)S(1)} %get-tuple-element.115), channel_id=1, source_target_pairs={{0,1},{1,2},{2,3},{3,0},{4,5},{5,6},{6,7},{7,4},{8,9},{9,10},{10,1... | collective-permute-start | bytes 1179656 | tf_op jit(solution)/shard_map/ppermute | solution.py:34
  192.2 11.3 %collective-permute-start.28 = (bf16[128,1536]{1,0:T(8,128)(2,1)S(1)}, bf16[128,1536]{1,0:T(8,128)(2,1)S(1)}, u32[]{:S(2)}, u32[]{:S(2)}) collective-permute-start(bf16[128,1536]{1,0:T(8,128)(2,1)S(1)} %get-tuple-element.114), channel_id=1, source_target_pairs={{0,2},{1,3},{2,0},{3,1},{4,6},{5,7},{6,4},{7,5},{8,10},{9,11},{10,... | collective-permute-start | bytes 1179656 | tf_op jit(solution)/shard_map/ppermute | solution.py:34
  (35 other events, 277.8 us)

commit v10 on v9

--- a/solution.py
+++ b/solution.py
@@ -402,7 +402,8 @@
 
     line = lax.optimization_barrier(
         [shift(moe_in, 0, 1), shift(moe_in, 0, -1), shift(moe_in, 0, 2)])
-    own_lo, own_hi = jnp.stack([moe_in, line[0]]), jnp.stack([line[1], line[2]])
+    own_lo = jnp.concatenate([moe_in, line[0]])
+    own_hi = jnp.concatenate([line[1], line[2]])
     minus_lo, plus_hi = shift(own_lo, 1, 1), shift(own_hi, 1, -1)
     minus_hi, plus_lo = shift(own_hi, 1, 1), shift(own_lo, 1, -1)
     own_lo, own_hi, last_own = share([own_lo, own_hi], 0)
@@ -426,9 +427,9 @@
     own_lo = wide(own_lo) + wide(plus_lo) + wide(minus_lo)
     own_hi = wide(own_hi) + wide(plus_hi) + wide(minus_hi)
     line = lax.optimization_barrier(
-        [shift(own_hi[0].astype(BF), 0, 1), shift(own_lo[1].astype(BF), 0, -1),
-         shift(own_hi[1].astype(BF), 0, 2)])
-    combined = own_lo[0] + wide(line[0]) + wide(line[1]) + wide(line[2])
+        [shift(own_hi[:count].astype(BF), 0, 1), shift(own_lo[count:].astype(BF), 0, -1),
+         shift(own_hi[count:].astype(BF), 0, 2)])
+    combined = own_lo[:count] + wide(line[0]) + wide(line[1]) + wide(line[2])
     hidden_out = (mixed.astype(F32) + combined).astype(BF)
 
     last = jnp.concatenate([piece.reshape(16, width) for piece in (

time: 206 us -> 205 us (level)
    unnamed x70 -> x72, local copies, waits for them, and re-layouts: 11.2 us -> 12.2 us
where the time goes in v10:
time: 205 us; the launch traced here: 203 us
  starting transfers between devices  64.4 us (31%)
  Pallas kernels  39.2 us (19%)
  waiting for transfers between devices  35.2 us (17%)
  local copies, waits for them, and re-layouts  23.1 us (11%)
  other arithmetic  16.1 us (8%)
  blocking collectives  14.7 us (7%)
  between operations  7.17 us (3%)
  matrix products  3.6 us (2%)
    ppermute x18, starting transfers between devices, shift(): return lax.ppermute(rows, WHOLE, pairs)  21.5 us
    pallas_call x1, Pallas kernels, attention(): pl.pallas_call(attention_kernel, out_shape=(rows, rows), in_specs=[vm] *...  20 us
    pallas_call x4, Pallas kernels, experts(): pl.pallas_call(expert_kernel, out_shape=(piece, piece, jax.ShapeDtypeStru...  19.1 us
    ppermute x18, waiting for transfers between devices, shift(): return lax.ppermute(rows, WHOLE, pairs)  17.8 us
    all_to_all x1, blocking collectives, body(): lax.all_to_all(jnp.broadcast_to(stats[None], (128, 128)), WHOLE, 0, 0, ti...  14.7 us
    unnamed x72, local copies, waits for them, and re-layouts  12.2 us
    all_to_all x1, starting transfers between devices, body(): mine = lax.all_to_all(split, 'seq', 0, 0, tiled=True)  9.02 us
    all_to_all x1, starting transfers between devices, body(): held = lax.all_to_all(payload, 'grp', 0, 0, tiled=True)  7.78 us
  transfers between devices with their start and end apart: 33, of which 14 were waited for; matrix products, arithmetic and copies ran while one was open for 11% of the time, Pallas kernels for 7%

profile of v10, /device:TPU:1, one launch (start us, length us, event | category | flops | bytes accessed | tf_op | source)
XLA Modules:
  0.0 203.4 jit_solution(12148559753221709310)
XLA Ops:
  6.0 4.1 %collective-permute-start = (bf16[128,1536]{1,0:T(8,128)(2,1)S(1)}, bf16[128,1536]{1,0:T(8,128)(2,1)S(1)}, u32[]{:S(2)}, u32[]{:S(2)}) collective-permute-start(bf16[128,1536]{1,0:T(8,128)(2,1)S(1)} %bitcast.167), channel_id=1, source_target_pairs={{0,32},{16,48},{32,64},{48,80},{64,96},{80,112},{1,33},{17,49},{33... | collective-permute-start | bytes 1179656 | tf_op jit(solution)/shard_map/ppermute | solution.py:334
  10.1 4.4 %collective-permute-start.1 = (bf16[128,1536]{1,0:T(8,128)(2,1)S(1)}, bf16[128,1536]{1,0:T(8,128)(2,1)S(1)}, u32[]{:S(2)}, u32[]{:S(2)}) collective-permute-start(bf16[128,1536]{1,0:T(8,128)(2,1)S(1)} %bitcast.168), channel_id=1, source_target_pairs={{0,64},{16,80},{32,96},{48,112},{1,65},{17,81},{33,97},{49,113},{2... | collective-permute-start | bytes 1179656 | tf_op jit(solution)/shard_map/ppermute | solution.py:335
  14.5 7.8 %all-to-all-start = ((bf16[16,16,1536]{2,1,0:T(8,128)(2,1)}), bf16[16,16,1536]{2,1,0:T(8,128)(2,1)S(1)}, u32[]{:S(2)}, u32[]{:S(2)}) async-start(bf16[16,16,1536]{2,1,0:T(8,128)(2,1)} %pad_maximum_fusion), calls=%async_computation | async-start | bytes 1572864 | tf_op jit(solution)/shard_map/all_to_all | solution.py:333
  37.4 2.7 %collective-permute-start.5 = (bf16[48,1536]{1,0:T(8,128)(2,1)S(1)}, bf16[48,1536]{1,0:T(8,128)(2,1)S(1)}, u32[]{:S(2)}, u32[]{:S(2)}) collective-permute-start(bf16[48,1536]{1,0:T(8,128)(2,1)S(1)} %bitcast.173), channel_id=1, source_target_pairs={{0,96},{16,112},{32,0},{48,16},{64,32},{80,48},{96,64},{112,80},{1... | collective-permute-start | bytes 442376 | tf_op jit(solution)/shard_map/ppermute | solution.py:369
  40.9 2.2 %collective-permute-done.4.refs_6_ = bf16[48,1536]{1,0:T(8,128)(2,1)S(1)} collective-permute-done((bf16[48,1536]{1,0:T(8,128)(2,1)S(1)}, bf16[48,1536]{1,0:T(8,128)(2,1)S(1)}, u32[]{:S(2)}, u32[]{:S(2)}) %collective-permute-start.4) | collective-permute-done | bytes 147488 | tf_op jit(solution)/shard_map/ppermute | solution.py:369
  43.8 1.8 collective-permute-done.6.refs_8_
  45.6 2.4 %collective-permute-start.10 = (bf16[48,1536]{1,0:T(8,128)(2,1)S(1)}, bf16[48,1536]{1,0:T(8,128)(2,1)S(1)}, u32[]{:S(2)}, u32[]{:S(2)}) collective-permute-start(bf16[48,1536]{1,0:T(8,128)(2,1)S(1)} %collective-permute-done.6.refs_8_), channel_id=1, source_target_pairs={{0,16},{16,0},{32,48},{48,32},{64,80},{80,64},{96,112},{112,96},{1... | collective-permute-start | bytes 442376 | tf_op jit(solution)/shard_map/ppermute | solution.py:38
  50.8 20.0 %attention_block.1 = (bf16[128,1536]{1,0:T(8,128)(2,1)}, bf16[128,1536]{1,0:T(8,128)(2,1)}) custom-call(bf16[128,1536]{1,0:T(8,128)(2,1)} %bitcast.166, bf16[128,1536]{1,0:T(8,128)(2,1)} %copy-done.12, bf16[128,1536]{1,0:T(8,128)(2,1)} %copy-done.13, bf16[128,1536]{1,0:T(8,128)(2,1)} %copy-done.25, bf16[128,1536]{1,0:T(8,128)(2,1)} %collective-permute-done.3.refs_4_, ...), custom_call_target="tpu_custom_call" | custom-call | flops 8589934592 | bytes 20971520 | tf_op jit(solution)/shard_map/attention_block/pallas_call | solution.py:192
  70.8 1.9 collective-permute-start.11
  76.8 2.8 %collective-permute-done.11 = bf16[128,1536]{1,0:T(8,128)(2,1)S(1)} collective-permute-done((bf16[128,1536]{1,0:T(8,128)(2,1)}, bf16[128,1536]{1,0:T(8,128)(2,1)S(1)}, u32[]{:S(2)}, u32[]{:S(2)}) %collective-permute-start.11) | collective-permute-done | bytes 393248 | tf_op jit(solution)/shard_map/ppermute | solution.py:34
  79.8 5.1 %collective-permute-done.13 = bf16[128,1536]{1,0:T(8,128)(2,1)S(1)} collective-permute-done((bf16[128,1536]{1,0:T(8,128)(2,1)}, bf16[128,1536]{1,0:T(8,128)(2,1)S(1)}, u32[]{:S(2)}, u32[]{:S(2)}) %collective-permute-start.13) | collective-permute-done | bytes 393248 | tf_op jit(solution)/shard_map/ppermute | solution.py:34
  86.0 1.9 collective-permute-start.15
  89.4 2.1 %copy-done.2 = bf16[5,1536,256]{2,1,0:T(8,128)(2,1)S(1)} copy-done((bf16[5,1536,256]{2,1,0:T(8,128)(2,1)S(1)}, bf16[5,1536,256]{2,1,0:T(8,128)(2,1)}, u32[]{:S(2)}) %copy-start.2) | copy-done | bytes 3932184
  91.5 2.1 %copy-done.4 = bf16[5,1536,256]{2,1,0:T(8,128)(2,1)S(1)} copy-done((bf16[5,1536,256]{2,1,0:T(8,128)(2,1)S(1)}, bf16[5,1536,256]{2,1,0:T(8,128)(2,1)}, u32[]{:S(2)}) %copy-start.4) | copy-done | bytes 3932184
  93.7 2.1 %copy-done.5 = bf16[5,256,1536]{2,1,0:T(8,128)(2,1)S(1)} copy-done((bf16[5,256,1536]{2,1,0:T(8,128)(2,1)S(1)}, bf16[5,256,1536]{2,1,0:T(8,128)(2,1)}, u32[]{:S(2)}) %copy-start.5) | copy-done | bytes 3932184
  95.8 4.8 %expert_block.4 = (bf16[256,1536]{1,0:T(8,128)(2,1)S(1)}, bf16[256,1536]{1,0:T(8,128)(2,1)S(1)}, bf16[2,8,1536]{2,1,0:T(8,128)(2,1)S(1)}) custom-call(bf16[256,1536]{1,0:T(8,128)(2,1)S(1)} %constant_dynamic-update-slice_fusion.p0, bf16[256,1536]{1,0:T(8,128)(2,1)S(1)} %constant_dynamic-update-slice_fusion.2.p1, s32[2]{0:T(128)S(1)} %get-tuple-element.152.first, ...), custom_call_target="tpu_custom_call" | custom-call | flops 7516192768 | bytes 12582912 | tf_op jit(solution)/shard_map/expert_block/pallas_call | solution.py:275
  100.6 2.7 %collective-permute-start.19 = (bf16[256,1536]{1,0:T(8,128)(2,1)S(1)}, bf16[256,1536]{1,0:T(8,128)(2,1)S(1)}, u32[]{:S(2)}, u32[]{:S(2)}) collective-permute-start(bf16[256,1536]{1,0:T(8,128)(2,1)S(1)} %collective-permute-done.15.p1), channel_id=1, source_target_pairs={{0,12},{1,13},{2,14},{3,15},{4,0},{5,1},{6,2},{7,3},{8,4},{9,5},{1... | collective-permute-start | bytes 2359304 | tf_op jit(solution)/shard_map/ppermute | solution.py:34
  103.3 4.8 %expert_block.5 = (bf16[256,1536]{1,0:T(8,128)(2,1)S(1)}, bf16[256,1536]{1,0:T(8,128)(2,1)S(1)}, bf16[2,8,1536]{2,1,0:T(8,128)(2,1)S(1)}) custom-call(bf16[256,1536]{1,0:T(8,128)(2,1)S(1)} %collective-permute-done.14.p0, bf16[256,1536]{1,0:T(8,128)(2,1)S(1)} %collective-permute-done.15.p1, s32[2]{0:T(128)S(1)} %get-tuple-element.153.first, ...), custom_call_target="tpu_custom_call" | custom-call | flops 7516192768 | bytes 12582912 | tf_op jit(solution)/shard_map/expert_block/pallas_call | solution.py:275
  109.9 4.8 %expert_block.6 = (bf16[256,1536]{1,0:T(8,128)(2,1)S(1)}, bf16[256,1536]{1,0:T(8,128)(2,1)S(1)}, bf16[2,8,1536]{2,1,0:T(8,128)(2,1)S(1)}) custom-call(bf16[256,1536]{1,0:T(8,128)(2,1)S(1)} %collective-permute-done.16.p0, bf16[256,1536]{1,0:T(8,128)(2,1)S(1)} %collective-permute-done.17.p1, s32[2]{0:T(128)S(1)} %get-tuple-element.154.first, ...), custom_call_target="tpu_custom_call" | custom-call | flops 7516192768 | bytes 12582912 | tf_op jit(solution)/shard_map/expert_block/pallas_call | solution.py:275
  114.7 4.8 %expert_block.7 = (bf16[256,1536]{1,0:T(8,128)(2,1)S(1)}, bf16[256,1536]{1,0:T(8,128)(2,1)S(1)}, bf16[2,8,1536]{2,1,0:T(8,128)(2,1)S(1)}) custom-call(bf16[256,1536]{1,0:T(8,128)(2,1)S(1)} %collective-permute-done.18.p0, bf16[256,1536]{1,0:T(8,128)(2,1)S(1)} %collective-permute-done.19.p1, s32[2]{0:T(128)S(1)} %get-tuple-element.155.first, ...), custom_call_target="tpu_custom_call" | custom-call | flops 7516192768 | bytes 12582912 | tf_op jit(solution)/shard_map/expert_block/pallas_call | solution.py:275
  122.3 5.0 %all-to-all-start.1 = ((bf16[16,3,1536]{2,1,0:T(4,128)(2,1)}), bf16[16,3,1536]{2,1,0:T(4,128)(2,1)S(1)}, u32[]{:S(2)}, u32[]{:S(2)}) async-start(bf16[16,3,1536]{2,1,0:T(4,128)(2,1)} %reshape.502), calls=%async_computation.1 | async-start | bytes 393216 | tf_op jit(solution)/shard_map/all_to_all | solution.py:438
  130.1 4.6 %all-to-all-done.1 = bf16[16,3,1536]{2,1,0:T(4,128)(2,1)S(1)} async-done(((bf16[16,3,1536]{2,1,0:T(4,128)(2,1)}), bf16[16,3,1536]{2,1,0:T(4,128)(2,1)S(1)}, u32[]{:S(2)}, u32[]{:S(2)}) %all-to-all-start.1) | async-done | bytes 147488 | tf_op jit(solution)/shard_map/all_to_all | solution.py:438
  136.9 9.0 %all-to-all-start.2 = ((bf16[8,3,192]{2,1,0:T(4,128)(2,1)}), bf16[8,3,192]{2,1,0:T(4,128)(2,1)S(1)}, u32[]{:S(2)}, u32[]{:S(2)}) async-start(bf16[8,3,192]{2,1,0:T(4,128)(2,1)} %bitcast.150), calls=%async_computation.2 | async-start | bytes 32768 | tf_op jit(solution)/shard_map/all_to_all | solution.py:444
  147.3 3.2 %all-to-all-done.2 = bf16[8,3,192]{2,1,0:T(4,128)(2,1)S(1)} async-done(((bf16[8,3,192]{2,1,0:T(4,128)(2,1)}), bf16[8,3,192]{2,1,0:T(4,128)(2,1)S(1)}, u32[]{:S(2)}, u32[]{:S(2)}) %all-to-all-start.2) | async-done | bytes 9248 | tf_op jit(solution)/shard_map/all_to_all | solution.py:444
  151.3 5.1 %all-to-all-start.3 = ((bf16[128,3,192]{2,1,0:T(4,128)(2,1)}), bf16[128,3,192]{2,1,0:T(4,128)(2,1)}, u32[]{:S(2)}, u32[]{:S(2)}) async-start(bf16[128,3,192]{2,1,0:T(4,128)(2,1)} %broadcast_in_dim.276), calls=%async_computation.3 | async-start | bytes 524288 | tf_op jit(solution)/shard_map/all_to_all | solution.py:446
  156.5 2.2 %add_convert_fusion.1 = bf16[256,1536]{1,0:T(8,128)(2,1)} fusion(bf16[256,1536]{1,0:T(8,128)(2,1)} %collective-permute-done.22, bf16[256,1536]{1,0:T(8,128)(2,1)S(1)} %get-tuple-element.95), kind=kLoop, calls=%fused_computation.8 | loop fusion | flops 1572864 | bytes 2359296 | tf_op jit(solution)/shard_map/convert_element_type | solution.py:423
  160.2 2.2 %add_convert_fusion.2 = bf16[256,1536]{1,0:T(8,128)(2,1)} fusion(bf16[256,1536]{1,0:T(8,128)(2,1)} %collective-permute-done.23, bf16[256,1536]{1,0:T(8,128)(2,1)S(1)} %get-tuple-element.89), kind=kLoop, calls=%fused_computation.9 | loop fusion | flops 1572864 | bytes 2359296 | tf_op jit(solution)/shard_map/convert_element_type | solution.py:424
  163.7 4.0 %all-to-all-done.3 = bf16[128,3,192]{2,1,0:T(4,128)(2,1)} async-done(((bf16[128,3,192]{2,1,0:T(4,128)(2,1)}), bf16[128,3,192]{2,1,0:T(4,128)(2,1)}, u32[]{:S(2)}, u32[]{:S(2)}) %all-to-all-start.3) | async-done | bytes 147488 | tf_op jit(solution)/shard_map/all_to_all | solution.py:446
  169.1 1.7 fusion.51
  171.1 14.7 %all_to_all.29 = f32[128,1,128]{2,1,0:T(1,128)S(1)} all-to-all(f32[128,1,128]{2,1,0:T(1,128)S(1)} %broadcast_in_dim.278), channel_id=1, replica_groups=mesh['seq'=8,'grp'=16] {'seq','grp'}, dimensions={0} | all-to-all | bytes 131072 | tf_op jit(solution)/shard_map/all_to_all | solution.py:453
  192.8 2.2 %collective-permute-done.27 = bf16[128,1536]{1,0:T(8,128)(2,1)S(1)} collective-permute-done((bf16[128,1536]{1,0:T(8,128)(2,1)S(1)}, bf16[128,1536]{1,0:T(8,128)(2,1)S(1)}, u32[]{:S(2)}, u32[]{:S(2)}) %collective-permute-start.27) | collective-permute-done | bytes 393248 | tf_op jit(solution)/shard_map/ppermute | solution.py:34
  195.0 7.4 %collective-permute-done.26 = bf16[128,1536]{1,0:T(8,128)(2,1)S(1)} collective-permute-done((bf16[128,1536]{1,0:T(8,128)(2,1)S(1)}, bf16[128,1536]{1,0:T(8,128)(2,1)S(1)}, u32[]{:S(2)}, u32[]{:S(2)}) %collective-permute-start.26) | collective-permute-done | bytes 393248 | tf_op jit(solution)/shard_map/ppermute | solution.py:34
  (229 shorter events, 49.7 us)
Async XLA Ops:
  6.0 28.9 %collective-permute-start = (bf16[128,1536]{1,0:T(8,128)(2,1)S(1)}, bf16[128,1536]{1,0:T(8,128)(2,1)S(1)}, u32[]{:S(2)}, u32[]{:S(2)}) collective-permute-start(bf16[128,1536]{1,0:T(8,128)(2,1)S(1)} %bitcast.167), channel_id=1, source_target_pairs={{0,32},{16,48},{32,64},{48,80},{64,96},{80,112},{1,33},{17,49},{33... | collective-permute-start | bytes 1179656 | tf_op jit(solution)/shard_map/ppermute | solution.py:334
  10.1 24.9 %collective-permute-start.1 = (bf16[128,1536]{1,0:T(8,128)(2,1)S(1)}, bf16[128,1536]{1,0:T(8,128)(2,1)S(1)}, u32[]{:S(2)}, u32[]{:S(2)}) collective-permute-start(bf16[128,1536]{1,0:T(8,128)(2,1)S(1)} %bitcast.168), channel_id=1, source_target_pairs={{0,64},{16,80},{32,96},{48,112},{1,65},{17,81},{33,97},{49,113},{2... | collective-permute-start | bytes 1179656 | tf_op jit(solution)/shard_map/ppermute | solution.py:335
  14.5 22.2 %all-to-all-start = ((bf16[16,16,1536]{2,1,0:T(8,128)(2,1)}), bf16[16,16,1536]{2,1,0:T(8,128)(2,1)S(1)}, u32[]{:S(2)}, u32[]{:S(2)}) async-start(bf16[16,16,1536]{2,1,0:T(8,128)(2,1)} %pad_maximum_fusion), calls=%async_computation | async-start | bytes 1572864 | tf_op jit(solution)/shard_map/all_to_all | solution.py:333
  35.0 13.6 %collective-permute-start.2 = (bf16[128,1536]{1,0:T(8,128)(2,1)S(1)}, bf16[128,1536]{1,0:T(8,128)(2,1)S(1)}, u32[]{:S(2)}, u32[]{:S(2)}) collective-permute-start(bf16[128,1536]{1,0:T(8,128)(2,1)S(1)} %get-tuple-element.120), channel_id=1, source_target_pairs={{0,16},{16,0},{32,48},{48,32},{64,80},{80,64},{96,112},{112,96},{1... | collective-permute-start | bytes 1179656 | tf_op jit(solution)/shard_map/ppermute | solution.py:38
  36.6 12.1 %collective-permute-start.3 = (bf16[128,1536]{1,0:T(8,128)(2,1)S(1)}, bf16[128,1536]{1,0:T(8,128)(2,1)}, u32[]{:S(2)}, u32[]{:S(2)}) collective-permute-start(bf16[128,1536]{1,0:T(8,128)(2,1)S(1)} %get-tuple-element.119), channel_id=1, source_target_pairs={{0,16},{16,0},{32,48},{48,32},{64,80},{80,64},{96,112},{112,96},{1... | collective-permute-start | bytes 1179656 | tf_op jit(solution)/shard_map/ppermute | solution.py:38
  37.3 5.8 %collective-permute-start.4 = (bf16[48,1536]{1,0:T(8,128)(2,1)S(1)}, bf16[48,1536]{1,0:T(8,128)(2,1)S(1)}, u32[]{:S(2)}, u32[]{:S(2)}) collective-permute-start(bf16[48,1536]{1,0:T(8,128)(2,1)S(1)} %bitcast.172), channel_id=1, source_target_pairs={{0,32},{16,48},{32,64},{48,80},{64,96},{80,112},{96,0},{112,16},{1... | collective-permute-start | bytes 442376 | tf_op jit(solution)/shard_map/ppermute | solution.py:369
  37.4 6.5 %collective-permute-start.5 = (bf16[48,1536]{1,0:T(8,128)(2,1)S(1)}, bf16[48,1536]{1,0:T(8,128)(2,1)S(1)}, u32[]{:S(2)}, u32[]{:S(2)}) collective-permute-start(bf16[48,1536]{1,0:T(8,128)(2,1)S(1)} %bitcast.173), channel_id=1, source_target_pairs={{0,96},{16,112},{32,0},{48,16},{64,32},{80,48},{96,64},{112,80},{1... | collective-permute-start | bytes 442376 | tf_op jit(solution)/shard_map/ppermute | solution.py:369
  40.0 5.6 %collective-permute-start.6 = (bf16[48,1536]{1,0:T(8,128)(2,1)S(1)}, bf16[48,1536]{1,0:T(8,128)(2,1)S(1)}, u32[]{:S(2)}, u32[]{:S(2)}) collective-permute-start(bf16[48,1536]{1,0:T(8,128)(2,1)S(1)} %bitcast.174), channel_id=1, source_target_pairs={{0,64},{16,80},{32,96},{48,112},{64,0},{80,16},{96,32},{112,48},{1... | collective-permute-start | bytes 442376 | tf_op jit(solution)/shard_map/ppermute | solution.py:369
  45.6 3.5 %collective-permute-start.10 = (bf16[48,1536]{1,0:T(8,128)(2,1)S(1)}, bf16[48,1536]{1,0:T(8,128)(2,1)S(1)}, u32[]{:S(2)}, u32[]{:S(2)}) collective-permute-start(bf16[48,1536]{1,0:T(8,128)(2,1)S(1)} %collective-permute-done.6.refs_8_), channel_id=1, source_target_pairs={{0,16},{16,0},{32,48},{48,32},{64,80},{80,64},{96,112},{112,96},{1... | collective-permute-start | bytes 442376 | tf_op jit(solution)/shard_map/ppermute | solution.py:38
  48.1 1.6 collective-permute-start.8
  48.6 2.2 %collective-permute-start.9 = (bf16[48,1536]{1,0:T(8,128)(2,1)S(1)}, bf16[48,1536]{1,0:T(8,128)(2,1)}, u32[]{:S(2)}, u32[]{:S(2)}) collective-permute-start(bf16[48,1536]{1,0:T(8,128)(2,1)S(1)} %collective-permute-done.5.refs_7_), channel_id=1, source_target_pairs={{0,16},{16,0},{32,48},{48,32},{64,80},{80,64},{96,112},{112,96},{1... | collective-permute-start | bytes 442376 | tf_op jit(solution)/shard_map/ppermute | solution.py:38
  70.8 8.8 %collective-permute-start.11 = (bf16[128,1536]{1,0:T(8,128)(2,1)}, bf16[128,1536]{1,0:T(8,128)(2,1)S(1)}, u32[]{:S(2)}, u32[]{:S(2)}) collective-permute-start(bf16[128,1536]{1,0:T(8,128)(2,1)} %get-tuple-element.69), channel_id=1, source_target_pairs={{0,1},{1,2},{2,3},{3,0},{4,5},{5,6},{6,7},{7,4},{8,9},{9,10},{10,1... | collective-permute-start | bytes 1179656 | tf_op jit(solution)/shard_map/ppermute | solution.py:34
  72.7 7.1 %collective-permute-start.12 = (bf16[128,1536]{1,0:T(8,128)(2,1)}, bf16[128,1536]{1,0:T(8,128)(2,1)S(1)}, u32[]{:S(2)}, u32[]{:S(2)}) collective-permute-start(bf16[128,1536]{1,0:T(8,128)(2,1)} %get-tuple-element.69), channel_id=1, source_target_pairs={{0,3},{1,0},{2,1},{3,2},{4,7},{5,4},{6,5},{7,6},{8,11},{9,8},{10,9... | collective-permute-start | bytes 1179656 | tf_op jit(solution)/shard_map/ppermute | solution.py:34
  74.0 11.0 %collective-permute-start.13 = (bf16[128,1536]{1,0:T(8,128)(2,1)}, bf16[128,1536]{1,0:T(8,128)(2,1)S(1)}, u32[]{:S(2)}, u32[]{:S(2)}) collective-permute-start(bf16[128,1536]{1,0:T(8,128)(2,1)} %get-tuple-element.69), channel_id=1, source_target_pairs={{0,2},{1,3},{2,0},{3,1},{4,6},{5,7},{6,4},{7,5},{8,10},{9,11},{10,... | collective-permute-start | bytes 1179656 | tf_op jit(solution)/shard_map/ppermute | solution.py:34
  85.0 15.5 %collective-permute-start.14 = (bf16[256,1536]{1,0:T(8,128)(2,1)S(1)}, bf16[256,1536]{1,0:T(8,128)(2,1)S(1)}, u32[]{:S(2)}, u32[]{:S(2)}) collective-permute-start(bf16[256,1536]{1,0:T(8,128)(2,1)S(1)} %constant_dynamic-update-slice_fusion.p0), channel_id=1, source_target_pairs={{0,4},{1,5},{2,6},{3,7},{4,8},{5,9},{6,10},{7,11},{8,12},{9,13},{1... | collective-permute-start | bytes 2359304 | tf_op jit(solution)/shard_map/ppermute | solution.py:34
  86.0 14.5 %collective-permute-start.15 = (bf16[256,1536]{1,0:T(8,128)(2,1)S(1)}, bf16[256,1536]{1,0:T(8,128)(2,1)S(1)}, u32[]{:S(2)}, u32[]{:S(2)}) collective-permute-start(bf16[256,1536]{1,0:T(8,128)(2,1)S(1)} %constant_dynamic-update-slice_fusion.2.p1), channel_id=1, source_target_pairs={{0,12},{1,13},{2,14},{3,15},{4,0},{5,1},{6,2},{7,3},{8,4},{9,5},{1... | collective-permute-start | bytes 2359304 | tf_op jit(solution)/shard_map/ppermute | solution.py:34
  88.0 21.9 %collective-permute-start.17 = (bf16[256,1536]{1,0:T(8,128)(2,1)S(1)}, bf16[256,1536]{1,0:T(8,128)(2,1)S(1)}, u32[]{:S(2)}, u32[]{:S(2)}) collective-permute-start(bf16[256,1536]{1,0:T(8,128)(2,1)S(1)} %constant_dynamic-update-slice_fusion.p0), channel_id=1, source_target_pairs={{0,12},{1,13},{2,14},{3,15},{4,0},{5,1},{6,2},{7,3},{8,4},{9,5},{1... | collective-permute-start | bytes 2359304 | tf_op jit(solution)/shard_map/ppermute | solution.py:34
  89.1 20.8 %collective-permute-start.16 = (bf16[256,1536]{1,0:T(8,128)(2,1)S(1)}, bf16[256,1536]{1,0:T(8,128)(2,1)S(1)}, u32[]{:S(2)}, u32[]{:S(2)}) collective-permute-start(bf16[256,1536]{1,0:T(8,128)(2,1)S(1)} %constant_dynamic-update-slice_fusion.2.p1), channel_id=1, source_target_pairs={{0,4},{1,5},{2,6},{3,7},{4,8},{5,9},{6,10},{7,11},{8,12},{9,13},{1... | collective-permute-start | bytes 2359304 | tf_op jit(solution)/shard_map/ppermute | solution.py:34
  100.6 14.1 %collective-permute-start.18 = (bf16[256,1536]{1,0:T(8,128)(2,1)S(1)}, bf16[256,1536]{1,0:T(8,128)(2,1)S(1)}, u32[]{:S(2)}, u32[]{:S(2)}) collective-permute-start(bf16[256,1536]{1,0:T(8,128)(2,1)S(1)} %collective-permute-done.14.p0), channel_id=1, source_target_pairs={{0,4},{1,5},{2,6},{3,7},{4,8},{5,9},{6,10},{7,11},{8,12},{9,13},{1... | collective-permute-start | bytes 2359304 | tf_op jit(solution)/shard_map/ppermute | solution.py:34
  100.6 14.1 %collective-permute-start.19 = (bf16[256,1536]{1,0:T(8,128)(2,1)S(1)}, bf16[256,1536]{1,0:T(8,128)(2,1)S(1)}, u32[]{:S(2)}, u32[]{:S(2)}) collective-permute-start(bf16[256,1536]{1,0:T(8,128)(2,1)S(1)} %collective-permute-done.15.p1), channel_id=1, source_target_pairs={{0,12},{1,13},{2,14},{3,15},{4,0},{5,1},{6,2},{7,3},{8,4},{9,5},{1... | collective-permute-start | bytes 2359304 | tf_op jit(solution)/shard_map/ppermute | solution.py:34
  122.3 12.3 %all-to-all-start.1 = ((bf16[16,3,1536]{2,1,0:T(4,128)(2,1)}), bf16[16,3,1536]{2,1,0:T(4,128)(2,1)S(1)}, u32[]{:S(2)}, u32[]{:S(2)}) async-start(bf16[16,3,1536]{2,1,0:T(4,128)(2,1)} %reshape.502), calls=%async_computation.1 | async-start | bytes 393216 | tf_op jit(solution)/shard_map/all_to_all | solution.py:438
  127.3 29.2 %collective-permute-start.22 = (bf16[256,1536]{1,0:T(8,128)(2,1)}, bf16[256,1536]{1,0:T(8,128)(2,1)}, u32[]{:S(2)}, u32[]{:S(2)}) collective-permute-start(bf16[256,1536]{1,0:T(8,128)(2,1)} %copy-done.9), channel_id=1, source_target_pairs={{0,4},{1,5},{2,6},{3,7},{4,8},{5,9},{6,10},{7,11},{8,12},{9,13},{1... | collective-permute-start | bytes 2359304 | tf_op jit(solution)/shard_map/ppermute | solution.py:34
  128.7 27.8 %collective-permute-start.23 = (bf16[256,1536]{1,0:T(8,128)(2,1)}, bf16[256,1536]{1,0:T(8,128)(2,1)}, u32[]{:S(2)}, u32[]{:S(2)}) collective-permute-start(bf16[256,1536]{1,0:T(8,128)(2,1)} %copy-done.8), channel_id=1, source_target_pairs={{0,12},{1,13},{2,14},{3,15},{4,0},{5,1},{6,2},{7,3},{8,4},{9,5},{1... | collective-permute-start | bytes 2359304 | tf_op jit(solution)/shard_map/ppermute | solution.py:34
  136.9 13.7 %all-to-all-start.2 = ((bf16[8,3,192]{2,1,0:T(4,128)(2,1)}), bf16[8,3,192]{2,1,0:T(4,128)(2,1)S(1)}, u32[]{:S(2)}, u32[]{:S(2)}) async-start(bf16[8,3,192]{2,1,0:T(4,128)(2,1)} %bitcast.150), calls=%async_computation.2 | async-start | bytes 32768 | tf_op jit(solution)/shard_map/all_to_all | solution.py:444
  145.9 40.4 %collective-permute-start.20 = (bf16[256,1536]{1,0:T(8,128)(2,1)}, bf16[256,1536]{1,0:T(8,128)(2,1)}, u32[]{:S(2)}, u32[]{:S(2)}) collective-permute-start(bf16[256,1536]{1,0:T(8,128)(2,1)} %copy-done.7), channel_id=1, source_target_pairs={{0,12},{1,13},{2,14},{3,15},{4,0},{5,1},{6,2},{7,3},{8,4},{9,5},{1... | collective-permute-start | bytes 2359304 | tf_op jit(solution)/shard_map/ppermute | solution.py:34
  145.9 40.3 %collective-permute-start.21 = (bf16[256,1536]{1,0:T(8,128)(2,1)}, bf16[256,1536]{1,0:T(8,128)(2,1)}, u32[]{:S(2)}, u32[]{:S(2)}) collective-permute-start(bf16[256,1536]{1,0:T(8,128)(2,1)} %copy-done.6), channel_id=1, source_target_pairs={{0,4},{1,5},{2,6},{3,7},{4,8},{5,9},{6,10},{7,11},{8,12},{9,13},{1... | collective-permute-start | bytes 2359304 | tf_op jit(solution)/shard_map/ppermute | solution.py:34
  151.3 16.4 %all-to-all-start.3 = ((bf16[128,3,192]{2,1,0:T(4,128)(2,1)}), bf16[128,3,192]{2,1,0:T(4,128)(2,1)}, u32[]{:S(2)}, u32[]{:S(2)}) async-start(bf16[128,3,192]{2,1,0:T(4,128)(2,1)} %broadcast_in_dim.276), calls=%async_computation.3 | async-start | bytes 524288 | tf_op jit(solution)/shard_map/all_to_all | solution.py:446
  158.7 27.5 %collective-permute-start.25 = (bf16[256,1536]{1,0:T(8,128)(2,1)}, bf16[256,1536]{1,0:T(8,128)(2,1)}, u32[]{:S(2)}, u32[]{:S(2)}) collective-permute-start(bf16[256,1536]{1,0:T(8,128)(2,1)} %add_convert_fusion.1), channel_id=1, source_target_pairs={{0,4},{1,5},{2,6},{3,7},{4,8},{5,9},{6,10},{7,11},{8,12},{9,13},{1... | collective-permute-start | bytes 2359304 | tf_op jit(solution)/shard_map/ppermute | solution.py:34
  162.4 23.9 %collective-permute-start.24 = (bf16[256,1536]{1,0:T(8,128)(2,1)}, bf16[256,1536]{1,0:T(8,128)(2,1)S(1)}, u32[]{:S(2)}, u32[]{:S(2)}) collective-permute-start(bf16[256,1536]{1,0:T(8,128)(2,1)} %add_convert_fusion.2), channel_id=1, source_target_pairs={{0,12},{1,13},{2,14},{3,15},{4,0},{5,1},{6,2},{7,3},{8,4},{9,5},{1... | collective-permute-start | bytes 2359304 | tf_op jit(solution)/shard_map/ppermute | solution.py:34
  188.0 7.0 %collective-permute-start.27 = (bf16[128,1536]{1,0:T(8,128)(2,1)S(1)}, bf16[128,1536]{1,0:T(8,128)(2,1)S(1)}, u32[]{:S(2)}, u32[]{:S(2)}) collective-permute-start(bf16[128,1536]{1,0:T(8,128)(2,1)S(1)} %slice.158), channel_id=1, source_target_pairs={{0,3},{1,0},{2,1},{3,2},{4,7},{5,4},{6,5},{7,6},{8,11},{9,8},{10,9... | collective-permute-start | bytes 1179656 | tf_op jit(solution)/shard_map/ppermute | solution.py:34
  190.0 12.4 %collective-permute-start.26 = (bf16[128,1536]{1,0:T(8,128)(2,1)S(1)}, bf16[128,1536]{1,0:T(8,128)(2,1)S(1)}, u32[]{:S(2)}, u32[]{:S(2)}) collective-permute-start(bf16[128,1536]{1,0:T(8,128)(2,1)S(1)} %get-tuple-element.115), channel_id=1, source_target_pairs={{0,1},{1,2},{2,3},{3,0},{4,5},{5,6},{6,7},{7,4},{8,9},{9,10},{10,1... | collective-permute-start | bytes 1179656 | tf_op jit(solution)/shard_map/ppermute | solution.py:34
  191.1 11.3 %collective-permute-start.28 = (bf16[128,1536]{1,0:T(8,128)(2,1)S(1)}, bf16[128,1536]{1,0:T(8,128)(2,1)S(1)}, u32[]{:S(2)}, u32[]{:S(2)}) collective-permute-start(bf16[128,1536]{1,0:T(8,128)(2,1)S(1)} %get-tuple-element.114), channel_id=1, source_target_pairs={{0,2},{1,3},{2,0},{3,1},{4,6},{5,7},{6,4},{7,5},{8,10},{9,11},{10,... | collective-permute-start | bytes 1179656 | tf_op jit(solution)/shard_map/ppermute | solution.py:34
  (35 other events, 286.2 us)
